TPU v7x, 32 devices: a whole 2x2x4 slice. The times are simulated.
32 devices in a mesh: dp: 4 (over z), blk: 2 (over x), ulys: 4 (over y, core).
Axes of the slice: x: 2, y: 2, z: 4, core: 2. Of those that a mesh axis runs over, the one named last changes fastest.
Arguments:
- hidden: float32 [6144, 768], P(('dp', 'blk', 'ulys')), may hold values from -6 to 6
- time_embed: float32 [4, 768], P('dp'), may hold values from -6 to 6
- segment_ids: int32 [4, 1536], P('dp', 'blk'), may hold values from 0 to 7, never falling along the last dimension, each value on 1 to 384 neighbouring positions
- key_valid: int32 [4, 1536], P('dp', 'blk'), may hold values 0 or 1
- out_grad: float32 [6144, 768], P(('dp', 'blk', 'ulys')), may hold values from -6 to 6
- w_query: float32 [768, 768], P(('blk', 'ulys')), may hold values from -0.21875 to 0.21875
- b_query: float32 [768], P(('blk', 'ulys')), may hold values from -3 to 3
- w_key: float32 [768, 768], P(('blk', 'ulys')), may hold values from -0.21875 to 0.21875
- w_value: float32 [768, 768], P(('blk', 'ulys')), may hold values from -0.21875 to 0.21875
- b_value: float32 [768], P(('blk', 'ulys')), may hold values from -3 to 3
- w_out: float32 [768, 768], P(('blk', 'ulys')), may hold values from -3 to 3
- b_out: float32 [768], P(('blk', 'ulys')), may hold values from -3 to 3
- w_up: float32 [768, 3072], P(('blk', 'ulys')), may hold values from -0.21875 to 0.21875
- b_up: float32 [3072], P(('blk', 'ulys')), may hold values from -3 to 3
- w_down: float32 [3072, 768], P(('blk', 'ulys')), may hold values from -0.109375 to 0.109375
- b_down: float32 [768], P(('blk', 'ulys')), may hold values from -3 to 3
- pre_gain: float32 [768], P(('blk', 'ulys')), may hold values from 0.5 to 1.5
- pre_shift: float32 [768], P(('blk', 'ulys')), may hold values from -3 to 3
- mlp_gain: float32 [768], P(('blk', 'ulys')), may hold values from 0.5 to 1.5
- mlp_shift: float32 [768], P(('blk', 'ulys')), may hold values from -3 to 3
Outputs:
- output: float32 [6144, 768], P(('dp', 'blk', 'ulys'))
- hidden_grad: float32 [6144, 768], P(('dp', 'blk', 'ulys'))
- grad_query: float32 [768, 768], P(('blk', 'ulys'))
- grad_qbias: float32 [768], P(('blk', 'ulys'))
- grad_key: float32 [768, 768], P(('blk', 'ulys'))
- grad_value: float32 [768, 768], P(('blk', 'ulys'))
- grad_vbias: float32 [768], P(('blk', 'ulys'))
- grad_outproj: float32 [768, 768], P(('blk', 'ulys'))
- grad_obias: float32 [768], P(('blk', 'ulys'))
- grad_upproj: float32 [768, 3072], P(('blk', 'ulys'))
- grad_upbias: float32 [3072], P(('blk', 'ulys'))
- grad_downproj: float32 [3072, 768], P(('blk', 'ulys'))
- grad_downbias: float32 [768], P(('blk', 'ulys'))
- prenorm_gain_gradient: float32 [768], P(('blk', 'ulys'))
- prenorm_shift_gradient: float32 [768], P(('blk', 'ulys'))
- grad_mlpgain: float32 [768], P(('blk', 'ulys'))
- grad_mlpshift: float32 [768], P(('blk', 'ulys'))
Inputs may be any that keep to these rules, and one draw needn't show every extreme that they name: `segment_ids`: segment ids never fall along a sequence; a document holds at most 384 tokens, and some document of each sequence holds exactly that many.
All inputs are finite; a program needn't handle non-finite values. No bound on the sum of `key_valid` on one device may be relied on, other than what follows from the above.
Results may differ from a plain program's by a relative error of at most 0.0003.
Values sent between devices are 32-bit elements; how exact they have to be, the bound alone decides.
No kernel may reach another device: no remote copies, remote signals or barrier semaphores. Data moves between devices by JAX's collectives and lax.ppermute only.
A program may use at most 192 MiB of HBM per device.

v0:
```python
import math

import jax
import jax.numpy as jnp
from jax import lax
from jax.sharding import PartitionSpec as P

HEAD_DIM = 64


HIGH = lax.Precision.HIGHEST
floor_score = -1e30


def layer_normalize(values, gain, shift):
    average = jnp.mean(values, axis=-1, keepdims=True)
    centred = values - average
    variance = jnp.mean(centred * centred, axis=-1, keepdims=True)
    return centred * lax.rsqrt(variance + 1e-05) * gain + shift


def gelu_tanh(values):
    return (
        0.5
        * values
        * (1.0 + jnp.tanh(0.7978845608028654 * (values + 0.044715 * values * values * values)))
    )


def matmul(left, right):
    return jnp.dot(left, right, precision=HIGH)


def matmul_left_t(left, right):
    return lax.dot_general(left, right, (((0,), (0,)), ((), ())), precision=HIGH)


def matmul_right_t(left, right):
    return lax.dot_general(left, right, (((1,), (1,)), ((), ())), precision=HIGH)


def local(
    hidden,
    time_embed,
    segment_ids,
    key_valid,
    out_grad,
    w_query,
    b_query,
    w_key,
    w_value,
    b_value,
    w_out,
    b_out,
    w_up,
    b_up,
    w_down,
    b_down,
    pre_gain,
    pre_shift,
    mlp_gain,
    mlp_shift,
):
    (
        full_query,
        full_qbias,
        full_key,
        full_value,
        full_vbias,
        full_out,
        full_obias,
        full_up,
        full_upbias,
        full_down,
        full_downbias,
        complete_prenorm_gain,
        complete_prenorm_shift,
        full_mlpgain,
        full_mlpshift,
    ) = (
        lax.all_gather(w_query, ("blk", "ulys"), axis=0, tiled=True),
        lax.all_gather(b_query, ("blk", "ulys"), axis=0, tiled=True),
        lax.all_gather(w_key, ("blk", "ulys"), axis=0, tiled=True),
        lax.all_gather(w_value, ("blk", "ulys"), axis=0, tiled=True),
        lax.all_gather(b_value, ("blk", "ulys"), axis=0, tiled=True),
        lax.all_gather(w_out, ("blk", "ulys"), axis=0, tiled=True),
        lax.all_gather(b_out, ("blk", "ulys"), axis=0, tiled=True),
        lax.all_gather(w_up, ("blk", "ulys"), axis=0, tiled=True),
        lax.all_gather(b_up, ("blk", "ulys"), axis=0, tiled=True),
        lax.all_gather(w_down, ("blk", "ulys"), axis=0, tiled=True),
        lax.all_gather(b_down, ("blk", "ulys"), axis=0, tiled=True),
        lax.all_gather(pre_gain, ("blk", "ulys"), axis=0, tiled=True),
        lax.all_gather(pre_shift, ("blk", "ulys"), axis=0, tiled=True),
        lax.all_gather(mlp_gain, ("blk", "ulys"), axis=0, tiled=True),
        lax.all_gather(mlp_shift, ("blk", "ulys"), axis=0, tiled=True),
    )
    residual_input = hidden + time_embed
    normalized_rows, prenorm_backward = jax.vjp(
        layer_normalize, residual_input, complete_prenorm_gain, complete_prenorm_shift
    )
    query = matmul(normalized_rows, full_query) + full_qbias
    keys = matmul(normalized_rows, full_key)
    values = matmul(normalized_rows, full_value) + full_vbias
    query_heads, key_heads, value_heads = (
        lax.all_to_all(query, "ulys", split_axis=1, concat_axis=0, tiled=True),
        lax.all_to_all(keys, "ulys", split_axis=1, concat_axis=0, tiled=True),
        lax.all_to_all(values, "ulys", split_axis=1, concat_axis=0, tiled=True),
    )
    group = query_heads.shape[0]
    width = query_heads.shape[1]
    heads_here = width // HEAD_DIM
    blk_count = lax.axis_size("blk")
    blk_here = lax.axis_index("blk")
    length = group * blk_count
    scale = HEAD_DIM ** (-0.5)
    segments_here = segment_ids[0]
    query_codes = segments_here.astype(jnp.float32)
    key_codes = jnp.where(key_valid[0] == 1, segments_here, -1).astype(jnp.float32)
    query_rows = blk_here * group + jnp.arange(group, dtype=jnp.int32)
    query_split = query_heads.reshape(group, heads_here, HEAD_DIM)
    key_value = jnp.concatenate([key_heads, value_heads], axis=1)

    def block_scores(kv_block, code_block, key_rows):
        key_split = kv_block[:, :width].reshape(-1, heads_here, HEAD_DIM)
        value_split = kv_block[:, width:].reshape(-1, heads_here, HEAD_DIM)
        scores = jnp.einsum("qhd,khd->hqk", query_split, key_split, precision=HIGH) * scale
        allowed = (query_codes[:, None] == code_block[None, :]) | (
            query_rows[:, None] == key_rows[None, :]
        )
        return (scores, allowed[None], key_split, value_split)

    def over_blocks(state, piece, update):
        kv_piece, code_piece = piece
        rows = kv_piece.shape[0]
        size = math.gcd(rows, group)
        count = rows // size
        kv_blocks = kv_piece.reshape(count, size, kv_piece.shape[1])
        code_blocks = code_piece.reshape(count, size)
        offsets = jnp.arange(count, dtype=jnp.int32) * size

        def visit(carried, item):
            kv_block, code_block, offset = item
            key_rows = offset + jnp.arange(size, dtype=jnp.int32)
            carried = update(carried, kv_block, code_block, key_rows)
            return (carried, None)

        state, unused = lax.scan(visit, state, (kv_blocks, code_blocks, offsets))
        return state

    def forward_update(state, kv_block, code_block, key_rows):
        running_max, total, accum = state
        scores, allowed, key_split, value_split = block_scores(kv_block, code_block, key_rows)
        masked = jnp.where(allowed, scores, floor_score)
        new_max = jnp.maximum(running_max, jnp.max(masked, axis=2))
        weights = jnp.where(allowed, jnp.exp(masked - new_max[:, :, None]), 0.0)
        factor = jnp.exp(running_max - new_max)
        total = total * factor + jnp.sum(weights, axis=2)
        weighted = jnp.einsum("hqk,khd->qhd", weights, value_split, precision=HIGH)
        accum = accum.reshape(group, heads_here, HEAD_DIM) * factor.T[:, :, None] + weighted
        return (new_max, total, accum.reshape(group, width))

    start_state = (
        jnp.full((heads_here, group), floor_score, jnp.float32),
        jnp.zeros((heads_here, group), jnp.float32),
        jnp.zeros((group, width), jnp.float32),
    )
    running_max, total, accum = over_blocks(
        start_state,
        (
            lax.all_gather(key_value, "blk", axis=0, tiled=True),
            lax.all_gather(key_codes, "blk", axis=0, tiled=True),
        ),
        forward_update,
    )
    normalizer = running_max + jnp.log(total)
    attended_heads = (accum.reshape(group, heads_here, HEAD_DIM) / total.T[:, :, None]).reshape(
        group, width
    )
    attended = lax.all_to_all(attended_heads, "ulys", split_axis=0, concat_axis=1, tiled=True)
    middle = residual_input + matmul(attended, full_out) + full_obias
    mlp_in, mlp_back = jax.vjp(layer_normalize, middle, full_mlpgain, full_mlpshift)
    pre_act = matmul(mlp_in, full_up) + full_upbias
    activated, gelu_back = jax.vjp(gelu_tanh, pre_act)
    output = middle + matmul(activated, full_down) + full_downbias
    back_query, back_key, back_value, back_out, back_up, back_down = (
        lax.all_gather(w_query, ("blk", "ulys"), axis=0, tiled=True),
        lax.all_gather(w_key, ("blk", "ulys"), axis=0, tiled=True),
        lax.all_gather(w_value, ("blk", "ulys"), axis=0, tiled=True),
        lax.all_gather(w_out, ("blk", "ulys"), axis=0, tiled=True),
        lax.all_gather(w_up, ("blk", "ulys"), axis=0, tiled=True),
        lax.all_gather(w_down, ("blk", "ulys"), axis=0, tiled=True),
    )
    grad_downbias = jnp.sum(out_grad, axis=0)
    grad_downproj = matmul_left_t(activated, out_grad)
    act_grad = matmul_right_t(out_grad, back_down)
    (pre_grad,) = gelu_back(act_grad)
    grad_upproj = matmul_left_t(mlp_in, pre_grad)
    grad_upbias = jnp.sum(pre_grad, axis=0)
    mlp_in_grad = matmul_right_t(pre_grad, back_up)
    middle_part, grad_mlpgain, grad_mlpshift = mlp_back(mlp_in_grad)
    middle_grad = out_grad + middle_part
    grad_outproj = matmul_left_t(attended, middle_grad)
    grad_obias = jnp.sum(middle_grad, axis=0)
    attended_grad = matmul_right_t(middle_grad, back_out)
    grad_heads = lax.all_to_all(attended_grad, "ulys", split_axis=1, concat_axis=0, tiled=True)
    grad_split = grad_heads.reshape(group, heads_here, HEAD_DIM)
    row_dots = jnp.sum(grad_split * attended_heads.reshape(group, heads_here, HEAD_DIM), axis=2).T

    def backward_from(first_row):

        def backward_update(state, kv_block, code_block, key_rows):
            query_grad, pair_grads = state
            scores, allowed, key_split, value_split = block_scores(kv_block, code_block, key_rows)
            weights = jnp.exp(jnp.where(allowed, scores - normalizer[:, :, None], floor_score))
            values_grad = jnp.einsum("hqk,qhd->khd", weights, grad_split, precision=HIGH)
            weights_grad = jnp.einsum("qhd,khd->hqk", grad_split, value_split, precision=HIGH)
            score_grad = weights * (weights_grad - row_dots[:, :, None]) * scale
            query_grad = query_grad + jnp.einsum(
                "hqk,khd->qhd", score_grad, key_split, precision=HIGH
            ).reshape(group, width)
            keys_grad = jnp.einsum("hqk,qhd->khd", score_grad, query_split, precision=HIGH)
            size = key_rows.shape[0]
            block_grad = jnp.concatenate(
                [keys_grad.reshape(size, width), values_grad.reshape(size, width)], axis=1
            )
            place = key_rows[0] - first_row
            current = lax.dynamic_slice_in_dim(pair_grads, place, size, 0)
            pair_grads = lax.dynamic_update_slice_in_dim(pair_grads, current + block_grad, place, 0)
            return (query_grad, pair_grads)

        return backward_update

    back_state = (
        jnp.zeros((group, width), jnp.float32),
        jnp.zeros((length, 2 * width), jnp.float32),
    )
    query_grad, pair_grads = over_blocks(
        back_state,
        (
            lax.all_gather(key_value, "blk", axis=0, tiled=True),
            lax.all_gather(key_codes, "blk", axis=0, tiled=True),
        ),
        backward_from(0),
    )
    local_pairs = lax.psum_scatter(pair_grads, "blk", scatter_dimension=0, tiled=True)
    token_query_grad, token_keys_grad, token_values_grad = (
        lax.all_to_all(query_grad, "ulys", split_axis=0, concat_axis=1, tiled=True),
        lax.all_to_all(local_pairs[:, :width], "ulys", split_axis=0, concat_axis=1, tiled=True),
        lax.all_to_all(local_pairs[:, width:], "ulys", split_axis=0, concat_axis=1, tiled=True),
    )
    grad_query = matmul_left_t(normalized_rows, token_query_grad)
    grad_qbias = jnp.sum(token_query_grad, axis=0)
    grad_key = matmul_left_t(normalized_rows, token_keys_grad)
    grad_value = matmul_left_t(normalized_rows, token_values_grad)
    grad_vbias = jnp.sum(token_values_grad, axis=0)
    normalized_gradient = (
        matmul_right_t(token_query_grad, back_query)
        + matmul_right_t(token_keys_grad, back_key)
        + matmul_right_t(token_values_grad, back_value)
    )
    residual_slice, prenorm_gain_gradient, prenorm_shift_gradient = prenorm_backward(
        normalized_gradient
    )
    hidden_grad = middle_grad + residual_slice
    shard_sums = (
        lax.psum_scatter(grad_query, ("blk", "ulys"), scatter_dimension=0, tiled=True),
        lax.psum_scatter(grad_qbias, ("blk", "ulys"), scatter_dimension=0, tiled=True),
        lax.psum_scatter(grad_key, ("blk", "ulys"), scatter_dimension=0, tiled=True),
        lax.psum_scatter(grad_value, ("blk", "ulys"), scatter_dimension=0, tiled=True),
        lax.psum_scatter(grad_vbias, ("blk", "ulys"), scatter_dimension=0, tiled=True),
        lax.psum_scatter(grad_outproj, ("blk", "ulys"), scatter_dimension=0, tiled=True),
        lax.psum_scatter(grad_obias, ("blk", "ulys"), scatter_dimension=0, tiled=True),
        lax.psum_scatter(grad_upproj, ("blk", "ulys"), scatter_dimension=0, tiled=True),
        lax.psum_scatter(grad_upbias, ("blk", "ulys"), scatter_dimension=0, tiled=True),
        lax.psum_scatter(grad_downproj, ("blk", "ulys"), scatter_dimension=0, tiled=True),
        lax.psum_scatter(grad_downbias, ("blk", "ulys"), scatter_dimension=0, tiled=True),
        lax.psum_scatter(prenorm_gain_gradient, ("blk", "ulys"), scatter_dimension=0, tiled=True),
        lax.psum_scatter(prenorm_shift_gradient, ("blk", "ulys"), scatter_dimension=0, tiled=True),
        lax.psum_scatter(grad_mlpgain, ("blk", "ulys"), scatter_dimension=0, tiled=True),
        lax.psum_scatter(grad_mlpshift, ("blk", "ulys"), scatter_dimension=0, tiled=True),
    )
    totals = lax.psum(
        (
            shard_sums[0],
            shard_sums[1],
            shard_sums[2],
            shard_sums[3],
            shard_sums[4],
            shard_sums[5],
            shard_sums[6],
            shard_sums[7],
            shard_sums[8],
            shard_sums[9],
            shard_sums[10],
            shard_sums[11],
            shard_sums[12],
            shard_sums[13],
            shard_sums[14],
        ),
        "dp",
    )
    return (output, hidden_grad) + tuple(totals)


def solution(mesh):
    placed = (
        P(("dp", "blk", "ulys"), None),
        P("dp", None),
        P("dp", "blk"),
        P("dp", "blk"),
        P(("dp", "blk", "ulys"), None),
        P(("blk", "ulys"), None),
        P(("blk", "ulys")),
        P(("blk", "ulys"), None),
        P(("blk", "ulys"), None),
        P(("blk", "ulys")),
        P(("blk", "ulys"), None),
        P(("blk", "ulys")),
        P(("blk", "ulys"), None),
        P(("blk", "ulys")),
        P(("blk", "ulys"), None),
        P(("blk", "ulys")),
        P(("blk", "ulys")),
        P(("blk", "ulys")),
        P(("blk", "ulys")),
        P(("blk", "ulys")),
    )
    return jax.shard_map(
        local,
        mesh=mesh,
        in_specs=placed,
        out_specs=(
            P(("dp", "blk", "ulys"), None),
            P(("dp", "blk", "ulys"), None),
            P(("blk", "ulys"), None),
            P(("blk", "ulys")),
            P(("blk", "ulys"), None),
            P(("blk", "ulys"), None),
            P(("blk", "ulys")),
            P(("blk", "ulys"), None),
            P(("blk", "ulys")),
            P(("blk", "ulys"), None),
            P(("blk", "ulys")),
            P(("blk", "ulys"), None),
            P(("blk", "ulys")),
            P(("blk", "ulys")),
            P(("blk", "ulys")),
            P(("blk", "ulys")),
            P(("blk", "ulys")),
        ),
        check_vma=False,
    )
```

profile of v0, /device:TPU:0, one launch (start us, length us, event | category | flops | bytes accessed | tf_op | source)
XLA Modules:
  0.0 1022.3 jit_solution(7947573977653093022)
XLA Ops:
  18.0 26.4 %all-reduce.18 = (f32[768]{0:T(1024)S(1)}, f32[768]{0:T(1024)S(1)}, f32[768]{0:T(1024)S(1)}, f32[768]{0:T(1024)}, f32[768]{0:T(1024)}, /*index=5*/f32[768]{0:T(1024)}, f32[768]{0:T(1024)}) all-reduce(f32[768]{0:T(1024)S(1)} %dynamic-update-slice.2, ...), channel_id=1, replica_groups=mesh['dp'=4,'blk'=2,'ulys'=4] {'blk','ulys'}, use_global_device_ids=true, to_apply=%add.2 | all-reduce | flops 5376 | bytes 43008
  55.1 19.6 %all-gather.10.cloned.1.call-done = f32[768,768]{1,0:T(8,128)} async-done(((f32[96,768]{1,0:T(8,128)}), f32[768,768]{1,0:T(8,128)}) %all-gather.10.cloned.1.call-update) | async-done | bytes 2359312 | tf_op jit(solution)/shard_map/all_gather | solution.py:83
  85.7 12.1 %all-to-all-done = f32[192,4,192]{0,2,1:T(8,128)S(1)} async-done(((f32[192,4,192]{0,2,1:T(8,128)}), f32[192,4,192]{0,2,1:T(8,128)S(1)}, u32[]{:S(2)}, u32[]{:S(2)}) %all-to-all-start) | async-done | bytes 589856 | tf_op jit(solution)/shard_map/all_to_all | solution.py:106
  129.3 16.9 %all-gather.14.cloned.1.call-done = f32[1536,384]{0,1:T(8,128)} async-done(((f32[768,384]{0,1:T(8,128)}), f32[1536,384]{0,1:T(8,128)}) %all-gather.14.cloned.1.call-update) | async-done | bytes 2359312 | tf_op jit(solution)/shard_map/all_gather | solution.py:170
  150.3 49.9 %while.28 = (s32[]{:T(128)}, f32[3,768]{1,0:T(4,128)S(1)}, f32[3,768]{1,0:T(4,128)}, f32[768,192]{0,1:T(8,128)S(1)}, f32[768]{0:T(1024)}, /*index=5*/f32[2,768]{...) while((s32[]{:T(128)}, f32[3,768]{1,0:T(4,128)S(1)}, ...), condition=%wide.region_5.6_spmd.clone, body=%wide.region_2.5_spmd.clone.sunk | while | flops 2741222400 | bytes 31506652 | solution.py:147
  205.9 22.6 %all-gather.1 = f32[8,1,384]{2,1,0:T(1,128)} all-gather(f32[1,1,384]{2,1,0:T(1,128)S(1)} %reshape.337), channel_id=1, replica_groups=mesh['dp'=4,'blk'=2,'ulys'=4] {'blk','ulys'}, dimensions={0}, use_global_device_ids=true | all-gather | bytes 13824 | tf_op jit(solution)/shard_map/all_gather | solution.py:89
  234.9 10.0 all-gather.20.cloned.1.call-done
  244.9 9.0 convolution_add_fusion
  254.0 50.8 %all-gather.22.cloned.1.call-done = f32[3072,768]{1,0:T(8,128)} async-done(((f32[384,768]{1,0:T(8,128)}), f32[3072,768]{1,0:T(8,128)}) %all-gather.22.cloned.1.call-update) | async-done | bytes 9437200 | tf_op jit(solution)/shard_map/all_gather | solution.py:90
  304.7 14.4 %fusion.64 = (f32[3072]{0:T(1024)}, f32[192,3072]{1,0:T(8,128)S(1)}) fusion(f32[192,3072]{1,0:T(8,128)S(1)} %convolution_add_fusion, f32[192,768]{1,0:T(8,128)} %param.28, f32[3072,768]{1,0:T(8,128)} %all-gather.22.cloned.1.call-done), kind=kOutput, calls=%fused_computation.123 | convolution fusion | flops 5449970688 | bytes 14757888 | tf_op jit(solution)/shard_map/dot_general | solution.py:39
  319.2 10.1 multiply_reduce_fusion
  340.4 11.0 %all-to-all-done.4 = f32[192,4,192]{2,0,1:T(8,128)} async-done(((f32[192,4,192]{2,0,1:T(8,128)}), f32[192,4,192]{2,0,1:T(8,128)}, u32[]{:S(2)}, u32[]{:S(2)}) %all-to-all-start.4) | async-done | bytes 589856 | tf_op jit(solution)/shard_map/all_to_all | solution.py:205
  357.8 123.8 %while.29 = (s32[]{:T(128)}, f32[768,192]{0,1:T(8,128)S(1)}, f32[1536,384]{0,1:T(8,128)}, f32[2,768,384]{1,2,0:T(8,128)}, f32[768]{0:T(1024)S(1)}, /*index=5*/f3...) while((s32[]{:T(128)}, f32[768,192]{0,1:T(8,128)S(1)}, ...), condition=%wide.region_12.13_spmd.clone, body=%wide.region_11.12_spmd.clone.sunk | while | flops 6813353472 | bytes 72011080 | solution.py:147
  390.5 8.8 fusion.165
  399.4 8.7 fusion.163
  439.0 8.8 fusion.165
  447.8 8.7 fusion.163
  486.8 14.1 %all_to_all.146 = f32[4,192,192]{2,1,0:T(8,128)S(1)} all-to-all(f32[4,192,192]{2,1,0:T(8,128)S(1)} %bitcast.210), channel_id=1, replica_groups=mesh['dp'=4,'blk'=2,'ulys'=4] {'ulys'}, dimensions={0} | all-to-all | bytes 1179648 | tf_op jit(solution)/shard_map/all_to_all | solution.py:247
  506.5 10.0 reduce-scatter.8.cloned.1.call-done
  518.1 14.2 %all_to_all.147 = f32[4,192,192]{2,1,0:T(8,128)S(1)} all-to-all(f32[4,192,192]{2,1,0:T(8,128)S(1)} %bitcast.211), channel_id=1, replica_groups=mesh['dp'=4,'blk'=2,'ulys'=4] {'ulys'}, dimensions={0} | all-to-all | bytes 1179648 | tf_op jit(solution)/shard_map/all_to_all | solution.py:249
  538.2 20.1 %all_to_all.148 = f32[4,192,192]{2,1,0:T(8,128)S(1)} all-to-all(f32[4,192,192]{2,1,0:T(8,128)S(1)} %bitcast.212), channel_id=1, replica_groups=mesh['dp'=4,'blk'=2,'ulys'=4] {'ulys'}, dimensions={0} | all-to-all | bytes 1179648 | tf_op jit(solution)/shard_map/all_to_all | solution.py:248
  565.1 10.9 %fusion.37 = f32[768,3072]{1,0:T(8,128)} fusion(f32[192,3072]{1,0:T(8,128)S(1)} %copy-done.13, f32[192,768]{1,0:T(8,128)S(1)} %copy-done.6, f32[768]{0:T(1024)S(1)} %copy-done.36, f32[768]{0:T(1024)S(1)} %copy-done.35, f32[192]{0:T(256)} %fusion.50, f32[192]{0:T(256)} %copy-done.40), kind=kOutput, calls=%fused_computation.82 | convolution fusion | flops 5436407808 | bytes 12393984 | tf_op jit(solution)/shard_map/dot_general | solution.py:35
  577.7 11.7 %fusion.36 = f32[3072,768]{1,0:T(8,128)} fusion(f32[192,768]{1,0:T(8,128)} %param.28, f32[192,3072]{1,0:T(8,128)S(1)} %copy-done.3), kind=kOutput, calls=%fused_computation.65 | convolution fusion | flops 5440536576 | bytes 12386304 | tf_op jit(solution)/shard_map/dot_general | solution.py:35
  589.5 25.1 %reduce-scatter.10.cloned.1.call-done = f32[96,768]{1,0:T(8,128)} async-done(((f32[768,768]{1,0:T(8,128)}), f32[96,768]{1,0:T(8,128)}) %reduce-scatter.10.cloned.1.call-update) | async-done | bytes 294928 | tf_op jit(solution)/shard_map/reduce_scatter | solution.py:266
  614.6 46.2 %reduce-scatter.14.cloned.1.call-done = f32[96,768]{1,0:T(8,128)} async-done(((f32[768,768]{1,0:T(8,128)}), f32[96,768]{1,0:T(8,128)}) %reduce-scatter.14.cloned.1.call-update) | async-done | bytes 294928 | tf_op jit(solution)/shard_map/reduce_scatter | solution.py:269
  660.8 45.7 %reduce-scatter.12.cloned.1.call-done = f32[96,768]{1,0:T(8,128)} async-done(((f32[768,768]{1,0:T(8,128)}), f32[96,768]{1,0:T(8,128)}) %reduce-scatter.12.cloned.1.call-update) | async-done | bytes 294928 | tf_op jit(solution)/shard_map/reduce_scatter | solution.py:268
  706.5 80.4 %reduce-scatter.18.cloned.1.call-done = f32[96,3072]{1,0:T(8,128)} async-done(((f32[768,3072]{1,0:T(8,128)}), f32[96,3072]{1,0:T(8,128)}) %reduce-scatter.18.cloned.1.call-update) | async-done | bytes 1179664 | tf_op jit(solution)/shard_map/reduce_scatter | solution.py:273
  787.0 80.3 %reduce-scatter.20.cloned.1.call-done = f32[384,768]{1,0:T(8,128)} async-done(((f32[3072,768]{1,0:T(8,128)}), f32[384,768]{1,0:T(8,128)}) %reduce-scatter.20.cloned.1.call-update) | async-done | bytes 1179664 | tf_op jit(solution)/shard_map/reduce_scatter | solution.py:275
  888.4 26.3 %all-reduce.17 = (f32[768]{0:T(1024)}, f32[768]{0:T(1024)}, f32[768]{0:T(1024)}, f32[768]{0:T(1024)}, f32[3072]{0:T(1024)}, /*index=5*/f32[768]{0:T(1024)}, f32[...) all-reduce(f32[768]{0:T(1024)} %dynamic-update-slice.7, ...), channel_id=1, replica_groups=mesh['dp'=4,'blk'=2,'ulys'=4] {'blk','ulys'}, use_global_device_ids=true, to_apply=%add.7 | all-reduce | flops 9984 | bytes 79872
  926.1 13.0 %all-reduce.19 = (f32[96]{0:T(128)}, f32[96]{0:T(128)}, f32[96]{0:T(128)}, f32[384]{0:T(512)}, f32[96]{0:T(128)}, /*index=5*/f32[96]{0:T(128)}, f32[96]{0:T(128)}, f32[96]{0:T(128)}, f32[96]{0:T(128)}) all-reduce(f32[96]{0:T(128)} %dynamic-slice.9, f32[96]{0:T(128)} %dynamic-slice.11, ...), channel_id=1, replica_groups=mesh['dp'=4,'blk'=2,'ulys'=4] {'dp'}, use_global_device_ids=true, to_apply=%region_20.21 | all-reduce | flops 1152 | bytes 9216 | tf_op jit(solution)/shard_map/psum | solution.py:282
  943.3 10.4 %fusion.35 = f32[192,768]{1,0:T(8,128)} fusion(f32[192,768]{1,0:T(8,128)S(1)} %copy-done.6, f32[3072,768]{1,0:T(8,128)} %all-gather.22.cloned.1.call-done, f32[192,3072]{1,0:T(8,128)S(1)} %copy-done.3, f32[768]{0:T(1024)S(1)} %copy-done.51), kind=kOutput, calls=%fused_computation.63 | convolution fusion | flops 5440831488 | bytes 12979200 | tf_op jit(solution)/shard_map/dot_general | solution.py:31
  953.6 52.7 %all-reduce.23.cloned.1.call-done = (f32[96,768]{1,0:T(8,128)}, f32[96,768]{1,0:T(8,128)}, f32[96,768]{1,0:T(8,128)}, f32[96,768]{1,0:T(8,128)}, f32[96,3072]{1,0:T(8,128)}, /*index=5*/f32[384,768]{1,0:T(8,128)}) async-done(((f32[96,768]{1,0:T(8,128)}, f32[96,768]{1,0:T(8,128)}, f32[96,768]{1,0:T(8,128)}, f32[96,768]{1,0:T(8,128)}, f32[96,3072]{1,0:T(8,128)}, /*index=5*/f32[384,768]{1,0:T(8,128)}), ...) | async-done | bytes 3538960 | tf_op jit(solution)/shard_map/psum | solution.py:282
  (334 shorter events, 265.8 us)
Async XLA Ops:
  7.2 39.7 %copy-start = (f32[192,768]{1,0:T(8,128)S(1)}, f32[192,768]{1,0:T(8,128)}, u32[]{:S(2)}) copy-start(f32[192,768]{1,0:T(8,128)} %param.24) | copy-start | bytes 1769476
  7.2 39.7 %all-gather.12.cloned.1.call-start = ((), (), s32[]{:S(2)}) async-start(), calls=%async_computation.16 | async-start | bytes 2654208 | tf_op jit(solution)/shard_map/all_gather | solution.py:84
  7.9 66.7 %all-gather.10.cloned.1.call-start = ((), (), s32[]{:S(2)}) async-start(), calls=%async_computation.15 | async-start | bytes 2654208 | tf_op jit(solution)/shard_map/all_gather | solution.py:83
  8.7 99.4 %all-gather.16.cloned.1.call-start = ((), (), s32[]{:S(2)}) async-start(), calls=%async_computation.18 | async-start | bytes 2654208 | tf_op jit(solution)/shard_map/all_gather | solution.py:81
  44.4 30.3 %copy-start.31 = (f32[768]{0:T(1024)}, f32[768]{0:T(1024)S(1)}, u32[]{:S(2)}) copy-start(f32[768]{0:T(1024)S(1)} %get-tuple-element.345) | copy-start | bytes 9220
  44.4 30.3 %copy-start.37 = (f32[768]{0:T(1024)}, f32[768]{0:T(1024)S(1)}, u32[]{:S(2)}) copy-start(f32[768]{0:T(1024)S(1)} %get-tuple-element.344) | copy-start | bytes 9220
  45.6 29.1 %copy-start.42 = (f32[192]{0:T(256)}, f32[192]{0:T(256)S(1)}, u32[]{:S(2)}) copy-start(f32[192]{0:T(256)S(1)} %broadcast_multiply_fusion.1) | copy-start | bytes 2308
  46.9 27.8 %copy-start.47 = (f32[192]{0:T(256)}, f32[192]{0:T(256)S(1)}, u32[]{:S(2)}) copy-start(f32[192]{0:T(256)S(1)} %fusion.49) | copy-start | bytes 2308
  51.6 29.5 %all-to-all-start.1 = ((f32[192,4,192]{0,2,1:T(8,128)}), f32[192,4,192]{0,2,1:T(8,128)S(1)}, u32[]{:S(2)}, u32[]{:S(2)}) async-start(f32[192,4,192]{0,2,1:T(8,128)} %bitcast.3), calls=%async_computation.1 | async-start | bytes 1572864 | tf_op jit(solution)/shard_map/all_to_all | solution.py:107
  81.1 16.7 %all-to-all-start = ((f32[192,4,192]{0,2,1:T(8,128)}), f32[192,4,192]{0,2,1:T(8,128)S(1)}, u32[]{:S(2)}, u32[]{:S(2)}) async-start(f32[192,4,192]{0,2,1:T(8,128)} %bitcast.1), calls=%async_computation | async-start | bytes 1572864 | tf_op jit(solution)/shard_map/all_to_all | solution.py:106
  84.6 61.6 %all-gather.14.cloned.1.call-start = ((), (), s32[]{:S(2)}) async-start(), calls=%async_computation.17 | async-start | bytes 3538944 | tf_op jit(solution)/shard_map/all_gather | solution.py:170
  99.9 129.6 %all-gather.18.cloned.1.call-start = ((), (), s32[]{:S(2)}) async-start(), calls=%async_computation.19 | async-start | bytes 2654208 | tf_op jit(solution)/shard_map/all_gather | solution.py:86
  100.5 144.4 %all-gather.20.cloned.1.call-start = ((), (), s32[]{:S(2)}) async-start(), calls=%async_computation.20 | async-start | bytes 10616832 | tf_op jit(solution)/shard_map/all_gather | solution.py:88
  101.1 203.6 %all-gather.22.cloned.1.call-start = ((), (), s32[]{:S(2)}) async-start(), calls=%async_computation.21 | async-start | bytes 10616832 | tf_op jit(solution)/shard_map/all_gather | solution.py:90
  113.2 15.2 %all-to-all-start.2 = ((f32[192,4,192]{2,0,1:T(8,128)}), f32[192,4,192]{2,0,1:T(8,128)S(1)}, u32[]{:S(2)}, u32[]{:S(2)}) async-start(f32[192,4,192]{2,0,1:T(8,128)} %copy.98), calls=%async_computation.2 | async-start | bytes 1572864 | tf_op jit(solution)/shard_map/all_to_all | solution.py:105
  200.2 28.3 %copy-start.19 = (f32[768,192]{0,1:T(8,128)}, f32[768,192]{0,1:T(8,128)S(1)}, u32[]{:S(2)}) copy-start(f32[768,192]{0,1:T(8,128)S(1)} %get-tuple-element.134) | copy-start | bytes 1769476
  202.2 27.3 %copy-start.56 = (f32[768]{0:T(1024)S(1)}, f32[768]{0:T(1024)}, u32[]{:S(2)}) copy-start(f32[768]{0:T(1024)} %get-tuple-element.347) | copy-start | bytes 9220
  202.2 26.3 %all-to-all-start.3 = ((f32[4,192,192]{2,1,0:T(8,128)}), f32[4,192,192]{2,1,0:T(8,128)S(1)}, u32[]{:S(2)}, u32[]{:S(2)}) async-start(f32[4,192,192]{2,1,0:T(8,128)} %bitcast.9), calls=%async_computation.3 | async-start | bytes 1572864 | tf_op jit(solution)/shard_map/all_to_all | solution.py:179
  253.9 65.2 %copy-start.2 = (f32[192,3072]{1,0:T(8,128)}, f32[192,3072]{1,0:T(8,128)S(1)}, u32[]{:S(2)}) copy-start(f32[192,3072]{1,0:T(8,128)S(1)} %convolution_add_fusion) | copy-start | bytes 7077892
  335.4 20.0 %copy-start.20 = (f32[768,192]{0,1:T(8,128)S(1)}, f32[768,192]{0,1:T(8,128)}, u32[]{:S(2)}) copy-start(f32[768,192]{0,1:T(8,128)} %copy-done.19) | copy-start | bytes 1769476
  335.4 16.1 %all-to-all-start.4 = ((f32[192,4,192]{2,0,1:T(8,128)}), f32[192,4,192]{2,0,1:T(8,128)}, u32[]{:S(2)}, u32[]{:S(2)}) async-start(f32[192,4,192]{2,0,1:T(8,128)} %copy.103), calls=%async_computation.4 | async-start | bytes 1572864 | tf_op jit(solution)/shard_map/all_to_all | solution.py:205
  339.7 176.8 %reduce-scatter.8.cloned.1.call-start = ((), (), s32[]{:S(2)}) async-start(), calls=%async_computation.22 | async-start | bytes 3538944 | tf_op jit(solution)/shard_map/reduce_scatter | solution.py:245
  481.6 107.9 %reduce-scatter.16.cloned.1.call-start = ((), (), s32[]{:S(2)}) async-start(), calls=%async_computation.26 | async-start | bytes 2654208 | tf_op jit(solution)/shard_map/reduce_scatter | solution.py:271
  486.4 128.2 %reduce-scatter.10.cloned.1.call-start = ((), (), s32[]{:S(2)}) async-start(), calls=%async_computation.23 | async-start | bytes 2654208 | tf_op jit(solution)/shard_map/reduce_scatter | solution.py:266
  486.7 16.0 %copy-start.33 = (f32[768]{0:T(1024)S(1)}, f32[768]{0:T(1024)}, u32[]{:S(2)}) copy-start(f32[768]{0:T(1024)} %copy-done.31) | copy-start | bytes 9220
  486.7 16.0 %copy-start.39 = (f32[768]{0:T(1024)S(1)}, f32[768]{0:T(1024)}, u32[]{:S(2)}) copy-start(f32[768]{0:T(1024)} %copy-done.37) | copy-start | bytes 9220
  506.4 154.4 %reduce-scatter.14.cloned.1.call-start = ((), (), s32[]{:S(2)}) async-start(), calls=%async_computation.25 | async-start | bytes 2654208 | tf_op jit(solution)/shard_map/reduce_scatter | solution.py:269
  537.8 168.7 %reduce-scatter.12.cloned.1.call-start = ((), (), s32[]{:S(2)}) async-start(), calls=%async_computation.24 | async-start | bytes 2654208 | tf_op jit(solution)/shard_map/reduce_scatter | solution.py:268
  565.0 222.0 %reduce-scatter.18.cloned.1.call-start = ((), (), s32[]{:S(2)}) async-start(), calls=%async_computation.27 | async-start | bytes 10616832 | tf_op jit(solution)/shard_map/reduce_scatter | solution.py:273
  576.0 291.3 %reduce-scatter.20.cloned.1.call-start = ((), (), s32[]{:S(2)}) async-start(), calls=%async_computation.28 | async-start | bytes 10616832 | tf_op jit(solution)/shard_map/reduce_scatter | solution.py:275
  589.4 279.8 %copy-start.60 = (f32[96]{0:T(128)S(1)}, f32[96]{0:T(128)}, u32[]{:S(2)}) copy-start(f32[96]{0:T(128)} %param.39) | copy-start | bytes 1156
  589.4 416.9 %all-reduce.23.cloned.1.call-start = ((), (), s32[]{:S(2)}) async-start(), calls=%async_computation.29 | async-start | bytes 7077888 | tf_op jit(solution)/shard_map/psum | solution.py:282
  (55 other events, 353.4 us)
Sparse Core Ops, SparseCore 0:
  9.9 32.0 all-gather.11
  43.9 30.6 all-gather.9
  76.5 31.5 all-gather.15
  110.1 36.0 all-gather.13
  147.9 29.0 all-gather.17
  178.8 66.0 all-gather.19
  246.8 57.9 all-gather.21
  481.7 34.7 reduce-scatter.7
  520.2 48.6 reduce-scatter.15
  572.1 42.4 reduce-scatter.9
  618.3 42.4 reduce-scatter.13
  664.0 42.4 reduce-scatter.11
  710.4 76.4 reduce-scatter.17
  790.7 76.4 reduce-scatter.19
  870.2 136.1 all-reduce.22
where the time goes:
time: 1030 us; the launch traced here: 1020 us
  waiting for transfers between devices  476 us (46%)
  matrix products  211 us (20%)
  blocking collectives  141 us (14%)
  local copies, waits for them, and re-layouts  91.2 us (9%)
  loops' own time  40.3 us (4%)
  other arithmetic  25.8 us (3%)
  starting transfers between devices  19.3 us (2%)
  between operations  17.2 us (2%)
    reduce_scatter x1, waiting for transfers between devices, local(): lax.psum_scatter(grad_upproj, ('blk', 'ulys'), scatter_dimension=0, tiled...  80.4 us
    reduce_scatter x1, waiting for transfers between devices, local(): lax.psum_scatter(grad_downproj, ('blk', 'ulys'), scatter_dimension=0, til...  80.3 us
    psum x1, waiting for transfers between devices, local(): lax.psum((shard_sums[0], shard_sums[1], shard_sums[2], shard_sums[3], sha...  52.7 us
    unnamed x2, blocking collectives  52.7 us
    all_gather x1, waiting for transfers between devices, local(): lax.all_gather(w_down, ('blk', 'ulys'), axis=0, tiled=True)  50.8 us
    reduce_scatter x1, waiting for transfers between devices, local(): lax.psum_scatter(grad_value, ('blk', 'ulys'), scatter_dimension=0, tiled=...  46.2 us
    reduce_scatter x1, waiting for transfers between devices, local(): lax.psum_scatter(grad_key, ('blk', 'ulys'), scatter_dimension=0, tiled=True)  45.7 us
    dot_general x6, matrix products, matmul_right_t(): lax.dot_general(left, right, (((1,), (1,)), ((), ())), precision=HIGH)  40.7 us
  transfers between devices with their start and end apart: 20, of which 15 were waited for; matrix products, arithmetic and copies ran while one was open for 18% of the time, Pallas kernels for 0%

commit v1 on v0

v1 whole, which is shorter than its diff:
```python
import functools
import math

import jax, jax.numpy as jnp
from jax import lax
from jax.experimental import pallas as pl
from jax.experimental.pallas import tpu as pltpu
from jax.sharding import PartitionSpec as P

HEAD_DIM = 64
FLOOR = -1e30
BF = jnp.bfloat16
F32 = jnp.float32
NT = (((1,), (1,)), ((), ()))
NN = (((1,), (0,)), ((), ()))


def split(x):
    hi = x.astype(BF)
    return hi, (x - hi.astype(F32)).astype(BF)


def mm(a, b, dims=NN):
    return lax.dot_general(a, b, dims, preferred_element_type=F32)


def attend_kernel(tile, heads, seg_ref, qcode_ref, kcode_ref, q_ref, k_ref, v_ref,
                  out_ref, lse_ref, qc, kc, vt, m_s, l_s, acc):
    group, keys = q_ref.shape[0], k_ref.shape[0]
    nq, nk = group // tile, keys // tile
    scale = HEAD_DIM ** -0.5
    for h in range(heads):
        lane = slice(h * HEAD_DIM, (h + 1) * HEAD_DIM)
        hi, lo = split(q_ref[:, lane] * scale)
        qc[h] = jnp.concatenate([hi, hi, lo], axis=1)
        hi, lo = split(k_ref[:, lane])
        kc[h] = jnp.concatenate([hi, lo, hi], axis=1)
    for j in range(nk):
        rows = slice(j * tile, (j + 1) * tile)
        vtile = v_ref[rows, :].T
        for h in range(heads):
            hi, lo = split(vtile[h * HEAD_DIM:(h + 1) * HEAD_DIM])
            vt[h, j] = jnp.concatenate([hi, lo], axis=0)

    def per_q(i, _):
        qrow = pl.ds(pl.multiple_of(i * tile, tile), tile)
        m_s[...] = jnp.full_like(m_s, FLOOR)
        l_s[...] = jnp.zeros_like(l_s)
        acc[...] = jnp.zeros_like(acc)
        first, last = seg_ref[0, 2 * i], seg_ref[0, 2 * i + 1]
        qcode = qcode_ref[:, qrow]

        def per_k(j, _):
            @pl.when((seg_ref[0, 2 * (nq + j) + 1] >= first) & (seg_ref[0, 2 * (nq + j)] <= last))
            def _():
                krow = pl.ds(pl.multiple_of(j * tile, tile), tile)
                kcode = kcode_ref[krow, :]
                gap = (i - j) * tile
                same = (lax.broadcasted_iota(jnp.int32, (tile, tile), 0)
                        - lax.broadcasted_iota(jnp.int32, (tile, tile), 1)) == gap
                allowed = (kcode == qcode) | same
                for h in range(heads):
                    s = mm(kc[h, krow, :], qc[h, qrow, :], NT)
                    s = jnp.where(allowed, s, FLOOR)
                    m_old = m_s[h]
                    m_new = jnp.maximum(m_old, jnp.max(s, axis=0, keepdims=True))
                    p = jnp.where(allowed, jnp.exp(s - m_new), 0.0)
                    factor = jnp.exp(m_old - m_new)
                    m_s[h] = m_new
                    l_s[h] = l_s[h] * factor + jnp.sum(p, axis=0, keepdims=True)
                    hi, lo = split(p)
                    v128 = vt[h, j]
                    acc[h] = acc[h] * factor + mm(v128, hi) + mm(v128, lo)
            return 0

        lax.fori_loop(0, nk, per_k, 0)
        parts = []
        for h in range(heads):
            total = l_s[h]
            parts.append((acc[h, :HEAD_DIM] + acc[h, HEAD_DIM:]) / total)
            lse_ref[h:h + 1, qrow] = m_s[h] + jnp.log(total)
        out_ref[qrow, :] = jnp.concatenate(parts, axis=0).T
        return 0

    lax.fori_loop(0, nq, per_q, 0)


def attend(segs, qcode, kcode, q, k, v, tile):
    group, width = q.shape
    keys = k.shape[0]
    heads = width // HEAD_DIM
    vm = pl.BlockSpec(memory_space=pltpu.VMEM)
    return pl.pallas_call(
        functools.partial(attend_kernel, tile, heads),
        out_shape=(jax.ShapeDtypeStruct((group, width), F32),
                   jax.ShapeDtypeStruct((8, group), F32)),
        in_specs=[pl.BlockSpec(memory_space=pltpu.SMEM)] + [vm] * 5,
        out_specs=(vm, vm),
        scratch_shapes=[
            pltpu.VMEM((heads, group, 3 * HEAD_DIM), BF),
            pltpu.VMEM((heads, keys, 3 * HEAD_DIM), BF),
            pltpu.VMEM((heads, keys // tile, 2 * HEAD_DIM, tile), BF),
            pltpu.VMEM((heads, 1, tile), F32),
            pltpu.VMEM((heads, 1, tile), F32),
            pltpu.VMEM((heads, 2 * HEAD_DIM, tile), F32),
        ],
        compiler_params=pltpu.CompilerParams(vmem_limit_bytes=40 << 20),
        cost_estimate=pl.CostEstimate(flops=4 * group * keys * width * 2, bytes_accessed=4 * width * (2 * group + 2 * keys),
                                      transcendentals=group * keys * heads),
        name="attend",
    )(segs, qcode, kcode, q, k, v)


def attend_back_kernel(tile, heads, seg_ref, qcode_ref, kcode_ref, q_ref, k_ref, v_ref, o_ref, do_ref, lse_ref,
                       dq_ref, dk_ref, dv_ref, qc, kc, vc, dc, q2, d2, kt, dot_s, dqa, dka, dva):
    group, keys = q_ref.shape[0], k_ref.shape[0]
    nq, nk = group // tile, keys // tile
    scale = HEAD_DIM ** -0.5
    for h in range(heads):
        lane = slice(h * HEAD_DIM, (h + 1) * HEAD_DIM)
        hi, lo = split(q_ref[:, lane] * scale)
        qc[h] = jnp.concatenate([hi, hi, lo], axis=1)
        q2[h] = jnp.concatenate([hi, lo], axis=1)
        hi, lo = split(do_ref[:, lane])
        dc[h] = jnp.concatenate([hi, hi, lo], axis=1)
        d2[h] = jnp.concatenate([hi, lo], axis=1)
        hi, lo = split(k_ref[:, lane])
        kc[h] = jnp.concatenate([hi, lo, hi], axis=1)
        hi, lo = split(v_ref[:, lane])
        vc[h] = jnp.concatenate([hi, lo, hi], axis=1)
    for j in range(nk):
        rows = slice(j * tile, (j + 1) * tile)
        ktile = k_ref[rows, :].T
        for h in range(heads):
            hi, lo = split(ktile[h * HEAD_DIM:(h + 1) * HEAD_DIM])
            kt[h, j] = jnp.concatenate([hi, lo], axis=0)
    for i in range(nq):
        rows = slice(i * tile, (i + 1) * tile)
        prod = (o_ref[rows, :] * do_ref[rows, :]).T
        for h in range(heads):
            dot_s[h, :, rows] = jnp.sum(prod[h * HEAD_DIM:(h + 1) * HEAD_DIM], axis=0, keepdims=True)
    dqa[...] = jnp.zeros_like(dqa)

    def per_k(j, _):
        krow = pl.ds(pl.multiple_of(j * tile, tile), tile)
        kcode = kcode_ref[krow, :]
        kfirst, klast = seg_ref[0, 2 * (nq + j)], seg_ref[0, 2 * (nq + j) + 1]
        dka[...] = jnp.zeros_like(dka)
        dva[...] = jnp.zeros_like(dva)

        def per_q(i, _):
            @pl.when((klast >= seg_ref[0, 2 * i]) & (kfirst <= seg_ref[0, 2 * i + 1]))
            def _():
                qrow = pl.ds(pl.multiple_of(i * tile, tile), tile)
                gap = (i - j) * tile
                same = (lax.broadcasted_iota(jnp.int32, (tile, tile), 0)
                        - lax.broadcasted_iota(jnp.int32, (tile, tile), 1)) == gap
                allowed = (kcode == qcode_ref[:, qrow]) | same
                for h in range(heads):
                    s = mm(kc[h, krow, :], qc[h, qrow, :], NT)
                    p = jnp.exp(jnp.where(allowed, s - lse_ref[h:h + 1, qrow], FLOOR))
                    dp = mm(vc[h, krow, :], dc[h, qrow, :], NT)
                    ds = p * (dp - dot_s[h, :, qrow])
                    hi, lo = split(p)
                    d128 = d2[h, qrow, :]
                    dva[h] += mm(hi, d128) + mm(lo, d128)
                    hi, lo = split(ds)
                    q128 = q2[h, qrow, :]
                    dka[h] += mm(hi, q128) + mm(lo, q128)
                    k128 = kt[h, j]
                    dqa[h, i] += mm(k128, hi) + mm(k128, lo)
            return 0

        lax.fori_loop(0, nq, per_q, 0)
        dk_ref[krow, :] = jnp.concatenate([dka[h, :, :HEAD_DIM] + dka[h, :, HEAD_DIM:] for h in range(heads)], axis=1)
        dv_ref[krow, :] = jnp.concatenate([dva[h, :, :HEAD_DIM] + dva[h, :, HEAD_DIM:] for h in range(heads)], axis=1)
        return 0

    lax.fori_loop(0, nk, per_k, 0)
    for i in range(nq):
        parts = [(dqa[h, i, :HEAD_DIM] + dqa[h, i, HEAD_DIM:]) * scale for h in range(heads)]
        dq_ref[i * tile:(i + 1) * tile, :] = jnp.concatenate(parts, axis=0).T


def attend_back(segs, qcode, kcode, q, k, v, o, do, lse, tile):
    group, width = q.shape
    keys = k.shape[0]
    heads = width // HEAD_DIM
    vm = pl.BlockSpec(memory_space=pltpu.VMEM)
    H3, H2 = 3 * HEAD_DIM, 2 * HEAD_DIM
    return pl.pallas_call(
        functools.partial(attend_back_kernel, tile, heads),
        out_shape=(jax.ShapeDtypeStruct((group, width), F32),
                   jax.ShapeDtypeStruct((keys, width), F32),
                   jax.ShapeDtypeStruct((keys, width), F32)),
        in_specs=[pl.BlockSpec(memory_space=pltpu.SMEM)] + [vm] * 8,
        out_specs=(vm, vm, vm),
        scratch_shapes=[
            pltpu.VMEM((heads, group, H3), BF),
            pltpu.VMEM((heads, keys, H3), BF),
            pltpu.VMEM((heads, keys, H3), BF),
            pltpu.VMEM((heads, group, H3), BF),
            pltpu.VMEM((heads, group, H2), BF),
            pltpu.VMEM((heads, group, H2), BF),
            pltpu.VMEM((heads, keys // tile, H2, tile), BF),
            pltpu.VMEM((heads, 1, group), F32),
            pltpu.VMEM((heads, group // tile, H2, tile), F32),
            pltpu.VMEM((heads, tile, H2), F32),
            pltpu.VMEM((heads, tile, H2), F32),
        ],
        compiler_params=pltpu.CompilerParams(vmem_limit_bytes=48 << 20),
        cost_estimate=pl.CostEstimate(flops=10 * group * keys * width * 2, bytes_accessed=4 * width * (4 * group + 4 * keys),
                                      transcendentals=group * keys * heads),
        name="attend_back",
    )(segs, qcode, kcode, q, k, v, o, do, lse)


HIGH = lax.Precision.HIGH
SQRT_2_PI = 0.7978845608028654
CUBIC = 0.044715
TILE = 256


def dot(left, right):
    return jnp.dot(left, right, precision=HIGH)


def dot_left_t(left, right):
    return lax.dot_general(left, right, (((0,), (0,)), ((), ())), precision=HIGH)


def dot_right_t(left, right):
    return lax.dot_general(left, right, (((1,), (1,)), ((), ())), precision=HIGH)


def normalize(values):
    centred = values - jnp.mean(values, axis=-1, keepdims=True)
    inverse = lax.rsqrt(jnp.mean(centred * centred, axis=-1, keepdims=True) + 1e-05)
    return centred * inverse, inverse


def normalize_back(grad, gain, xhat, inverse):
    scaled = grad * gain
    mean = jnp.mean(scaled, axis=-1, keepdims=True)
    lean = jnp.mean(scaled * xhat, axis=-1, keepdims=True)
    return (scaled - mean - xhat * lean) * inverse


def swap(value, axis, mask):
    count = lax.axis_size(axis)
    return lax.ppermute(value, axis, [(i, i ^ mask) for i in range(count)])


def bits_of(axis):
    return lax.axis_size(axis).bit_length() - 1


def gather_axis(value, axis):
    here = lax.axis_index(axis)
    bits = bits_of(axis)
    shape = value.shape
    for level in range(bits):
        bit = bits - 1 - level
        other = swap(value, axis, 1 << bit)
        low = (here >> bit) & 1 == 0
        value = jnp.stack([jnp.where(low, value, other), jnp.where(low, other, value)], axis=level)
    return value.reshape((1 << bits,) + shape)


def scatter_axis(value, axis):
    here = lax.axis_index(axis)
    bits = bits_of(axis)
    shape = value.shape[1:]
    value = value.reshape((2,) * bits + shape)
    for bit in range(bits):
        level = bits - 1 - bit
        zero, one = (lax.index_in_dim(value, i, level, keepdims=False) for i in (0, 1))
        low = (here >> bit) & 1 == 0
        value = jnp.where(low, zero, one) + swap(jnp.where(low, one, zero), axis, 1 << bit)
    return value.reshape(shape)


def sum_half(value, masks):
    here = lax.axis_index("dp")
    sides = {1: (here ^ (here >> 1)) & 1, 3: here >> 1}
    for mask in masks:
        zero, one = jnp.split(value, 2, axis=0)
        low = sides[mask] == 0
        value = jnp.where(low, zero, one) + swap(jnp.where(low, one, zero), "dp", mask)
    for mask in masks[::-1]:
        other = swap(value, "dp", mask)
        low = sides[mask] == 0
        value = jnp.concatenate([jnp.where(low, value, other), jnp.where(low, other, value)], axis=0)
    return value


def sum_sequences(value):
    if lax.axis_size("dp") != 4 or value.shape[0] % 64:
        return lax.psum(value, "dp")
    first, second = jnp.split(value, 2, axis=0)
    return jnp.concatenate([sum_half(first, (1, 3)), sum_half(second, (3, 1))], axis=0)


def halo_moves(group, reach, blocks):
    moves = []
    shift = 1
    while reach > 0 and shift < blocks:
        rows = min(group, reach)
        moves.append((rows, True, [(i, i - shift) for i in range(shift, blocks)]))
        moves.append((rows, False, [(i, i + shift) for i in range(blocks - shift)]))
        reach -= rows
        shift += 1
    return moves


def halo_get(value, reach, axis=0):
    blocks, group = lax.axis_size("blk"), value.shape[axis]
    if blocks == 2 and reach <= group:
        first = lax.slice_in_dim(value, 0, reach, axis=axis)
        last = lax.slice_in_dim(value, group - reach, group, axis=axis)
        return swap(jnp.where(lax.axis_index("blk") == 0, last, first), "blk", 1)
    parts = []
    for rows, right, moves in halo_moves(group, reach, blocks):
        start = 0 if right else group - rows
        parts.append(lax.ppermute(lax.slice_in_dim(value, start, start + rows, axis=axis), "blk", moves))
    return jnp.concatenate(parts, axis=axis)


def halo_add(value, halo, reach):
    blocks, group = lax.axis_size("blk"), value.shape[0]
    if blocks == 2 and reach <= group:
        back = swap(halo, "blk", 1)
        spare = ((0, group - reach), (0, 0))
        return value + jnp.where(lax.axis_index("blk") == 0, jnp.pad(back, ((group - reach, 0), (0, 0))), jnp.pad(back, spare))
    start = 0
    for rows, right, moves in halo_moves(group, reach, blocks):
        back = lax.ppermute(halo[start:start + rows], "blk", [(j, i) for i, j in moves])
        start += rows
        room = group - rows
        value = value + jnp.pad(back, ((0, room), (0, 0)) if right else ((room, 0), (0, 0)))
    return value


def local(
    hidden,
    time_embed,
    segment_ids,
    key_valid,
    out_grad,
    w_query,
    b_query,
    w_key,
    w_value,
    b_value,
    w_out,
    b_out,
    w_up,
    b_up,
    w_down,
    b_down,
    pre_gain,
    pre_shift,
    mlp_gain,
    mlp_shift,
):
    blocks, splits = lax.axis_size("blk"), lax.axis_size("ulys")
    here_b, here_u = lax.axis_index("blk"), lax.axis_index("ulys")
    both = ("blk", "ulys")
    owners = blocks * splits
    tokens, width = hidden.shape
    group = tokens * splits
    part = width // splits
    rows = w_query.shape[0]
    units = w_up.shape[1]
    unit_rows = w_down.shape[0]
    share = units // splits
    reach = group * blocks // 4

    def mine(value):
        return lax.dynamic_slice_in_dim(value, here_u * tokens, tokens, 0)

    small = jnp.concatenate([b_query, b_value, b_out, b_down, pre_gain, pre_shift, mlp_gain, mlp_shift, b_up])
    small_rows = -(-small.shape[0] // (3 * part))
    small_rows += -small_rows % 8
    small_pad = jnp.pad(small, (0, small_rows * 3 * part - small.shape[0])).reshape(1, small_rows, 3 * part)
    qkv_cut = jnp.stack([w_query, w_key, w_value], axis=1).reshape(rows, 3, splits, part)
    qkv_cut = qkv_cut.transpose(2, 0, 1, 3).reshape(splits, rows, 3 * part)
    message = jnp.concatenate([qkv_cut, jnp.broadcast_to(small_pad, (splits, small_rows, 3 * part))], axis=1)
    message = jnp.broadcast_to(message[None], (blocks,) + message.shape).reshape(owners, rows + small_rows, 3 * part)
    message = lax.all_to_all(message, both, 0, 0, tiled=True)
    base = gather_axis(hidden + time_embed, "ulys").reshape(group, width)
    own_segments = segment_ids[0] + 1
    own_codes = jnp.stack([own_segments, jnp.where(key_valid[0] == 1, own_segments, 0)]).astype(jnp.float32)
    halo_codes = halo_get(own_codes, reach, axis=1)
    w_qkv = message[:, :rows].reshape(width, 3 * part)
    smalls = message[:, rows:].reshape(owners, -1)
    vectors = [smalls[:, i * rows:(i + 1) * rows].reshape(width) for i in range(8)]
    full_qbias, full_vbias, full_obias, full_downbias, gain1, shift1, gain2, shift2 = vectors
    up_bias = smalls[:, 8 * rows:8 * rows + unit_rows].reshape(blocks, splits, unit_rows)
    up_bias = lax.dynamic_index_in_dim(up_bias, here_u, 1, keepdims=False).reshape(share)

    xhat1, inverse1 = normalize(base)
    normed = xhat1 * gain1 + shift1
    bias_here = jnp.concatenate(
        [
            lax.dynamic_slice_in_dim(full_qbias, here_u * part, part),
            jnp.zeros((part,), jnp.float32),
            lax.dynamic_slice_in_dim(full_vbias, here_u * part, part),
        ]
    )
    qkv = dot(normed, w_qkv) + bias_here
    query, key_value = qkv[:, :part], qkv[:, part:]

    window = group + halo_codes.shape[1]
    spare = -window % TILE
    halo = halo_get(key_value, reach)
    all_kv = jnp.pad(jnp.concatenate([key_value, halo], axis=0), ((0, spare), (0, 0)))
    all_codes = jnp.pad(jnp.concatenate([own_codes, halo_codes], axis=1), ((0, 0), (0, spare)))
    all_keys, all_values = all_kv[:, :part], all_kv[:, part:]
    window_segments = all_codes[0].astype(jnp.int32).reshape(-1, TILE)
    query_segments = own_segments.reshape(-1, TILE)
    bounds = jnp.concatenate(
        [
            jnp.stack([query_segments[:, 0], query_segments[:, -1]], axis=1),
            jnp.stack(
                [
                    jnp.min(jnp.where(window_segments == 0, 1 << 20, window_segments), axis=1),
                    jnp.max(window_segments, axis=1),
                ],
                axis=1,
            ),
        ],
        axis=0,
    ).reshape(1, -1)
    query_codes = own_codes[:1]
    key_codes = all_codes[1][:, None]
    attended, normalizer = attend(bounds, query_codes, key_codes, query, all_keys, all_values, TILE)

    full_out = lax.all_gather(w_out, both, axis=0, tiled=True)
    up_cut = w_up.reshape(rows, blocks, splits, unit_rows).transpose(2, 0, 1, 3).reshape(splits, rows, share)
    up_cut = jnp.broadcast_to(up_cut[None], (blocks,) + up_cut.shape).reshape(owners, rows, share)
    up_here = lax.all_to_all(up_cut, both, 0, 0, tiled=True).reshape(width, share)
    down_here = gather_axis(w_down, "blk").reshape(share, width)
    out_grads = gather_axis(out_grad, "ulys").reshape(group, width)

    attended_all = gather_axis(attended, "ulys")
    middle = base + full_obias
    for i in range(splits):
        middle = middle + dot(attended_all[i], full_out[i * part:(i + 1) * part])
    xhat2, inverse2 = normalize(middle)
    mlp_in = xhat2 * gain2 + shift2
    pre_act = dot(mlp_in, up_here) + up_bias
    curve = jnp.tanh(SQRT_2_PI * (pre_act + CUBIC * pre_act * pre_act * pre_act))
    activated = 0.5 * pre_act * (1.0 + curve)
    slope = 0.5 * (1.0 + curve) + 0.5 * pre_act * (1.0 - curve * curve) * SQRT_2_PI * (
        1.0 + 3.0 * CUBIC * pre_act * pre_act
    )
    pre_grad = dot_right_t(out_grads, down_here) * slope
    mlp_in_grads = dot_right_t(pre_grad, up_here)
    mlp_in_grad = scatter_axis(mlp_in_grads.reshape(splits, tokens, width), "ulys")
    grad_down = dot_left_t(activated, out_grads)
    grad_up = dot_left_t(mlp_in, pre_grad)
    output = scatter_axis(dot(activated, down_here).reshape(splits, tokens, width), "ulys")
    output = output + mine(middle) + full_downbias

    feed_grads = jnp.concatenate(
        [grad_down.reshape(blocks, unit_rows, width), grad_up.reshape(blocks, splits * rows, share)], axis=1
    )
    feed_grads = lax.psum_scatter(feed_grads, "blk", scatter_dimension=0, tiled=False)
    feed_grads = lax.psum(feed_grads, "dp")
    total_down = feed_grads[:unit_rows]
    total_up = lax.all_to_all(feed_grads[unit_rows:].reshape(splits, rows, share), "ulys", 0, 0, tiled=True)
    total_up = total_up.reshape(splits, rows, blocks, unit_rows).transpose(1, 2, 0, 3).reshape(rows, units)

    middle_grad = out_grad + normalize_back(mlp_in_grad, gain2, mine(xhat2), mine(inverse2))
    middle_grads = gather_axis(middle_grad, "ulys").reshape(group, width)
    out_here = lax.dynamic_slice_in_dim(full_out, here_u * part, part, 0)
    attended_grad = dot_right_t(middle_grads, out_here)
    grad_out = dot_left_t(attended, middle_grads)

    query_grad, keys_grad, values_grad = attend_back(
        bounds, query_codes, key_codes, query, all_keys, all_values, attended, attended_grad, normalizer, TILE
    )
    pair_grad = jnp.concatenate([keys_grad, values_grad], axis=1)
    pair_grad = halo_add(pair_grad[:group], pair_grad[group:window], reach)
    qkv_grad = jnp.concatenate([query_grad, pair_grad], axis=1)
    grad_qkv = dot_left_t(normed, qkv_grad)
    normed_grads = dot_right_t(qkv_grad, w_qkv)
    normed_grad = scatter_axis(normed_grads.reshape(splits, tokens, width), "ulys")
    hidden_grad = middle_grad + normalize_back(normed_grad, gain1, mine(xhat1), mine(inverse1))

    column_sums = jnp.sum(qkv_grad, axis=0)
    place = lambda piece: lax.dynamic_update_slice_in_dim(jnp.zeros((width,), jnp.float32), piece, here_u * part, 0)
    terms = [
        place(column_sums[:part]),
        place(column_sums[2 * part:]),
        jnp.sum(middle_grad, axis=0),
        jnp.sum(out_grad, axis=0),
        jnp.sum(normed_grads * xhat1, axis=0),
        jnp.sum(normed_grads, axis=0),
        jnp.sum(mlp_in_grads * xhat2, axis=0),
        jnp.sum(mlp_in_grads, axis=0),
    ]
    up_terms = lax.dynamic_update_slice_in_dim(
        jnp.zeros((blocks, splits, unit_rows), jnp.float32),
        jnp.sum(pre_grad, axis=0).reshape(blocks, 1, unit_rows),
        here_u,
        1,
    ).reshape(owners, unit_rows)
    terms = jnp.concatenate([term.reshape(owners, rows) for term in terms] + [up_terms], axis=1)
    terms = jnp.pad(terms, ((0, 0), (0, small_rows * 3 * part - terms.shape[1])))
    terms = terms.reshape(blocks, splits, small_rows, 3 * part)
    tail = jnp.concatenate([grad_qkv.reshape(blocks, splits, rows, 3 * part), terms], axis=2)
    tail = tail.reshape(blocks, splits * (rows + small_rows), 3 * part)
    tail = jnp.concatenate([tail, grad_out.reshape(blocks, -1, 3 * part)], axis=1)
    tail_rows = tail.shape[1]
    tail = jnp.pad(tail, ((0, 0), (0, -tail_rows % 64), (0, 0)))
    if blocks == 2:
        tail = scatter_axis(tail, "blk")
    else:
        tail = lax.psum_scatter(tail, "blk", scatter_dimension=0, tiled=False)
    tail = sum_sequences(tail)
    cut = splits * (rows + small_rows)
    total_out = tail[cut:tail_rows].reshape(rows, width)
    total_out = lax.ppermute(
        total_out, both, [(i * splits + j, j * blocks + i) for i in range(blocks) for j in range(splits)]
    )
    tail = lax.all_to_all(tail[:cut].reshape(splits, rows + small_rows, 3 * part), "ulys", 0, 0, tiled=True)
    total_qkv = tail[:, :rows].reshape(splits, rows, 3, part).transpose(2, 1, 0, 3).reshape(3, rows, width)
    sums = jnp.sum(tail[:, rows:], axis=0).reshape(-1)
    vector = [sums[i * rows:(i + 1) * rows] for i in range(8)]
    return (
        output,
        hidden_grad,
        total_qkv[0],
        vector[0],
        total_qkv[1],
        total_qkv[2],
        vector[1],
        total_out,
        vector[2],
        total_up,
        sums[8 * rows:8 * rows + unit_rows],
        total_down,
        vector[3],
        vector[4],
        vector[5],
        vector[6],
        vector[7],
    )


def solution(mesh):
    tokens = P(("dp", "blk", "ulys"), None)
    matrix = P(("blk", "ulys"), None)
    vector = P(("blk", "ulys"))
    return jax.shard_map(
        local,
        mesh=mesh,
        in_specs=(
            tokens,
            P("dp", None),
            P("dp", "blk"),
            P("dp", "blk"),
            tokens,
            matrix,
            vector,
            matrix,
            matrix,
            vector,
            matrix,
            vector,
            matrix,
            vector,
            matrix,
            vector,
            vector,
            vector,
            vector,
            vector,
        ),
        out_specs=(
            tokens,
            tokens,
            matrix,
            vector,
            matrix,
            matrix,
            vector,
            matrix,
            vector,
            matrix,
            vector,
            matrix,
            vector,
            vector,
            vector,
            vector,
            vector,
        ),
        check_vma=False,
    )
```

time: 1030 us -> 530 us (0.51)
  waiting for transfers between devices: 476 us -> 186 us
  matrix products: 211 us -> 67.5 us
  blocking collectives: 141 us -> 0 us
  starting transfers between devices: 19.3 us -> 82.3 us
  other arithmetic: 25.8 us -> 69.5 us
  loops' own time: 40.3 us -> 0 us
  Pallas kernels: 0 us -> 26.1 us
  local copies, waits for them, and re-layouts: 91.2 us -> 74.1 us
    reduce_scatter x7 -> x1, waiting for transfers between devices: 288 us -> 0.02 us  [local(): lax.psum_scatter(feed_grads, 'blk', scatter_dimension=0, tiled=False)]
    dot_general x31 -> x15, matrix products: 205 us -> 67.5 us  [the longest x7 25.2 us: dot(): return jnp.dot(left, right, precision=HIGH)]
    ppermute x0 -> x28, waiting for transfers between devices: none -> 126 us  [the longest x27 126 us: swap(): return lax.ppermute(value, axis, [(i, i ^ mask) for i in range(count)])]
    all_gather x7 -> x1, waiting for transfers between devices: 104 us -> 0.01 us  [local(): full_out = lax.all_gather(w_out, both, axis=0, tiled=True)]
    ppermute x0 -> x28, starting transfers between devices: none -> 65.4 us  [the longest x27 61.7 us: swap(): return lax.ppermute(value, axis, [(i, i ^ mask) for i in range(count)])]
    unnamed x2 -> x0, blocking collectives: 52.7 us -> none
    all_to_all x3 -> x0, blocking collectives: 48.4 us -> none  [the longest x1 20.1 us: local(): lax.all_to_all(local_pairs[:, :width], 'ulys', split_axis=0, concat_axis=...]
    another operation x2 -> x0, loops' own time: 40.3 us -> none  [over_blocks(): state, unused = lax.scan(visit, state, (kv_blocks, code_blocks, offsets))]
  transfers between devices with their start and end apart: 20 -> 35, of which waited for: 15 -> 18; matrix products, arithmetic and copies ran while one was open for 18% -> 32% of each run, Pallas kernels for 0% -> 5%
where the time goes in v1:
time: 530 us; the launch traced here: 521 us
  waiting for transfers between devices  186 us (35%)
  starting transfers between devices  82.3 us (16%)
  local copies, waits for them, and re-layouts  74.1 us (14%)
  other arithmetic  69.5 us (13%)
  matrix products  67.5 us (13%)
  Pallas kernels  26.1 us (5%)
  between operations  15.1 us (3%)
    ppermute x27, waiting for transfers between devices, swap(): return lax.ppermute(value, axis, [(i, i ^ mask) for i in range(count)])  126 us
    ppermute x27, starting transfers between devices, swap(): return lax.ppermute(value, axis, [(i, i ^ mask) for i in range(count)])  61.7 us
    psum x1, waiting for transfers between devices, local(): feed_grads = lax.psum(feed_grads, 'dp')  47.9 us
    dot_general x7, matrix products, dot(): return jnp.dot(left, right, precision=HIGH)  25.2 us
    another operation x18, other arithmetic, gather_axis(): jnp.stack([jnp.where(low, value, other), jnp.where(low, other, value)], a...  24.2 us
    dot_general x4, matrix products, dot_right_t(): lax.dot_general(left, right, (((1,), (1,)), ((), ())), precision=HIGH)  24.2 us
    dot_general x4, matrix products, dot_left_t(): lax.dot_general(left, right, (((0,), (0,)), ((), ())), precision=HIGH)  18.1 us
    pallas_call x1, Pallas kernels, attend_back(): pl.pallas_call(functools.partial(attend_back_kernel, tile, heads), out_sh...  17.3 us
  transfers between devices with their start and end apart: 35, of which 18 were waited for; matrix products, arithmetic and copies ran while one was open for 32% of the time, Pallas kernels for 5%

profile of v1, /device:TPU:0, one launch (start us, length us, event | category | flops | bytes accessed | tf_op | source)
XLA Modules:
  0.0 520.9 jit_solution(16632600912481829282)
XLA Ops:
  21.7 5.9 %collective-permute-done = f32[192,768]{1,0:T(8,128)} collective-permute-done((f32[192,768]{1,0:T(8,128)S(1)}, f32[192,768]{1,0:T(8,128)}, u32[]{:S(2)}, u32[]{:S(2)}) %collective-permute-start) | collective-permute-done | bytes 589856 | tf_op jit(solution)/shard_map/ppermute | solution.py:251
  30.1 9.1 %collective-permute-start.2 = (f32[2,384]{1,0:T(2,128)S(1)}, f32[2,384]{1,0:T(2,128)S(1)}, u32[]{:S(2)}, u32[]{:S(2)}) collective-permute-start(f32[2,384]{1,0:T(2,128)S(1)} %slice_select_fusion.5), channel_id=1, source_target_pairs={{0,4},{4,0},{1,5},{5,1},{2,6},{6,2},{3,7},{7,3},{8,12},{12,8},{9,1... | collective-permute-start | bytes 9224 | tf_op jit(solution)/shard_map/ppermute | solution.py:251
  42.8 7.3 %collective-permute-done.2 = f32[2,384]{1,0:T(2,128)S(1)} collective-permute-done((f32[2,384]{1,0:T(2,128)S(1)}, f32[2,384]{1,0:T(2,128)S(1)}, u32[]{:S(2)}, u32[]{:S(2)}) %collective-permute-start.2) | collective-permute-done | bytes 3104 | tf_op jit(solution)/shard_map/ppermute | solution.py:251
  67.6 9.9 %collective-permute-done.3 = f32[384,384]{1,0:T(8,128)S(1)} collective-permute-done((f32[384,384]{1,0:T(8,128)}, f32[384,384]{1,0:T(8,128)S(1)}, u32[]{:S(2)}, u32[]{:S(2)}) %collective-permute-start.3) | collective-permute-done | bytes 589856 | tf_op jit(solution)/shard_map/ppermute | solution.py:251
  78.1 8.8 %attend.1 = (f32[768,192]{1,0:T(8,128)S(1)}, f32[8,768]{1,0:T(8,128)S(1)}) custom-call(s32[1,16]{1,0:T(1,128)S(1)} %reshape.389.seg_ref, f32[1,768]{1,0:T(1,128)S(1)} %slice.289.qcode_ref, f32[1280,1]{1,0:T(8,128)S(1)} %copy.152.kcode_ref, f32[768,192]{1,0:T(8,128)S(1)} %slice.296.q_ref, f32[1280,192]{1,0:T(8,128)S(1)} %get-tuple-element.109.k_ref, ...), custom_call_target="tpu_custom_call" | custom-call | flops 1509949440 | bytes 3145728 | tf_op jit(solution)/shard_map/attend/pallas_call | solution.py:93
  92.9 6.1 %collective-permute-done.4 = f32[768,192]{0,1:T(8,128)S(1)} collective-permute-done((f32[768,192]{0,1:T(8,128)S(1)}, f32[768,192]{0,1:T(8,128)S(1)}, u32[]{:S(2)}, u32[]{:S(2)}) %collective-permute-start.4) | collective-permute-done | bytes 589856 | tf_op jit(solution)/shard_map/ppermute | solution.py:251
  117.1 4.4 all-to-all-start.1
  154.2 8.0 %fusion.9 = (f32[768,768]{0,1:T(8,128)}, f32[768,768]{1,0:T(8,128)}) fusion(f32[768]{0:T(1024)S(1)} %add.258, f32[768,768]{1,0:T(8,128)} %bitcast.27, f32[768,768]{1,0:T(8,128)} %subtract_multiply_fusion, f32[768]{0:T(1024)S(1)} %add.254, f32[768]{0:T(1024)S(1)} %mul.216), kind=kOutput, calls=%fused_computation.16 | convolution fusion | flops 2724397056 | bytes 9446400 | tf_op jit(solution)/shard_map/dot_general | solution.py:225
  165.4 7.8 %fusion.65 = (f32[768]{0:T(1024)}, f32[768,768]{0,1:T(8,128)S(1)}) fusion(f32[768,768]{0,1:T(8,128)} %copy.161, f32[768,768]{1,0:T(8,128)} %bitcast.209, f32[768,768]{1,0:T(8,128)} %bitcast.206), kind=kOutput, calls=%fused_computation.191 | convolution fusion | flops 2729114880 | bytes 9440256 | tf_op jit(solution)/shard_map/dot_general | solution.py:233
  173.2 9.0 %fusion.50 = (f32[768]{0:T(1024)}, f32[768]{0:T(1024)}, f32[768,768]{1,0:T(8,128)S(1)}) fusion(f32[768,768]{1,0:T(8,128)S(1)} %copy-done.6, f32[768,768]{0,1:T(8,128)S(1)} %get-tuple-element.160, f32[768,768]{1,0:T(8,128)} %bitcast.27), kind=kOutput, calls=%fused_computation.179 | convolution fusion | flops 2719676928 | bytes 9443328 | tf_op jit(solution)/shard_map/dot_general | solution.py:233
  195.6 5.9 %fusion.17 = f32[768,768]{1,0:T(8,128)S(1)} fusion(f32[768,768]{0,1:T(8,128)S(1)} %copy-done.22, f32[768,768]{1,0:T(8,128)S(1)} %copy-done.7, f32[768]{0:T(1024)S(1)} %add.254, f32[768]{0:T(1024)S(1)} %mul.216), kind=kOutput, calls=%fused_computation.41 | convolution fusion | flops 2719088640 | bytes 7084032 | tf_op jit(solution)/shard_map/dot_general | solution.py:229
  201.5 4.7 collective-permute-done.12
  211.5 10.6 %collective-permute-done.13 = f32[192,768]{1,0:T(8,128)} collective-permute-done((f32[192,768]{1,0:T(8,128)S(1)}, f32[192,768]{1,0:T(8,128)}, u32[]{:S(2)}, u32[]{:S(2)}) %collective-permute-start.13) | collective-permute-done | bytes 589856 | tf_op jit(solution)/shard_map/ppermute | solution.py:251
  225.2 4.4 add_bitcast_fusion
  233.0 3.8 add_multiply_fusion
  239.9 5.5 %fusion.15 = f32[2,2,192,768]{3,2,0,1:T(8,128)S(1)} fusion(f32[768,768,1,1]{1,0,2,3:T(8,128)} %bitcast.207, f32[2,2,192,768]{3,2,1,0:T(8,128)} %bitcast.212), kind=kOutput, calls=%fused_computation.29 | convolution fusion | flops 2717908992 | bytes 7077888 | tf_op jit(solution)/shard_map/dot_general | solution.py:225
  250.8 17.3 %attend_back.1 = (f32[768,192]{1,0:T(8,128)S(1)}, f32[1280,192]{1,0:T(8,128)S(1)}, f32[1280,192]{1,0:T(8,128)}) custom-call(s32[1,16]{1,0:T(1,128)S(1)} %reshape.389.seg_ref, f32[1,768]{1,0:T(1,128)S(1)} %slice.289.qcode_ref, f32[1280,1]{1,0:T(8,128)S(1)} %copy.152.kcode_ref, f32[768,192]{1,0:T(8,128)S(1)} %copy-done.3, f32[1280,192]{1,0:T(8,128)} %copy-done.1, ...), custom_call_target="tpu_custom_call" | custom-call | flops 3774873600 | bytes 6291456 | tf_op jit(solution)/shard_map/attend_back/pallas_call | solution.py:191
  278.1 8.4 %collective-permute-done.15 = f32[384,384]{1,0:T(8,128)} collective-permute-done((f32[384,384]{1,0:T(8,128)}, f32[384,384]{1,0:T(8,128)}, u32[]{:S(2)}, u32[]{:S(2)}) %collective-permute-start.15) | collective-permute-done | bytes 589856 | tf_op jit(solution)/shard_map/ppermute | solution.py:251
  289.0 6.2 %fusion.19 = f32[2,4,96,576]{3,2,1,0:T(8,128)} fusion(f32[2,4,96,768]{3,2,1,0:T(8,128)} %bitcast.208, f32[768,384]{1,0:T(8,128)S(1)} %fusion.25, f32[768,192]{1,0:T(8,128)S(1)} %get-tuple-element.24), kind=kOutput, calls=%fused_computation.48 | convolution fusion | flops 2038874112 | bytes 5898240 | tf_op jit(solution)/shard_map/dot_general | solution.py:229
  295.2 4.6 fusion.51
  311.4 27.8 %collective-permute-done.18 = f32[576,576]{1,0:T(8,128)} collective-permute-done((f32[576,576]{1,0:T(8,128)}, f32[576,576]{1,0:T(8,128)}, u32[]{:S(2)}, u32[]{:S(2)}) %collective-permute-start.18) | collective-permute-done | bytes 1327136 | tf_op jit(solution)/shard_map/ppermute | solution.py:251
  340.8 3.9 collective-permute-start.19
  344.7 4.0 collective-permute-start.23
  353.8 10.9 %collective-permute-done.23 = f32[144,576]{1,0:T(8,128)S(1)} collective-permute-done((f32[144,576]{1,0:T(8,128)S(1)}, f32[144,576]{1,0:T(8,128)S(1)}, u32[]{:S(2)}, u32[]{:S(2)}) %collective-permute-start.23) | collective-permute-done | bytes 331808 | tf_op jit(solution)/shard_map/ppermute | solution.py:251
  370.7 4.8 collective-permute-done.20
  378.9 5.8 %collective-permute-start.26 = (f32[144,576]{1,0:T(8,128)S(1)}, f32[144,576]{1,0:T(8,128)S(1)}, u32[]{:S(2)}, u32[]{:S(2)}) collective-permute-start(f32[144,576]{1,0:T(8,128)S(1)} %pad_maximum_fusion.20), channel_id=1, source_target_pairs={{0,24},{8,16},{16,8},{24,0},{1,25},{9,17},{17,9},{25,1},{2,26},{10... | collective-permute-start | bytes 995336 | tf_op jit(solution)/shard_map/ppermute | solution.py:251
  385.0 15.6 %collective-permute-start.22 = (f32[144,576]{1,0:T(8,128)S(1)}, f32[144,576]{1,0:T(8,128)S(1)}, u32[]{:S(2)}, u32[]{:S(2)}) collective-permute-start(f32[144,576]{1,0:T(8,128)S(1)} %pad_maximum_fusion.19), channel_id=1, source_target_pairs={{0,8},{8,0},{16,24},{24,16},{1,9},{9,1},{17,25},{25,17},{2,10},{10... | collective-permute-start | bytes 995336 | tf_op jit(solution)/shard_map/ppermute | solution.py:251
  403.2 21.5 %collective-permute-done.22 = f32[144,576]{1,0:T(8,128)S(1)} collective-permute-done((f32[144,576]{1,0:T(8,128)S(1)}, f32[144,576]{1,0:T(8,128)S(1)}, u32[]{:S(2)}, u32[]{:S(2)}) %collective-permute-start.22) | collective-permute-done | bytes 331808 | tf_op jit(solution)/shard_map/ppermute | solution.py:251
  425.8 4.3 all-to-all-start.2
  436.9 47.9 %all-reduce.9.cloned.1.call-done = f32[768,768]{1,0:T(8,128)} async-done(((f32[768,768]{1,0:T(8,128)}), f32[768,768]{1,0:T(8,128)}) %all-reduce.9.cloned.1.call-update) | async-done | bytes 2359312 | tf_op jit(solution)/shard_map/psum | solution.py:470
  487.9 4.4 all-to-all-start.3
  499.9 8.4 %all-to-all-done.3 = f32[4,96,768]{2,1,0:T(8,128)} async-done(((f32[4,96,768]{2,1,0:T(8,128)}), f32[4,96,768]{2,1,0:T(8,128)}, u32[]{:S(2)}, u32[]{:S(2)}) %all-to-all-start.3) | async-done | bytes 1179680 | tf_op jit(solution)/shard_map/all_to_all | solution.py:472
  (334 shorter events, 199.1 us)
Async XLA Ops:
  9.1 18.6 %collective-permute-start = (f32[192,768]{1,0:T(8,128)S(1)}, f32[192,768]{1,0:T(8,128)}, u32[]{:S(2)}, u32[]{:S(2)}) collective-permute-start(f32[192,768]{1,0:T(8,128)S(1)} %broadcast_add_fusion), channel_id=1, source_target_pairs={{0,2},{1,3},{2,0},{3,1},{4,6},{5,7},{6,4},{7,5},{8,10},{9,11},{10,... | collective-permute-start | bytes 1769480 | tf_op jit(solution)/shard_map/ppermute | solution.py:251
  17.2 35.8 %all-to-all-start = ((f32[8,104,576]{2,1,0:T(8,128)}), f32[8,104,576]{2,1,0:T(8,128)S(1)}, u32[]{:S(2)}, u32[]{:S(2)}) async-start(f32[8,104,576]{2,1,0:T(8,128)} %bitcast.220), calls=%async_computation | async-start | bytes 4259840 | tf_op jit(solution)/shard_map/all_to_all | solution.py:390
  20.9 121.1 %all-gather.2.cloned.1.call-start = ((), (), s32[]{:S(2)}) async-start(), calls=%async_computation.5 | async-start | bytes 2654208 | tf_op jit(solution)/shard_map/all_gather | solution.py:439
  30.1 25.9 %collective-permute-start.1 = (f32[2,192,768]{2,1,0:T(8,128)}, f32[2,192,768]{2,1,0:T(8,128)}, u32[]{:S(2)}, u32[]{:S(2)}) collective-permute-start(f32[2,192,768]{2,1,0:T(8,128)} %pad_maximum_fusion.11), channel_id=1, source_target_pairs={{0,1},{1,0},{2,3},{3,2},{4,5},{5,4},{6,7},{7,6},{8,9},{9,8},{10,11... | collective-permute-start | bytes 3538952 | tf_op jit(solution)/shard_map/ppermute | solution.py:251
  30.1 20.0 %collective-permute-start.2 = (f32[2,384]{1,0:T(2,128)S(1)}, f32[2,384]{1,0:T(2,128)S(1)}, u32[]{:S(2)}, u32[]{:S(2)}) collective-permute-start(f32[2,384]{1,0:T(2,128)S(1)} %slice_select_fusion.5), channel_id=1, source_target_pairs={{0,4},{4,0},{1,5},{5,1},{2,6},{6,2},{3,7},{7,3},{8,12},{12,8},{9,1... | collective-permute-start | bytes 9224 | tf_op jit(solution)/shard_map/ppermute | solution.py:251
  39.2 50.6 %collective-permute-start.9 = (f32[192,768]{1,0:T(8,128)}, f32[192,768]{1,0:T(8,128)}, u32[]{:S(2)}, u32[]{:S(2)}) collective-permute-start(f32[192,768]{1,0:T(8,128)} %param.24), channel_id=1, source_target_pairs={{0,2},{1,3},{2,0},{3,1},{4,6},{5,7},{6,4},{7,5},{8,10},{9,11},{10,... | collective-permute-start | bytes 1769480 | tf_op jit(solution)/shard_map/ppermute | solution.py:251
  65.2 12.3 %collective-permute-start.3 = (f32[384,384]{1,0:T(8,128)}, f32[384,384]{1,0:T(8,128)S(1)}, u32[]{:S(2)}, u32[]{:S(2)}) collective-permute-start(f32[384,384]{1,0:T(8,128)} %slice_select_fusion), channel_id=1, source_target_pairs={{0,4},{4,0},{1,5},{5,1},{2,6},{6,2},{3,7},{7,3},{8,12},{12,8},{9,1... | collective-permute-start | bytes 1769480 | tf_op jit(solution)/shard_map/ppermute | solution.py:251
  87.7 11.2 %collective-permute-start.4 = (f32[768,192]{0,1:T(8,128)S(1)}, f32[768,192]{0,1:T(8,128)S(1)}, u32[]{:S(2)}, u32[]{:S(2)}) collective-permute-start(f32[768,192]{0,1:T(8,128)S(1)} %copy.153), channel_id=1, source_target_pairs={{0,2},{1,3},{2,0},{3,1},{4,6},{5,7},{6,4},{7,5},{8,10},{9,11},{10,... | collective-permute-start | bytes 1769480 | tf_op jit(solution)/shard_map/ppermute | solution.py:251
  89.3 32.2 %collective-permute-start.6 = (f32[384,768]{1,0:T(8,128)}, f32[384,768]{1,0:T(8,128)}, u32[]{:S(2)}, u32[]{:S(2)}) collective-permute-start(f32[384,768]{1,0:T(8,128)} %param.34), channel_id=1, source_target_pairs={{0,4},{4,0},{1,5},{5,1},{2,6},{6,2},{3,7},{7,3},{8,12},{12,8},{9,1... | collective-permute-start | bytes 3538952 | tf_op jit(solution)/shard_map/ppermute | solution.py:251
  92.9 35.7 %collective-permute-start.10 = (f32[2,192,768]{2,1,0:T(8,128)}, f32[2,192,768]{2,1,0:T(8,128)}, u32[]{:S(2)}, u32[]{:S(2)}) collective-permute-start(f32[2,192,768]{2,1,0:T(8,128)} %pad_maximum_fusion.14), channel_id=1, source_target_pairs={{0,1},{1,0},{2,3},{3,2},{4,5},{5,4},{6,7},{7,6},{8,9},{9,8},{10,11... | collective-permute-start | bytes 3538952 | tf_op jit(solution)/shard_map/ppermute | solution.py:251
  105.4 26.2 %collective-permute-start.5 = (f32[2,768,192]{1,2,0:T(8,128)}, f32[2,768,192]{1,2,0:T(8,128)}, u32[]{:S(2)}, u32[]{:S(2)}) collective-permute-start(f32[2,768,192]{1,2,0:T(8,128)} %copy.156), channel_id=1, source_target_pairs={{0,1},{1,0},{2,3},{3,2},{4,5},{5,4},{6,7},{7,6},{8,9},{9,8},{10,11... | collective-permute-start | bytes 3538952 | tf_op jit(solution)/shard_map/ppermute | solution.py:251
  117.1 37.1 %all-to-all-start.1 = ((f32[8,96,768]{2,1,0:T(8,128)}), f32[8,96,768]{2,1,0:T(8,128)}, u32[]{:S(2)}, u32[]{:S(2)}) async-start(f32[8,96,768]{2,1,0:T(8,128)} %bitcast.217), calls=%async_computation.1 | async-start | bytes 4718592 | tf_op jit(solution)/shard_map/all_to_all | solution.py:442
  121.5 249.2 %reduce-scatter.2.cloned.1.call-start = ((), (), s32[]{:S(2)}) async-start(), calls=%async_computation.6 | async-start | bytes 7077888 | tf_op jit(solution)/shard_map/reduce_scatter | solution.py:469
  190.7 15.5 %collective-permute-start.12 = (f32[192,768]{1,0:T(8,128)S(1)}, f32[192,768]{1,0:T(8,128)S(1)}, u32[]{:S(2)}, u32[]{:S(2)}) collective-permute-start(f32[192,768]{1,0:T(8,128)S(1)} %select_bitcast_fusion.19), channel_id=1, source_target_pairs={{0,2},{1,3},{2,0},{3,1},{4,6},{5,7},{6,4},{7,5},{8,10},{9,11},{10,... | collective-permute-start | bytes 1769480 | tf_op jit(solution)/shard_map/ppermute | solution.py:251
  207.2 14.9 %collective-permute-start.13 = (f32[192,768]{1,0:T(8,128)S(1)}, f32[192,768]{1,0:T(8,128)}, u32[]{:S(2)}, u32[]{:S(2)}) collective-permute-start(f32[192,768]{1,0:T(8,128)S(1)} %get-tuple-element.91), channel_id=1, source_target_pairs={{0,2},{1,3},{2,0},{3,1},{4,6},{5,7},{6,4},{7,5},{8,10},{9,11},{10,... | collective-permute-start | bytes 1769480 | tf_op jit(solution)/shard_map/ppermute | solution.py:251
  211.4 273.3 %all-reduce.9.cloned.1.call-start = ((), (), s32[]{:S(2)}) async-start(), calls=%async_computation.7 | async-start | bytes 4718592 | tf_op jit(solution)/shard_map/psum | solution.py:470
  224.3 21.0 %collective-permute-start.14 = (f32[2,192,768]{2,1,0:T(8,128)}, f32[2,192,768]{2,1,0:T(8,128)}, u32[]{:S(2)}, u32[]{:S(2)}) collective-permute-start(f32[2,192,768]{2,1,0:T(8,128)} %pad_maximum_fusion.15), channel_id=1, source_target_pairs={{0,1},{1,0},{2,3},{3,2},{4,5},{5,4},{6,7},{7,6},{8,9},{9,8},{10,11... | collective-permute-start | bytes 3538952 | tf_op jit(solution)/shard_map/ppermute | solution.py:251
  270.2 16.3 %collective-permute-start.15 = (f32[384,384]{1,0:T(8,128)}, f32[384,384]{1,0:T(8,128)}, u32[]{:S(2)}, u32[]{:S(2)}) collective-permute-start(f32[384,384]{1,0:T(8,128)} %pad_maximum_fusion.18), channel_id=1, source_target_pairs={{0,4},{4,0},{1,5},{5,1},{2,6},{6,2},{3,7},{7,3},{8,12},{12,8},{9,1... | collective-permute-start | bytes 1769480 | tf_op jit(solution)/shard_map/ppermute | solution.py:251
  273.3 33.3 %collective-permute-start.7 = (f32[2,192,768]{2,1,0:T(8,128)}, f32[2,192,768]{2,1,0:T(8,128)}, u32[]{:S(2)}, u32[]{:S(2)}) collective-permute-start(f32[2,192,768]{2,1,0:T(8,128)} %select_bitcast_fusion.9), channel_id=1, source_target_pairs={{0,1},{1,0},{2,3},{3,2},{4,5},{5,4},{6,7},{7,6},{8,9},{9,8},{10,11... | collective-permute-start | bytes 3538952 | tf_op jit(solution)/shard_map/ppermute | solution.py:251
  304.8 34.3 %collective-permute-start.18 = (f32[576,576]{1,0:T(8,128)}, f32[576,576]{1,0:T(8,128)}, u32[]{:S(2)}, u32[]{:S(2)}) collective-permute-start(f32[576,576]{1,0:T(8,128)} %select_bitcast_fusion.2), channel_id=1, source_target_pairs={{0,4},{4,0},{1,5},{5,1},{2,6},{6,2},{3,7},{7,3},{8,12},{12,8},{9,1... | collective-permute-start | bytes 3981320 | tf_op jit(solution)/shard_map/ppermute | solution.py:251
  309.5 41.4 %collective-permute-start.16 = (f32[2,192,768]{2,1,0:T(8,128)S(1)}, f32[2,192,768]{2,1,0:T(8,128)S(1)}, u32[]{:S(2)}, u32[]{:S(2)}) collective-permute-start(f32[2,192,768]{2,1,0:T(8,128)S(1)} %select_bitcast_fusion.3), channel_id=1, source_target_pairs={{0,1},{1,0},{2,3},{3,2},{4,5},{5,4},{6,7},{7,6},{8,9},{9,8},{10,11... | collective-permute-start | bytes 3538952 | tf_op jit(solution)/shard_map/ppermute | solution.py:251
  309.6 39.1 %collective-permute-start.8 = (f32[192,768]{1,0:T(8,128)S(1)}, f32[192,768]{1,0:T(8,128)S(1)}, u32[]{:S(2)}, u32[]{:S(2)}) collective-permute-start(f32[192,768]{1,0:T(8,128)S(1)} %select_bitcast_fusion.22), channel_id=1, source_target_pairs={{0,2},{1,3},{2,0},{3,1},{4,6},{5,7},{6,4},{7,5},{8,10},{9,11},{10,... | collective-permute-start | bytes 1769480 | tf_op jit(solution)/shard_map/ppermute | solution.py:251
  340.8 12.9 %collective-permute-start.19 = (f32[144,576]{1,0:T(8,128)S(1)}, f32[144,576]{1,0:T(8,128)S(1)}, u32[]{:S(2)}, u32[]{:S(2)}) collective-permute-start(f32[144,576]{1,0:T(8,128)S(1)} %get-tuple-element.114), channel_id=1, source_target_pairs={{0,8},{8,0},{16,24},{24,16},{1,9},{9,1},{17,25},{25,17},{2,10},{10... | collective-permute-start | bytes 995336 | tf_op jit(solution)/shard_map/ppermute | solution.py:251
  344.7 20.0 %collective-permute-start.23 = (f32[144,576]{1,0:T(8,128)S(1)}, f32[144,576]{1,0:T(8,128)S(1)}, u32[]{:S(2)}, u32[]{:S(2)}) collective-permute-start(f32[144,576]{1,0:T(8,128)S(1)} %get-tuple-element.115), channel_id=1, source_target_pairs={{0,24},{8,16},{16,8},{24,0},{1,25},{9,17},{17,9},{25,1},{2,26},{10... | collective-permute-start | bytes 995336 | tf_op jit(solution)/shard_map/ppermute | solution.py:251
  365.0 10.5 %collective-permute-start.20 = (f32[72,576]{1,0:T(8,128)S(1)}, f32[72,576]{1,0:T(8,128)S(1)}, u32[]{:S(2)}, u32[]{:S(2)}) collective-permute-start(f32[72,576]{1,0:T(8,128)S(1)} %slice_select_fusion.4), channel_id=1, source_target_pairs={{0,24},{8,16},{16,8},{24,0},{1,25},{9,17},{17,9},{25,1},{2,26},{10... | collective-permute-start | bytes 497672 | tf_op jit(solution)/shard_map/ppermute | solution.py:251
  375.5 9.4 %collective-permute-start.21 = (f32[72,576]{1,0:T(8,128)S(1)}, f32[72,576]{1,0:T(8,128)S(1)}, u32[]{:S(2)}, u32[]{:S(2)}) collective-permute-start(f32[72,576]{1,0:T(8,128)S(1)} %select_add_fusion.3), channel_id=1, source_target_pairs={{0,24},{8,16},{16,8},{24,0},{1,25},{9,17},{17,9},{25,1},{2,26},{10... | collective-permute-start | bytes 497672 | tf_op jit(solution)/shard_map/ppermute | solution.py:251
  378.9 23.5 %collective-permute-start.26 = (f32[144,576]{1,0:T(8,128)S(1)}, f32[144,576]{1,0:T(8,128)S(1)}, u32[]{:S(2)}, u32[]{:S(2)}) collective-permute-start(f32[144,576]{1,0:T(8,128)S(1)} %pad_maximum_fusion.20), channel_id=1, source_target_pairs={{0,24},{8,16},{16,8},{24,0},{1,25},{9,17},{17,9},{25,1},{2,26},{10... | collective-permute-start | bytes 995336 | tf_op jit(solution)/shard_map/ppermute | solution.py:251
  385.0 39.7 %collective-permute-start.22 = (f32[144,576]{1,0:T(8,128)S(1)}, f32[144,576]{1,0:T(8,128)S(1)}, u32[]{:S(2)}, u32[]{:S(2)}) collective-permute-start(f32[144,576]{1,0:T(8,128)S(1)} %pad_maximum_fusion.19), channel_id=1, source_target_pairs={{0,8},{8,0},{16,24},{24,16},{1,9},{9,1},{17,25},{25,17},{2,10},{10... | collective-permute-start | bytes 995336 | tf_op jit(solution)/shard_map/ppermute | solution.py:251
  401.4 28.7 %collective-permute-start.17 = (f32[192,768]{1,0:T(8,128)}, f32[192,768]{1,0:T(8,128)}, u32[]{:S(2)}, u32[]{:S(2)}) collective-permute-start(f32[192,768]{1,0:T(8,128)} %select_bitcast_fusion.16), channel_id=1, source_target_pairs={{0,2},{1,3},{2,0},{3,1},{4,6},{5,7},{6,4},{7,5},{8,10},{9,11},{10,... | collective-permute-start | bytes 1769480 | tf_op jit(solution)/shard_map/ppermute | solution.py:251
  425.8 62.1 %all-to-all-start.2 = ((f32[4,104,576]{2,1,0:T(8,128)}), f32[4,104,576]{2,1,0:T(8,128)}, u32[]{:S(2)}, u32[]{:S(2)}) async-start(f32[4,104,576]{2,1,0:T(8,128)} %bitcast.227), calls=%async_computation.2 | async-start | bytes 2129920 | tf_op jit(solution)/shard_map/all_to_all | solution.py:528
  433.1 60.2 %collective-permute-start.27 = (f32[96,768]{1,0:T(8,128)}, f32[96,768]{1,0:T(8,128)}, u32[]{:S(2)}, u32[]{:S(2)}) collective-permute-start(f32[96,768]{1,0:T(8,128)} %reshape.415), channel_id=1, source_target_pairs={{0,0},{1,2},{2,4},{3,6},{4,1},{5,3},{6,5},{7,7},{8,8},{9,10},{10,1... | collective-permute-start | bytes 884744 | tf_op jit(solution)/shard_map/ppermute | solution.py:525
  487.9 20.3 %all-to-all-start.3 = ((f32[4,96,768]{2,1,0:T(8,128)}), f32[4,96,768]{2,1,0:T(8,128)}, u32[]{:S(2)}, u32[]{:S(2)}) async-start(f32[4,96,768]{2,1,0:T(8,128)} %bitcast.226), calls=%async_computation.4 | async-start | bytes 2359296 | tf_op jit(solution)/shard_map/all_to_all | solution.py:472
  (50 other events, 288.0 us)
Sparse Core Ops, SparseCore 0:
  23.7 43.4 all-gather.1
  211.6 61.7 reduce-scatter.1
  370.8 113.8 all-reduce.8

commit v2 on v1

v2 whole, which is shorter than its diff:
```python
import functools
import math

import jax
import jax.numpy as jnp
from jax import lax
from jax.experimental import pallas as pl
from jax.experimental.pallas import tpu as pltpu
from jax.sharding import PartitionSpec as P

HEAD_DIM = 64
FLOOR = -1e30
SQRT_2_PI = 0.7978845608028654
CUBIC = 0.044715
EXTRA = 16
TILE = 256
EDGE = 128
BF = jnp.bfloat16
F32 = jnp.float32
NN = (((1,), (0,)), ((), ()))
NT = (((1,), (1,)), ((), ()))
TN = (((0,), (0,)), ((), ()))
VM = pl.BlockSpec(memory_space=pltpu.VMEM)
SM = pl.BlockSpec(memory_space=pltpu.SMEM)
LIMITS = {"attend_own": 10, "attend_edge": 10, "back_edge": 12, "back_own": 12, "act": 14, "weights": 16, "feed_grads": 12, "place": 8, "hidden": 6, "middle": 6, "last_grads": 16, "pack": 8}


def split(x):
    hi = x.astype(BF)
    return hi, (x - hi.astype(F32)).astype(BF)


def mm(a, b, dims=NN):
    return lax.dot_general(a, b, dims, preferred_element_type=F32)


def mm3(a, b, dims=NN):
    return mm(a[0], b[0], dims) + (mm(a[0], b[1], dims) + mm(a[1], b[0], dims))


def at(start, size, step=8):
    return pl.ds(pl.multiple_of(start, step), size)


def call(kernel, name, outs, ins, scratch=(), flops=0, smem=1, limit=16, wide=False):
    size = sum(math.prod(x.shape) * x.dtype.itemsize for x in list(outs) + list(ins[smem:]))
    return pl.pallas_call(
        kernel,
        out_shape=tuple(outs),
        in_specs=[SM] * smem + [VM] * (len(ins) - smem),
        out_specs=tuple(VM for _ in outs),
        scratch_shapes=list(scratch),
        compiler_params=pltpu.CompilerParams(vmem_limit_bytes=(48 if wide else LIMITS.get(name, limit)) << 20),
        cost_estimate=pl.CostEstimate(flops=3 * flops, bytes_accessed=size, transcendentals=0),
        name=name,
    )(*ins)


def arr(shape, dtype=F32):
    return jax.ShapeDtypeStruct(tuple(shape), dtype)


def norm(x):
    centred = x - jnp.mean(x, axis=-1, keepdims=True)
    inverse = lax.rsqrt(jnp.mean(centred * centred, axis=-1, keepdims=True) + 1e-05)
    return centred * inverse, inverse


def norm_back(grad, gain, xhat, inverse):
    scaled = grad * gain
    mean = jnp.mean(scaled, axis=-1, keepdims=True)
    lean = jnp.mean(scaled * xhat, axis=-1, keepdims=True)
    return (scaled - mean - xhat * lean) * inverse


def pick(index, choices):
    value = choices[0]
    for i in range(1, len(choices)):
        value = jnp.where(index == i, choices[i], value)
    return value


def pack_kernel(blocks, idx, wq, wk, wv, wup, wout, near, far, near2, far2):
    part, share = near.shape[2] // 3, near2.shape[2]
    splits = wq.shape[1] // part
    unit = share // blocks
    for r in range(splits):
        first, second, k = (near, near2, r) if r < 2 else (far, far2, r - 2)
        for u in range(splits):

            @pl.when(idx[0, r] == u)
            def _():
                for i, w in enumerate((wq, wk, wv)):
                    first[k, :, i * part:(i + 1) * part] = w[:, u * part:(u + 1) * part]
                for b in range(blocks):
                    lane = (b * splits + u) * unit
                    second[k, :, b * unit:(b + 1) * unit] = wup[:, lane:lane + unit]
    near2[2] = wout[...]
    far2[2] = wout[...]


def qkv_kernel(pieces, splits, edge, idx, *refs):
    base, rest = refs[:splits], refs[splits:]
    count = max(p[0] for p in pieces) + 1
    weights = rest[:count]
    (q_ref, kv_ref, edge_ref, base_ref, small_ref, wh, wl, w32, nh, nl) = rest[count:count + 10]
    got = base + weights
    tokens = base[0].shape[0] - EXTRA
    part = q_ref.shape[1]
    rows = w32.shape[0] // len(pieces)
    small = None
    for r in range(splits):
        rest = got[r][tokens:, :]
        small = rest if small is None else small + rest
    small_ref[...] = small
    gain, shift = small[4:5], small[5:6]
    for r in range(splits):
        row = at(idx[0, r] * tokens, tokens, 16)
        x = got[r][:tokens, :]
        base_ref[row, :] = x
        xhat, _ = norm(x)
        nh[row, :], nl[row, :] = split(xhat * gain + shift)
    for i, (n, lead) in enumerate(pieces):
        w32[at(idx[0, splits + i] * rows, rows), :] = got[splits + n][lead, :rows, :]
    wh[...], wl[...] = split(w32[...])
    u = idx[0, 0]
    qb = pick(u, [small[0:1, i * part:(i + 1) * part] for i in range(splits)])
    vb = pick(u, [small[1:2, i * part:(i + 1) * part] for i in range(splits)])
    bias = jnp.concatenate([qb, jnp.zeros_like(qb), vb], axis=1)
    step = nh.shape[0] // 2

    def rows_of(i, _):
        row = at(i * step, step, 16)
        out = mm3((nh[row, :], nl[row, :]), (wh[...], wl[...])) + bias
        q_ref[row, :] = out[:, :part]
        kv_ref[row, :] = out[:, part:]
        return 0

    lax.fori_loop(0, 2, rows_of, 0)
    reach = edge_ref.shape[0]
    edge_ref[...] = kv_ref[at(idx[0, edge], reach), :]


def span_hits(seg, i, j):
    return (seg[0, 2 * j + 1] >= seg[0, 2 * i]) & (seg[0, 2 * j] <= seg[0, 2 * i + 1])


def prepare(src, width, first, count, size, pairs, flipped):
    heads = width // HEAD_DIM
    for scratch, start in pairs:
        for h in range(heads):
            hi, lo = split(src[:, start + h * HEAD_DIM:start + (h + 1) * HEAD_DIM])
            scratch[h] = jnp.concatenate([hi, lo, hi], axis=1)
    for j in range(count):
        turned = src[j * size:(j + 1) * size, first:first + width].T
        for h in range(heads):
            hi, lo = split(turned[h * HEAD_DIM:(h + 1) * HEAD_DIM])
            flipped[h, j] = jnp.concatenate([hi, lo], axis=0)


def columns(codes, out, size):
    for j in range(out.shape[0] // size):
        row = codes[:, j * size:(j + 1) * size]
        out[j * size:(j + 1) * size, :] = jnp.broadcast_to(row, (128, size)).T


def same_row(i, j):
    return (lax.broadcasted_iota(jnp.int32, (TILE, TILE), 0)
            - lax.broadcasted_iota(jnp.int32, (TILE, TILE), 1)) == (i - j) * TILE


def attend_add(heads, qc, keys, flipped, m_s, l_s, acc, i, j, size, allowed):
    qrow = at(i * TILE, TILE, TILE)
    krow = at(j * size, size, size)
    for h in range(heads):
        s = jnp.where(allowed, mm(keys[h, krow, :], qc[h, qrow, :], NT), FLOOR)
        m_old = m_s[h, i]
        m_new = jnp.maximum(m_old, jnp.max(s, axis=0, keepdims=True))
        p = jnp.where(allowed, jnp.exp(s - m_new), 0.0)
        factor = jnp.exp(m_old - m_new)
        m_s[h, i] = m_new
        l_s[h, i] = l_s[h, i] * factor + jnp.sum(p, axis=0, keepdims=True)
        hi, lo = split(p)
        v128 = flipped[h, j]
        acc[h, i] = acc[h, i] * factor + mm(v128, hi) + mm(v128, lo)


def attend_own_kernel(heads, seg_ref, qcode_ref, kcode_ref, q_ref, kv_ref, qc, m_s, l_s, acc, kc, vt, kcol):
    group, width = q_ref.shape
    nq = group // TILE
    for h in range(heads):
        hi, lo = split(q_ref[:, h * HEAD_DIM:(h + 1) * HEAD_DIM] * HEAD_DIM ** -0.5)
        qc[h] = jnp.concatenate([hi, hi, lo], axis=1)
    prepare(kv_ref, width, width, nq, TILE, [(kc, 0)], vt)
    columns(kcode_ref, kcol, TILE)
    m_s[...] = jnp.full_like(m_s, FLOOR)
    l_s[...] = jnp.zeros_like(l_s)
    acc[...] = jnp.zeros_like(acc)

    def per_q(i, _):
        def per_k(j, _):
            @pl.when(span_hits(seg_ref, i, j))
            def _():
                allowed = kcol[at(j * TILE, TILE, TILE), :1] == qcode_ref[:, at(i * TILE, TILE, TILE)]
                attend_add(heads, qc, kc, vt, m_s, l_s, acc, i, j, TILE, allowed | same_row(i, j))
            return 0

        lax.fori_loop(0, nq, per_k, 0)
        return 0

    lax.fori_loop(0, nq, per_q, 0)


def attend_edge_kernel(heads, seg_ref, qcode_ref, hcode_ref, halo_ref, qc, m_in, l_in, acc_in,
                       out_ref, wide_ref, lse_ref, kh, vh, hcol, m_s, l_s, acc):
    group, width = out_ref.shape
    nq, nh = group // TILE, halo_ref.shape[0] // EDGE
    m_s[...] = m_in[...]
    l_s[...] = l_in[...]
    acc[...] = acc_in[...]
    if nh:
        prepare(halo_ref, width, width, nh, EDGE, [(kh, 0)], vh)
        columns(hcode_ref, hcol, EDGE)

    def per_q(i, _):
        qrow = at(i * TILE, TILE, TILE)

        def per_edge(j, _):
            @pl.when(span_hits(seg_ref, i, nq + j))
            def _():
                allowed = hcol[at(j * EDGE, EDGE, EDGE), :1] == qcode_ref[:, qrow]
                attend_add(heads, qc, kh, vh, m_s, l_s, acc, i, j, EDGE, allowed)
            return 0

        if nh:
            lax.fori_loop(0, nh, per_edge, 0)
        parts = []
        for h in range(heads):
            total = l_s[h, i]
            parts.append((acc[h, i, :HEAD_DIM] + acc[h, i, HEAD_DIM:]) / total)
            lse_ref[h:h + 1, qrow] = m_s[h, i] + jnp.log(total)
        out_ref[qrow, :] = jnp.concatenate(parts, axis=0).T
        return 0

    lax.fori_loop(0, nq, per_q, 0)
    wide_ref[:, :width] = out_ref[:group // 2, :]
    wide_ref[:, width:] = out_ref[group // 2:, :]


def attend_own(segs, qcode, kcode, q, kv):
    group, width = q.shape
    heads, nq = width // HEAD_DIM, group // TILE
    return call(
        functools.partial(attend_own_kernel, heads), "attend_own",
        [arr((heads, group, 3 * HEAD_DIM), BF), arr((heads, nq, 1, TILE)), arr((heads, nq, 1, TILE)),
         arr((heads, nq, 2 * HEAD_DIM, TILE))],
        [segs, qcode, kcode, q, kv],
        [pltpu.VMEM((heads, group, 3 * HEAD_DIM), BF), pltpu.VMEM((heads, nq, 2 * HEAD_DIM, TILE), BF),
         pltpu.VMEM((group, 128), F32)],
        flops=4 * group * group * width)


def attend_edge(segs, qcode, hcode, halo, state):
    heads, group, _ = state[0].shape
    reach, width = halo.shape[0], halo.shape[1] // 2
    nq, nh = group // TILE, reach // EDGE
    return call(
        functools.partial(attend_edge_kernel, heads), "attend_edge",
        [arr((group, width)), arr((group // 2, 2 * width)), arr((8, group))],
        [segs, qcode, hcode, halo, *state],
        [pltpu.VMEM((heads, reach, 3 * HEAD_DIM), BF), pltpu.VMEM((heads, nh, 2 * HEAD_DIM, EDGE), BF),
         pltpu.VMEM((reach, 128), F32)]
        + [pltpu.VMEM(x.shape, x.dtype) for x in state[1:]],
        flops=2 * group * reach * width, wide=reach > group)


def back_add(heads, qc, q2, dc, d2, dot_s, lse_ref, keys, values, flipped, dqa, dka, dva, i, j, size, allowed):
    qrow = at(i * TILE, TILE, TILE)
    krow = at(j * size, size, size)
    for h in range(heads):
        s = mm(keys[h, krow, :], qc[h, qrow, :], NT)
        p = jnp.exp(jnp.where(allowed, s - lse_ref[h:h + 1, qrow], FLOOR))
        dp = mm(values[h, krow, :], dc[h, qrow, :], NT)
        ds = p * (dp - dot_s[h, :, qrow])
        hi, lo = split(p)
        d128 = d2[h, qrow, :]
        dva[h] += mm(hi, d128) + mm(lo, d128)
        hi, lo = split(ds)
        q128 = q2[h, qrow, :]
        dka[h] += mm(hi, q128) + mm(lo, q128)
        k128 = flipped[h, j]
        dqa[h, i] += mm(k128, hi) + mm(k128, lo)


def back_over(heads, seg_ref, nq, count, size, first, out, dka, dva, visit):
    width = heads * HEAD_DIM

    def folded(acc):
        return jnp.concatenate([acc[h, :, :HEAD_DIM] + acc[h, :, HEAD_DIM:] for h in range(heads)], axis=1)

    def per_k(j, _):
        dka[...] = jnp.zeros_like(dka)
        dva[...] = jnp.zeros_like(dva)

        def per_q(i, _):
            @pl.when(span_hits(seg_ref, i, first + j))
            def _():
                visit(i, j)
            return 0

        lax.fori_loop(0, nq, per_q, 0)
        krow = at(j * size, size, size)
        out[krow, :width] = folded(dka)
        out[krow, width:] = folded(dva)
        return 0

    lax.fori_loop(0, count, per_k, 0)


def back_edge_kernel(heads, splits, idx, seg_ref, qcode_ref, hcode_ref, q_ref, halo_ref, o_ref, lse_ref, qc,
                     oh_ref, ol_ref, *refs):
    mg, (dhalo_ref, q2, dc, d2, dot_s, dqa, gh, gl, kh, vh, kth, hcol, prod_s, dka, dva) = (
        refs[:splits], refs[splits:])
    group, width = q_ref.shape
    nq, nh = group // TILE, halo_ref.shape[0] // EDGE
    tokens = group // splits
    if nh:
        prepare(halo_ref, width, 0, nh, EDGE, [(kh, 0), (vh, width)], kth)
        columns(hcode_ref, hcol, EDGE)
    for h in range(heads):
        hi, lo = split(q_ref[:, h * HEAD_DIM:(h + 1) * HEAD_DIM] * HEAD_DIM ** -0.5)
        q2[h] = jnp.concatenate([hi, lo], axis=1)
    dqa[...] = jnp.zeros_like(dqa)
    wrow = at(idx[0, 0] * width, width, 16)
    w_pair = (oh_ref[wrow, :], ol_ref[wrow, :])
    for r in range(splits):
        row = at(idx[0, r] * tokens, tokens, 16)
        gh[row, :], gl[row, :] = split(mg[r][...])
    step = group // 2
    for i in range(2):
        row = slice(i * step, (i + 1) * step)
        grad = mm3((gh[row, :], gl[row, :]), w_pair, NT)
        prod_s[row, :] = grad * o_ref[row, :]
        for h in range(heads):
            hi, lo = split(grad[:, h * HEAD_DIM:(h + 1) * HEAD_DIM])
            dc[h, row, :] = jnp.concatenate([hi, hi, lo], axis=1)
            d2[h, row, :] = jnp.concatenate([hi, lo], axis=1)
    for i in range(nq):
        rows = slice(i * TILE, (i + 1) * TILE)
        prod = prod_s[rows, :].T
        for h in range(heads):
            dot_s[h, :, rows] = jnp.sum(prod[h * HEAD_DIM:(h + 1) * HEAD_DIM], axis=0, keepdims=True)

    def visit(i, j):
        allowed = hcol[at(j * EDGE, EDGE, EDGE), :1] == qcode_ref[:, at(i * TILE, TILE, TILE)]
        back_add(heads, qc, q2, dc, d2, dot_s, lse_ref, kh, vh, kth, dqa, dka, dva, i, j, EDGE, allowed)

    if nh:
        back_over(heads, seg_ref, nq, nh, EDGE, nq, dhalo_ref, dka, dva, visit)


def back_own_kernel(heads, seg_ref, qcode_ref, kcode_ref, kv_ref, lse_ref, qc, q2, dc, d2, dot_s, dq_in,
                    dq_ref, dkv_ref, kc, vc, kt, kcol, dqa, dka, dva):
    group, width = dq_ref.shape
    nq = group // TILE
    prepare(kv_ref, width, 0, nq, TILE, [(kc, 0), (vc, width)], kt)
    columns(kcode_ref, kcol, TILE)
    dqa[...] = dq_in[...]

    def visit(i, j):
        allowed = kcol[at(j * TILE, TILE, TILE), :1] == qcode_ref[:, at(i * TILE, TILE, TILE)]
        back_add(heads, qc, q2, dc, d2, dot_s, lse_ref, kc, vc, kt, dqa, dka, dva, i, j, TILE, allowed | same_row(i, j))

    back_over(heads, seg_ref, nq, nq, TILE, 0, dkv_ref, dka, dva, visit)
    for i in range(nq):
        parts = [(dqa[h, i, :HEAD_DIM] + dqa[h, i, HEAD_DIM:]) * HEAD_DIM ** -0.5 for h in range(heads)]
        dq_ref[i * TILE:(i + 1) * TILE, :] = jnp.concatenate(parts, axis=0).T


def attend_back_edge(idx, segs, qcode, hcode, q, halo, o, lse, qc, oh, ol, mg):
    group, width = q.shape
    reach = halo.shape[0]
    heads = width // HEAD_DIM
    nq, nh = group // TILE, reach // EDGE
    full = oh.shape[1]
    H3, H2 = 3 * HEAD_DIM, 2 * HEAD_DIM
    return call(
        functools.partial(back_edge_kernel, heads, len(mg)), "back_edge",
        [arr((reach, 2 * width)), arr((heads, group, H2), BF), arr((heads, group, H3), BF), arr((heads, group, H2), BF),
         arr((heads, 1, group)), arr((heads, nq, H2, TILE)), arr((group, full), BF), arr((group, full), BF)],
        [idx, segs, qcode, hcode, q, halo, o, lse, qc, oh, ol, *mg],
        [
            pltpu.VMEM((heads, reach, H3), BF),
            pltpu.VMEM((heads, reach, H3), BF),
            pltpu.VMEM((heads, nh, H2, EDGE), BF),
            pltpu.VMEM((reach, 128), F32),
            pltpu.VMEM((group, width), F32),
            pltpu.VMEM((heads, EDGE, H2), F32),
            pltpu.VMEM((heads, EDGE, H2), F32),
        ],
        flops=2 * group * full * width, smem=2, wide=reach > group)


def attend_back_own(segs, qcode, kcode, kv, lse, qc, q2, dc, d2, dot_s, dqa):
    heads, group, _ = qc.shape
    width = kv.shape[1] // 2
    nq = group // TILE
    H3, H2 = 3 * HEAD_DIM, 2 * HEAD_DIM
    return call(
        functools.partial(back_own_kernel, heads), "back_own",
        [arr((group, width)), arr((group, 2 * width))],
        [segs, qcode, kcode, kv, lse, qc, q2, dc, d2, dot_s, dqa],
        [
            pltpu.VMEM((heads, group, H3), BF),
            pltpu.VMEM((heads, group, H3), BF),
            pltpu.VMEM((heads, nq, H2, TILE), BF),
            pltpu.VMEM((group, 128), F32),
            pltpu.VMEM((heads, nq, H2, TILE), F32),
            pltpu.VMEM((heads, TILE, H2), F32),
            pltpu.VMEM((heads, TILE, H2), F32),
        ],
        flops=10 * group * group * width)


def weights_kernel(full, splits, idx, *refs):
    count = max([p[0] for p in full]) + 1
    weights, (uh, ul, oh, ol, u32, o32) = refs[:count], refs[count:count + 6]
    got = weights
    owners = len(full)
    rows = u32.shape[0] // owners
    for i, (n, lead) in enumerate(full):
        row = at(idx[0, splits + i] * rows, rows)
        u32[row, :] = got[n][lead]
        o32[row, :] = got[n][2]
    uh[...], ul[...] = split(u32[...])
    oh[...], ol[...] = split(o32[...])


def act_kernel(splits, whole, first, place, idx, *refs):
    got, (gh, gl, dh, dl, act_ref) = refs[:-5], refs[-5:]
    tokens = got[0].shape[0]
    down = got[splits:]
    unit = down[0].shape[0]
    blocks = dh.shape[0] // unit
    for r in range(splits):
        row = at(idx[0, r] * tokens, tokens, 16)
        gh[row, :], gl[row, :] = split(got[r][...])
    for i in range(blocks):
        if i < whole:
            row = at(idx[0, first + i] * unit, unit, 16)
            dh[row, :], dl[row, :] = split(down[i][...])
            continue
        size = unit // 4
        for z in range(4):
            quarter = idx[0, place] ^ (0, 3, 1, 2)[z]
            row = at(idx[0, first + i] * unit + quarter * size, size, 16)
            dh[row, :], dl[row, :] = split(down[whole + 4 * (i - whole) + z][...])
    step = gh.shape[0] // 2

    def rows_of(i, _):
        row = at(i * step, step, 16)
        act_ref[row, :] = mm3((gh[row, :], gl[row, :]), (dh[...], dl[...]), NT)
        return 0

    lax.fori_loop(0, 2, rows_of, 0)


def feed_kernel(splits, idx, small, base, *refs):
    (oh, ol, uh, ul, act, keep, send, mine, inv_ref, ah, al, ph, plo, mh, ml, vec, b32, x2, g32, r32) = (
        refs[splits:splits + 20])
    att = refs[:splits]
    tokens = keep.shape[1]
    group = b32.shape[0]
    part = att[0].shape[1] // 2
    gain, shift = small[6:7, :], small[7:8, :]
    up_bias = small[pl.ds(8 + idx[0, 0], 1), :]
    vec[...] = jnp.zeros_like(vec)
    step = group // 2

    def rows_of(i, _):
        row = at(i * step, step, 16)
        middle = base[row, :] + small[2:3, :]
        for s in range(splits):
            wrow = at(idx[0, s] * part, part, 16)
            piece = jnp.where(i == 0, att[s][:, :part], att[s][:, part:])
            middle = middle + mm3(split(piece), (oh[wrow, :], ol[wrow, :]))
        b32[row, :] = middle
        xhat, inverse = norm(middle)
        x2[row, :] = xhat
        g32[row, :] = jnp.broadcast_to(inverse, g32[row, :].shape)
        pair = split(xhat * gain + shift)
        mh[row, :], ml[row, :] = pair
        pre = mm3(pair, (uh[...], ul[...])) + up_bias
        square = pre * pre
        curve = jnp.tanh(SQRT_2_PI * (pre + CUBIC * square * pre))
        half = 0.5 * (1.0 + curve)
        ah[row, :], al[row, :] = split(pre * half)
        slope = half + 0.5 * pre * (1.0 - curve * curve) * SQRT_2_PI * (1.0 + 3.0 * CUBIC * square)
        grad = act[row, :] * slope
        pair = split(grad)
        ph[row, :], plo[row, :] = pair
        back = mm3(pair, (uh[...], ul[...]), NT)
        vec[0:1, :] += jnp.sum(grad, axis=0, keepdims=True)
        vec[1:2, :] += jnp.sum(back * xhat, axis=0, keepdims=True)
        vec[2:3, :] += jnp.sum(back, axis=0, keepdims=True)
        r32[row, :] = back
        return 0

    lax.fori_loop(0, 2, rows_of, 0)
    for r in range(splits):
        row = at(idx[0, r] * tokens, tokens)
        target = send if r % 2 else keep
        target[r // 2] = r32[row, :]
    row = at(idx[0, 0] * tokens, tokens)
    mine[0] = b32[row, :]
    mine[1] = x2[row, :]
    inv_ref[...] = g32[row, :]


def feed_grads_kernel(splits, first, down_rows, up_rows, idx, ah, al, ph, plo, mh, ml, gh, gl, dh, dl,
                      keep, send, *refs):
    outs, r32 = refs[:-1], refs[-1]
    downs, ups = outs[:len(outs) // 2], outs[len(outs) // 2:]
    tokens = keep.shape[1]
    step = r32.shape[0] // 2

    def left(a, b):
        def rows_of(i, _):
            lane = at(i * step, step, 128)
            r32[at(i * step, step), :] = mm3((a[0][:, lane], a[1][:, lane]), (b[0][...], b[1][...]), TN)
            return 0

        lax.fori_loop(0, 2, rows_of, 0)

    def deal(targets, rows, place):
        for target in targets:
            for c in range(target.shape[0]):
                target[c] = r32[at(idx[0, place + c], rows), :]
            place += target.shape[0]
        return place

    left((ah, al), (gh, gl))
    place = deal(downs, down_rows, first)
    left((mh, ml), (ph, plo))
    deal(ups, up_rows, place)

    def rows_of(i, _):
        row = at(i * step, step, 16)
        r32[row, :] = mm3((ah[row, :], al[row, :]), (dh[...], dl[...]))
        return 0

    lax.fori_loop(0, 2, rows_of, 0)
    for r in range(splits):
        target = send if r % 2 else keep
        target[r // 2] = r32[at(idx[0, r] * tokens, tokens), :]


def middle_kernel(small, keep, core, far, og, mine, inv, mg_ref, vec_ref):
    grad = keep[0] + core[0] + far[...]
    out = og[...] + norm_back(grad, small[6:7, :], mine[1], inv[:, :1])
    mg_ref[...] = out
    vec_ref[...] = jnp.zeros_like(vec_ref)
    vec_ref[0:1, :] = jnp.sum(out, axis=0, keepdims=True)
    vec_ref[1:2, :] = jnp.sum(og[...], axis=0, keepdims=True)


def last_grads_kernel(splits, first, edge, rows, idx, small, dq, dkv, back, base, att, vec1, vec2, gh, gl, wh, wl,
                      keep, send, *refs):
    tails, (qh, ql, xhat, r32, o32, s32, n32, vec) = refs[:-8], refs[-8:]
    part = dq.shape[1]
    width = xhat.shape[1]
    tokens = keep.shape[1]
    gain, shift = small[4:5, :], small[5:6, :]
    u = idx[0, 0]
    s32[:, :part] = dq[...]
    s32[:, part:] = dkv[...]
    s32[at(idx[0, edge], back.shape[0]), part:] += back[...]
    qkv = s32[...]
    qh[...], ql[...] = split(qkv)
    sums = jnp.sum(qkv, axis=0, keepdims=True)
    xhat[...], _ = norm(base[...])
    vec[...] = jnp.zeros_like(vec)
    step = n32.shape[0] // 2

    def rows_of(i, _):
        row = at(i * step, step, 16)
        grad = mm3((qh[row, :], ql[row, :]), (wh[...], wl[...]), NT)
        n32[row, :] = grad
        vec[4:5, :] += jnp.sum(grad * xhat[row, :], axis=0, keepdims=True)
        vec[5:6, :] += jnp.sum(grad, axis=0, keepdims=True)
        return 0

    lax.fori_loop(0, 2, rows_of, 0)
    for r in range(splits):
        target = send if r % 2 else keep
        target[r // 2] = n32[at(idx[0, r] * tokens, tokens), :]
    step = width // 2
    for i in range(2):
        lane = slice(i * step, (i + 1) * step)
        pair = split(xhat[:, lane] * gain[:, lane] + shift[:, lane])
        r32[lane, :] = mm3(pair, (qh[...], ql[...]), TN)
    o32[...] = mm3(split(att[...]), (gh[...], gl[...]), TN)
    for i in range(splits):

        @pl.when(u == i)
        def _():
            vec[0:1, i * part:(i + 1) * part] = sums[:, :part]
            vec[1:2, i * part:(i + 1) * part] = sums[:, 2 * part:]

    vec[2:4, :] = vec2[0:2, :]
    vec[6:8, :] = vec1[1:3, :]
    vec[pl.ds(8 + u, 1), :] = vec1[0:1, :]
    wide = r32.shape[1]
    outs = width // 128
    vecs = outs * EXTRA // rows
    lane_blocks = -(-wide // 128)
    spare = lane_blocks * 128 - wide
    near = 2 * lane_blocks
    total = sum(t.shape[0] for t in tails)
    spot = 0
    for t in tails:
        for c in range(t.shape[0]):
            for j in range(splits):
                row = at(idx[0, first + spot * splits + j], rows)
                start = j * lane_blocks + (outs + vecs if j >= 2 else 0)
                for k in range(lane_blocks - 1):
                    t[c, start + k] = r32[row, k * 128:(k + 1) * 128]
                k = lane_blocks - 1
                t[c, start + k, :, :128 - spare] = r32[row, k * 128:]
                t[c, start + k, :, 128 - spare:] = jnp.zeros((rows, spare), F32)
            row = at(idx[0, first + total * splits + spot], rows)
            for k in range(outs):
                t[c, near + k] = o32[row, k * 128:(k + 1) * 128]
            for k in range(outs * EXTRA // 8):
                block, low = divmod(8 * k, rows)
                lane, high = divmod(8 * k, EXTRA)
                t[c, near + outs + block, low:low + 8, :] = vec[high:high + 8, lane * 128:(lane + 1) * 128]
            spot += 1


def hidden_kernel(idx, small, base, keep, core, far, mg, out):
    tokens = mg.shape[0]
    xhat, inverse = norm(base[at(idx[0, 0] * tokens, tokens), :])
    out[...] = mg[...] + norm_back(keep[0] + core[0] + far[...], small[4:5, :], xhat, inverse)


def place_kernel(splits, first, rows, idx, *refs):
    pieces, (gq, gk, gv, go) = refs[:-4], refs[-4:]
    part = gq.shape[1] // splits
    for z, piece in enumerate(pieces):
        row = at(idx[0, first + z] * rows, rows)
        count = gq.shape[1] // 128
        for k in range(count):
            go[row, k * 128:(k + 1) * 128] = piece[5 * splits + k]
        for r in range(splits):
            whole = jnp.concatenate([piece[5 * r + k] for k in range(5)], axis=1)
            for i in range(splits):

                @pl.when(idx[0, r] == i)
                def _():
                    for n, out in enumerate((gq, gk, gv)):
                        out[row, i * part:(i + 1) * part] = whole[:, n * part:(n + 1) * part]


def place_feed_kernel(splits, blocks, unit, first, idx, *refs):
    pieces, (gd, gu) = refs[:-2], refs[-2:]
    downs, ups = pieces[:len(pieces) // 2], pieces[len(pieces) // 2:]
    for z, (down, up) in enumerate(zip(downs, ups)):
        gd[at(idx[0, first + z] * down.shape[0], down.shape[0]), :] = down[...]
        rows = up.shape[1]
        row = at(idx[0, first + z] * rows, rows)
        for r in range(splits):
            for i in range(splits):

                @pl.when(idx[0, r] == i)
                def _():
                    for n in range(blocks):
                        start = (n * splits + i) * unit
                        gu[row, start:start + unit] = up[r, :, n * unit:(n + 1) * unit]


def swap(value, axis, mask):
    count = lax.axis_size(axis)
    return lax.ppermute(value, axis, [(i, i ^ mask) for i in range(count)])


def across(value):
    return swap(value, "ulys", 2)


def beside(value):
    return swap(value, "ulys", 1)


def over(value):
    return swap(value, "blk", 1)


def gather_splits(value):
    far = across(value)
    return [value, beside(value), far, beside(far)]


def after(value, *marks):
    return lax.optimization_barrier((value,) + marks)[0]


def corner(value):
    return lax.slice(value, (0,) * value.ndim, (1,) * (value.ndim - 2) + (8, 128))


def collect(value):
    near = swap(value, "dp", 3)
    return [value, near, swap(value, "dp", 1), swap(near, "dp", 1)]


def halo_moves(group, reach, blocks):
    moves = []
    shift = 1
    while reach > 0 and shift < blocks:
        rows = min(group, reach)
        moves.append((rows, True, [(i, i - shift) for i in range(shift, blocks)]))
        moves.append((rows, False, [(i, i + shift) for i in range(blocks - shift)]))
        reach -= rows
        shift += 1
    return moves


def halo_get(value, reach, axis=0):
    blocks, group = lax.axis_size("blk"), value.shape[axis]
    parts = []
    for rows, right, moves in halo_moves(group, reach, blocks):
        start = 0 if right else group - rows
        parts.append(lax.ppermute(lax.slice_in_dim(value, start, start + rows, axis=axis), "blk", moves))
    return jnp.concatenate(parts, axis=axis)


def halo_add(value, halo, reach):
    blocks, group = lax.axis_size("blk"), value.shape[0]
    start = 0
    for rows, right, moves in halo_moves(group, reach, blocks):
        back = lax.ppermute(halo[start:start + rows], "blk", [(j, i) for i, j in moves])
        start += rows
        room = group - rows
        value = value + jnp.pad(back, ((0, room), (0, 0)) if right else ((room, 0), (0, 0)))
    return value


def local(
    hidden,
    time_embed,
    segment_ids,
    key_valid,
    out_grad,
    w_query,
    b_query,
    w_key,
    w_value,
    b_value,
    w_out,
    b_out,
    w_up,
    b_up,
    w_down,
    b_down,
    pre_gain,
    pre_shift,
    mlp_gain,
    mlp_shift,
):
    blocks, splits = lax.axis_size("blk"), lax.axis_size("ulys")
    b, u, d = (lax.axis_index(name) for name in ("blk", "ulys", "dp"))
    both = ("blk", "ulys")
    owners = blocks * splits
    tokens, width = hidden.shape
    group = tokens * splits
    part = width // splits
    rows = w_query.shape[0]
    unit = w_down.shape[0]
    units = unit * owners
    share = units // splits
    reach = group * blocks // 4
    fast = blocks == 2 and splits == 4 and lax.axis_size("dp") == 4 and reach <= group and group == width

    if fast:
        f1, f3 = (d ^ (d >> 1)) & 1, d >> 1
        quarters = [2 * (f1 ^ s) + (f3 ^ t) for s in range(2) for t in range(2)]
        owner_list = [(b ^ x) * splits + (u ^ r) for x in range(2) for r in range(4)]
        block_list = [b, b ^ 1]
        edge_row = jnp.where(b == 0, group - reach, 0)
        down_rows, up_rows, tail_rows = unit // 4, rows // 4, rows // 4
        down_table = [(b ^ x) * unit + q * down_rows for x in range(2) for q in quarters]
        up_table = [
            ((b ^ x) * splits + (u ^ r)) * rows + q * up_rows for q in quarters for x in range(2) for r in range(4)
        ]
        tail_table = [
            ((b ^ x) * splits + (u ^ r)) * rows + q * tail_rows for x in range(2) for q in quarters for r in range(4)
        ] + [(b ^ x) * rows + q * tail_rows for x in range(2) for q in quarters]
        chunks = 8
    else:
        quarters = []
        owner_list = list(range(owners))
        block_list = list(range(blocks))
        edge_row = 0
        down_rows, up_rows, tail_rows = unit, rows, rows
        down_table = [i * unit for i in range(blocks)]
        up_table = [i * rows for i in range(owners)]
        tail_table = up_table + [i * rows for i in range(blocks)]
        chunks = blocks
    entries, spots = [], []
    for values in (
        [u ^ r for r in range(splits)], owner_list, block_list, [d], [edge_row], down_table + up_table, tail_table,
        quarters,
    ):
        spots.append(len(entries))
        entries += values
    _, _, at_block, at_d, at_edge, at_feed, at_tail, at_quarter = spots
    idx = jnp.stack([jnp.asarray(v, jnp.int32) for v in entries]).reshape(1, -1)

    segments = segment_ids[0] + 1
    codes = jnp.stack([segments, jnp.where(key_valid[0] == 1, segments, 0)]).astype(F32)
    small = jnp.stack([b_query, b_value, b_out, b_down, pre_gain, pre_shift, mlp_gain, mlp_shift])
    small = lax.dynamic_update_slice(jnp.zeros((EXTRA, width), F32), small, (0, (b * splits + u) * rows))
    small = lax.dynamic_update_slice(small, b_up[None], (8 + u, b * unit))
    if fast:
        small = lax.dynamic_update_slice(small, codes, (12, 0))
        other = over(small)
        small = small + other
        halo_codes = jnp.where(b == 0, other[12:14, :reach], other[12:14, group - reach:group])
    else:
        small = lax.psum(small, "blk")
        halo_codes = halo_get(codes, reach, axis=1)
    tiles = codes[0].reshape(-1, TILE)
    edges = halo_codes[0].reshape(-1, EDGE)
    bounds = jnp.concatenate(
        [
            jnp.stack([tiles[:, 0], tiles[:, -1]], axis=1).reshape(-1),
            jnp.stack([jnp.min(jnp.where(edges == 0, 1e6, edges), axis=1), jnp.max(edges, axis=1)], axis=1).reshape(-1),
        ]
    ).astype(jnp.int32).reshape(1, -1)
    query_codes, key_codes, edge_codes = codes[:1], codes[1:], halo_codes[1:]
    idx, bounds, query_codes, key_codes, edge_codes, small = lax.optimization_barrier(
        (idx, bounds, query_codes, key_codes, edge_codes, small)
    )
    base = jnp.concatenate([hidden + time_embed, small], axis=0)

    if fast:
        near, far, near2, far2 = call(
            functools.partial(pack_kernel, blocks), "pack",
            [arr((2, rows, 3 * part))] * 2 + [arr((3, rows, share))] * 2,
            [idx, w_query, w_key, w_value, w_up, w_out])
        pieces = [(i, i % 2) for i in range(8)]
        far = across(far)
        far_base = across(after(base, corner(far)))
        qkv_arrays = [near, beside(near), far, beside(far)]
        near = over(near)
        far = over(far)
        qkv_arrays += [near, beside(near), far, beside(far)]
        base_all = [base, beside(base), far_base, beside(far_base)]

        far2 = across(after(far2, corner(far_base)))
        feed_arrays = [near2, beside(near2), far2, beside(far2)]
        near2 = over(after(near2, corner(far)))
        feed_arrays += [near2, beside(near2)]
        whole = 1
        down_quarter = lax.dynamic_slice_in_dim(w_down, d * (unit // 4), unit // 4, 0)
        down_quarter = over(after(down_quarter, corner(far)))
    else:
        cut = jnp.stack([w_query, w_key, w_value], axis=1).reshape(rows, 3, splits, part)
        cut = cut.transpose(2, 0, 1, 3).reshape(splits, rows, 3 * part)
        cut = jnp.broadcast_to(cut[None], (blocks,) + cut.shape).reshape(owners, rows, 3 * part)
        got = lax.all_to_all(cut, both, 0, 0, tiled=True)
        qkv_arrays = [got[i:i + 1] for i in range(owners)]
        cut = w_up.reshape(rows, blocks, splits, unit).transpose(2, 0, 1, 3).reshape(splits, rows, share)
        cut = jnp.broadcast_to(cut[None], (blocks,) + cut.shape).reshape(owners, rows, share)
        got = lax.all_to_all(cut, both, 0, 0, tiled=True)
        outs = lax.all_gather(w_out, both, axis=0, tiled=False)
        feed_arrays = [jnp.stack([got[i], got[i], outs[i]]) for i in range(owners)]
        pieces = [(i, 0) for i in range(owners)]
        whole = blocks
        base_all = gather_splits(base)
        gathered = lax.all_gather(w_down, "blk", axis=0, tiled=False)
        down = [gathered[i] for i in range(blocks)]

    query, key_value, edge_kv, base, small, qkv_hi, qkv_lo = call(
        functools.partial(qkv_kernel, pieces, splits, at_edge), "qkv",
        [arr((group, part)), arr((group, 2 * part)), arr((reach if fast else 8, 2 * part)), arr((group, width)),
         arr((EXTRA, width)), arr((width, 3 * part), BF), arr((width, 3 * part), BF)],
        [idx, *base_all, *qkv_arrays],
        [pltpu.VMEM((width, 3 * part), F32), pltpu.VMEM((group, width), BF), pltpu.VMEM((group, width), BF)],
        flops=2 * group * width * 3 * part)
    halo = over(edge_kv) if fast else halo_get(key_value, reach)
    state = attend_own(bounds, query_codes, key_codes, query, key_value)
    attended, attended_wide, lse = attend_edge(bounds, query_codes, edge_codes, halo, state)

    grads = gather_splits(after(out_grad, corner(edge_kv)))
    if fast:
        down = [w_down] + collect(after(down_quarter, corner(state[3])))
        far2 = over(after(far2, corner(halo)))
    og_hi, og_lo, down_hi, down_lo, act_grad = call(
        functools.partial(act_kernel, splits, whole, at_block, at_d), "act",
        [arr((group, width), BF)] * 2 + [arr((share, width), BF)] * 2 + [arr((group, share))],
        [idx, *grads, *down],
        flops=2 * group * width * share)
    if fast:
        far2 = after(far2, corner(act_grad))
        feed_arrays += [far2, beside(far2)]
    up_hi, up_lo, out_hi, out_lo = call(
        functools.partial(weights_kernel, pieces, splits), "weights",
        [arr((width, share), BF)] * 2 + [arr((width, width), BF)] * 2,
        [idx, *feed_arrays],
        [pltpu.VMEM((width, share), F32), pltpu.VMEM((width, width), F32)])

    attended_all = gather_splits(attended_wide)
    pair = [arr((group, share), BF)] * 2
    keep, send, mine, inverse2, act_hi, act_lo, pre_hi, pre_lo, in_hi, in_lo, vec_feed = call(
        functools.partial(feed_kernel, splits), "feed",
        [arr((2, tokens, width))] * 2 + [arr((2, tokens, width)), arr((tokens, 128))] + pair * 2
        + [arr((group, width), BF)] * 2 + [arr((8, width))],
        [idx, small, base, *attended_all, out_hi, out_lo, up_hi, up_lo, act_grad],
        [pltpu.VMEM((group, width), F32), pltpu.VMEM((group, width), F32), pltpu.VMEM((group, 128), F32),
         pltpu.VMEM((group, width), F32)],
        flops=2 * group * width * (width + 2 * share))
    core = beside(send)
    near_sum = keep[1] + core[1]
    far_sum = across(near_sum)

    if fast:
        feed_outs = [arr((4, down_rows, width))] * 2 + [arr((8 * splits // 2, up_rows, share))] * 2
    else:
        feed_outs = [arr((blocks, down_rows, width)), arr((owners, up_rows, share))]
    keep_out, send_out, *feed_grads = call(
        functools.partial(feed_grads_kernel, splits, at_feed, down_rows, up_rows), "feed_grads",
        [arr((2, tokens, width))] * 2 + feed_outs,
        [idx, after(act_hi, corner(near_sum)), act_lo, pre_hi, pre_lo, in_hi, in_lo, og_hi, og_lo, down_hi, down_lo],
        [pltpu.VMEM((group, width), F32)],
        flops=6 * group * width * share)
    if fast:
        down_keep, down_send, up_keep, up_send = feed_grads
        down_got = over(down_send)
        up_got = swap(up_send, "dp", 1)

    middle_grad, vec_middle = call(
        middle_kernel, "middle",
        [arr((tokens, width)), arr((8, width))],
        [small, keep, core, after(far_sum, corner(keep_out)), out_grad, mine, inverse2], smem=0)
    middle_all = gather_splits(middle_grad)

    halo_grad, q2, dc, d2, dots, dq_part, mg_hi, mg_lo = attend_back_edge(
        idx, bounds, query_codes, edge_codes, query, halo, attended, lse, state[0], out_hi, out_lo, middle_all)
    query_grad, kv_grad = attend_back_own(
        bounds, query_codes, key_codes, key_value, lse, state[0], q2, dc, d2, dots, dq_part)
    if fast:
        returned = over(halo_grad)
        mark = corner(halo_grad)
        part_down = down_keep + after(down_got, mark)
        part_up = up_keep.reshape(2, 2, splits, up_rows, share) + after(up_got, mark).reshape(
            2, 2, splits, up_rows, share)
        down_got = swap(part_down[2:], "dp", 1)
        up_got = swap(part_up[1], "dp", 3)
    else:
        kv_grad = halo_add(kv_grad, halo_grad, reach)
        returned = jnp.zeros((8, 2 * part), F32)

    lane_blocks = -(-3 * part // 128)
    outs, vecs = width // 128, width // 128 * EXTRA // tail_rows
    total_blocks = splits * lane_blocks + outs + vecs
    tail_outs = [arr((4, total_blocks, tail_rows, 128))] * 2 if fast else [arr((blocks, total_blocks, tail_rows, 128))]
    keep_in, send_in, *tail = call(
        functools.partial(last_grads_kernel, splits, at_tail, at_edge, tail_rows), "last_grads",
        [arr((2, tokens, width))] * 2 + tail_outs,
        [idx, small, query_grad, kv_grad, returned, base, attended, vec_feed, vec_middle, mg_hi, mg_lo, qkv_hi, qkv_lo],
        [pltpu.VMEM((group, 3 * part), BF), pltpu.VMEM((group, 3 * part), BF), pltpu.VMEM((group, width), F32),
         pltpu.VMEM((width, 3 * part), F32), pltpu.VMEM((part, width), F32), pltpu.VMEM((group, 3 * part), F32),
         pltpu.VMEM((group, width), F32), pltpu.VMEM((EXTRA, width), F32)],
        flops=2 * group * width * 7 * part)
    to_owner = [(i * splits + j, j * blocks + i) for i in range(blocks) for j in range(splits)]
    near = 2 * lane_blocks
    if fast:
        tail_got = over(tail[1])
        core_in = beside(send_in)
        far_in = across(keep_in[1] + core_in[1])

        mark = corner(keep_in)
        part_down = part_down[:2] + after(down_got, mark)
        part_up = part_up[0] + after(up_got, mark)
        down_got = swap(part_down[1], "dp", 3)
        up_got = over(part_up[1])
        part_down = part_down[0] + down_got
        part_up = part_up[0] + up_got

        part_tail = tail[0] + tail_got
        mark = corner(part_tail)
        part_tail = part_tail[:2] + swap(part_tail[2:], "dp", 1)
        far_up = across(after(part_up[2:], mark))
        core_up = beside(jnp.stack([part_up[1], far_up[1]]))
        part_tail = part_tail[0] + swap(part_tail[1], "dp", 3)
        part_up = jnp.stack([part_up[0], core_up[0], far_up[0], core_up[1]])

        all_down = collect(after(part_down, mark))
        far_tail = across(part_tail[near + outs:])
        core_tail = beside(
            jnp.concatenate([
                part_tail[lane_blocks:near], part_tail[near + outs:near + outs + vecs] + far_tail[:vecs],
                far_tail[vecs + lane_blocks:]])
        )
        vec = part_tail[near + outs:near + outs + vecs] + far_tail[:vecs] + core_tail[lane_blocks:lane_blocks + vecs]
        owned = lax.ppermute(part_tail[near:near + outs], both, to_owner)
        part_tail = jnp.concatenate([
            part_tail[:lane_blocks], core_tail[:lane_blocks], far_tail[vecs:vecs + lane_blocks],
            core_tail[lane_blocks + vecs:], owned])
        all_tail = collect(part_tail)
        all_up = collect(part_up)
        total_down, total_up = call(
            functools.partial(place_feed_kernel, splits, blocks, unit, at_quarter), "place_feed",
            [arr((unit, width)), arr((rows, units))],
            [idx, *all_down, *all_up])
        total_query, total_key, total_value, total_out = call(
            functools.partial(place_kernel, splits, at_quarter, tail_rows), "place",
            [arr((rows, width))] * 4,
            [idx, *all_tail])
    else:
        core_in = beside(send_in)
        far_in = across(keep_in[1] + core_in[1])
        total_down, total_up, tail = [
            lax.psum(lax.psum_scatter(g.reshape((blocks, -1) + g.shape[1:]), "blk", scatter_dimension=0, tiled=False), "dp")
            for g in (*feed_grads, *tail)
        ]
        total_down = total_down.reshape(unit, width)
        total_up = lax.all_to_all(total_up, "ulys", 0, 0, tiled=True)
        total_up = total_up.reshape(splits, rows, blocks, unit).transpose(1, 2, 0, 3).reshape(rows, units)
        tail = tail[0]
        total_out = lax.ppermute(tail[near:near + outs], both, to_owner).transpose(1, 0, 2).reshape(rows, width)
        vec = lax.psum(tail[near + outs:near + outs + vecs], "ulys")
        got = jnp.concatenate([tail[:near], tail[near + outs + vecs:]]).reshape(splits, lane_blocks, rows, 128)
        got = lax.all_to_all(got, "ulys", 0, 0, tiled=True).transpose(2, 0, 1, 3).reshape(rows, splits, lane_blocks * 128)
        total_query, total_key, total_value = (
            got[:, :, i * part:(i + 1) * part].reshape(rows, width) for i in range(3)
        )
    (hidden_grad,) = call(
        hidden_kernel, "hidden",
        [arr((tokens, width))],
        [idx, small, base, keep_in, core_in, far_in, middle_grad])

    core_out = beside(after(send_out, corner(keep_in)))
    far_out = across(keep_out[1] + core_out[1])
    output = mine[0] + small[3:4] + keep_out[0] + core_out[0] + far_out

    vec = vec.reshape(outs, EXTRA, 128).transpose(1, 0, 2).reshape(EXTRA, width)
    vector = lax.dynamic_slice(vec, (0, (b * splits + u) * rows), (8, rows))
    up_vector = lax.dynamic_slice(vec, (8 + u, b * unit), (1, unit))[0]
    return (
        output,
        hidden_grad,
        total_query,
        vector[0],
        total_key,
        total_value,
        vector[1],
        total_out,
        vector[2],
        total_up,
        up_vector,
        total_down,
        vector[3],
        vector[4],
        vector[5],
        vector[6],
        vector[7],
    )


def solution(mesh):
    tokens = P(("dp", "blk", "ulys"), None)
    matrix = P(("blk", "ulys"), None)
    vector = P(("blk", "ulys"))
    return jax.shard_map(
        local,
        mesh=mesh,
        in_specs=(
            tokens,
            P("dp", None),
            P("dp", "blk"),
            P("dp", "blk"),
            tokens,
            matrix,
            vector,
            matrix,
            matrix,
            vector,
            matrix,
            vector,
            matrix,
            vector,
            matrix,
            vector,
            vector,
            vector,
            vector,
            vector,
        ),
        out_specs=(
            tokens,
            tokens,
            matrix,
            vector,
            matrix,
            matrix,
            vector,
            matrix,
            vector,
            matrix,
            vector,
            matrix,
            vector,
            vector,
            vector,
            vector,
            vector,
        ),
        check_vma=False,
    )
```

time: 530 us -> 391 us (0.74)
  the two profiles are of different devices: /device:TPU:0 before, /device:TPU:5 now
where the time goes in v2:
time: 391 us; the launch traced here: 388 us
  waiting for transfers between devices  183 us (47%)
  Pallas kernels  94.9 us (24%)
  starting transfers between devices  87.5 us (22%)
  local copies, waits for them, and re-layouts  17.2 us (4%)
  other arithmetic  4.1 us (1%)
    ppermute x61, waiting for transfers between devices, swap(): return lax.ppermute(value, axis, [(i, i ^ mask) for i in range(count)])  179 us
    pallas_call x15, Pallas kernels, call(): pl.pallas_call(kernel, out_shape=tuple(outs), in_specs=[SM] * smem + [VM]...  94.9 us
    ppermute x61, starting transfers between devices, swap(): return lax.ppermute(value, axis, [(i, i ^ mask) for i in range(count)])  84.4 us
    unnamed x36, local copies, waits for them, and re-layouts  12.5 us
  transfers between devices with their start and end apart: 62, of which 22 were waited for; matrix products, arithmetic and copies ran while one was open for 1% of the time, Pallas kernels for 19%

profile of v2, /device:TPU:5, one launch (start us, length us, event | category | flops | bytes accessed | tf_op | source)
XLA Modules:
  0.0 387.8 jit_solution(7638450141794585083)
XLA Ops:
  20.3 8.2 %collective-permute-done.5.refs_6_ = f32[2,96,576]{2,1,0:T(8,128)S(1)} collective-permute-done((f32[2,96,576]{2,1,0:T(8,128)S(1)}, f32[2,96,576]{2,1,0:T(8,128)S(1)}, u32[]{:S(2)}, u32[]{:S(2)}) %collective-permute-start.5) | collective-permute-done | bytes 442400 | tf_op jit(solution)/shard_map/ppermute | solution.py:684
  31.8 10.4 %collective-permute-done.2.refs_2_ = f32[208,768]{1,0:T(8,128)} collective-permute-done((f32[208,768]{1,0:T(8,128)S(1)}, f32[208,768]{1,0:T(8,128)}, u32[]{:S(2)}, u32[]{:S(2)}) %collective-permute-start.2) | collective-permute-done | bytes 639008 | tf_op jit(solution)/shard_map/ppermute | solution.py:684
  45.6 15.5 %collective-permute-done.16.refs_2_ = f32[3,96,768]{2,1,0:T(8,128)S(1)} collective-permute-done((f32[3,96,768]{2,1,0:T(8,128)S(1)}, f32[3,96,768]{2,1,0:T(8,128)S(1)}, u32[]{:S(2)}, u32[]{:S(2)}) %collective-permute-start.16) | collective-permute-done | bytes 884768 | tf_op jit(solution)/shard_map/ppermute | solution.py:684
  67.6 7.6 %qkv.1 = (f32[768,192]{1,0:T(8,128)S(1)}, f32[768,384]{1,0:T(8,128)S(1)}, f32[384,384]{1,0:T(8,128)S(1)}, f32[768,768]{1,0:T(8,128)S(1)}, f32[16,768]{1,0:T(8,12...) custom-call(s32[1,100]{1,0:T(1,128)S(1)} %bitcast.145, f32[208,768]{1,0:T(8,128)S(1)} %pad_maximum_fusion.refs_0_, ...), custom_call_target="tpu_custom_call" | custom-call | flops 2038431744 | bytes 12632064 | tf_op jit(solution)/shard_map/qkv/pallas_call | solution.py:47
  77.0 25.3 %collective-permute-done.25.refs_5_ = f32[96,768]{1,0:T(8,128)S(1)} collective-permute-done((f32[96,768]{1,0:T(8,128)S(1)}, f32[96,768]{1,0:T(8,128)S(1)}, u32[]{:S(2)}, u32[]{:S(2)}) %collective-permute-start.25) | collective-permute-done | bytes 294944 | tf_op jit(solution)/shard_map/ppermute | solution.py:684
  103.6 8.8 %attend_own.1 = (bf16[3,768,192]{2,1,0:T(8,128)(2,1)S(1)}, f32[3,3,1,256]{3,2,1,0:T(1,128)S(1)}, f32[3,3,1,256]{3,2,1,0:T(1,128)S(1)}, f32[3,3,128,256]{3,2,1,0:T(8,128)S(1)}) custom-call(s32[1,12]{1,0:T(1,128)S(1)} %maximum_convert_fusion.seg_ref, f32[1,768]{1,0:T(1,128)S(1)} %get-tuple-element.105.qcode_ref, f32[1,768]{1,0:T(1,128)S(1)} %get-tuple-element.108.kcode_ref, ...), custom_call_target="tpu_custom_call" | custom-call | flops 1358954496 | bytes 3858432 | tf_op jit(solution)/shard_map/attend_own/pallas_call | solution.py:47
  114.3 3.3 attend_edge.1
  119.8 3.2 collective-permute-done.26.refs_6_
  123.0 4.3 %collective-permute-start.28 = (f32[96,768]{1,0:T(8,128)S(1)}, f32[96,768]{1,0:T(8,128)S(1)}, u32[]{:S(2)}, u32[]{:S(2)}) collective-permute-start(f32[96,768]{1,0:T(8,128)S(1)} %collective-permute-done.26.refs_6_), channel_id=1, source_target_pairs={{0,8},{8,0},{16,24},{24,16},{1,9},{9,1},{17,25},{25,17},{2,10},{10... | collective-permute-start | bytes 884744 | tf_op jit(solution)/shard_map/ppermute | solution.py:684
  130.2 5.8 %collective-permute-done.28.refs_8_ = f32[96,768]{1,0:T(8,128)S(1)} collective-permute-done((f32[96,768]{1,0:T(8,128)S(1)}, f32[96,768]{1,0:T(8,128)S(1)}, u32[]{:S(2)}, u32[]{:S(2)}) %collective-permute-start.28) | collective-permute-done | bytes 294944 | tf_op jit(solution)/shard_map/ppermute | solution.py:684
  136.5 5.2 %act.1 = (bf16[768,768]{1,0:T(8,128)(2,1)S(1)}, bf16[768,768]{1,0:T(8,128)(2,1)S(1)}, bf16[768,768]{1,0:T(8,128)(2,1)S(1)}, bf16[768,768]{1,0:T(8,128)(2,1)S(1)}, f32[768,768]{1,0:T(8,128)S(1)}) custom-call(s32[1,100]{1,0:T(1,128)S(1)} %bitcast.146, f32[192,768]{1,0:T(8,128)S(1)} %copy-done.1, f32[192,768]{1,0:T(8,128)} %collective-permute-done.22.refs_1_, ...), custom_call_target="tpu_custom_call" | custom-call | flops 2717908992 | bytes 11796480 | tf_op jit(solution)/shard_map/act/pallas_call | solution.py:47
  143.8 17.6 %feed.1 = (f32[2,192,768]{2,1,0:T(8,128)S(1)}, f32[2,192,768]{2,1,0:T(8,128)S(1)}, f32[2,192,768]{2,1,0:T(8,128)S(1)}, f32[192,128]{1,0:T(8,128)S(1)}, bf16[768,...) custom-call(s32[1,100]{1,0:T(1,128)S(1)} %bitcast.148, ...), custom_call_target="tpu_custom_call" | custom-call | flops 8153726976 | bytes 22585344 | tf_op jit(solution)/shard_map/feed/pallas_call | solution.py:47
  166.0 13.1 %collective-permute-done.30.far = f32[192,768]{1,0:T(8,128)S(1)} collective-permute-done((f32[192,768]{1,0:T(8,128)S(1)}, f32[192,768]{1,0:T(8,128)S(1)}, u32[]{:S(2)}, u32[]{:S(2)}) %collective-permute-start.30) | collective-permute-done | bytes 589856 | tf_op jit(solution)/shard_map/ppermute | solution.py:684
  181.0 10.7 %feed_grads.1 = (f32[2,192,768]{2,1,0:T(8,128)S(1)}, f32[2,192,768]{2,1,0:T(8,128)S(1)}, f32[4,96,768]{2,1,0:T(8,128)S(1)}, f32[4,96,768]{2,1,0:T(8,128)S(1)}, f...) custom-call(s32[1,100]{1,0:T(1,128)S(1)} %bitcast.149, bf16[768,768]{1,0:T(8,128)(2,1)S(1)} %get-tuple-element.126.ah, ...), custom_call_target="tpu_custom_call" | custom-call | flops 8153726976 | bytes 18874368 | tf_op jit(solution)/shard_map/feed_grads/pallas_call | solution.py:47
  199.1 6.2 %back_edge.1 = (f32[384,384]{1,0:T(8,128)S(1)}, bf16[3,768,128]{2,1,0:T(8,128)(2,1)S(1)}, bf16[3,768,192]{2,1,0:T(8,128)(2,1)S(1)}, bf16[3,768,128]{2,1,0:T(8,12...) custom-call(s32[1,100]{1,0:T(1,128)S(1)} %bitcast.150, ...), custom_call_target="tpu_custom_call" | custom-call | flops 679477248 | bytes 13604352 | tf_op jit(solution)/shard_map/back_edge/pallas_call | solution.py:47
  205.4 12.3 %collective-permute-done.48 = f32[4,96,768]{2,1,0:T(8,128)S(1)} collective-permute-done((f32[4,96,768]{2,1,0:T(8,128)S(1)}, f32[4,96,768]{2,1,0:T(8,128)S(1)}, u32[]{:S(2)}, u32[]{:S(2)}) %collective-permute-start.48) | collective-permute-done | bytes 1179680 | tf_op jit(solution)/shard_map/ppermute | solution.py:684
  221.0 14.9 %back_own.1 = (f32[768,192]{1,0:T(8,128)S(1)}, f32[768,384]{1,0:T(8,128)S(1)}) custom-call(s32[1,12]{1,0:T(1,128)S(1)} %maximum_convert_fusion.seg_ref, f32[1,768]{1,0:T(1,128)S(1)} %get-tuple-element.105.qcode_ref, f32[1,768]{1,0:T(1,128)S(1)} %get-tuple-element.108.kcode_ref, f32[768,384]{1,0:T(8,128)S(1)} %get-tuple-element.110.kv_ref, ...), custom_call_target="tpu_custom_call" | custom-call | flops 3397386240 | bytes 7117824 | tf_op jit(solution)/shard_map/back_own/pallas_call | solution.py:47
  236.0 9.8 %last_grads.1 = (f32[2,192,768]{2,1,0:T(8,128)S(1)}, f32[2,192,768]{2,1,0:T(8,128)S(1)}, f32[4,30,24,128]{3,2,1,0:T(8,128)S(1)}, f32[4,30,24,128]{3,2,1,0:T(8,128)S(1)}) custom-call(s32[1,100]{1,0:T(1,128)S(1)} %bitcast.151, f32[16,768]{1,0:T(8,128)S(1)} %get-tuple-element.102.small, f32[768,192]{1,0:T(8,128)S(1)} %get-tuple-element.149.dq, ...), custom_call_target="tpu_custom_call" | custom-call | flops 4756340736 | bytes 14843904 | tf_op jit(solution)/shard_map/last_grads/pallas_call | solution.py:47
  247.1 5.3 %collective-permute-start.35 = (f32[2,192,768]{2,1,0:T(8,128)S(1)}, f32[2,192,768]{2,1,0:T(8,128)S(1)}, u32[]{:S(2)}, u32[]{:S(2)}) collective-permute-start(f32[2,192,768]{2,1,0:T(8,128)S(1)} %get-tuple-element.159), channel_id=1, source_target_pairs={{0,1},{1,0},{2,3},{3,2},{4,5},{5,4},{6,7},{7,6},{8,9},{9,8},{10,11... | collective-permute-start | bytes 3538952 | tf_op jit(solution)/shard_map/ppermute | solution.py:684
  252.9 28.5 %collective-permute-done.56 = f32[4,24,768]{2,1,0:T(8,128)S(1)} collective-permute-done((f32[4,24,768]{2,1,0:T(8,128)S(1)}, f32[4,24,768]{2,1,0:T(8,128)S(1)}, u32[]{:S(2)}, u32[]{:S(2)}) %collective-permute-start.56) | collective-permute-done | bytes 294944 | tf_op jit(solution)/shard_map/ppermute | solution.py:684
  283.5 10.8 %collective-permute-done.40 = f32[2,30,24,128]{3,2,1,0:T(8,128)S(1)} collective-permute-done((f32[2,30,24,128]{3,2,1,0:T(8,128)S(1)}, f32[2,30,24,128]{3,2,1,0:T(8,128)S(1)}, u32[]{:S(2)}, u32[]{:S(2)}) %collective-permute-start.40) | collective-permute-done | bytes 737312 | tf_op jit(solution)/shard_map/ppermute | solution.py:684
  294.8 3.2 collective-permute-start.51
  298.0 14.4 %collective-permute-start.58 = (f32[2,24,768]{2,1,0:T(8,128)S(1)}, f32[2,24,768]{2,1,0:T(8,128)S(1)}, u32[]{:S(2)}, u32[]{:S(2)}) collective-permute-start(f32[2,24,768]{2,1,0:T(8,128)S(1)} %pad_maximum_fusion.3), channel_id=1, source_target_pairs={{0,1},{1,0},{2,3},{3,2},{4,5},{5,4},{6,7},{7,6},{8,9},{9,8},{10,11... | collective-permute-start | bytes 442376 | tf_op jit(solution)/shard_map/ppermute | solution.py:684
  314.0 5.1 %collective-permute-done.42 = f32[14,24,128]{2,1,0:T(8,128)S(1)} collective-permute-done((f32[14,24,128]{2,1,0:T(8,128)S(1)}, f32[14,24,128]{2,1,0:T(8,128)S(1)}, u32[]{:S(2)}, u32[]{:S(2)}) %collective-permute-start.42) | collective-permute-done | bytes 172064 | tf_op jit(solution)/shard_map/ppermute | solution.py:684
  319.1 4.0 %collective-permute-start.43 = (f32[14,24,128]{2,1,0:T(8,128)S(1)}, f32[14,24,128]{2,1,0:T(8,128)S(1)}, u32[]{:S(2)}, u32[]{:S(2)}) collective-permute-start(f32[14,24,128]{2,1,0:T(8,128)S(1)} %pad_maximum_fusion.2), channel_id=1, source_target_pairs={{0,1},{1,0},{2,3},{3,2},{4,5},{5,4},{6,7},{7,6},{8,9},{9,8},{10,11... | collective-permute-start | bytes 516104 | tf_op jit(solution)/shard_map/ppermute | solution.py:684
  328.6 3.4 collective-permute-done.44
  332.1 4.0 %collective-permute-start.52 = (f32[96,768]{1,0:T(8,128)S(1)}, f32[96,768]{1,0:T(8,128)S(1)}, u32[]{:S(2)}, u32[]{:S(2)}) collective-permute-start(f32[96,768]{1,0:T(8,128)S(1)} %fusion.7.refs_0_), channel_id=1, source_target_pairs={{0,8},{8,0},{16,24},{24,16},{1,9},{9,1},{17,25},{25,17},{2,10},{10... | collective-permute-start | bytes 884744 | tf_op jit(solution)/shard_map/ppermute | solution.py:684
  345.7 10.5 %collective-permute-done.53.refs_3_ = f32[96,768]{1,0:T(8,128)S(1)} collective-permute-done((f32[96,768]{1,0:T(8,128)S(1)}, f32[96,768]{1,0:T(8,128)S(1)}, u32[]{:S(2)}, u32[]{:S(2)}) %collective-permute-start.53) | collective-permute-done | bytes 294944 | tf_op jit(solution)/shard_map/ppermute | solution.py:684
  356.2 6.3 %collective-permute-done.61.refs_7_ = f32[4,24,768]{2,1,0:T(8,128)S(1)} collective-permute-done((f32[4,24,768]{2,1,0:T(8,128)S(1)}, f32[4,24,768]{2,1,0:T(8,128)S(1)}, u32[]{:S(2)}, u32[]{:S(2)}) %collective-permute-start.61) | collective-permute-done | bytes 294944 | tf_op jit(solution)/shard_map/ppermute | solution.py:684
  367.1 3.7 collective-permute-done.45.refs_1_
  371.4 6.3 %collective-permute-done.46.refs_2_ = f32[26,24,128]{2,1,0:T(8,128)S(1)} collective-permute-done((f32[26,24,128]{2,1,0:T(8,128)S(1)}, f32[26,24,128]{2,1,0:T(8,128)S(1)}, u32[]{:S(2)}, u32[]{:S(2)}) %collective-permute-start.46) | collective-permute-done | bytes 319520 | tf_op jit(solution)/shard_map/ppermute | solution.py:684
  377.7 6.8 %collective-permute-done.47.refs_3_ = f32[26,24,128]{2,1,0:T(8,128)S(1)} collective-permute-done((f32[26,24,128]{2,1,0:T(8,128)S(1)}, f32[26,24,128]{2,1,0:T(8,128)S(1)}, u32[]{:S(2)}, u32[]{:S(2)}) %collective-permute-start.47) | collective-permute-done | bytes 319520 | tf_op jit(solution)/shard_map/ppermute | solution.py:684
  (207 shorter events, 91.8 us)
Async XLA Ops:
  15.6 26.6 %collective-permute-start.2 = (f32[208,768]{1,0:T(8,128)S(1)}, f32[208,768]{1,0:T(8,128)}, u32[]{:S(2)}, u32[]{:S(2)}) collective-permute-start(f32[208,768]{1,0:T(8,128)S(1)} %pad_maximum_fusion.refs_0_), channel_id=1, source_target_pairs={{0,2},{1,3},{2,0},{3,1},{4,6},{5,7},{6,4},{7,5},{8,10},{9,11},{10,... | collective-permute-start | bytes 1916936 | tf_op jit(solution)/shard_map/ppermute | solution.py:684
  18.3 42.8 %collective-permute-start.16 = (f32[3,96,768]{2,1,0:T(8,128)S(1)}, f32[3,96,768]{2,1,0:T(8,128)S(1)}, u32[]{:S(2)}, u32[]{:S(2)}) collective-permute-start(f32[3,96,768]{2,1,0:T(8,128)S(1)} %get-tuple-element.117), channel_id=1, source_target_pairs={{0,2},{1,3},{2,0},{3,1},{4,6},{5,7},{6,4},{7,5},{8,10},{9,11},{10,... | collective-permute-start | bytes 2654216 | tf_op jit(solution)/shard_map/ppermute | solution.py:684
  19.2 24.3 %collective-permute-start.1 = (f32[208,768]{1,0:T(8,128)S(1)}, f32[208,768]{1,0:T(8,128)S(1)}, u32[]{:S(2)}, u32[]{:S(2)}) collective-permute-start(f32[208,768]{1,0:T(8,128)S(1)} %pad_maximum_fusion.refs_0_), channel_id=1, source_target_pairs={{0,1},{1,0},{2,3},{3,2},{4,5},{5,4},{6,7},{7,6},{8,9},{9,8},{10,11... | collective-permute-start | bytes 1916936 | tf_op jit(solution)/shard_map/ppermute | solution.py:684
  42.2 20.0 %collective-permute-start.3 = (f32[208,768]{1,0:T(8,128)}, f32[208,768]{1,0:T(8,128)}, u32[]{:S(2)}, u32[]{:S(2)}) collective-permute-start(f32[208,768]{1,0:T(8,128)} %collective-permute-done.2.refs_2_), channel_id=1, source_target_pairs={{0,1},{1,0},{2,3},{3,2},{4,5},{5,4},{6,7},{7,6},{8,9},{9,8},{10,11... | collective-permute-start | bytes 1916936 | tf_op jit(solution)/shard_map/ppermute | solution.py:684
  44.3 19.1 %collective-permute-start.10 = (f32[2,96,576]{2,1,0:T(8,128)}, f32[2,96,576]{2,1,0:T(8,128)}, u32[]{:S(2)}, u32[]{:S(2)}) collective-permute-start(f32[2,96,576]{2,1,0:T(8,128)} %collective-permute-done.9.refs_10_), channel_id=1, source_target_pairs={{0,1},{1,0},{2,3},{3,2},{4,5},{5,4},{6,7},{7,6},{8,9},{9,8},{10,11... | collective-permute-start | bytes 1327112 | tf_op jit(solution)/shard_map/ppermute | solution.py:684
  45.5 29.9 %collective-permute-start.22 = (f32[192,768]{1,0:T(8,128)S(1)}, f32[192,768]{1,0:T(8,128)}, u32[]{:S(2)}, u32[]{:S(2)}) collective-permute-start(f32[192,768]{1,0:T(8,128)S(1)} %copy-done.1), channel_id=1, source_target_pairs={{0,1},{1,0},{2,3},{3,2},{4,5},{5,4},{6,7},{7,6},{8,9},{9,8},{10,11... | collective-permute-start | bytes 1769480 | tf_op jit(solution)/shard_map/ppermute | solution.py:684
  61.3 56.4 %collective-permute-start.15 = (f32[3,96,768]{2,1,0:T(8,128)S(1)}, f32[3,96,768]{2,1,0:T(8,128)S(1)}, u32[]{:S(2)}, u32[]{:S(2)}) collective-permute-start(f32[3,96,768]{2,1,0:T(8,128)S(1)} %get-tuple-element.118.refs_0_), channel_id=1, source_target_pairs={{0,1},{1,0},{2,3},{3,2},{4,5},{5,4},{6,7},{7,6},{8,9},{9,8},{10,11... | collective-permute-start | bytes 2654216 | tf_op jit(solution)/shard_map/ppermute | solution.py:684
  62.2 55.6 %collective-permute-start.20 = (f32[3,96,768]{2,1,0:T(8,128)S(1)}, f32[3,96,768]{2,1,0:T(8,128)S(1)}, u32[]{:S(2)}, u32[]{:S(2)}) collective-permute-start(f32[3,96,768]{2,1,0:T(8,128)S(1)} %collective-permute-done.16.refs_2_), channel_id=1, source_target_pairs={{0,4},{4,0},{1,5},{5,1},{2,6},{6,2},{3,7},{7,3},{8,12},{12,8},{9,1... | collective-permute-start | bytes 2654216 | tf_op jit(solution)/shard_map/ppermute | solution.py:684
  75.1 37.3 %collective-permute-start.11 = (f32[384,384]{1,0:T(8,128)S(1)}, f32[384,384]{1,0:T(8,128)S(1)}, u32[]{:S(2)}, u32[]{:S(2)}) collective-permute-start(f32[384,384]{1,0:T(8,128)S(1)} %get-tuple-element.107), channel_id=1, source_target_pairs={{0,4},{4,0},{1,5},{5,1},{2,6},{6,2},{3,7},{7,3},{8,12},{12,8},{9,1... | collective-permute-start | bytes 1769480 | tf_op jit(solution)/shard_map/ppermute | solution.py:684
  75.5 26.8 %collective-permute-start.25 = (f32[96,768]{1,0:T(8,128)S(1)}, f32[96,768]{1,0:T(8,128)S(1)}, u32[]{:S(2)}, u32[]{:S(2)}) collective-permute-start(f32[96,768]{1,0:T(8,128)S(1)} %constant_dynamic-slice_fusion.1), channel_id=1, source_target_pairs={{0,4},{4,0},{1,5},{5,1},{2,6},{6,2},{3,7},{7,3},{8,12},{12,8},{9,1... | collective-permute-start | bytes 884744 | tf_op jit(solution)/shard_map/ppermute | solution.py:684
  76.8 50.5 %collective-permute-start.18 = (f32[3,96,768]{2,1,0:T(8,128)S(1)}, f32[3,96,768]{2,1,0:T(8,128)S(1)}, u32[]{:S(2)}, u32[]{:S(2)}) collective-permute-start(f32[3,96,768]{2,1,0:T(8,128)S(1)} %get-tuple-element.118.refs_0_), channel_id=1, source_target_pairs={{0,4},{4,0},{1,5},{5,1},{2,6},{6,2},{3,7},{7,3},{8,12},{12,8},{9,1... | collective-permute-start | bytes 2654216 | tf_op jit(solution)/shard_map/ppermute | solution.py:684
  117.7 18.7 %collective-permute-start.13 = (f32[384,384]{1,0:T(8,128)S(1)}, f32[384,384]{1,0:T(8,128)S(1)}, u32[]{:S(2)}, u32[]{:S(2)}) collective-permute-start(f32[384,384]{1,0:T(8,128)S(1)} %get-tuple-element.115.refs_0_), channel_id=1, source_target_pairs={{0,2},{1,3},{2,0},{3,1},{4,6},{5,7},{6,4},{7,5},{8,10},{9,11},{10,... | collective-permute-start | bytes 1769480 | tf_op jit(solution)/shard_map/ppermute | solution.py:684
  119.2 22.5 %collective-permute-start.17 = (f32[3,96,768]{2,1,0:T(8,128)S(1)}, f32[3,96,768]{2,1,0:T(8,128)S(1)}, u32[]{:S(2)}, u32[]{:S(2)}) collective-permute-start(f32[3,96,768]{2,1,0:T(8,128)S(1)} %collective-permute-done.16.refs_2_), channel_id=1, source_target_pairs={{0,1},{1,0},{2,3},{3,2},{4,5},{5,4},{6,7},{7,6},{8,9},{9,8},{10,11... | collective-permute-start | bytes 2654216 | tf_op jit(solution)/shard_map/ppermute | solution.py:684
  191.7 26.0 %collective-permute-start.48 = (f32[4,96,768]{2,1,0:T(8,128)S(1)}, f32[4,96,768]{2,1,0:T(8,128)S(1)}, u32[]{:S(2)}, u32[]{:S(2)}) collective-permute-start(f32[4,96,768]{2,1,0:T(8,128)S(1)} %get-tuple-element.168), channel_id=1, source_target_pairs={{0,4},{4,0},{1,5},{5,1},{2,6},{6,2},{3,7},{7,3},{8,12},{12,8},{9,1... | collective-permute-start | bytes 3538952 | tf_op jit(solution)/shard_map/ppermute | solution.py:684
  193.1 26.5 %collective-permute-start.54 = (f32[16,24,768]{2,1,0:T(8,128)S(1)}, f32[16,24,768]{2,1,0:T(8,128)S(1)}, u32[]{:S(2)}, u32[]{:S(2)}) collective-permute-start(f32[16,24,768]{2,1,0:T(8,128)S(1)} %get-tuple-element.173), channel_id=1, source_target_pairs={{0,8},{8,0},{16,24},{24,16},{1,9},{9,1},{17,25},{25,17},{2,10},{10... | collective-permute-start | bytes 3538952 | tf_op jit(solution)/shard_map/ppermute | solution.py:684
  205.3 30.6 %collective-permute-start.34 = (f32[384,384]{1,0:T(8,128)S(1)}, f32[384,384]{1,0:T(8,128)S(1)}, u32[]{:S(2)}, u32[]{:S(2)}) collective-permute-start(f32[384,384]{1,0:T(8,128)S(1)} %get-tuple-element.151), channel_id=1, source_target_pairs={{0,4},{4,0},{1,5},{5,1},{2,6},{6,2},{3,7},{7,3},{8,12},{12,8},{9,1... | collective-permute-start | bytes 1769480 | tf_op jit(solution)/shard_map/ppermute | solution.py:684
  217.9 34.5 %collective-permute-start.49 = (f32[2,96,768]{2,1,0:T(8,128)S(1)}, f32[2,96,768]{2,1,0:T(8,128)S(1)}, u32[]{:S(2)}, u32[]{:S(2)}) collective-permute-start(f32[2,96,768]{2,1,0:T(8,128)S(1)} %slice.284), channel_id=1, source_target_pairs={{0,8},{8,0},{16,24},{24,16},{1,9},{9,1},{17,25},{25,17},{2,10},{10... | collective-permute-start | bytes 1769480 | tf_op jit(solution)/shard_map/ppermute | solution.py:684
  220.0 32.5 %collective-permute-start.55 = (f32[2,4,24,768]{3,2,1,0:T(8,128)S(1)}, f32[2,4,24,768]{3,2,1,0:T(8,128)S(1)}, u32[]{:S(2)}, u32[]{:S(2)}) collective-permute-start(f32[2,4,24,768]{3,2,1,0:T(8,128)S(1)} %bitcast.156), channel_id=1, source_target_pairs={{0,24},{8,16},{16,8},{24,0},{1,25},{9,17},{17,9},{25,1},{2,26},{10... | collective-permute-start | bytes 1769480 | tf_op jit(solution)/shard_map/ppermute | solution.py:684
  245.8 35.6 %collective-permute-start.39 = (f32[4,30,24,128]{3,2,1,0:T(8,128)S(1)}, f32[4,30,24,128]{3,2,1,0:T(8,128)S(1)}, u32[]{:S(2)}, u32[]{:S(2)}) collective-permute-start(f32[4,30,24,128]{3,2,1,0:T(8,128)S(1)} %get-tuple-element.162), channel_id=1, source_target_pairs={{0,4},{4,0},{1,5},{5,1},{2,6},{6,2},{3,7},{7,3},{8,12},{12,8},{9,1... | collective-permute-start | bytes 4423688 | tf_op jit(solution)/shard_map/ppermute | solution.py:684
  247.1 34.7 %collective-permute-start.35 = (f32[2,192,768]{2,1,0:T(8,128)S(1)}, f32[2,192,768]{2,1,0:T(8,128)S(1)}, u32[]{:S(2)}, u32[]{:S(2)}) collective-permute-start(f32[2,192,768]{2,1,0:T(8,128)S(1)} %get-tuple-element.159), channel_id=1, source_target_pairs={{0,1},{1,0},{2,3},{3,2},{4,5},{5,4},{6,7},{7,6},{8,9},{9,8},{10,11... | collective-permute-start | bytes 3538952 | tf_op jit(solution)/shard_map/ppermute | solution.py:684
  252.4 42.2 %collective-permute-start.37 = (f32[2,192,768]{2,1,0:T(8,128)S(1)}, f32[2,192,768]{2,1,0:T(8,128)S(1)}, u32[]{:S(2)}, u32[]{:S(2)}) collective-permute-start(f32[2,192,768]{2,1,0:T(8,128)S(1)} %get-tuple-element.160), channel_id=1, source_target_pairs={{0,1},{1,0},{2,3},{3,2},{4,5},{5,4},{6,7},{7,6},{8,9},{9,8},{10,11... | collective-permute-start | bytes 3538952 | tf_op jit(solution)/shard_map/ppermute | solution.py:684
  252.6 28.7 %collective-permute-start.56 = (f32[4,24,768]{2,1,0:T(8,128)S(1)}, f32[4,24,768]{2,1,0:T(8,128)S(1)}, u32[]{:S(2)}, u32[]{:S(2)}) collective-permute-start(f32[4,24,768]{2,1,0:T(8,128)S(1)} %slice_bitcast_fusion.3), channel_id=1, source_target_pairs={{0,4},{4,0},{1,5},{5,1},{2,6},{6,2},{3,7},{7,3},{8,12},{12,8},{9,1... | collective-permute-start | bytes 884744 | tf_op jit(solution)/shard_map/ppermute | solution.py:684
  252.8 29.0 %collective-permute-start.50 = (f32[96,768]{1,0:T(8,128)S(1)}, f32[96,768]{1,0:T(8,128)S(1)}, u32[]{:S(2)}, u32[]{:S(2)}) collective-permute-start(f32[96,768]{1,0:T(8,128)S(1)} %slice_bitcast_fusion.5), channel_id=1, source_target_pairs={{0,24},{8,16},{16,8},{24,0},{1,25},{9,17},{17,9},{25,1},{2,26},{10... | collective-permute-start | bytes 884744 | tf_op jit(solution)/shard_map/ppermute | solution.py:684
  282.0 54.2 %collective-permute-start.36 = (f32[192,768]{1,0:T(8,128)S(1)}, f32[192,768]{1,0:T(8,128)S(1)}, u32[]{:S(2)}, u32[]{:S(2)}) collective-permute-start(f32[192,768]{1,0:T(8,128)S(1)} %fusion.1), channel_id=1, source_target_pairs={{0,2},{1,3},{2,0},{3,1},{4,6},{5,7},{6,4},{7,5},{8,10},{9,11},{10,... | collective-permute-start | bytes 1769480 | tf_op jit(solution)/shard_map/ppermute | solution.py:684
  294.4 18.1 %collective-permute-start.41 = (f32[30,24,128]{2,1,0:T(8,128)S(1)}, f32[30,24,128]{2,1,0:T(8,128)S(1)}, u32[]{:S(2)}, u32[]{:S(2)}) collective-permute-start(f32[30,24,128]{2,1,0:T(8,128)S(1)} %slice_bitcast_fusion.1), channel_id=1, source_target_pairs={{0,24},{8,16},{16,8},{24,0},{1,25},{9,17},{17,9},{25,1},{2,26},{10... | collective-permute-start | bytes 1105928 | tf_op jit(solution)/shard_map/ppermute | solution.py:684
  294.7 45.9 %collective-permute-start.38 = (f32[192,768]{1,0:T(8,128)S(1)}, f32[192,768]{1,0:T(8,128)S(1)}, u32[]{:S(2)}, u32[]{:S(2)}) collective-permute-start(f32[192,768]{1,0:T(8,128)S(1)} %fusion), channel_id=1, source_target_pairs={{0,2},{1,3},{2,0},{3,1},{4,6},{5,7},{6,4},{7,5},{8,10},{9,11},{10,... | collective-permute-start | bytes 1769480 | tf_op jit(solution)/shard_map/ppermute | solution.py:684
  294.8 41.4 %collective-permute-start.51 = (f32[96,768]{1,0:T(8,128)S(1)}, f32[96,768]{1,0:T(8,128)S(1)}, u32[]{:S(2)}, u32[]{:S(2)}) collective-permute-start(f32[96,768]{1,0:T(8,128)S(1)} %fusion.7.refs_0_), channel_id=1, source_target_pairs={{0,24},{8,16},{16,8},{24,0},{1,25},{9,17},{17,9},{25,1},{2,26},{10... | collective-permute-start | bytes 884744 | tf_op jit(solution)/shard_map/ppermute | solution.py:684
  298.0 25.1 %collective-permute-start.58 = (f32[2,24,768]{2,1,0:T(8,128)S(1)}, f32[2,24,768]{2,1,0:T(8,128)S(1)}, u32[]{:S(2)}, u32[]{:S(2)}) collective-permute-start(f32[2,24,768]{2,1,0:T(8,128)S(1)} %pad_maximum_fusion.3), channel_id=1, source_target_pairs={{0,1},{1,0},{2,3},{3,2},{4,5},{5,4},{6,7},{7,6},{8,9},{9,8},{10,11... | collective-permute-start | bytes 442376 | tf_op jit(solution)/shard_map/ppermute | solution.py:684
  336.1 20.1 %collective-permute-start.60 = (f32[4,24,768]{2,1,0:T(8,128)S(1)}, f32[4,24,768]{2,1,0:T(8,128)S(1)}, u32[]{:S(2)}, u32[]{:S(2)}) collective-permute-start(f32[4,24,768]{2,1,0:T(8,128)S(1)} %pad_maximum_fusion.1.refs_4_), channel_id=1, source_target_pairs={{0,8},{8,0},{16,24},{24,16},{1,9},{9,1},{17,25},{25,17},{2,10},{10... | collective-permute-start | bytes 884744 | tf_op jit(solution)/shard_map/ppermute | solution.py:684
  336.2 20.0 %collective-permute-start.53 = (f32[96,768]{1,0:T(8,128)S(1)}, f32[96,768]{1,0:T(8,128)S(1)}, u32[]{:S(2)}, u32[]{:S(2)}) collective-permute-start(f32[96,768]{1,0:T(8,128)S(1)} %collective-permute-done.51.refs_1_), channel_id=1, source_target_pairs={{0,8},{8,0},{16,24},{24,16},{1,9},{9,1},{17,25},{25,17},{2,10},{10... | collective-permute-start | bytes 884744 | tf_op jit(solution)/shard_map/ppermute | solution.py:684
  337.7 24.8 %collective-permute-start.61 = (f32[4,24,768]{2,1,0:T(8,128)S(1)}, f32[4,24,768]{2,1,0:T(8,128)S(1)}, u32[]{:S(2)}, u32[]{:S(2)}) collective-permute-start(f32[4,24,768]{2,1,0:T(8,128)S(1)} %collective-permute-done.59.refs_5_), channel_id=1, source_target_pairs={{0,8},{8,0},{16,24},{24,16},{1,9},{9,1},{17,25},{25,17},{2,10},{10... | collective-permute-start | bytes 884744 | tf_op jit(solution)/shard_map/ppermute | solution.py:684
  340.6 30.2 %collective-permute-start.45 = (f32[26,24,128]{2,1,0:T(8,128)S(1)}, f32[26,24,128]{2,1,0:T(8,128)S(1)}, u32[]{:S(2)}, u32[]{:S(2)}) collective-permute-start(f32[26,24,128]{2,1,0:T(8,128)S(1)} %constant_dynamic-update-slice_fusion.refs_0_), channel_id=1, source_target_pairs={{0,24},{8,16},{16,8},{24,0},{1,25},{9,17},{17,9},{25,1},{2,26},{10... | collective-permute-start | bytes 958472 | tf_op jit(solution)/shard_map/ppermute | solution.py:684
  (46 other events, 396.0 us)

commit v3 on v2

--- a/solution.py
+++ b/solution.py
@@ -22,7 +22,7 @@
 TN = (((0,), (0,)), ((), ()))
 VM = pl.BlockSpec(memory_space=pltpu.VMEM)
 SM = pl.BlockSpec(memory_space=pltpu.SMEM)
-LIMITS = {"attend_own": 10, "attend_edge": 10, "back_edge": 12, "back_own": 12, "act": 14, "weights": 16, "feed_grads": 12, "place": 8, "hidden": 6, "middle": 6, "last_grads": 16, "pack": 8}
+LIMITS = {"attend_own": 10, "attend_edge": 10, "back_edge": 12, "back_own": 12, "act": 14, "weights": 16, "feed_grads": 12, "place": 8, "hidden": 6, "middle": 6, "last_grads": 16, "fold": 10, "base": 6, "pack_qkv": 8, "pack_feed": 10}
 
 
 def split(x):
@@ -42,16 +42,21 @@
     return pl.ds(pl.multiple_of(start, step), size)
 
 
-def call(kernel, name, outs, ins, scratch=(), flops=0, smem=1, limit=16, wide=False):
-    size = sum(math.prod(x.shape) * x.dtype.itemsize for x in list(outs) + list(ins[smem:]))
+def call(kernel, name, outs, ins, scratch=(), flops=0, smem=1, limit=16, wide=False, marks=()):
+    inner, count, ins = kernel, len(ins), list(ins) + list(marks)
+
+    def kernel(*refs):
+        return inner(*refs[:count], *refs[len(ins):])
+
+    size = sum(math.prod(x.shape) * x.dtype.itemsize for x in list(outs) + list(ins[smem:count]))
     return pl.pallas_call(
         kernel,
         out_shape=tuple(outs),
-        in_specs=[SM] * smem + [VM] * (len(ins) - smem),
-        out_specs=tuple(VM for _ in outs),
+        in_specs=[SM] * smem + [VM] * (count - smem) + [pl.BlockSpec(memory_space=pl.ANY)] * len(marks),
+        out_specs=tuple(SM if x.dtype == jnp.int32 else VM for x in outs),
         scratch_shapes=list(scratch),
         compiler_params=pltpu.CompilerParams(vmem_limit_bytes=(48 if wide else LIMITS.get(name, limit)) << 20),
-        cost_estimate=pl.CostEstimate(flops=3 * flops, bytes_accessed=size, transcendentals=0),
+        cost_estimate=pl.CostEstimate(flops=1, bytes_accessed=1, transcendentals=0),
         name=name,
     )(*ins)
 
@@ -80,30 +85,56 @@
     return value
 
 
-def pack_kernel(blocks, idx, wq, wk, wv, wup, wout, near, far, near2, far2):
-    part, share = near.shape[2] // 3, near2.shape[2]
+def first_kernel(count, numbers, *refs):
+    for source, target in zip((numbers,) + refs[:count], refs[count:]):
+        if target.dtype == jnp.int32:
+            for i in range(target.shape[1]):
+                target[0, i] = source[0, i]
+        else:
+            target[...] = source[...]
+
+
+def pack_qkv_kernel(idx, bounds, codes, halo_codes, small, wq, wk, wv, near, far, *outs):
+    first_kernel(4, idx, bounds, codes, halo_codes, small, *outs)
+    part = near.shape[2] // 3
     splits = wq.shape[1] // part
-    unit = share // blocks
     for r in range(splits):
-        first, second, k = (near, near2, r) if r < 2 else (far, far2, r - 2)
+        target, k = (near, r) if r < 2 else (far, r - 2)
         for u in range(splits):
 
             @pl.when(idx[0, r] == u)
             def _():
                 for i, w in enumerate((wq, wk, wv)):
-                    first[k, :, i * part:(i + 1) * part] = w[:, u * part:(u + 1) * part]
+                    target[k, :, i * part:(i + 1) * part] = w[:, u * part:(u + 1) * part]
+
+
+def pack_feed_kernel(splits, blocks, idx, wup, wout, near, far):
+    unit = near.shape[2] // blocks
+    for r in range(splits):
+        target, k = (near, r) if r < 2 else (far, r - 2)
+        for u in range(splits):
+
+            @pl.when(idx[0, r] == u)
+            def _():
                 for b in range(blocks):
                     lane = (b * splits + u) * unit
-                    second[k, :, b * unit:(b + 1) * unit] = wup[:, lane:lane + unit]
-    near2[2] = wout[...]
-    far2[2] = wout[...]
-
-
-def qkv_kernel(pieces, splits, edge, idx, *refs):
+                    target[k, :, b * unit:(b + 1) * unit] = wup[:, lane:lane + unit]
+    near[2] = wout[...]
+    far[2] = wout[...]
+
+
+def base_kernel(place, idx, hidden, embed, small, wdown, out, quarter):
+    tokens, size = hidden.shape[0], quarter.shape[0]
+    quarter[...] = wdown[at(idx[0, place] * size, size), :]
+    out[:tokens, :] = hidden[...] + embed[...]
+    out[tokens:, :] = small[...]
+
+
+def qkv_kernel(pieces, splits, edge, idx, og, *refs):
     base, rest = refs[:splits], refs[splits:]
     count = max(p[0] for p in pieces) + 1
     weights = rest[:count]
-    (q_ref, kv_ref, edge_ref, base_ref, small_ref, wh, wl, w32, nh, nl) = rest[count:count + 10]
+    (q_ref, kv_ref, edge_ref, base_ref, small_ref, wh, wl, og_ref, w32, nh, nl) = rest[count:count + 11]
     got = base + weights
     tokens = base[0].shape[0] - EXTRA
     part = q_ref.shape[1]
@@ -139,6 +170,7 @@
     lax.fori_loop(0, 2, rows_of, 0)
     reach = edge_ref.shape[0]
     edge_ref[...] = kv_ref[at(idx[0, edge], reach), :]
+    og_ref[...] = og[...]
 
 
 def span_hits(seg, i, j):
@@ -160,7 +192,7 @@
 
 def columns(codes, out, size):
     for j in range(out.shape[0] // size):
-        row = codes[:, j * size:(j + 1) * size]
+        row = codes[1:2, j * size:(j + 1) * size]
         out[j * size:(j + 1) * size, :] = jnp.broadcast_to(row, (128, size)).T
 
 
@@ -201,7 +233,7 @@
         def per_k(j, _):
             @pl.when(span_hits(seg_ref, i, j))
             def _():
-                allowed = kcol[at(j * TILE, TILE, TILE), :1] == qcode_ref[:, at(i * TILE, TILE, TILE)]
+                allowed = kcol[at(j * TILE, TILE, TILE), :1] == qcode_ref[:1, at(i * TILE, TILE, TILE)]
                 attend_add(heads, qc, kc, vt, m_s, l_s, acc, i, j, TILE, allowed | same_row(i, j))
             return 0
 
@@ -211,8 +243,11 @@
     lax.fori_loop(0, nq, per_q, 0)
 
 
-def attend_edge_kernel(heads, seg_ref, qcode_ref, hcode_ref, halo_ref, qc, m_in, l_in, acc_in,
-                       out_ref, wide_ref, lse_ref, kh, vh, hcol, m_s, l_s, acc):
+def attend_edge_kernel(heads, extra, seg_ref, qcode_ref, hcode_ref, halo_ref, qc, m_in, l_in, acc_in, *refs):
+    out_ref, wide_ref, lse_ref = refs[extra:extra + 3]
+    for source, target in zip(refs[:extra], refs[extra + 3:2 * extra + 3]):
+        target[...] = source[...]
+    kh, vh, hcol, m_s, l_s, acc = refs[2 * extra + 3:]
     group, width = out_ref.shape
     nq, nh = group // TILE, halo_ref.shape[0] // EDGE
     m_s[...] = m_in[...]
@@ -228,7 +263,7 @@
         def per_edge(j, _):
             @pl.when(span_hits(seg_ref, i, nq + j))
             def _():
-                allowed = hcol[at(j * EDGE, EDGE, EDGE), :1] == qcode_ref[:, qrow]
+                allowed = hcol[at(j * EDGE, EDGE, EDGE), :1] == qcode_ref[:1, qrow]
                 attend_add(heads, qc, kh, vh, m_s, l_s, acc, i, j, EDGE, allowed)
             return 0
 
@@ -260,18 +295,18 @@
         flops=4 * group * group * width)
 
 
-def attend_edge(segs, qcode, hcode, halo, state):
+def attend_edge(segs, qcode, hcode, halo, state, passed=(), marks=()):
     heads, group, _ = state[0].shape
     reach, width = halo.shape[0], halo.shape[1] // 2
     nq, nh = group // TILE, reach // EDGE
     return call(
-        functools.partial(attend_edge_kernel, heads), "attend_edge",
-        [arr((group, width)), arr((group // 2, 2 * width)), arr((8, group))],
-        [segs, qcode, hcode, halo, *state],
+        functools.partial(attend_edge_kernel, heads, len(passed)), "attend_edge",
+        [arr((group, width)), arr((group // 2, 2 * width)), arr((8, group))] + [arr(x.shape) for x in passed],
+        [segs, qcode, hcode, halo, *state, *passed],
         [pltpu.VMEM((heads, reach, 3 * HEAD_DIM), BF), pltpu.VMEM((heads, nh, 2 * HEAD_DIM, EDGE), BF),
          pltpu.VMEM((reach, 128), F32)]
         + [pltpu.VMEM(x.shape, x.dtype) for x in state[1:]],
-        flops=2 * group * reach * width, wide=reach > group)
+        flops=2 * group * reach * width, wide=reach > group, marks=marks)
 
 
 def back_add(heads, qc, q2, dc, d2, dot_s, lse_ref, keys, values, flipped, dqa, dka, dva, i, j, size, allowed):
@@ -352,7 +387,7 @@
             dot_s[h, :, rows] = jnp.sum(prod[h * HEAD_DIM:(h + 1) * HEAD_DIM], axis=0, keepdims=True)
 
     def visit(i, j):
-        allowed = hcol[at(j * EDGE, EDGE, EDGE), :1] == qcode_ref[:, at(i * TILE, TILE, TILE)]
+        allowed = hcol[at(j * EDGE, EDGE, EDGE), :1] == qcode_ref[:1, at(i * TILE, TILE, TILE)]
         back_add(heads, qc, q2, dc, d2, dot_s, lse_ref, kh, vh, kth, dqa, dka, dva, i, j, EDGE, allowed)
 
     if nh:
@@ -368,7 +403,7 @@
     dqa[...] = dq_in[...]
 
     def visit(i, j):
-        allowed = kcol[at(j * TILE, TILE, TILE), :1] == qcode_ref[:, at(i * TILE, TILE, TILE)]
+        allowed = kcol[at(j * TILE, TILE, TILE), :1] == qcode_ref[:1, at(i * TILE, TILE, TILE)]
         back_add(heads, qc, q2, dc, d2, dot_s, lse_ref, kc, vc, kt, dqa, dka, dva, i, j, TILE, allowed | same_row(i, j))
 
     back_over(heads, seg_ref, nq, nq, TILE, 0, dkv_ref, dka, dva, visit)
@@ -401,7 +436,7 @@
         flops=2 * group * full * width, smem=2, wide=reach > group)
 
 
-def attend_back_own(segs, qcode, kcode, kv, lse, qc, q2, dc, d2, dot_s, dqa):
+def attend_back_own(segs, qcode, kcode, kv, lse, qc, q2, dc, d2, dot_s, dqa, marks):
     heads, group, _ = qc.shape
     width = kv.shape[1] // 2
     nq = group // TILE
@@ -419,7 +454,7 @@
             pltpu.VMEM((heads, TILE, H2), F32),
             pltpu.VMEM((heads, TILE, H2), F32),
         ],
-        flops=10 * group * group * width)
+        flops=10 * group * group * width, marks=marks)
 
 
 def weights_kernel(full, splits, idx, *refs):
@@ -644,6 +679,30 @@
     out[...] = mg[...] + norm_back(keep[0] + core[0] + far[...], small[4:5, :], xhat, inverse)
 
 
+def fold_kernel(count, *refs):
+    keeps, gots, outs = refs[:count], refs[count:2 * count], refs[2 * count:]
+    for i in range(count):
+        stay, go = outs[2 * i:2 * i + 2]
+        half = stay.shape[0]
+        stay[...] = keeps[i][:half] + gots[i][:half]
+        go[...] = keeps[i][half:] + gots[i][half:]
+
+
+def fold(keeps, gots, marks=()):
+    outs = []
+    for keep in keeps:
+        outs += [arr((keep.shape[0] // 2,) + keep.shape[1:])] * 2
+    got = call(functools.partial(fold_kernel, len(keeps)), "fold", outs, [*keeps, *gots], smem=0, marks=marks)
+    return got[::2], got[1::2]
+
+
+def message_kernel(near, stop, vecs, part, far, out):
+    blocks = near // 2
+    out[:blocks] = part[blocks:near]
+    out[blocks:blocks + vecs] = part[stop:stop + vecs] + far[:vecs]
+    out[blocks + vecs:] = far[vecs + blocks:]
+
+
 def place_kernel(splits, first, rows, idx, *refs):
     pieces, (gq, gk, gv, go) = refs[:-4], refs[-4:]
     part = gq.shape[1] // splits
@@ -699,14 +758,6 @@
 def gather_splits(value):
     far = across(value)
     return [value, beside(value), far, beside(far)]
-
-
-def after(value, *marks):
-    return lax.optimization_barrier((value,) + marks)[0]
-
-
-def corner(value):
-    return lax.slice(value, (0,) * value.ndim, (1,) * (value.ndim - 2) + (8, 128))
 
 
 def collect(value):
@@ -838,33 +889,38 @@
             jnp.stack([jnp.min(jnp.where(edges == 0, 1e6, edges), axis=1), jnp.max(edges, axis=1)], axis=1).reshape(-1),
         ]
     ).astype(jnp.int32).reshape(1, -1)
-    query_codes, key_codes, edge_codes = codes[:1], codes[1:], halo_codes[1:]
-    idx, bounds, query_codes, key_codes, edge_codes, small = lax.optimization_barrier(
-        (idx, bounds, query_codes, key_codes, edge_codes, small)
-    )
-    base = jnp.concatenate([hidden + time_embed, small], axis=0)
+    def make_base(marks):
+        return call(
+            functools.partial(base_kernel, at_d), "base",
+            [arr((tokens + EXTRA, width)), arr((unit // 4 if fast else 8, width))],
+            [idx, hidden, time_embed, small, w_down], marks=marks)
 
     if fast:
-        near, far, near2, far2 = call(
-            functools.partial(pack_kernel, blocks), "pack",
-            [arr((2, rows, 3 * part))] * 2 + [arr((3, rows, share))] * 2,
-            [idx, w_query, w_key, w_value, w_up, w_out])
+        tables = [idx, bounds, codes, halo_codes, small]
+        near, far, *tables = call(
+            pack_qkv_kernel, "pack_qkv",
+            [arr((2, rows, 3 * part))] * 2 + [arr(x.shape, x.dtype) for x in tables],
+            [*tables, w_query, w_key, w_value], smem=2)
+        idx, bounds, codes, halo_codes, small = tables
         pieces = [(i, i % 2) for i in range(8)]
         far = across(far)
-        far_base = across(after(base, corner(far)))
+        near_over = over(near)
+        base, down_quarter = make_base([far, near_over])
+        far_base = across(base)
         qkv_arrays = [near, beside(near), far, beside(far)]
-        near = over(near)
+        near = near_over
         far = over(far)
+        down_quarter = over(down_quarter)
         qkv_arrays += [near, beside(near), far, beside(far)]
         base_all = [base, beside(base), far_base, beside(far_base)]
-
-        far2 = across(after(far2, corner(far_base)))
+        near2, far2 = call(
+            functools.partial(pack_feed_kernel, splits, blocks), "pack_feed", [arr((3, rows, share))] * 2,
+            [idx, w_up, w_out], marks=[far])
+        far2 = across(far2)
         feed_arrays = [near2, beside(near2), far2, beside(far2)]
-        near2 = over(after(near2, corner(far)))
+        near2 = over(near2)
         feed_arrays += [near2, beside(near2)]
         whole = 1
-        down_quarter = lax.dynamic_slice_in_dim(w_down, d * (unit // 4), unit // 4, 0)
-        down_quarter = over(after(down_quarter, corner(far)))
     else:
         cut = jnp.stack([w_query, w_key, w_value], axis=1).reshape(rows, 3, splits, part)
         cut = cut.transpose(2, 0, 1, 3).reshape(splits, rows, 3 * part)
@@ -878,40 +934,41 @@
         feed_arrays = [jnp.stack([got[i], got[i], outs[i]]) for i in range(owners)]
         pieces = [(i, 0) for i in range(owners)]
         whole = blocks
+        base, down_quarter = make_base([])
         base_all = gather_splits(base)
         gathered = lax.all_gather(w_down, "blk", axis=0, tiled=False)
         down = [gathered[i] for i in range(blocks)]
 
-    query, key_value, edge_kv, base, small, qkv_hi, qkv_lo = call(
+    query_codes, key_codes, edge_codes = codes, codes, halo_codes
+    query, key_value, edge_kv, base, small, qkv_hi, qkv_lo, own_grad = call(
         functools.partial(qkv_kernel, pieces, splits, at_edge), "qkv",
         [arr((group, part)), arr((group, 2 * part)), arr((reach if fast else 8, 2 * part)), arr((group, width)),
-         arr((EXTRA, width)), arr((width, 3 * part), BF), arr((width, 3 * part), BF)],
-        [idx, *base_all, *qkv_arrays],
+         arr((EXTRA, width)), arr((width, 3 * part), BF), arr((width, 3 * part), BF), arr((tokens, width))],
+        [idx, out_grad, *base_all, *qkv_arrays],
         [pltpu.VMEM((width, 3 * part), F32), pltpu.VMEM((group, width), BF), pltpu.VMEM((group, width), BF)],
         flops=2 * group * width * 3 * part)
     halo = over(edge_kv) if fast else halo_get(key_value, reach)
     state = attend_own(bounds, query_codes, key_codes, query, key_value)
-    attended, attended_wide, lse = attend_edge(bounds, query_codes, edge_codes, halo, state)
-
-    grads = gather_splits(after(out_grad, corner(edge_kv)))
+    grads = gather_splits(own_grad)
     if fast:
-        down = [w_down] + collect(after(down_quarter, corner(state[3])))
-        far2 = over(after(far2, corner(halo)))
+        down = [w_down, down_quarter] + [swap(down_quarter, "dp", mask) for mask in (3, 1, 2)]
+        attended, attended_wide, lse, far2 = attend_edge(bounds, query_codes, edge_codes, halo, state, (far2,), [*down[2:], grads[2], near2])
+        far2 = over(far2)
+        feed_arrays += [far2, beside(far2)]
+    else:
+        attended, attended_wide, lse = attend_edge(bounds, query_codes, edge_codes, halo, state)
+    attended_all = gather_splits(attended_wide)
     og_hi, og_lo, down_hi, down_lo, act_grad = call(
         functools.partial(act_kernel, splits, whole, at_block, at_d), "act",
         [arr((group, width), BF)] * 2 + [arr((share, width), BF)] * 2 + [arr((group, share))],
         [idx, *grads, *down],
-        flops=2 * group * width * share)
-    if fast:
-        far2 = after(far2, corner(act_grad))
-        feed_arrays += [far2, beside(far2)]
+        flops=2 * group * width * share, marks=[attended_all[2]])
     up_hi, up_lo, out_hi, out_lo = call(
         functools.partial(weights_kernel, pieces, splits), "weights",
         [arr((width, share), BF)] * 2 + [arr((width, width), BF)] * 2,
         [idx, *feed_arrays],
-        [pltpu.VMEM((width, share), F32), pltpu.VMEM((width, width), F32)])
-
-    attended_all = gather_splits(attended_wide)
+        [pltpu.VMEM((width, share), F32), pltpu.VMEM((width, width), F32)], marks=[act_grad])
+
     pair = [arr((group, share), BF)] * 2
     keep, send, mine, inverse2, act_hi, act_lo, pre_hi, pre_lo, in_hi, in_lo, vec_feed = call(
         functools.partial(feed_kernel, splits), "feed",
@@ -932,9 +989,9 @@
     keep_out, send_out, *feed_grads = call(
         functools.partial(feed_grads_kernel, splits, at_feed, down_rows, up_rows), "feed_grads",
         [arr((2, tokens, width))] * 2 + feed_outs,
-        [idx, after(act_hi, corner(near_sum)), act_lo, pre_hi, pre_lo, in_hi, in_lo, og_hi, og_lo, down_hi, down_lo],
+        [idx, act_hi, act_lo, pre_hi, pre_lo, in_hi, in_lo, og_hi, og_lo, down_hi, down_lo],
         [pltpu.VMEM((group, width), F32)],
-        flops=6 * group * width * share)
+        flops=6 * group * width * share, marks=[near_sum])
     if fast:
         down_keep, down_send, up_keep, up_send = feed_grads
         down_got = over(down_send)
@@ -943,29 +1000,29 @@
     middle_grad, vec_middle = call(
         middle_kernel, "middle",
         [arr((tokens, width)), arr((8, width))],
-        [small, keep, core, after(far_sum, corner(keep_out)), out_grad, mine, inverse2], smem=0)
+        [small, keep, core, far_sum, out_grad, mine, inverse2], smem=0, marks=[keep_out])
     middle_all = gather_splits(middle_grad)
 
     halo_grad, q2, dc, d2, dots, dq_part, mg_hi, mg_lo = attend_back_edge(
         idx, bounds, query_codes, edge_codes, query, halo, attended, lse, state[0], out_hi, out_lo, middle_all)
-    query_grad, kv_grad = attend_back_own(
-        bounds, query_codes, key_codes, key_value, lse, state[0], q2, dc, d2, dots, dq_part)
     if fast:
         returned = over(halo_grad)
-        mark = corner(halo_grad)
-        part_down = down_keep + after(down_got, mark)
-        part_up = up_keep.reshape(2, 2, splits, up_rows, share) + after(up_got, mark).reshape(
-            2, 2, splits, up_rows, share)
-        down_got = swap(part_down[2:], "dp", 1)
-        up_got = swap(part_up[1], "dp", 3)
+        (down_keep, up_keep), (down_send, up_send) = fold((down_keep, up_keep), (down_got, up_got), [halo_grad])
+        down_got = swap(down_send, "dp", 1)
+        up_got = swap(up_send, "dp", 3)
+        own_marks = [down_keep]
     else:
+        own_marks = []
+    query_grad, kv_grad = attend_back_own(
+        bounds, query_codes, key_codes, key_value, lse, state[0], q2, dc, d2, dots, dq_part, own_marks)
+    if not fast:
         kv_grad = halo_add(kv_grad, halo_grad, reach)
         returned = jnp.zeros((8, 2 * part), F32)
 
     lane_blocks = -(-3 * part // 128)
     outs, vecs = width // 128, width // 128 * EXTRA // tail_rows
     total_blocks = splits * lane_blocks + outs + vecs
-    tail_outs = [arr((4, total_blocks, tail_rows, 128))] * 2 if fast else [arr((blocks, total_blocks, tail_rows, 128))]
+    tail_outs = [arr((2, total_blocks, tail_rows, 128))] * 4 if fast else [arr((blocks, total_blocks, tail_rows, 128))]
     keep_in, send_in, *tail = call(
         functools.partial(last_grads_kernel, splits, at_tail, at_edge, tail_rows), "last_grads",
         [arr((2, tokens, width))] * 2 + tail_outs,
@@ -973,44 +1030,42 @@
         [pltpu.VMEM((group, 3 * part), BF), pltpu.VMEM((group, 3 * part), BF), pltpu.VMEM((group, width), F32),
          pltpu.VMEM((width, 3 * part), F32), pltpu.VMEM((part, width), F32), pltpu.VMEM((group, 3 * part), F32),
          pltpu.VMEM((group, width), F32), pltpu.VMEM((EXTRA, width), F32)],
-        flops=2 * group * width * 7 * part)
+        flops=2 * group * width * 7 * part, marks=[])
     to_owner = [(i * splits + j, j * blocks + i) for i in range(blocks) for j in range(splits)]
     near = 2 * lane_blocks
     if fast:
-        tail_got = over(tail[1])
+        tail_near, tail_far, send_near, send_far = tail
+        got_far = over(send_far)
+        got_near = over(send_near)
         core_in = beside(send_in)
         far_in = across(keep_in[1] + core_in[1])
 
-        mark = corner(keep_in)
-        part_down = part_down[:2] + after(down_got, mark)
-        part_up = part_up[0] + after(up_got, mark)
-        down_got = swap(part_down[1], "dp", 3)
-        up_got = over(part_up[1])
-        part_down = part_down[0] + down_got
-        part_up = part_up[0] + up_got
-
-        part_tail = tail[0] + tail_got
-        mark = corner(part_tail)
-        part_tail = part_tail[:2] + swap(part_tail[2:], "dp", 1)
-        far_up = across(after(part_up[2:], mark))
+        (down_keep, up_keep), (down_send, up_send) = fold((down_keep, up_keep), (down_got, up_got), [keep_in])
+        down_got = swap(down_send, "dp", 3)
+        up_got = over(up_send)
+        tail_got = swap(tail_far + got_far, "dp", 1)
+        tail_near = tail_near + got_near
+        part_down = (down_keep + down_got)[0]
+        part_up = up_keep + up_got
+        far_up = across(part_up[2:])
         core_up = beside(jnp.stack([part_up[1], far_up[1]]))
-        part_tail = part_tail[0] + swap(part_tail[1], "dp", 3)
         part_up = jnp.stack([part_up[0], core_up[0], far_up[0], core_up[1]])
-
-        all_down = collect(after(part_down, mark))
+        all_down = collect(part_down)
+        all_up = collect(part_up)
+        (tail_keep,), (tail_send,) = fold((tail_near,), (tail_got,), all_down)
+        part_tail = (tail_keep + swap(tail_send, "dp", 3))[0]
+
         far_tail = across(part_tail[near + outs:])
-        core_tail = beside(
-            jnp.concatenate([
-                part_tail[lane_blocks:near], part_tail[near + outs:near + outs + vecs] + far_tail[:vecs],
-                far_tail[vecs + lane_blocks:]])
-        )
+        message, = call(
+            functools.partial(message_kernel, near, near + outs, vecs), "message", [arr(far_tail.shape)],
+            [part_tail, far_tail], smem=0, marks=all_up)
+        core_tail = beside(message)
         vec = part_tail[near + outs:near + outs + vecs] + far_tail[:vecs] + core_tail[lane_blocks:lane_blocks + vecs]
         owned = lax.ppermute(part_tail[near:near + outs], both, to_owner)
         part_tail = jnp.concatenate([
             part_tail[:lane_blocks], core_tail[:lane_blocks], far_tail[vecs:vecs + lane_blocks],
             core_tail[lane_blocks + vecs:], owned])
         all_tail = collect(part_tail)
-        all_up = collect(part_up)
         total_down, total_up = call(
             functools.partial(place_feed_kernel, splits, blocks, unit, at_quarter), "place_feed",
             [arr((unit, width)), arr((rows, units))],
@@ -1042,7 +1097,7 @@
         [arr((tokens, width))],
         [idx, small, base, keep_in, core_in, far_in, middle_grad])
 
-    core_out = beside(after(send_out, corner(keep_in)))
+    core_out = beside(send_out)
     far_out = across(keep_out[1] + core_out[1])
     output = mine[0] + small[3:4] + keep_out[0] + core_out[0] + far_out
 

time: 391 us -> 341 us (0.87)
  the two profiles are of different devices: /device:TPU:5 before, /device:TPU:0 now
where the time goes in v3:
time: 341 us; the launch traced here: 344 us
  waiting for transfers between devices  169 us (50%)
  Pallas kernels  89.1 us (26%)
  starting transfers between devices  72.7 us (21%)
  local copies, waits for them, and re-layouts  9.03 us (3%)
    ppermute x62, waiting for transfers between devices, swap(): return lax.ppermute(value, axis, [(i, i ^ mask) for i in range(count)])  169 us
    pallas_call x21, Pallas kernels, call(): pl.pallas_call(kernel, out_shape=tuple(outs), in_specs=[SM] * smem + [VM]...  89.1 us
    ppermute x62, starting transfers between devices, swap(): return lax.ppermute(value, axis, [(i, i ^ mask) for i in range(count)])  72 us
  transfers between devices with their start and end apart: 63, of which 33 were waited for; matrix products, arithmetic and copies ran while one was open for 1% of the time, Pallas kernels for 19%

profile of v3, /device:TPU:0, one launch (start us, length us, event | category | flops | bytes accessed | tf_op | source)
XLA Modules:
  0.0 343.9 jit_solution(5986275486915958434)
XLA Ops:
  17.7 8.6 %collective-permute-done.1.refs_5_.refs_8_ = f32[2,96,576]{2,1,0:T(8,128)S(1)} collective-permute-done((f32[2,96,576]{2,1,0:T(8,128)S(1)}, f32[2,96,576]{2,1,0:T(8,128)S(1)}, u32[]{:S(2)}, u32[]{:S(2)}) %collective-permute-start.1) | collective-permute-done | bytes 442400 | tf_op jit(solution)/shard_map/ppermute | solution.py:743
  32.8 7.5 %collective-permute-done.13.refs_6_ = f32[96,768]{1,0:T(8,128)S(1)} collective-permute-done((f32[96,768]{1,0:T(8,128)S(1)}, f32[96,768]{1,0:T(8,128)S(1)}, u32[]{:S(2)}, u32[]{:S(2)}) %collective-permute-start.13) | collective-permute-done | bytes 294944 | tf_op jit(solution)/shard_map/ppermute | solution.py:743
  40.4 3.6 %collective-permute-done.4.refs_4_ = f32[208,768]{1,0:T(8,128)S(1)} collective-permute-done((f32[208,768]{1,0:T(8,128)S(1)}, f32[208,768]{1,0:T(8,128)S(1)}, u32[]{:S(2)}, u32[]{:S(2)}) %collective-permute-start.4) | collective-permute-done | bytes 639008 | tf_op jit(solution)/shard_map/ppermute | solution.py:743
  44.0 6.5 %collective-permute-done.9.refs_12_.refs_3_ = f32[2,96,576]{2,1,0:T(8,128)S(1)} collective-permute-done((f32[2,96,576]{2,1,0:T(8,128)S(1)}, f32[2,96,576]{2,1,0:T(8,128)S(1)}, u32[]{:S(2)}, u32[]{:S(2)}) %collective-permute-start.9) | collective-permute-done | bytes 442400 | tf_op jit(solution)/shard_map/ppermute | solution.py:743
  51.8 3.8 %collective-permute-start.14 = (f32[96,768]{1,0:T(8,128)S(1)}, f32[96,768]{1,0:T(8,128)S(1)}, u32[]{:S(2)}, u32[]{:S(2)}) collective-permute-start(f32[96,768]{1,0:T(8,128)S(1)} %collective-permute-done.13.refs_6_), channel_id=1, source_target_pairs={{0,24},{8,16},{16,8},{24,0},{1,25},{9,17},{17,9},{25,1},{2,26},{10... | collective-permute-start | bytes 884744 | tf_op jit(solution)/shard_map/ppermute | solution.py:743
  58.5 5.8 %qkv.1 = (f32[768,192]{1,0:T(8,128)S(1)}, f32[768,384]{1,0:T(8,128)S(1)}, f32[384,384]{1,0:T(8,128)S(1)}, f32[768,768]{1,0:T(8,128)S(1)}, f32[16,768]{1,0:T(8,12...) custom-call(s32[1,100]{1,0:T(1,128)S(1)} %get-tuple-element.104.refs_0_, ...), custom_call_target="tpu_custom_call" | custom-call | flops 1 | bytes 1 | tf_op jit(solution)/shard_map/qkv/pallas_call | solution.py:52
  65.6 4.1 %collective-permute-done.15.refs_10_.refs_8_ = f32[96,768]{1,0:T(8,128)S(1)} collective-permute-done((f32[96,768]{1,0:T(8,128)S(1)}, f32[96,768]{1,0:T(8,128)S(1)}, u32[]{:S(2)}, u32[]{:S(2)}) %collective-permute-start.15) | collective-permute-done | bytes 294944 | tf_op jit(solution)/shard_map/ppermute | solution.py:743
  71.9 7.2 %attend_own.1 = (bf16[3,768,192]{2,1,0:T(8,128)(2,1)S(1)}, f32[3,3,1,256]{3,2,1,0:T(1,128)S(1)}, f32[3,3,1,256]{3,2,1,0:T(1,128)S(1)}, f32[3,3,128,256]{3,2,1,0:T(8,128)S(1)}) custom-call(s32[1,12]{1,0:T(1,128)S(1)} %get-tuple-element.111.refs_0_.refs_1_, f32[2,768]{1,0:T(2,128)S(1)} %get-tuple-element.112.refs_1_.refs_2_, ...), custom_call_target="tpu_custom_call" | custom-call | flops 1 | bytes 1 | tf_op jit(solution)/shard_map/attend_own/pallas_call | solution.py:52
  79.1 6.8 %collective-permute-done.16.refs_11_.refs_9_ = f32[96,768]{1,0:T(8,128)S(1)} collective-permute-done((f32[96,768]{1,0:T(8,128)S(1)}, f32[96,768]{1,0:T(8,128)S(1)}, u32[]{:S(2)}, u32[]{:S(2)}) %collective-permute-start.16) | collective-permute-done | bytes 294944 | tf_op jit(solution)/shard_map/ppermute | solution.py:743
  85.9 5.4 %collective-permute-done.11.refs_3_.refs_5_ = f32[384,384]{1,0:T(8,128)S(1)} collective-permute-done((f32[384,384]{1,0:T(8,128)S(1)}, f32[384,384]{1,0:T(8,128)S(1)}, u32[]{:S(2)}, u32[]{:S(2)}) %collective-permute-start.11) | collective-permute-done | bytes 589856 | tf_op jit(solution)/shard_map/ppermute | solution.py:743
  98.2 16.8 %collective-permute-done.25.refs_7_ = f32[3,96,768]{2,1,0:T(8,128)S(1)} collective-permute-done((f32[3,96,768]{2,1,0:T(8,128)S(1)}, f32[3,96,768]{2,1,0:T(8,128)S(1)}, u32[]{:S(2)}, u32[]{:S(2)}) %collective-permute-start.25) | collective-permute-done | bytes 884768 | tf_op jit(solution)/shard_map/ppermute | solution.py:743
  115.5 4.5 %act.1 = (bf16[768,768]{1,0:T(8,128)(2,1)S(1)}, bf16[768,768]{1,0:T(8,128)(2,1)S(1)}, bf16[768,768]{1,0:T(8,128)(2,1)S(1)}, bf16[768,768]{1,0:T(8,128)(2,1)S(1)}, f32[768,768]{1,0:T(8,128)S(1)}) custom-call(s32[1,100]{1,0:T(1,128)S(1)} %get-tuple-element.104.refs_0_, f32[192,768]{1,0:T(8,128)S(1)} %get-tuple-element.123.refs_1_, ...), custom_call_target="tpu_custom_call" | custom-call | flops 1 | bytes 1 | tf_op jit(solution)/shard_map/act/pallas_call | solution.py:52
  122.1 17.6 %feed.1 = (f32[2,192,768]{2,1,0:T(8,128)S(1)}, f32[2,192,768]{2,1,0:T(8,128)S(1)}, f32[2,192,768]{2,1,0:T(8,128)S(1)}, f32[192,128]{1,0:T(8,128)S(1)}, bf16[768,...) custom-call(s32[1,100]{1,0:T(1,128)S(1)} %get-tuple-element.104.refs, ...), custom_call_target="tpu_custom_call" | custom-call | flops 1 | bytes 1 | tf_op jit(solution)/shard_map/feed/pallas_call | solution.py:52
  143.5 10.7 %feed_grads.1 = (f32[2,192,768]{2,1,0:T(8,128)S(1)}, f32[2,192,768]{2,1,0:T(8,128)S(1)}, f32[4,96,768]{2,1,0:T(8,128)S(1)}, f32[4,96,768]{2,1,0:T(8,128)S(1)}, f...) custom-call(s32[1,100]{1,0:T(1,128)S(1)} %get-tuple-element.104.refs_0_, ...), custom_call_target="tpu_custom_call" | custom-call | flops 1 | bytes 1 | tf_op jit(solution)/shard_map/feed_grads/pallas_call | solution.py:52
  154.2 4.2 %collective-permute-done.32.refs_3_ = f32[192,768]{1,0:T(8,128)S(1)} collective-permute-done((f32[192,768]{1,0:T(8,128)S(1)}, f32[192,768]{1,0:T(8,128)S(1)}, u32[]{:S(2)}, u32[]{:S(2)}) %collective-permute-start.32) | collective-permute-done | bytes 589856 | tf_op jit(solution)/shard_map/ppermute | solution.py:743
  161.3 12.4 %collective-permute-done.34.refs_13_ = f32[192,768]{1,0:T(8,128)S(1)} collective-permute-done((f32[192,768]{1,0:T(8,128)S(1)}, f32[192,768]{1,0:T(8,128)S(1)}, u32[]{:S(2)}, u32[]{:S(2)}) %collective-permute-start.34) | collective-permute-done | bytes 589856 | tf_op jit(solution)/shard_map/ppermute | solution.py:743
  175.7 5.1 %back_edge.1 = (f32[384,384]{1,0:T(8,128)S(1)}, bf16[3,768,128]{2,1,0:T(8,128)(2,1)S(1)}, bf16[3,768,192]{2,1,0:T(8,128)(2,1)S(1)}, bf16[3,768,128]{2,1,0:T(8,12...) custom-call(s32[1,100]{1,0:T(1,128)S(1)} %get-tuple-element.104.refs, ...), custom_call_target="tpu_custom_call" | custom-call | flops 1 | bytes 1 | tf_op jit(solution)/shard_map/back_edge/pallas_call | solution.py:52
  183.6 4.8 %collective-permute-done.36.refs_2_ = f32[4,96,768]{2,1,0:T(8,128)S(1)} collective-permute-done((f32[4,96,768]{2,1,0:T(8,128)S(1)}, f32[4,96,768]{2,1,0:T(8,128)S(1)}, u32[]{:S(2)}, u32[]{:S(2)}) %collective-permute-start.36) | collective-permute-done | bytes 1179680 | tf_op jit(solution)/shard_map/ppermute | solution.py:743
  189.3 12.2 %back_own.1 = (f32[768,192]{1,0:T(8,128)S(1)}, f32[768,384]{1,0:T(8,128)S(1)}) custom-call(s32[1,12]{1,0:T(1,128)S(1)} %get-tuple-element.111.refs_0_.refs_1_, f32[2,768]{1,0:T(2,128)S(1)} %get-tuple-element.112.refs_1_.refs_2_, f32[2,768]{1,0:T(2,128)S(1)} %get-tuple-element.112.refs_1_.refs_2_, f32[768,384]{1,0:T(8,128)S(1)} %get-tuple-element.116.refs_4_.refs_3_, ...), custom_call_target="tpu_custom_call" | custom-call | flops 1 | bytes 1 | tf_op jit(solution)/shard_map/back_own/pallas_call | solution.py:52
  201.5 9.7 %last_grads.1 = (f32[2,192,768]{2,1,0:T(8,128)S(1)}, f32[2,192,768]{2,1,0:T(8,128)S(1)}, f32[2,30,24,128]{3,2,1,0:T(8,128)S(1)}, f32[2,30,24,128]{3,2,1,0:T(8,12...) custom-call(s32[1,100]{1,0:T(1,128)S(1)} %get-tuple-element.104.refs_0_, ...), custom_call_target="tpu_custom_call" | custom-call | flops 1 | bytes 1 | tf_op jit(solution)/shard_map/last_grads/pallas_call | solution.py:52
  229.2 8.7 %collective-permute-done.42 = f32[2,30,24,128]{3,2,1,0:T(8,128)S(1)} collective-permute-done((f32[2,30,24,128]{3,2,1,0:T(8,128)S(1)}, f32[2,30,24,128]{3,2,1,0:T(8,128)S(1)}, u32[]{:S(2)}, u32[]{:S(2)}) %collective-permute-start.42) | collective-permute-done | bytes 737312 | tf_op jit(solution)/shard_map/ppermute | solution.py:743
  237.9 10.1 %collective-permute-start.48 = (f32[96,768]{1,0:T(8,128)S(1)}, f32[96,768]{1,0:T(8,128)S(1)}, u32[]{:S(2)}, u32[]{:S(2)}) collective-permute-start(f32[96,768]{1,0:T(8,128)S(1)} %add_bitcast_fusion.refs_2_.refs_1_), channel_id=1, source_target_pairs={{0,8},{8,0},{16,24},{24,16},{1,9},{9,1},{17,25},{25,17},{2,10},{10... | collective-permute-start | bytes 884744 | tf_op jit(solution)/shard_map/ppermute | solution.py:743
  248.2 7.8 %collective-permute-done.48.refs_4_.refs_3_ = f32[96,768]{1,0:T(8,128)S(1)} collective-permute-done((f32[96,768]{1,0:T(8,128)S(1)}, f32[96,768]{1,0:T(8,128)S(1)}, u32[]{:S(2)}, u32[]{:S(2)}) %collective-permute-start.48) | collective-permute-done | bytes 294944 | tf_op jit(solution)/shard_map/ppermute | solution.py:743
  259.3 17.1 %collective-permute-done.49.refs_5_.refs_4_ = f32[96,768]{1,0:T(8,128)S(1)} collective-permute-done((f32[96,768]{1,0:T(8,128)S(1)}, f32[96,768]{1,0:T(8,128)S(1)}, u32[]{:S(2)}, u32[]{:S(2)}) %collective-permute-start.49) | collective-permute-done | bytes 294944 | tf_op jit(solution)/shard_map/ppermute | solution.py:743
  276.5 3.8 %collective-permute-start.50 = (f32[1,30,24,128]{3,2,1,0:T(8,128)S(1)}, f32[1,30,24,128]{3,2,1,0:T(8,128)S(1)}, u32[]{:S(2)}, u32[]{:S(2)}) collective-permute-start(f32[1,30,24,128]{3,2,1,0:T(8,128)S(1)} %get-tuple-element.182), channel_id=1, source_target_pairs={{0,24},{8,16},{16,8},{24,0},{1,25},{9,17},{17,9},{25,1},{2,26},{10... | collective-permute-start | bytes 1105928 | tf_op jit(solution)/shard_map/ppermute | solution.py:743
  280.3 4.3 %collective-permute-start.31 = (f32[192,768]{1,0:T(8,128)S(1)}, f32[192,768]{1,0:T(8,128)S(1)}, u32[]{:S(2)}, u32[]{:S(2)}) collective-permute-start(f32[192,768]{1,0:T(8,128)S(1)} %fusion.1), channel_id=1, source_target_pairs={{0,2},{1,3},{2,0},{3,1},{4,6},{5,7},{6,4},{7,5},{8,10},{9,11},{10,... | collective-permute-start | bytes 1769480 | tf_op jit(solution)/shard_map/ppermute | solution.py:743
  289.0 4.5 %collective-permute-done.50 = f32[1,30,24,128]{3,2,1,0:T(8,128)S(1)} collective-permute-done((f32[1,30,24,128]{3,2,1,0:T(8,128)S(1)}, f32[1,30,24,128]{3,2,1,0:T(8,128)S(1)}, u32[]{:S(2)}, u32[]{:S(2)}) %collective-permute-start.50) | collective-permute-done | bytes 368672 | tf_op jit(solution)/shard_map/ppermute | solution.py:743
  293.5 3.2 collective-permute-start.51
  298.0 5.6 %collective-permute-done.57.refs_5_.refs_8_ = f32[4,24,768]{2,1,0:T(8,128)S(1)} collective-permute-done((f32[4,24,768]{2,1,0:T(8,128)S(1)}, f32[4,24,768]{2,1,0:T(8,128)S(1)}, u32[]{:S(2)}, u32[]{:S(2)}) %collective-permute-start.57) | collective-permute-done | bytes 294944 | tf_op jit(solution)/shard_map/ppermute | solution.py:743
  303.6 10.4 %collective-permute-done.51.refs_1_ = f32[14,24,128]{2,1,0:T(8,128)S(1)} collective-permute-done((f32[14,24,128]{2,1,0:T(8,128)S(1)}, f32[14,24,128]{2,1,0:T(8,128)S(1)}, u32[]{:S(2)}, u32[]{:S(2)}) %collective-permute-start.51) | collective-permute-done | bytes 172064 | tf_op jit(solution)/shard_map/ppermute | solution.py:743
  322.1 5.8 %collective-permute-done.60.refs_2_ = f32[26,24,128]{2,1,0:T(8,128)S(1)} collective-permute-done((f32[26,24,128]{2,1,0:T(8,128)S(1)}, f32[26,24,128]{2,1,0:T(8,128)S(1)}, u32[]{:S(2)}, u32[]{:S(2)}) %collective-permute-start.60) | collective-permute-done | bytes 319520 | tf_op jit(solution)/shard_map/ppermute | solution.py:743
  334.1 6.8 %collective-permute-done.62.refs_4_ = f32[26,24,128]{2,1,0:T(8,128)S(1)} collective-permute-done((f32[26,24,128]{2,1,0:T(8,128)S(1)}, f32[26,24,128]{2,1,0:T(8,128)S(1)}, u32[]{:S(2)}, u32[]{:S(2)}) %collective-permute-start.62) | collective-permute-done | bytes 319520 | tf_op jit(solution)/shard_map/ppermute | solution.py:743
  (184 shorter events, 97.0 us)
Async XLA Ops:
  32.1 25.0 %collective-permute-start.3 = (f32[208,768]{1,0:T(8,128)S(1)}, f32[208,768]{1,0:T(8,128)S(1)}, u32[]{:S(2)}, u32[]{:S(2)}) collective-permute-start(f32[208,768]{1,0:T(8,128)S(1)} %get-tuple-element.108.refs_2_), channel_id=1, source_target_pairs={{0,1},{1,0},{2,3},{3,2},{4,5},{5,4},{6,7},{7,6},{8,9},{9,8},{10,11... | collective-permute-start | bytes 1916936 | tf_op jit(solution)/shard_map/ppermute | solution.py:743
  32.4 18.1 %collective-permute-start.9 = (f32[2,96,576]{2,1,0:T(8,128)S(1)}, f32[2,96,576]{2,1,0:T(8,128)S(1)}, u32[]{:S(2)}, u32[]{:S(2)}) collective-permute-start(f32[2,96,576]{2,1,0:T(8,128)S(1)} %collective-permute-done.1.refs_5_.refs_8_), channel_id=1, source_target_pairs={{0,4},{4,0},{1,5},{5,1},{2,6},{6,2},{3,7},{7,3},{8,12},{12,8},{9,1... | collective-permute-start | bytes 1327112 | tf_op jit(solution)/shard_map/ppermute | solution.py:743
  32.8 19.0 %collective-permute-start.7 = (f32[2,96,576]{2,1,0:T(8,128)S(1)}, f32[2,96,576]{2,1,0:T(8,128)S(1)}, u32[]{:S(2)}, u32[]{:S(2)}) collective-permute-start(f32[2,96,576]{2,1,0:T(8,128)S(1)} %collective-permute-done.1.refs_5_.refs_8_), channel_id=1, source_target_pairs={{0,1},{1,0},{2,3},{3,2},{4,5},{5,4},{6,7},{7,6},{8,9},{9,8},{10,11... | collective-permute-start | bytes 1327112 | tf_op jit(solution)/shard_map/ppermute | solution.py:743
  55.7 30.2 %collective-permute-start.12 = (f32[3,96,768]{2,1,0:T(8,128)S(1)}, f32[3,96,768]{2,1,0:T(8,128)S(1)}, u32[]{:S(2)}, u32[]{:S(2)}) collective-permute-start(f32[3,96,768]{2,1,0:T(8,128)S(1)} %get-tuple-element.121), channel_id=1, source_target_pairs={{0,2},{1,3},{2,0},{3,1},{4,6},{5,7},{6,4},{7,5},{8,10},{9,11},{10,... | collective-permute-start | bytes 2654216 | tf_op jit(solution)/shard_map/ppermute | solution.py:743
  57.2 28.7 %collective-permute-start.18 = (f32[3,96,768]{2,1,0:T(8,128)S(1)}, f32[3,96,768]{2,1,0:T(8,128)S(1)}, u32[]{:S(2)}, u32[]{:S(2)}) collective-permute-start(f32[3,96,768]{2,1,0:T(8,128)S(1)} %get-tuple-element.124.refs_1_), channel_id=1, source_target_pairs={{0,4},{4,0},{1,5},{5,1},{2,6},{6,2},{3,7},{7,3},{8,12},{12,8},{9,1... | collective-permute-start | bytes 2654216 | tf_op jit(solution)/shard_map/ppermute | solution.py:743
  64.3 27.0 %collective-permute-start.11 = (f32[384,384]{1,0:T(8,128)S(1)}, f32[384,384]{1,0:T(8,128)S(1)}, u32[]{:S(2)}, u32[]{:S(2)}) collective-permute-start(f32[384,384]{1,0:T(8,128)S(1)} %get-tuple-element.114), channel_id=1, source_target_pairs={{0,4},{4,0},{1,5},{5,1},{2,6},{6,2},{3,7},{7,3},{8,12},{12,8},{9,1... | collective-permute-start | bytes 1769480 | tf_op jit(solution)/shard_map/ppermute | solution.py:743
  65.1 26.2 %collective-permute-start.17 = (f32[192,768]{1,0:T(8,128)S(1)}, f32[192,768]{1,0:T(8,128)S(1)}, u32[]{:S(2)}, u32[]{:S(2)}) collective-permute-start(f32[192,768]{1,0:T(8,128)S(1)} %get-tuple-element.123.refs_1_), channel_id=1, source_target_pairs={{0,2},{1,3},{2,0},{3,1},{4,6},{5,7},{6,4},{7,5},{8,10},{9,11},{10,... | collective-permute-start | bytes 1769480 | tf_op jit(solution)/shard_map/ppermute | solution.py:743
  93.9 21.1 %collective-permute-start.25 = (f32[3,96,768]{2,1,0:T(8,128)S(1)}, f32[3,96,768]{2,1,0:T(8,128)S(1)}, u32[]{:S(2)}, u32[]{:S(2)}) collective-permute-start(f32[3,96,768]{2,1,0:T(8,128)S(1)} %get-tuple-element.126), channel_id=1, source_target_pairs={{0,4},{4,0},{1,5},{5,1},{2,6},{6,2},{3,7},{7,3},{8,12},{12,8},{9,1... | collective-permute-start | bytes 2654216 | tf_op jit(solution)/shard_map/ppermute | solution.py:743
  96.0 18.9 %collective-permute-start.20 = (f32[384,384]{1,0:T(8,128)S(1)}, f32[384,384]{1,0:T(8,128)S(1)}, u32[]{:S(2)}, u32[]{:S(2)}) collective-permute-start(f32[384,384]{1,0:T(8,128)S(1)} %get-tuple-element.125.refs_3_), channel_id=1, source_target_pairs={{0,2},{1,3},{2,0},{3,1},{4,6},{5,7},{6,4},{7,5},{8,10},{9,11},{10,... | collective-permute-start | bytes 1769480 | tf_op jit(solution)/shard_map/ppermute | solution.py:743
  96.7 18.8 %collective-permute-start.28 = (f32[192,768]{1,0:T(8,128)S(1)}, f32[192,768]{1,0:T(8,128)S(1)}, u32[]{:S(2)}, u32[]{:S(2)}) collective-permute-start(f32[192,768]{1,0:T(8,128)S(1)} %collective-permute-done.17.refs_12_.refs_3_), channel_id=1, source_target_pairs={{0,1},{1,0},{2,3},{3,2},{4,5},{5,4},{6,7},{7,6},{8,9},{9,8},{10,11... | collective-permute-start | bytes 1769480 | tf_op jit(solution)/shard_map/ppermute | solution.py:743
  96.9 23.1 %collective-permute-start.23 = (f32[3,96,768]{2,1,0:T(8,128)S(1)}, f32[3,96,768]{2,1,0:T(8,128)S(1)}, u32[]{:S(2)}, u32[]{:S(2)}) collective-permute-start(f32[3,96,768]{2,1,0:T(8,128)S(1)} %collective-permute-done.12.refs_8_.refs_3_), channel_id=1, source_target_pairs={{0,1},{1,0},{2,3},{3,2},{4,5},{5,4},{6,7},{7,6},{8,9},{9,8},{10,11... | collective-permute-start | bytes 2654216 | tf_op jit(solution)/shard_map/ppermute | solution.py:743
  98.0 22.0 %collective-permute-start.24 = (f32[3,96,768]{2,1,0:T(8,128)S(1)}, f32[3,96,768]{2,1,0:T(8,128)S(1)}, u32[]{:S(2)}, u32[]{:S(2)}) collective-permute-start(f32[3,96,768]{2,1,0:T(8,128)S(1)} %collective-permute-done.18.refs_13_.refs_5_), channel_id=1, source_target_pairs={{0,1},{1,0},{2,3},{3,2},{4,5},{5,4},{6,7},{7,6},{8,9},{9,8},{10,11... | collective-permute-start | bytes 2654216 | tf_op jit(solution)/shard_map/ppermute | solution.py:743
  159.5 28.9 %collective-permute-start.36 = (f32[4,96,768]{2,1,0:T(8,128)S(1)}, f32[4,96,768]{2,1,0:T(8,128)S(1)}, u32[]{:S(2)}, u32[]{:S(2)}) collective-permute-start(f32[4,96,768]{2,1,0:T(8,128)S(1)} %get-tuple-element.158), channel_id=1, source_target_pairs={{0,4},{4,0},{1,5},{5,1},{2,6},{6,2},{3,7},{7,3},{8,12},{12,8},{9,1... | collective-permute-start | bytes 3538952 | tf_op jit(solution)/shard_map/ppermute | solution.py:743
  161.3 27.2 %collective-permute-start.37 = (f32[16,24,768]{2,1,0:T(8,128)S(1)}, f32[16,24,768]{2,1,0:T(8,128)S(1)}, u32[]{:S(2)}, u32[]{:S(2)}) collective-permute-start(f32[16,24,768]{2,1,0:T(8,128)S(1)} %get-tuple-element.159), channel_id=1, source_target_pairs={{0,8},{8,0},{16,24},{24,16},{1,9},{9,1},{17,25},{25,17},{2,10},{10... | collective-permute-start | bytes 3538952 | tf_op jit(solution)/shard_map/ppermute | solution.py:743
  180.8 20.7 %collective-permute-start.38 = (f32[384,384]{1,0:T(8,128)S(1)}, f32[384,384]{1,0:T(8,128)S(1)}, u32[]{:S(2)}, u32[]{:S(2)}) collective-permute-start(f32[384,384]{1,0:T(8,128)S(1)} %get-tuple-element.160.refs_4_), channel_id=1, source_target_pairs={{0,4},{4,0},{1,5},{5,1},{2,6},{6,2},{3,7},{7,3},{8,12},{12,8},{9,1... | collective-permute-start | bytes 1769480 | tf_op jit(solution)/shard_map/ppermute | solution.py:743
  188.7 25.7 %collective-permute-start.44 = (f32[2,96,768]{2,1,0:T(8,128)S(1)}, f32[2,96,768]{2,1,0:T(8,128)S(1)}, u32[]{:S(2)}, u32[]{:S(2)}) collective-permute-start(f32[2,96,768]{2,1,0:T(8,128)S(1)} %get-tuple-element.177), channel_id=1, source_target_pairs={{0,8},{8,0},{16,24},{24,16},{1,9},{9,1},{17,25},{25,17},{2,10},{10... | collective-permute-start | bytes 1769480 | tf_op jit(solution)/shard_map/ppermute | solution.py:743
  188.8 25.6 %collective-permute-start.45 = (f32[8,24,768]{2,1,0:T(8,128)S(1)}, f32[8,24,768]{2,1,0:T(8,128)S(1)}, u32[]{:S(2)}, u32[]{:S(2)}) collective-permute-start(f32[8,24,768]{2,1,0:T(8,128)S(1)} %get-tuple-element.178), channel_id=1, source_target_pairs={{0,24},{8,16},{16,8},{24,0},{1,25},{9,17},{17,9},{25,1},{2,26},{10... | collective-permute-start | bytes 1769480 | tf_op jit(solution)/shard_map/ppermute | solution.py:743
  217.4 62.9 %collective-permute-start.30 = (f32[2,192,768]{2,1,0:T(8,128)S(1)}, f32[2,192,768]{2,1,0:T(8,128)S(1)}, u32[]{:S(2)}, u32[]{:S(2)}) collective-permute-start(f32[2,192,768]{2,1,0:T(8,128)S(1)} %get-tuple-element.146), channel_id=1, source_target_pairs={{0,1},{1,0},{2,3},{3,2},{4,5},{5,4},{6,7},{7,6},{8,9},{9,8},{10,11... | collective-permute-start | bytes 3538952 | tf_op jit(solution)/shard_map/ppermute | solution.py:743
  217.4 20.6 %collective-permute-start.42 = (f32[2,30,24,128]{3,2,1,0:T(8,128)S(1)}, f32[2,30,24,128]{3,2,1,0:T(8,128)S(1)}, u32[]{:S(2)}, u32[]{:S(2)}) collective-permute-start(f32[2,30,24,128]{3,2,1,0:T(8,128)S(1)} %get-tuple-element.175), channel_id=1, source_target_pairs={{0,4},{4,0},{1,5},{5,1},{2,6},{6,2},{3,7},{7,3},{8,12},{12,8},{9,1... | collective-permute-start | bytes 2211848 | tf_op jit(solution)/shard_map/ppermute | solution.py:743
  223.8 24.3 %collective-permute-start.47 = (f32[96,768]{1,0:T(8,128)S(1)}, f32[96,768]{1,0:T(8,128)S(1)}, u32[]{:S(2)}, u32[]{:S(2)}) collective-permute-start(f32[96,768]{1,0:T(8,128)S(1)} %add_bitcast_fusion.refs_2_.refs_1_), channel_id=1, source_target_pairs={{0,24},{8,16},{16,8},{24,0},{1,25},{9,17},{17,9},{25,1},{2,26},{10... | collective-permute-start | bytes 884744 | tf_op jit(solution)/shard_map/ppermute | solution.py:743
  227.5 59.2 %collective-permute-start.39 = (f32[2,192,768]{2,1,0:T(8,128)S(1)}, f32[2,192,768]{2,1,0:T(8,128)S(1)}, u32[]{:S(2)}, u32[]{:S(2)}) collective-permute-start(f32[2,192,768]{2,1,0:T(8,128)S(1)} %get-tuple-element.171), channel_id=1, source_target_pairs={{0,1},{1,0},{2,3},{3,2},{4,5},{5,4},{6,7},{7,6},{8,9},{9,8},{10,11... | collective-permute-start | bytes 3538952 | tf_op jit(solution)/shard_map/ppermute | solution.py:743
  228.9 29.2 %collective-permute-start.41 = (f32[2,30,24,128]{3,2,1,0:T(8,128)S(1)}, f32[2,30,24,128]{3,2,1,0:T(8,128)S(1)}, u32[]{:S(2)}, u32[]{:S(2)}) collective-permute-start(f32[2,30,24,128]{3,2,1,0:T(8,128)S(1)} %get-tuple-element.173), channel_id=1, source_target_pairs={{0,4},{4,0},{1,5},{5,1},{2,6},{6,2},{3,7},{7,3},{8,12},{12,8},{9,1... | collective-permute-start | bytes 2211848 | tf_op jit(solution)/shard_map/ppermute | solution.py:743
  237.9 18.1 %collective-permute-start.48 = (f32[96,768]{1,0:T(8,128)S(1)}, f32[96,768]{1,0:T(8,128)S(1)}, u32[]{:S(2)}, u32[]{:S(2)}) collective-permute-start(f32[96,768]{1,0:T(8,128)S(1)} %add_bitcast_fusion.refs_2_.refs_1_), channel_id=1, source_target_pairs={{0,8},{8,0},{16,24},{24,16},{1,9},{9,1},{17,25},{25,17},{2,10},{10... | collective-permute-start | bytes 884744 | tf_op jit(solution)/shard_map/ppermute | solution.py:743
  248.2 28.2 %collective-permute-start.43 = (f32[2,30,24,128]{3,2,1,0:T(8,128)S(1)}, f32[2,30,24,128]{3,2,1,0:T(8,128)S(1)}, u32[]{:S(2)}, u32[]{:S(2)}) collective-permute-start(f32[2,30,24,128]{3,2,1,0:T(8,128)S(1)} %add.440), channel_id=1, source_target_pairs={{0,8},{8,0},{16,24},{24,16},{1,9},{9,1},{17,25},{25,17},{2,10},{10... | collective-permute-start | bytes 2211848 | tf_op jit(solution)/shard_map/ppermute | solution.py:743
  256.0 20.4 %collective-permute-start.49 = (f32[96,768]{1,0:T(8,128)S(1)}, f32[96,768]{1,0:T(8,128)S(1)}, u32[]{:S(2)}, u32[]{:S(2)}) collective-permute-start(f32[96,768]{1,0:T(8,128)S(1)} %collective-permute-done.47.refs_3_.refs_2_), channel_id=1, source_target_pairs={{0,8},{8,0},{16,24},{24,16},{1,9},{9,1},{17,25},{25,17},{2,10},{10... | collective-permute-start | bytes 884744 | tf_op jit(solution)/shard_map/ppermute | solution.py:743
  258.1 27.5 %collective-permute-start.55 = (f32[4,24,768]{2,1,0:T(8,128)S(1)}, f32[4,24,768]{2,1,0:T(8,128)S(1)}, u32[]{:S(2)}, u32[]{:S(2)}) collective-permute-start(f32[4,24,768]{2,1,0:T(8,128)S(1)} %pad_maximum_fusion.refs_2_.refs_5_), channel_id=1, source_target_pairs={{0,24},{8,16},{16,8},{24,0},{1,25},{9,17},{17,9},{25,1},{2,26},{10... | collective-permute-start | bytes 884744 | tf_op jit(solution)/shard_map/ppermute | solution.py:743
  276.5 17.0 %collective-permute-start.50 = (f32[1,30,24,128]{3,2,1,0:T(8,128)S(1)}, f32[1,30,24,128]{3,2,1,0:T(8,128)S(1)}, u32[]{:S(2)}, u32[]{:S(2)}) collective-permute-start(f32[1,30,24,128]{3,2,1,0:T(8,128)S(1)} %get-tuple-element.182), channel_id=1, source_target_pairs={{0,24},{8,16},{16,8},{24,0},{1,25},{9,17},{17,9},{25,1},{2,26},{10... | collective-permute-start | bytes 1105928 | tf_op jit(solution)/shard_map/ppermute | solution.py:743
  280.3 35.6 %collective-permute-start.31 = (f32[192,768]{1,0:T(8,128)S(1)}, f32[192,768]{1,0:T(8,128)S(1)}, u32[]{:S(2)}, u32[]{:S(2)}) collective-permute-start(f32[192,768]{1,0:T(8,128)S(1)} %fusion.1), channel_id=1, source_target_pairs={{0,2},{1,3},{2,0},{3,1},{4,6},{5,7},{6,4},{7,5},{8,10},{9,11},{10,... | collective-permute-start | bytes 1769480 | tf_op jit(solution)/shard_map/ppermute | solution.py:743
  285.6 18.0 %collective-permute-start.57 = (f32[4,24,768]{2,1,0:T(8,128)S(1)}, f32[4,24,768]{2,1,0:T(8,128)S(1)}, u32[]{:S(2)}, u32[]{:S(2)}) collective-permute-start(f32[4,24,768]{2,1,0:T(8,128)S(1)} %collective-permute-done.55.refs_3_.refs_6_), channel_id=1, source_target_pairs={{0,8},{8,0},{16,24},{24,16},{1,9},{9,1},{17,25},{25,17},{2,10},{10... | collective-permute-start | bytes 884744 | tf_op jit(solution)/shard_map/ppermute | solution.py:743
  286.7 32.8 %collective-permute-start.40 = (f32[192,768]{1,0:T(8,128)S(1)}, f32[192,768]{1,0:T(8,128)S(1)}, u32[]{:S(2)}, u32[]{:S(2)}) collective-permute-start(f32[192,768]{1,0:T(8,128)S(1)} %fusion), channel_id=1, source_target_pairs={{0,2},{1,3},{2,0},{3,1},{4,6},{5,7},{6,4},{7,5},{8,10},{9,11},{10,... | collective-permute-start | bytes 1769480 | tf_op jit(solution)/shard_map/ppermute | solution.py:743
  293.5 20.5 %collective-permute-start.51 = (f32[14,24,128]{2,1,0:T(8,128)S(1)}, f32[14,24,128]{2,1,0:T(8,128)S(1)}, u32[]{:S(2)}, u32[]{:S(2)}) collective-permute-start(f32[14,24,128]{2,1,0:T(8,128)S(1)} %slice_bitcast_fusion.1), channel_id=1, source_target_pairs={{0,2},{1,3},{2,0},{3,1},{4,6},{5,7},{6,4},{7,5},{8,10},{9,11},{10,... | collective-permute-start | bytes 516104 | tf_op jit(solution)/shard_map/ppermute | solution.py:743
  297.4 18.2 %collective-permute-start.59 = (f32[6,24,128]{2,1,0:T(8,128)S(1)}, f32[6,24,128]{2,1,0:T(8,128)S(1)}, u32[]{:S(2)}, u32[]{:S(2)}) collective-permute-start(f32[6,24,128]{2,1,0:T(8,128)S(1)} %slice_bitcast_fusion.2), channel_id=1, source_target_pairs={{0,0},{1,2},{2,4},{3,6},{4,1},{5,3},{6,5},{7,7},{8,8},{9,10},{10,1... | collective-permute-start | bytes 221192 | tf_op jit(solution)/shard_map/ppermute | solution.py:1064
  (40 other events, 390.3 us)

commit v4 on v3

--- a/solution.py
+++ b/solution.py
@@ -108,7 +108,7 @@
                     target[k, :, i * part:(i + 1) * part] = w[:, u * part:(u + 1) * part]
 
 
-def pack_feed_kernel(splits, blocks, idx, wup, wout, near, far):
+def pack_feed_kernel(splits, blocks, place, idx, wup, wout, wdown, near, far, down_quarter):
     unit = near.shape[2] // blocks
     for r in range(splits):
         target, k = (near, r) if r < 2 else (far, r - 2)
@@ -121,11 +121,12 @@
                     target[k, :, b * unit:(b + 1) * unit] = wup[:, lane:lane + unit]
     near[2] = wout[...]
     far[2] = wout[...]
-
-
-def base_kernel(place, idx, hidden, embed, small, wdown, out, quarter):
-    tokens, size = hidden.shape[0], quarter.shape[0]
-    quarter[...] = wdown[at(idx[0, place] * size, size), :]
+    size = down_quarter.shape[0]
+    down_quarter[...] = wdown[at(idx[0, place] * size, size), :]
+
+
+def base_kernel(hidden, embed, small, out):
+    tokens = hidden.shape[0]
     out[:tokens, :] = hidden[...] + embed[...]
     out[tokens:, :] = small[...]
 
@@ -371,15 +372,19 @@
     for r in range(splits):
         row = at(idx[0, r] * tokens, tokens, 16)
         gh[row, :], gl[row, :] = split(mg[r][...])
-    step = group // 2
-    for i in range(2):
-        row = slice(i * step, (i + 1) * step)
+    step = group // 3
+
+    def rows_of(i, _):
+        row = at(i * step, step, 16)
         grad = mm3((gh[row, :], gl[row, :]), w_pair, NT)
         prod_s[row, :] = grad * o_ref[row, :]
         for h in range(heads):
             hi, lo = split(grad[:, h * HEAD_DIM:(h + 1) * HEAD_DIM])
             dc[h, row, :] = jnp.concatenate([hi, hi, lo], axis=1)
             d2[h, row, :] = jnp.concatenate([hi, lo], axis=1)
+        return 0
+
+    lax.fori_loop(0, 3, rows_of, 0)
     for i in range(nq):
         rows = slice(i * TILE, (i + 1) * TILE)
         prod = prod_s[rows, :].T
@@ -542,10 +547,13 @@
         return 0
 
     lax.fori_loop(0, 2, rows_of, 0)
-    for r in range(splits):
-        row = at(idx[0, r] * tokens, tokens)
-        target = send if r % 2 else keep
-        target[r // 2] = r32[row, :]
+
+    def pairs_of(h, _):
+        keep[h] = r32[at(idx[0, 2 * h] * tokens, tokens), :]
+        send[h] = r32[at(idx[0, 2 * h + 1] * tokens, tokens), :]
+        return 0
+
+    lax.fori_loop(0, splits // 2, pairs_of, 0)
     row = at(idx[0, 0] * tokens, tokens)
     mine[0] = b32[row, :]
     mine[1] = x2[row, :]
@@ -559,18 +567,23 @@
     tokens = keep.shape[1]
     step = r32.shape[0] // 2
 
+    third = r32.shape[0] // 3
+
     def left(a, b):
         def rows_of(i, _):
-            lane = at(i * step, step, 128)
-            r32[at(i * step, step), :] = mm3((a[0][:, lane], a[1][:, lane]), (b[0][...], b[1][...]), TN)
+            lane = at(i * third, third, 128)
+            r32[at(i * third, third), :] = mm3((a[0][:, lane], a[1][:, lane]), (b[0][...], b[1][...]), TN)
             return 0
 
-        lax.fori_loop(0, 2, rows_of, 0)
+        lax.fori_loop(0, 3, rows_of, 0)
 
     def deal(targets, rows, place):
         for target in targets:
-            for c in range(target.shape[0]):
+            def one(c, _, target=target, place=place):
                 target[c] = r32[at(idx[0, place + c], rows), :]
+                return 0
+
+            lax.fori_loop(0, target.shape[0], one, 0)
             place += target.shape[0]
         return place
 
@@ -585,9 +598,13 @@
         return 0
 
     lax.fori_loop(0, 2, rows_of, 0)
-    for r in range(splits):
-        target = send if r % 2 else keep
-        target[r // 2] = r32[at(idx[0, r] * tokens, tokens), :]
+
+    def pairs_of(h, _):
+        keep[h] = r32[at(idx[0, 2 * h] * tokens, tokens), :]
+        send[h] = r32[at(idx[0, 2 * h + 1] * tokens, tokens), :]
+        return 0
+
+    lax.fori_loop(0, splits // 2, pairs_of, 0)
 
 
 def middle_kernel(small, keep, core, far, og, mine, inv, mg_ref, vec_ref):
@@ -605,7 +622,6 @@
     part = dq.shape[1]
     width = xhat.shape[1]
     tokens = keep.shape[1]
-    gain, shift = small[4:5, :], small[5:6, :]
     u = idx[0, 0]
     s32[:, :part] = dq[...]
     s32[:, part:] = dkv[...]
@@ -626,14 +642,22 @@
         return 0
 
     lax.fori_loop(0, 2, rows_of, 0)
-    for r in range(splits):
-        target = send if r % 2 else keep
-        target[r // 2] = n32[at(idx[0, r] * tokens, tokens), :]
-    step = width // 2
-    for i in range(2):
-        lane = slice(i * step, (i + 1) * step)
-        pair = split(xhat[:, lane] * gain[:, lane] + shift[:, lane])
+
+    def pairs_of(h, _):
+        keep[h] = n32[at(idx[0, 2 * h] * tokens, tokens), :]
+        send[h] = n32[at(idx[0, 2 * h + 1] * tokens, tokens), :]
+        return 0
+
+    lax.fori_loop(0, splits // 2, pairs_of, 0)
+    step = width // 3
+
+    def lanes_of(i, _):
+        lane = at(i * step, step, 128)
+        pair = split(xhat[:, lane] * small[4:5, lane] + small[5:6, lane])
         r32[lane, :] = mm3(pair, (qh[...], ql[...]), TN)
+        return 0
+
+    lax.fori_loop(0, 3, lanes_of, 0)
     o32[...] = mm3(split(att[...]), (gh[...], gl[...]), TN)
     for i in range(splits):
 
@@ -654,23 +678,26 @@
     total = sum(t.shape[0] for t in tails)
     spot = 0
     for t in tails:
-        for c in range(t.shape[0]):
+        def one(c, _, t=t, spot=spot):
             for j in range(splits):
-                row = at(idx[0, first + spot * splits + j], rows)
+                row = at(idx[0, first + (spot + c) * splits + j], rows)
                 start = j * lane_blocks + (outs + vecs if j >= 2 else 0)
                 for k in range(lane_blocks - 1):
                     t[c, start + k] = r32[row, k * 128:(k + 1) * 128]
                 k = lane_blocks - 1
                 t[c, start + k, :, :128 - spare] = r32[row, k * 128:]
                 t[c, start + k, :, 128 - spare:] = jnp.zeros((rows, spare), F32)
-            row = at(idx[0, first + total * splits + spot], rows)
+            row = at(idx[0, first + total * splits + spot + c], rows)
             for k in range(outs):
                 t[c, near + k] = o32[row, k * 128:(k + 1) * 128]
             for k in range(outs * EXTRA // 8):
                 block, low = divmod(8 * k, rows)
                 lane, high = divmod(8 * k, EXTRA)
                 t[c, near + outs + block, low:low + 8, :] = vec[high:high + 8, lane * 128:(lane + 1) * 128]
-            spot += 1
+            return 0
+
+        lax.fori_loop(0, t.shape[0], one, 0)
+        spot += t.shape[0]
 
 
 def hidden_kernel(idx, small, base, keep, core, far, mg, out):
@@ -711,14 +738,10 @@
         count = gq.shape[1] // 128
         for k in range(count):
             go[row, k * 128:(k + 1) * 128] = piece[5 * splits + k]
-        for r in range(splits):
-            whole = jnp.concatenate([piece[5 * r + k] for k in range(5)], axis=1)
-            for i in range(splits):
-
-                @pl.when(idx[0, r] == i)
-                def _():
-                    for n, out in enumerate((gq, gk, gv)):
-                        out[row, i * part:(i + 1) * part] = whole[:, n * part:(n + 1) * part]
+        for i in range(splits):
+            whole = jnp.concatenate([piece[5 * idx[0, i] + k] for k in range(5)], axis=1)
+            for n, out in enumerate((gq, gk, gv)):
+                out[row, i * part:(i + 1) * part] = whole[:, n * part:(n + 1) * part]
 
 
 def place_feed_kernel(splits, blocks, unit, first, idx, *refs):
@@ -728,14 +751,10 @@
         gd[at(idx[0, first + z] * down.shape[0], down.shape[0]), :] = down[...]
         rows = up.shape[1]
         row = at(idx[0, first + z] * rows, rows)
-        for r in range(splits):
-            for i in range(splits):
-
-                @pl.when(idx[0, r] == i)
-                def _():
-                    for n in range(blocks):
-                        start = (n * splits + i) * unit
-                        gu[row, start:start + unit] = up[r, :, n * unit:(n + 1) * unit]
+        for i in range(splits):
+            for n in range(blocks):
+                start = (n * splits + i) * unit
+                gu[row, start:start + unit] = up[idx[0, i], :, n * unit:(n + 1) * unit]
 
 
 def swap(value, axis, mask):
@@ -891,9 +910,7 @@
     ).astype(jnp.int32).reshape(1, -1)
     def make_base(marks):
         return call(
-            functools.partial(base_kernel, at_d), "base",
-            [arr((tokens + EXTRA, width)), arr((unit // 4 if fast else 8, width))],
-            [idx, hidden, time_embed, small, w_down], marks=marks)
+            base_kernel, "base", [arr((tokens + EXTRA, width))], [hidden, time_embed, small], smem=0, marks=marks)[0]
 
     if fast:
         tables = [idx, bounds, codes, halo_codes, small]
@@ -905,17 +922,18 @@
         pieces = [(i, i % 2) for i in range(8)]
         far = across(far)
         near_over = over(near)
-        base, down_quarter = make_base([far, near_over])
+        base = make_base([far, near_over])
         far_base = across(base)
         qkv_arrays = [near, beside(near), far, beside(far)]
         near = near_over
         far = over(far)
-        down_quarter = over(down_quarter)
         qkv_arrays += [near, beside(near), far, beside(far)]
         base_all = [base, beside(base), far_base, beside(far_base)]
-        near2, far2 = call(
-            functools.partial(pack_feed_kernel, splits, blocks), "pack_feed", [arr((3, rows, share))] * 2,
-            [idx, w_up, w_out], marks=[far])
+        near2, far2, down_quarter = call(
+            functools.partial(pack_feed_kernel, splits, blocks, at_d), "pack_feed",
+            [arr((3, rows, share))] * 2 + [arr((unit // 4, width))],
+            [idx, w_up, w_out, w_down], marks=[far])
+        down_quarter = over(down_quarter)
         far2 = across(far2)
         feed_arrays = [near2, beside(near2), far2, beside(far2)]
         near2 = over(near2)
@@ -934,7 +952,7 @@
         feed_arrays = [jnp.stack([got[i], got[i], outs[i]]) for i in range(owners)]
         pieces = [(i, 0) for i in range(owners)]
         whole = blocks
-        base, down_quarter = make_base([])
+        base = make_base([])
         base_all = gather_splits(base)
         gathered = lax.all_gather(w_down, "blk", axis=0, tiled=False)
         down = [gathered[i] for i in range(blocks)]
@@ -1019,6 +1037,8 @@
         kv_grad = halo_add(kv_grad, halo_grad, reach)
         returned = jnp.zeros((8, 2 * part), F32)
 
+    core_out = beside(send_out)
+    far_out = across(keep_out[1] + core_out[1])
     lane_blocks = -(-3 * part // 128)
     outs, vecs = width // 128, width // 128 * EXTRA // tail_rows
     total_blocks = splits * lane_blocks + outs + vecs
@@ -1030,7 +1050,7 @@
         [pltpu.VMEM((group, 3 * part), BF), pltpu.VMEM((group, 3 * part), BF), pltpu.VMEM((group, width), F32),
          pltpu.VMEM((width, 3 * part), F32), pltpu.VMEM((part, width), F32), pltpu.VMEM((group, 3 * part), F32),
          pltpu.VMEM((group, width), F32), pltpu.VMEM((EXTRA, width), F32)],
-        flops=2 * group * width * 7 * part, marks=[])
+        flops=2 * group * width * 7 * part, marks=[far_out])
     to_owner = [(i * splits + j, j * blocks + i) for i in range(blocks) for j in range(splits)]
     near = 2 * lane_blocks
     if fast:
@@ -1052,7 +1072,7 @@
         part_up = jnp.stack([part_up[0], core_up[0], far_up[0], core_up[1]])
         all_down = collect(part_down)
         all_up = collect(part_up)
-        (tail_keep,), (tail_send,) = fold((tail_near,), (tail_got,), all_down)
+        (tail_keep,), (tail_send,) = fold((tail_near,), (tail_got,), [*all_down, far_in])
         part_tail = (tail_keep + swap(tail_send, "dp", 3))[0]
 
         far_tail = across(part_tail[near + outs:])
@@ -1097,8 +1117,6 @@
         [arr((tokens, width))],
         [idx, small, base, keep_in, core_in, far_in, middle_grad])
 
-    core_out = beside(send_out)
-    far_out = across(keep_out[1] + core_out[1])
     output = mine[0] + small[3:4] + keep_out[0] + core_out[0] + far_out
 
     vec = vec.reshape(outs, EXTRA, 128).transpose(1, 0, 2).reshape(EXTRA, width)

time: 341 us -> 337 us (0.988); the launches traced: 344 us -> 333 us
  waiting for transfers between devices: 169 us -> 163 us
  starting transfers between devices: 72.7 us -> 67.2 us
    ppermute x62, waiting for transfers between devices: 169 us -> 163 us  [swap(): return lax.ppermute(value, axis, [(i, i ^ mask) for i in range(count)])]
    ppermute x62, starting transfers between devices: 72 us -> 66.5 us  [swap(): return lax.ppermute(value, axis, [(i, i ^ mask) for i in range(count)])]
  transfers between devices with their start and end apart: 63 -> 63, of which waited for: 33 -> 28; matrix products, arithmetic and copies ran while one was open for 1% -> 1% of each run, Pallas kernels for 19% -> 21%
where the time goes in v4:
time: 337 us; the launch traced here: 333 us
  waiting for transfers between devices  163 us (48%)
  Pallas kernels  91 us (27%)
  starting transfers between devices  67.2 us (20%)
  local copies, waits for them, and re-layouts  7.26 us (2%)
    ppermute x62, waiting for transfers between devices, swap(): return lax.ppermute(value, axis, [(i, i ^ mask) for i in range(count)])  163 us
    pallas_call x21, Pallas kernels, call(): pl.pallas_call(kernel, out_shape=tuple(outs), in_specs=[SM] * smem + [VM]...  91 us
    ppermute x62, starting transfers between devices, swap(): return lax.ppermute(value, axis, [(i, i ^ mask) for i in range(count)])  66.5 us
  transfers between devices with their start and end apart: 63, of which 28 were waited for; matrix products, arithmetic and copies ran while one was open for 1% of the time, Pallas kernels for 21%

profile of v4, /device:TPU:0, one launch (start us, length us, event | category | flops | bytes accessed | tf_op | source)
XLA Modules:
  0.0 333.1 jit_solution(11939952033696627722)
XLA Ops:
  17.7 8.6 %collective-permute-done.1.refs_3_.refs_8_ = f32[2,96,576]{2,1,0:T(8,128)S(1)} collective-permute-done((f32[2,96,576]{2,1,0:T(8,128)S(1)}, f32[2,96,576]{2,1,0:T(8,128)S(1)}, u32[]{:S(2)}, u32[]{:S(2)}) %collective-permute-start.1) | collective-permute-done | bytes 442400 | tf_op jit(solution)/shard_map/ppermute | solution.py:762
  30.3 8.5 %collective-permute-done.9.refs_12_.refs_4_ = f32[2,96,576]{2,1,0:T(8,128)S(1)} collective-permute-done((f32[2,96,576]{2,1,0:T(8,128)S(1)}, f32[2,96,576]{2,1,0:T(8,128)S(1)}, u32[]{:S(2)}, u32[]{:S(2)}) %collective-permute-start.9) | collective-permute-done | bytes 442400 | tf_op jit(solution)/shard_map/ppermute | solution.py:762
  45.6 6.9 %collective-permute-done.13.refs_6_ = f32[96,768]{1,0:T(8,128)S(1)} collective-permute-done((f32[96,768]{1,0:T(8,128)S(1)}, f32[96,768]{1,0:T(8,128)S(1)}, u32[]{:S(2)}, u32[]{:S(2)}) %collective-permute-start.13) | collective-permute-done | bytes 294944 | tf_op jit(solution)/shard_map/ppermute | solution.py:762
  52.5 3.6 %collective-permute-start.14 = (f32[96,768]{1,0:T(8,128)S(1)}, f32[96,768]{1,0:T(8,128)S(1)}, u32[]{:S(2)}, u32[]{:S(2)}) collective-permute-start(f32[96,768]{1,0:T(8,128)S(1)} %collective-permute-done.13.refs_6_), channel_id=1, source_target_pairs={{0,24},{8,16},{16,8},{24,0},{1,25},{9,17},{17,9},{25,1},{2,26},{10... | collective-permute-start | bytes 884744 | tf_op jit(solution)/shard_map/ppermute | solution.py:762
  56.1 5.8 %qkv.1 = (f32[768,192]{1,0:T(8,128)S(1)}, f32[768,384]{1,0:T(8,128)S(1)}, f32[384,384]{1,0:T(8,128)S(1)}, f32[768,768]{1,0:T(8,128)S(1)}, f32[16,768]{1,0:T(8,12...) custom-call(s32[1,100]{1,0:T(1,128)S(1)} %get-tuple-element.103.refs_0_, ...), custom_call_target="tpu_custom_call" | custom-call | flops 1 | bytes 1 | tf_op jit(solution)/shard_map/qkv/pallas_call | solution.py:52
  65.0 4.1 %collective-permute-done.15.refs_10_.refs_8_ = f32[96,768]{1,0:T(8,128)S(1)} collective-permute-done((f32[96,768]{1,0:T(8,128)S(1)}, f32[96,768]{1,0:T(8,128)S(1)}, u32[]{:S(2)}, u32[]{:S(2)}) %collective-permute-start.15) | collective-permute-done | bytes 294944 | tf_op jit(solution)/shard_map/ppermute | solution.py:762
  70.3 7.2 %attend_own.1 = (bf16[3,768,192]{2,1,0:T(8,128)(2,1)S(1)}, f32[3,3,1,256]{3,2,1,0:T(1,128)S(1)}, f32[3,3,1,256]{3,2,1,0:T(1,128)S(1)}, f32[3,3,128,256]{3,2,1,0:T(8,128)S(1)}) custom-call(s32[1,12]{1,0:T(1,128)S(1)} %get-tuple-element.109.refs_0_.refs_1_, f32[2,768]{1,0:T(2,128)S(1)} %get-tuple-element.110.refs_1_.refs_2_, ...), custom_call_target="tpu_custom_call" | custom-call | flops 1 | bytes 1 | tf_op jit(solution)/shard_map/attend_own/pallas_call | solution.py:52
  77.5 7.2 %collective-permute-done.16.refs_11_.refs_9_ = f32[96,768]{1,0:T(8,128)S(1)} collective-permute-done((f32[96,768]{1,0:T(8,128)S(1)}, f32[96,768]{1,0:T(8,128)S(1)}, u32[]{:S(2)}, u32[]{:S(2)}) %collective-permute-start.16) | collective-permute-done | bytes 294944 | tf_op jit(solution)/shard_map/ppermute | solution.py:762
  84.8 3.4 %attend_edge.1 = (f32[768,192]{1,0:T(8,128)S(1)}, f32[384,384]{1,0:T(8,128)S(1)}, f32[8,768]{1,0:T(8,128)S(1)}, f32[3,96,768]{2,1,0:T(8,128)S(1)}) custom-call(s32[1,12]{1,0:T(1,128)S(1)} %get-tuple-element.109.refs_0_.refs_1_, f32[2,768]{1,0:T(2,128)S(1)} %get-tuple-element.110.refs_1_.refs_2_, f32[2,384]{1,0:T(2,128)S(1)} %get-tuple-element.111.refs_2_.refs_3_, ...), custom_call_target="tpu_custom_call" | custom-call | flops 1 | bytes 1 | tf_op jit(solution)/shard_map/attend_edge/pallas_call | solution.py:52
  90.8 19.4 %collective-permute-done.25.refs_7_ = f32[3,96,768]{2,1,0:T(8,128)S(1)} collective-permute-done((f32[3,96,768]{2,1,0:T(8,128)S(1)}, f32[3,96,768]{2,1,0:T(8,128)S(1)}, u32[]{:S(2)}, u32[]{:S(2)}) %collective-permute-start.25) | collective-permute-done | bytes 884768 | tf_op jit(solution)/shard_map/ppermute | solution.py:762
  110.8 4.5 %act.1 = (bf16[768,768]{1,0:T(8,128)(2,1)S(1)}, bf16[768,768]{1,0:T(8,128)(2,1)S(1)}, bf16[768,768]{1,0:T(8,128)(2,1)S(1)}, bf16[768,768]{1,0:T(8,128)(2,1)S(1)}, f32[768,768]{1,0:T(8,128)S(1)}) custom-call(s32[1,100]{1,0:T(1,128)S(1)} %get-tuple-element.103.refs_0_, f32[192,768]{1,0:T(8,128)S(1)} %get-tuple-element.121.refs_1_, ...), custom_call_target="tpu_custom_call" | custom-call | flops 1 | bytes 1 | tf_op jit(solution)/shard_map/act/pallas_call | solution.py:52
  117.4 17.7 %feed.1 = (f32[2,192,768]{2,1,0:T(8,128)S(1)}, f32[2,192,768]{2,1,0:T(8,128)S(1)}, f32[2,192,768]{2,1,0:T(8,128)S(1)}, f32[192,128]{1,0:T(8,128)S(1)}, bf16[768,...) custom-call(s32[1,100]{1,0:T(1,128)S(1)} %get-tuple-element.103.refs, ...), custom_call_target="tpu_custom_call" | custom-call | flops 1 | bytes 1 | tf_op jit(solution)/shard_map/feed/pallas_call | solution.py:52
  138.9 11.2 %feed_grads.1 = (f32[2,192,768]{2,1,0:T(8,128)S(1)}, f32[2,192,768]{2,1,0:T(8,128)S(1)}, f32[4,96,768]{2,1,0:T(8,128)S(1)}, f32[4,96,768]{2,1,0:T(8,128)S(1)}, f...) custom-call(s32[1,100]{1,0:T(1,128)S(1)} %get-tuple-element.103.refs_0_, ...), custom_call_target="tpu_custom_call" | custom-call | flops 1 | bytes 1 | tf_op jit(solution)/shard_map/feed_grads/pallas_call | solution.py:52
  150.2 3.6 %collective-permute-done.32.refs_3_ = f32[192,768]{1,0:T(8,128)S(1)} collective-permute-done((f32[192,768]{1,0:T(8,128)S(1)}, f32[192,768]{1,0:T(8,128)S(1)}, u32[]{:S(2)}, u32[]{:S(2)}) %collective-permute-start.32) | collective-permute-done | bytes 589856 | tf_op jit(solution)/shard_map/ppermute | solution.py:762
  156.2 12.9 %collective-permute-done.34.refs_13_ = f32[192,768]{1,0:T(8,128)S(1)} collective-permute-done((f32[192,768]{1,0:T(8,128)S(1)}, f32[192,768]{1,0:T(8,128)S(1)}, u32[]{:S(2)}, u32[]{:S(2)}) %collective-permute-start.34) | collective-permute-done | bytes 589856 | tf_op jit(solution)/shard_map/ppermute | solution.py:762
  171.1 7.6 %back_edge.1 = (f32[384,384]{1,0:T(8,128)S(1)}, bf16[3,768,128]{2,1,0:T(8,128)(2,1)S(1)}, bf16[3,768,192]{2,1,0:T(8,128)(2,1)S(1)}, bf16[3,768,128]{2,1,0:T(8,12...) custom-call(s32[1,100]{1,0:T(1,128)S(1)} %get-tuple-element.103.refs, ...), custom_call_target="tpu_custom_call" | custom-call | flops 1 | bytes 1 | tf_op jit(solution)/shard_map/back_edge/pallas_call | solution.py:52
  178.8 4.0 %collective-permute-done.36.refs_2_ = f32[4,96,768]{2,1,0:T(8,128)S(1)} collective-permute-done((f32[4,96,768]{2,1,0:T(8,128)S(1)}, f32[4,96,768]{2,1,0:T(8,128)S(1)}, u32[]{:S(2)}, u32[]{:S(2)}) %collective-permute-start.36) | collective-permute-done | bytes 1179680 | tf_op jit(solution)/shard_map/ppermute | solution.py:762
  183.3 3.3 collective-permute-start.45
  186.6 12.2 %back_own.1 = (f32[768,192]{1,0:T(8,128)S(1)}, f32[768,384]{1,0:T(8,128)S(1)}) custom-call(s32[1,12]{1,0:T(1,128)S(1)} %get-tuple-element.109.refs_0_.refs_1_, f32[2,768]{1,0:T(2,128)S(1)} %get-tuple-element.110.refs_1_.refs_2_, f32[2,768]{1,0:T(2,128)S(1)} %get-tuple-element.110.refs_1_.refs_2_, f32[768,384]{1,0:T(8,128)S(1)} %get-tuple-element.114.refs_4_.refs_3_, ...), custom_call_target="tpu_custom_call" | custom-call | flops 1 | bytes 1 | tf_op jit(solution)/shard_map/back_own/pallas_call | solution.py:52
  198.9 10.2 %last_grads.1 = (f32[2,192,768]{2,1,0:T(8,128)S(1)}, f32[2,192,768]{2,1,0:T(8,128)S(1)}, f32[2,30,24,128]{3,2,1,0:T(8,128)S(1)}, f32[2,30,24,128]{3,2,1,0:T(8,12...) custom-call(s32[1,100]{1,0:T(1,128)S(1)} %get-tuple-element.103.refs_0_, ...), custom_call_target="tpu_custom_call" | custom-call | flops 1 | bytes 1 | tf_op jit(solution)/shard_map/last_grads/pallas_call | solution.py:52
  214.9 5.9 %collective-permute-done.52 = f32[4,24,768]{2,1,0:T(8,128)S(1)} collective-permute-done((f32[4,24,768]{2,1,0:T(8,128)S(1)}, f32[4,24,768]{2,1,0:T(8,128)S(1)}, u32[]{:S(2)}, u32[]{:S(2)}) %collective-permute-start.52) | collective-permute-done | bytes 294944 | tf_op jit(solution)/shard_map/ppermute | solution.py:762
  222.7 13.8 %collective-permute-done.42 = f32[2,30,24,128]{3,2,1,0:T(8,128)S(1)} collective-permute-done((f32[2,30,24,128]{3,2,1,0:T(8,128)S(1)}, f32[2,30,24,128]{3,2,1,0:T(8,128)S(1)}, u32[]{:S(2)}, u32[]{:S(2)}) %collective-permute-start.42) | collective-permute-done | bytes 737312 | tf_op jit(solution)/shard_map/ppermute | solution.py:762
  242.8 7.6 %collective-permute-done.41 = f32[2,30,24,128]{3,2,1,0:T(8,128)S(1)} collective-permute-done((f32[2,30,24,128]{3,2,1,0:T(8,128)S(1)}, f32[2,30,24,128]{3,2,1,0:T(8,128)S(1)}, u32[]{:S(2)}, u32[]{:S(2)}) %collective-permute-start.41) | collective-permute-done | bytes 737312 | tf_op jit(solution)/shard_map/ppermute | solution.py:762
  250.5 11.9 %collective-permute-done.48.refs_4_.refs_3_ = f32[96,768]{1,0:T(8,128)S(1)} collective-permute-done((f32[96,768]{1,0:T(8,128)S(1)}, f32[96,768]{1,0:T(8,128)S(1)}, u32[]{:S(2)}, u32[]{:S(2)}) %collective-permute-start.48) | collective-permute-done | bytes 294944 | tf_op jit(solution)/shard_map/ppermute | solution.py:762
  262.4 3.6 %collective-permute-done.49.refs_5_.refs_4_ = f32[96,768]{1,0:T(8,128)S(1)} collective-permute-done((f32[96,768]{1,0:T(8,128)S(1)}, f32[96,768]{1,0:T(8,128)S(1)}, u32[]{:S(2)}, u32[]{:S(2)}) %collective-permute-start.49) | collective-permute-done | bytes 294944 | tf_op jit(solution)/shard_map/ppermute | solution.py:762
  266.2 3.9 %collective-permute-start.55 = (f32[4,24,768]{2,1,0:T(8,128)S(1)}, f32[4,24,768]{2,1,0:T(8,128)S(1)}, u32[]{:S(2)}, u32[]{:S(2)}) collective-permute-start(f32[4,24,768]{2,1,0:T(8,128)S(1)} %pad_maximum_fusion.refs_2_.refs_5_), channel_id=1, source_target_pairs={{0,24},{8,16},{16,8},{24,0},{1,25},{9,17},{17,9},{25,1},{2,26},{10... | collective-permute-start | bytes 884744 | tf_op jit(solution)/shard_map/ppermute | solution.py:762
  270.8 14.6 %collective-permute-done.55.refs_3_.refs_6_ = f32[4,24,768]{2,1,0:T(8,128)S(1)} collective-permute-done((f32[4,24,768]{2,1,0:T(8,128)S(1)}, f32[4,24,768]{2,1,0:T(8,128)S(1)}, u32[]{:S(2)}, u32[]{:S(2)}) %collective-permute-start.55) | collective-permute-done | bytes 294944 | tf_op jit(solution)/shard_map/ppermute | solution.py:762
  285.4 11.5 %collective-permute-start.57 = (f32[4,24,768]{2,1,0:T(8,128)S(1)}, f32[4,24,768]{2,1,0:T(8,128)S(1)}, u32[]{:S(2)}, u32[]{:S(2)}) collective-permute-start(f32[4,24,768]{2,1,0:T(8,128)S(1)} %collective-permute-done.55.refs_3_.refs_6_), channel_id=1, source_target_pairs={{0,8},{8,0},{16,24},{24,16},{1,9},{9,1},{17,25},{25,17},{2,10},{10... | collective-permute-start | bytes 884744 | tf_op jit(solution)/shard_map/ppermute | solution.py:762
  299.8 4.2 %collective-permute-done.57.refs_5_.refs_8_ = f32[4,24,768]{2,1,0:T(8,128)S(1)} collective-permute-done((f32[4,24,768]{2,1,0:T(8,128)S(1)}, f32[4,24,768]{2,1,0:T(8,128)S(1)}, u32[]{:S(2)}, u32[]{:S(2)}) %collective-permute-start.57) | collective-permute-done | bytes 294944 | tf_op jit(solution)/shard_map/ppermute | solution.py:762
  313.0 4.9 %collective-permute-done.60.refs_2_ = f32[26,24,128]{2,1,0:T(8,128)S(1)} collective-permute-done((f32[26,24,128]{2,1,0:T(8,128)S(1)}, f32[26,24,128]{2,1,0:T(8,128)S(1)}, u32[]{:S(2)}, u32[]{:S(2)}) %collective-permute-start.60) | collective-permute-done | bytes 319520 | tf_op jit(solution)/shard_map/ppermute | solution.py:762
  317.9 5.9 %collective-permute-start.62 = (f32[26,24,128]{2,1,0:T(8,128)S(1)}, f32[26,24,128]{2,1,0:T(8,128)S(1)}, u32[]{:S(2)}, u32[]{:S(2)}) collective-permute-start(f32[26,24,128]{2,1,0:T(8,128)S(1)} %collective-permute-done.60.refs_2_), channel_id=1, source_target_pairs={{0,8},{8,0},{16,24},{24,16},{1,9},{9,1},{17,25},{25,17},{2,10},{10... | collective-permute-start | bytes 958472 | tf_op jit(solution)/shard_map/ppermute | solution.py:762
  324.4 6.5 %collective-permute-done.62.refs_4_ = f32[26,24,128]{2,1,0:T(8,128)S(1)} collective-permute-done((f32[26,24,128]{2,1,0:T(8,128)S(1)}, f32[26,24,128]{2,1,0:T(8,128)S(1)}, u32[]{:S(2)}, u32[]{:S(2)}) %collective-permute-start.62) | collective-permute-done | bytes 319520 | tf_op jit(solution)/shard_map/ppermute | solution.py:762
  (184 shorter events, 75.4 us)
Async XLA Ops:
  29.8 15.2 %collective-permute-start.3 = (f32[208,768]{1,0:T(8,128)S(1)}, f32[208,768]{1,0:T(8,128)S(1)}, u32[]{:S(2)}, u32[]{:S(2)}) collective-permute-start(f32[208,768]{1,0:T(8,128)S(1)} %base.1.refs_2_), channel_id=1, source_target_pairs={{0,1},{1,0},{2,3},{3,2},{4,5},{5,4},{6,7},{7,6},{8,9},{9,8},{10,11... | collective-permute-start | bytes 1916936 | tf_op jit(solution)/shard_map/ppermute | solution.py:762
  44.1 40.6 %collective-permute-start.12 = (f32[3,96,768]{2,1,0:T(8,128)S(1)}, f32[3,96,768]{2,1,0:T(8,128)S(1)}, u32[]{:S(2)}, u32[]{:S(2)}) collective-permute-start(f32[3,96,768]{2,1,0:T(8,128)S(1)} %get-tuple-element.119), channel_id=1, source_target_pairs={{0,2},{1,3},{2,0},{3,1},{4,6},{5,7},{6,4},{7,5},{8,10},{9,11},{10,... | collective-permute-start | bytes 2654216 | tf_op jit(solution)/shard_map/ppermute | solution.py:762
  45.0 39.7 %collective-permute-start.18 = (f32[3,96,768]{2,1,0:T(8,128)S(1)}, f32[3,96,768]{2,1,0:T(8,128)S(1)}, u32[]{:S(2)}, u32[]{:S(2)}) collective-permute-start(f32[3,96,768]{2,1,0:T(8,128)S(1)} %get-tuple-element.122.refs_1_), channel_id=1, source_target_pairs={{0,4},{4,0},{1,5},{5,1},{2,6},{6,2},{3,7},{7,3},{8,12},{12,8},{9,1... | collective-permute-start | bytes 2654216 | tf_op jit(solution)/shard_map/ppermute | solution.py:762
  62.0 22.8 %collective-permute-start.11 = (f32[384,384]{1,0:T(8,128)S(1)}, f32[384,384]{1,0:T(8,128)S(1)}, u32[]{:S(2)}, u32[]{:S(2)}) collective-permute-start(f32[384,384]{1,0:T(8,128)S(1)} %get-tuple-element.112), channel_id=1, source_target_pairs={{0,4},{4,0},{1,5},{5,1},{2,6},{6,2},{3,7},{7,3},{8,12},{12,8},{9,1... | collective-permute-start | bytes 1769480 | tf_op jit(solution)/shard_map/ppermute | solution.py:762
  64.3 20.4 %collective-permute-start.17 = (f32[192,768]{1,0:T(8,128)S(1)}, f32[192,768]{1,0:T(8,128)S(1)}, u32[]{:S(2)}, u32[]{:S(2)}) collective-permute-start(f32[192,768]{1,0:T(8,128)S(1)} %get-tuple-element.121.refs_1_), channel_id=1, source_target_pairs={{0,2},{1,3},{2,0},{3,1},{4,6},{5,7},{6,4},{7,5},{8,10},{9,11},{10,... | collective-permute-start | bytes 1769480 | tf_op jit(solution)/shard_map/ppermute | solution.py:762
  69.0 15.7 %collective-permute-start.16 = (f32[96,768]{1,0:T(8,128)S(1)}, f32[96,768]{1,0:T(8,128)S(1)}, u32[]{:S(2)}, u32[]{:S(2)}) collective-permute-start(f32[96,768]{1,0:T(8,128)S(1)} %collective-permute-done.13.refs_6_), channel_id=1, source_target_pairs={{0,16},{8,24},{16,0},{24,8},{1,17},{9,25},{17,1},{25,9},{2,18},{10... | collective-permute-start | bytes 884744 | tf_op jit(solution)/shard_map/ppermute | solution.py:762
  88.1 22.1 %collective-permute-start.25 = (f32[3,96,768]{2,1,0:T(8,128)S(1)}, f32[3,96,768]{2,1,0:T(8,128)S(1)}, u32[]{:S(2)}, u32[]{:S(2)}) collective-permute-start(f32[3,96,768]{2,1,0:T(8,128)S(1)} %get-tuple-element.124), channel_id=1, source_target_pairs={{0,4},{4,0},{1,5},{5,1},{2,6},{6,2},{3,7},{7,3},{8,12},{12,8},{9,1... | collective-permute-start | bytes 2654216 | tf_op jit(solution)/shard_map/ppermute | solution.py:762
  88.8 21.4 %collective-permute-start.20 = (f32[384,384]{1,0:T(8,128)S(1)}, f32[384,384]{1,0:T(8,128)S(1)}, u32[]{:S(2)}, u32[]{:S(2)}) collective-permute-start(f32[384,384]{1,0:T(8,128)S(1)} %get-tuple-element.123.refs_3_), channel_id=1, source_target_pairs={{0,2},{1,3},{2,0},{3,1},{4,6},{5,7},{6,4},{7,5},{8,10},{9,11},{10,... | collective-permute-start | bytes 1769480 | tf_op jit(solution)/shard_map/ppermute | solution.py:762
  89.7 21.1 %collective-permute-start.28 = (f32[192,768]{1,0:T(8,128)S(1)}, f32[192,768]{1,0:T(8,128)S(1)}, u32[]{:S(2)}, u32[]{:S(2)}) collective-permute-start(f32[192,768]{1,0:T(8,128)S(1)} %collective-permute-done.17.refs_12_.refs_3_), channel_id=1, source_target_pairs={{0,1},{1,0},{2,3},{3,2},{4,5},{5,4},{6,7},{7,6},{8,9},{9,8},{10,11... | collective-permute-start | bytes 1769480 | tf_op jit(solution)/shard_map/ppermute | solution.py:762
  89.7 25.6 %collective-permute-start.23 = (f32[3,96,768]{2,1,0:T(8,128)S(1)}, f32[3,96,768]{2,1,0:T(8,128)S(1)}, u32[]{:S(2)}, u32[]{:S(2)}) collective-permute-start(f32[3,96,768]{2,1,0:T(8,128)S(1)} %collective-permute-done.12.refs_8_.refs_3_), channel_id=1, source_target_pairs={{0,1},{1,0},{2,3},{3,2},{4,5},{5,4},{6,7},{7,6},{8,9},{9,8},{10,11... | collective-permute-start | bytes 2654216 | tf_op jit(solution)/shard_map/ppermute | solution.py:762
  90.6 24.7 %collective-permute-start.24 = (f32[3,96,768]{2,1,0:T(8,128)S(1)}, f32[3,96,768]{2,1,0:T(8,128)S(1)}, u32[]{:S(2)}, u32[]{:S(2)}) collective-permute-start(f32[3,96,768]{2,1,0:T(8,128)S(1)} %collective-permute-done.18.refs_13_.refs_5_), channel_id=1, source_target_pairs={{0,1},{1,0},{2,3},{3,2},{4,5},{5,4},{6,7},{7,6},{8,9},{9,8},{10,11... | collective-permute-start | bytes 2654216 | tf_op jit(solution)/shard_map/ppermute | solution.py:762
  138.2 15.7 %collective-permute-start.32 = (f32[192,768]{1,0:T(8,128)S(1)}, f32[192,768]{1,0:T(8,128)S(1)}, u32[]{:S(2)}, u32[]{:S(2)}) collective-permute-start(f32[192,768]{1,0:T(8,128)S(1)} %fusion.4.refs_11_), channel_id=1, source_target_pairs={{0,2},{1,3},{2,0},{3,1},{4,6},{5,7},{6,4},{7,5},{8,10},{9,11},{10,... | collective-permute-start | bytes 1769480 | tf_op jit(solution)/shard_map/ppermute | solution.py:762
  150.1 19.0 %collective-permute-start.30 = (f32[2,192,768]{2,1,0:T(8,128)S(1)}, f32[2,192,768]{2,1,0:T(8,128)S(1)}, u32[]{:S(2)}, u32[]{:S(2)}) collective-permute-start(f32[2,192,768]{2,1,0:T(8,128)S(1)} %get-tuple-element.144), channel_id=1, source_target_pairs={{0,1},{1,0},{2,3},{3,2},{4,5},{5,4},{6,7},{7,6},{8,9},{9,8},{10,11... | collective-permute-start | bytes 3538952 | tf_op jit(solution)/shard_map/ppermute | solution.py:762
  155.0 27.7 %collective-permute-start.36 = (f32[4,96,768]{2,1,0:T(8,128)S(1)}, f32[4,96,768]{2,1,0:T(8,128)S(1)}, u32[]{:S(2)}, u32[]{:S(2)}) collective-permute-start(f32[4,96,768]{2,1,0:T(8,128)S(1)} %get-tuple-element.156), channel_id=1, source_target_pairs={{0,4},{4,0},{1,5},{5,1},{2,6},{6,2},{3,7},{7,3},{8,12},{12,8},{9,1... | collective-permute-start | bytes 3538952 | tf_op jit(solution)/shard_map/ppermute | solution.py:762
  155.6 27.1 %collective-permute-start.37 = (f32[16,24,768]{2,1,0:T(8,128)S(1)}, f32[16,24,768]{2,1,0:T(8,128)S(1)}, u32[]{:S(2)}, u32[]{:S(2)}) collective-permute-start(f32[16,24,768]{2,1,0:T(8,128)S(1)} %get-tuple-element.157), channel_id=1, source_target_pairs={{0,8},{8,0},{16,24},{24,16},{1,9},{9,1},{17,25},{25,17},{2,10},{10... | collective-permute-start | bytes 3538952 | tf_op jit(solution)/shard_map/ppermute | solution.py:762
  169.2 29.7 %collective-permute-start.31 = (f32[192,768]{1,0:T(8,128)S(1)}, f32[192,768]{1,0:T(8,128)S(1)}, u32[]{:S(2)}, u32[]{:S(2)}) collective-permute-start(f32[192,768]{1,0:T(8,128)S(1)} %fusion.1), channel_id=1, source_target_pairs={{0,2},{1,3},{2,0},{3,1},{4,6},{5,7},{6,4},{7,5},{8,10},{9,11},{10,... | collective-permute-start | bytes 1769480 | tf_op jit(solution)/shard_map/ppermute | solution.py:762
  178.7 20.2 %collective-permute-start.38 = (f32[384,384]{1,0:T(8,128)S(1)}, f32[384,384]{1,0:T(8,128)S(1)}, u32[]{:S(2)}, u32[]{:S(2)}) collective-permute-start(f32[384,384]{1,0:T(8,128)S(1)} %get-tuple-element.158.refs_4_), channel_id=1, source_target_pairs={{0,4},{4,0},{1,5},{5,1},{2,6},{6,2},{3,7},{7,3},{8,12},{12,8},{9,1... | collective-permute-start | bytes 1769480 | tf_op jit(solution)/shard_map/ppermute | solution.py:762
  183.0 26.2 %collective-permute-start.44 = (f32[2,96,768]{2,1,0:T(8,128)S(1)}, f32[2,96,768]{2,1,0:T(8,128)S(1)}, u32[]{:S(2)}, u32[]{:S(2)}) collective-permute-start(f32[2,96,768]{2,1,0:T(8,128)S(1)} %get-tuple-element.175), channel_id=1, source_target_pairs={{0,8},{8,0},{16,24},{24,16},{1,9},{9,1},{17,25},{25,17},{2,10},{10... | collective-permute-start | bytes 1769480 | tf_op jit(solution)/shard_map/ppermute | solution.py:762
  183.3 27.2 %collective-permute-start.45 = (f32[8,24,768]{2,1,0:T(8,128)S(1)}, f32[8,24,768]{2,1,0:T(8,128)S(1)}, u32[]{:S(2)}, u32[]{:S(2)}) collective-permute-start(f32[8,24,768]{2,1,0:T(8,128)S(1)} %get-tuple-element.176), channel_id=1, source_target_pairs={{0,24},{8,16},{16,8},{24,0},{1,25},{9,17},{17,9},{25,1},{2,26},{10... | collective-permute-start | bytes 1769480 | tf_op jit(solution)/shard_map/ppermute | solution.py:762
  209.1 28.1 %collective-permute-start.39 = (f32[2,192,768]{2,1,0:T(8,128)S(1)}, f32[2,192,768]{2,1,0:T(8,128)S(1)}, u32[]{:S(2)}, u32[]{:S(2)}) collective-permute-start(f32[2,192,768]{2,1,0:T(8,128)S(1)} %get-tuple-element.169), channel_id=1, source_target_pairs={{0,1},{1,0},{2,3},{3,2},{4,5},{5,4},{6,7},{7,6},{8,9},{9,8},{10,11... | collective-permute-start | bytes 3538952 | tf_op jit(solution)/shard_map/ppermute | solution.py:762
  212.8 23.7 %collective-permute-start.42 = (f32[2,30,24,128]{3,2,1,0:T(8,128)S(1)}, f32[2,30,24,128]{3,2,1,0:T(8,128)S(1)}, u32[]{:S(2)}, u32[]{:S(2)}) collective-permute-start(f32[2,30,24,128]{3,2,1,0:T(8,128)S(1)} %get-tuple-element.173), channel_id=1, source_target_pairs={{0,4},{4,0},{1,5},{5,1},{2,6},{6,2},{3,7},{7,3},{8,12},{12,8},{9,1... | collective-permute-start | bytes 2211848 | tf_op jit(solution)/shard_map/ppermute | solution.py:762
  213.5 36.9 %collective-permute-start.41 = (f32[2,30,24,128]{3,2,1,0:T(8,128)S(1)}, f32[2,30,24,128]{3,2,1,0:T(8,128)S(1)}, u32[]{:S(2)}, u32[]{:S(2)}) collective-permute-start(f32[2,30,24,128]{3,2,1,0:T(8,128)S(1)} %get-tuple-element.171), channel_id=1, source_target_pairs={{0,4},{4,0},{1,5},{5,1},{2,6},{6,2},{3,7},{7,3},{8,12},{12,8},{9,1... | collective-permute-start | bytes 2211848 | tf_op jit(solution)/shard_map/ppermute | solution.py:762
  220.8 18.5 %collective-permute-start.53 = (f32[2,24,768]{2,1,0:T(8,128)S(1)}, f32[2,24,768]{2,1,0:T(8,128)S(1)}, u32[]{:S(2)}, u32[]{:S(2)}) collective-permute-start(f32[2,24,768]{2,1,0:T(8,128)S(1)} %slice.190), channel_id=1, source_target_pairs={{0,2},{1,3},{2,0},{3,1},{4,6},{5,7},{6,4},{7,5},{8,10},{9,11},{10,... | collective-permute-start | bytes 442376 | tf_op jit(solution)/shard_map/ppermute | solution.py:762
  222.0 19.4 %collective-permute-start.47 = (f32[96,768]{1,0:T(8,128)S(1)}, f32[96,768]{1,0:T(8,128)S(1)}, u32[]{:S(2)}, u32[]{:S(2)}) collective-permute-start(f32[96,768]{1,0:T(8,128)S(1)} %add_bitcast_fusion.refs_2_.refs_1_), channel_id=1, source_target_pairs={{0,24},{8,16},{16,8},{24,0},{1,25},{9,17},{17,9},{25,1},{2,26},{10... | collective-permute-start | bytes 884744 | tf_op jit(solution)/shard_map/ppermute | solution.py:762
  236.6 29.4 %collective-permute-start.43 = (f32[2,30,24,128]{3,2,1,0:T(8,128)S(1)}, f32[2,30,24,128]{3,2,1,0:T(8,128)S(1)}, u32[]{:S(2)}, u32[]{:S(2)}) collective-permute-start(f32[2,30,24,128]{3,2,1,0:T(8,128)S(1)} %add.440), channel_id=1, source_target_pairs={{0,8},{8,0},{16,24},{24,16},{1,9},{9,1},{17,25},{25,17},{2,10},{10... | collective-permute-start | bytes 2211848 | tf_op jit(solution)/shard_map/ppermute | solution.py:762
  237.2 28.8 %collective-permute-start.40 = (f32[192,768]{1,0:T(8,128)S(1)}, f32[192,768]{1,0:T(8,128)S(1)}, u32[]{:S(2)}, u32[]{:S(2)}) collective-permute-start(f32[192,768]{1,0:T(8,128)S(1)} %fusion), channel_id=1, source_target_pairs={{0,2},{1,3},{2,0},{3,1},{4,6},{5,7},{6,4},{7,5},{8,10},{9,11},{10,... | collective-permute-start | bytes 1769480 | tf_op jit(solution)/shard_map/ppermute | solution.py:762
  240.8 21.7 %collective-permute-start.48 = (f32[96,768]{1,0:T(8,128)S(1)}, f32[96,768]{1,0:T(8,128)S(1)}, u32[]{:S(2)}, u32[]{:S(2)}) collective-permute-start(f32[96,768]{1,0:T(8,128)S(1)} %add_bitcast_fusion.refs_2_.refs_1_), channel_id=1, source_target_pairs={{0,8},{8,0},{16,24},{24,16},{1,9},{9,1},{17,25},{25,17},{2,10},{10... | collective-permute-start | bytes 884744 | tf_op jit(solution)/shard_map/ppermute | solution.py:762
  241.4 24.5 %collective-permute-start.49 = (f32[96,768]{1,0:T(8,128)S(1)}, f32[96,768]{1,0:T(8,128)S(1)}, u32[]{:S(2)}, u32[]{:S(2)}) collective-permute-start(f32[96,768]{1,0:T(8,128)S(1)} %collective-permute-done.47.refs_3_.refs_2_), channel_id=1, source_target_pairs={{0,8},{8,0},{16,24},{24,16},{1,9},{9,1},{17,25},{25,17},{2,10},{10... | collective-permute-start | bytes 884744 | tf_op jit(solution)/shard_map/ppermute | solution.py:762
  266.1 30.8 %collective-permute-start.50 = (f32[1,30,24,128]{3,2,1,0:T(8,128)S(1)}, f32[1,30,24,128]{3,2,1,0:T(8,128)S(1)}, u32[]{:S(2)}, u32[]{:S(2)}) collective-permute-start(f32[1,30,24,128]{3,2,1,0:T(8,128)S(1)} %get-tuple-element.180), channel_id=1, source_target_pairs={{0,24},{8,16},{16,8},{24,0},{1,25},{9,17},{17,9},{25,1},{2,26},{10... | collective-permute-start | bytes 1105928 | tf_op jit(solution)/shard_map/ppermute | solution.py:762
  266.2 19.2 %collective-permute-start.55 = (f32[4,24,768]{2,1,0:T(8,128)S(1)}, f32[4,24,768]{2,1,0:T(8,128)S(1)}, u32[]{:S(2)}, u32[]{:S(2)}) collective-permute-start(f32[4,24,768]{2,1,0:T(8,128)S(1)} %pad_maximum_fusion.refs_2_.refs_5_), channel_id=1, source_target_pairs={{0,24},{8,16},{16,8},{24,0},{1,25},{9,17},{17,9},{25,1},{2,26},{10... | collective-permute-start | bytes 884744 | tf_op jit(solution)/shard_map/ppermute | solution.py:762
  270.1 29.7 %collective-permute-start.56 = (f32[4,24,768]{2,1,0:T(8,128)S(1)}, f32[4,24,768]{2,1,0:T(8,128)S(1)}, u32[]{:S(2)}, u32[]{:S(2)}) collective-permute-start(f32[4,24,768]{2,1,0:T(8,128)S(1)} %pad_maximum_fusion.refs_2_.refs_5_), channel_id=1, source_target_pairs={{0,8},{8,0},{16,24},{24,16},{1,9},{9,1},{17,25},{25,17},{2,10},{10... | collective-permute-start | bytes 884744 | tf_op jit(solution)/shard_map/ppermute | solution.py:762
  285.4 18.6 %collective-permute-start.57 = (f32[4,24,768]{2,1,0:T(8,128)S(1)}, f32[4,24,768]{2,1,0:T(8,128)S(1)}, u32[]{:S(2)}, u32[]{:S(2)}) collective-permute-start(f32[4,24,768]{2,1,0:T(8,128)S(1)} %collective-permute-done.55.refs_3_.refs_6_), channel_id=1, source_target_pairs={{0,8},{8,0},{16,24},{24,16},{1,9},{9,1},{17,25},{25,17},{2,10},{10... | collective-permute-start | bytes 884744 | tf_op jit(solution)/shard_map/ppermute | solution.py:762
  (40 other events, 438.1 us)

commit v5 on v4

--- a/solution.py
+++ b/solution.py
@@ -1072,13 +1072,13 @@
         part_up = jnp.stack([part_up[0], core_up[0], far_up[0], core_up[1]])
         all_down = collect(part_down)
         all_up = collect(part_up)
-        (tail_keep,), (tail_send,) = fold((tail_near,), (tail_got,), [*all_down, far_in])
+        (tail_keep,), (tail_send,) = fold((tail_near,), (tail_got,), [*all_down, all_up[1], far_in])
         part_tail = (tail_keep + swap(tail_send, "dp", 3))[0]
 
         far_tail = across(part_tail[near + outs:])
         message, = call(
             functools.partial(message_kernel, near, near + outs, vecs), "message", [arr(far_tail.shape)],
-            [part_tail, far_tail], smem=0, marks=all_up)
+            [part_tail, far_tail], smem=0, marks=[])
         core_tail = beside(message)
         vec = part_tail[near + outs:near + outs + vecs] + far_tail[:vecs] + core_tail[lane_blocks:lane_blocks + vecs]
         owned = lax.ppermute(part_tail[near:near + outs], both, to_owner)

time: 337 us -> 321 us (0.953)
  waiting for transfers between devices: 163 us -> 144 us
  starting transfers between devices: 67.2 us -> 70.6 us
    ppermute x62, waiting for transfers between devices: 163 us -> 144 us  [swap(): return lax.ppermute(value, axis, [(i, i ^ mask) for i in range(count)])]
    ppermute x62, starting transfers between devices: 66.5 us -> 70 us  [swap(): return lax.ppermute(value, axis, [(i, i ^ mask) for i in range(count)])]
  transfers between devices with their start and end apart: 63 -> 63, of which waited for: 28 -> 30; matrix products, arithmetic and copies ran while one was open for 1% -> 1% of each run, Pallas kernels for 21% -> 22%
where the time goes in v5:
time: 321 us; the launch traced here: 317 us
  waiting for transfers between devices  144 us (45%)
  Pallas kernels  91 us (28%)
  starting transfers between devices  70.6 us (22%)
  local copies, waits for them, and re-layouts  7.26 us (2%)
    ppermute x62, waiting for transfers between devices, swap(): return lax.ppermute(value, axis, [(i, i ^ mask) for i in range(count)])  144 us
    pallas_call x21, Pallas kernels, call(): pl.pallas_call(kernel, out_shape=tuple(outs), in_specs=[SM] * smem + [VM]...  91 us
    ppermute x62, starting transfers between devices, swap(): return lax.ppermute(value, axis, [(i, i ^ mask) for i in range(count)])  70 us
  transfers between devices with their start and end apart: 63, of which 30 were waited for; matrix products, arithmetic and copies ran while one was open for 1% of the time, Pallas kernels for 22%

profile of v5, /device:TPU:0, one launch (start us, length us, event | category | flops | bytes accessed | tf_op | source)
XLA Modules:
  0.0 317.3 jit_solution(14461241677744555541)
XLA Ops:
  3.8 2.9 collective-permute-start
  17.7 8.6 %collective-permute-done.1.refs_3_.refs_8_ = f32[2,96,576]{2,1,0:T(8,128)S(1)} collective-permute-done((f32[2,96,576]{2,1,0:T(8,128)S(1)}, f32[2,96,576]{2,1,0:T(8,128)S(1)}, u32[]{:S(2)}, u32[]{:S(2)}) %collective-permute-start.1) | collective-permute-done | bytes 442400 | tf_op jit(solution)/shard_map/ppermute | solution.py:762
  30.3 8.5 %collective-permute-done.9.refs_12_.refs_4_ = f32[2,96,576]{2,1,0:T(8,128)S(1)} collective-permute-done((f32[2,96,576]{2,1,0:T(8,128)S(1)}, f32[2,96,576]{2,1,0:T(8,128)S(1)}, u32[]{:S(2)}, u32[]{:S(2)}) %collective-permute-start.9) | collective-permute-done | bytes 442400 | tf_op jit(solution)/shard_map/ppermute | solution.py:762
  38.8 2.8 collective-permute-done.4.refs_4_
  45.6 6.9 %collective-permute-done.13.refs_6_ = f32[96,768]{1,0:T(8,128)S(1)} collective-permute-done((f32[96,768]{1,0:T(8,128)S(1)}, f32[96,768]{1,0:T(8,128)S(1)}, u32[]{:S(2)}, u32[]{:S(2)}) %collective-permute-start.13) | collective-permute-done | bytes 294944 | tf_op jit(solution)/shard_map/ppermute | solution.py:762
  52.5 3.6 %collective-permute-start.14 = (f32[96,768]{1,0:T(8,128)S(1)}, f32[96,768]{1,0:T(8,128)S(1)}, u32[]{:S(2)}, u32[]{:S(2)}) collective-permute-start(f32[96,768]{1,0:T(8,128)S(1)} %collective-permute-done.13.refs_6_), channel_id=1, source_target_pairs={{0,24},{8,16},{16,8},{24,0},{1,25},{9,17},{17,9},{25,1},{2,26},{10... | collective-permute-start | bytes 884744 | tf_op jit(solution)/shard_map/ppermute | solution.py:762
  56.1 5.8 %qkv.1 = (f32[768,192]{1,0:T(8,128)S(1)}, f32[768,384]{1,0:T(8,128)S(1)}, f32[384,384]{1,0:T(8,128)S(1)}, f32[768,768]{1,0:T(8,128)S(1)}, f32[16,768]{1,0:T(8,12...) custom-call(s32[1,100]{1,0:T(1,128)S(1)} %get-tuple-element.103.refs_0_, ...), custom_call_target="tpu_custom_call" | custom-call | flops 1 | bytes 1 | tf_op jit(solution)/shard_map/qkv/pallas_call | solution.py:52
  65.0 4.1 %collective-permute-done.15.refs_10_.refs_8_ = f32[96,768]{1,0:T(8,128)S(1)} collective-permute-done((f32[96,768]{1,0:T(8,128)S(1)}, f32[96,768]{1,0:T(8,128)S(1)}, u32[]{:S(2)}, u32[]{:S(2)}) %collective-permute-start.15) | collective-permute-done | bytes 294944 | tf_op jit(solution)/shard_map/ppermute | solution.py:762
  70.3 7.2 %attend_own.1 = (bf16[3,768,192]{2,1,0:T(8,128)(2,1)S(1)}, f32[3,3,1,256]{3,2,1,0:T(1,128)S(1)}, f32[3,3,1,256]{3,2,1,0:T(1,128)S(1)}, f32[3,3,128,256]{3,2,1,0:T(8,128)S(1)}) custom-call(s32[1,12]{1,0:T(1,128)S(1)} %get-tuple-element.109.refs_0_.refs_1_, f32[2,768]{1,0:T(2,128)S(1)} %get-tuple-element.110.refs_1_.refs_2_, ...), custom_call_target="tpu_custom_call" | custom-call | flops 1 | bytes 1 | tf_op jit(solution)/shard_map/attend_own/pallas_call | solution.py:52
  77.5 7.2 %collective-permute-done.16.refs_11_.refs_9_ = f32[96,768]{1,0:T(8,128)S(1)} collective-permute-done((f32[96,768]{1,0:T(8,128)S(1)}, f32[96,768]{1,0:T(8,128)S(1)}, u32[]{:S(2)}, u32[]{:S(2)}) %collective-permute-start.16) | collective-permute-done | bytes 294944 | tf_op jit(solution)/shard_map/ppermute | solution.py:762
  84.8 3.4 %attend_edge.1 = (f32[768,192]{1,0:T(8,128)S(1)}, f32[384,384]{1,0:T(8,128)S(1)}, f32[8,768]{1,0:T(8,128)S(1)}, f32[3,96,768]{2,1,0:T(8,128)S(1)}) custom-call(s32[1,12]{1,0:T(1,128)S(1)} %get-tuple-element.109.refs_0_.refs_1_, f32[2,768]{1,0:T(2,128)S(1)} %get-tuple-element.110.refs_1_.refs_2_, f32[2,384]{1,0:T(2,128)S(1)} %get-tuple-element.111.refs_2_.refs_3_, ...), custom_call_target="tpu_custom_call" | custom-call | flops 1 | bytes 1 | tf_op jit(solution)/shard_map/attend_edge/pallas_call | solution.py:52
  91.6 18.6 %collective-permute-done.25.refs_7_ = f32[3,96,768]{2,1,0:T(8,128)S(1)} collective-permute-done((f32[3,96,768]{2,1,0:T(8,128)S(1)}, f32[3,96,768]{2,1,0:T(8,128)S(1)}, u32[]{:S(2)}, u32[]{:S(2)}) %collective-permute-start.25) | collective-permute-done | bytes 884768 | tf_op jit(solution)/shard_map/ppermute | solution.py:762
  110.8 4.5 %act.1 = (bf16[768,768]{1,0:T(8,128)(2,1)S(1)}, bf16[768,768]{1,0:T(8,128)(2,1)S(1)}, bf16[768,768]{1,0:T(8,128)(2,1)S(1)}, bf16[768,768]{1,0:T(8,128)(2,1)S(1)}, f32[768,768]{1,0:T(8,128)S(1)}) custom-call(s32[1,100]{1,0:T(1,128)S(1)} %get-tuple-element.103.refs_0_, f32[192,768]{1,0:T(8,128)S(1)} %get-tuple-element.121.refs_1_, ...), custom_call_target="tpu_custom_call" | custom-call | flops 1 | bytes 1 | tf_op jit(solution)/shard_map/act/pallas_call | solution.py:52
  117.4 17.7 %feed.1 = (f32[2,192,768]{2,1,0:T(8,128)S(1)}, f32[2,192,768]{2,1,0:T(8,128)S(1)}, f32[2,192,768]{2,1,0:T(8,128)S(1)}, f32[192,128]{1,0:T(8,128)S(1)}, bf16[768,...) custom-call(s32[1,100]{1,0:T(1,128)S(1)} %get-tuple-element.103.refs, ...), custom_call_target="tpu_custom_call" | custom-call | flops 1 | bytes 1 | tf_op jit(solution)/shard_map/feed/pallas_call | solution.py:52
  135.6 2.5 collective-permute-done.29.refs_2_
  138.9 11.2 %feed_grads.1 = (f32[2,192,768]{2,1,0:T(8,128)S(1)}, f32[2,192,768]{2,1,0:T(8,128)S(1)}, f32[4,96,768]{2,1,0:T(8,128)S(1)}, f32[4,96,768]{2,1,0:T(8,128)S(1)}, f...) custom-call(s32[1,100]{1,0:T(1,128)S(1)} %get-tuple-element.103.refs_0_, ...), custom_call_target="tpu_custom_call" | custom-call | flops 1 | bytes 1 | tf_op jit(solution)/shard_map/feed_grads/pallas_call | solution.py:52
  150.2 3.6 %collective-permute-done.32.refs_3_ = f32[192,768]{1,0:T(8,128)S(1)} collective-permute-done((f32[192,768]{1,0:T(8,128)S(1)}, f32[192,768]{1,0:T(8,128)S(1)}, u32[]{:S(2)}, u32[]{:S(2)}) %collective-permute-start.32) | collective-permute-done | bytes 589856 | tf_op jit(solution)/shard_map/ppermute | solution.py:762
  156.4 12.7 %collective-permute-done.34.refs_13_ = f32[192,768]{1,0:T(8,128)S(1)} collective-permute-done((f32[192,768]{1,0:T(8,128)S(1)}, f32[192,768]{1,0:T(8,128)S(1)}, u32[]{:S(2)}, u32[]{:S(2)}) %collective-permute-start.34) | collective-permute-done | bytes 589856 | tf_op jit(solution)/shard_map/ppermute | solution.py:762
  171.1 7.6 %back_edge.1 = (f32[384,384]{1,0:T(8,128)S(1)}, bf16[3,768,128]{2,1,0:T(8,128)(2,1)S(1)}, bf16[3,768,192]{2,1,0:T(8,128)(2,1)S(1)}, bf16[3,768,128]{2,1,0:T(8,12...) custom-call(s32[1,100]{1,0:T(1,128)S(1)} %get-tuple-element.103.refs, ...), custom_call_target="tpu_custom_call" | custom-call | flops 1 | bytes 1 | tf_op jit(solution)/shard_map/back_edge/pallas_call | solution.py:52
  179.9 2.8 collective-permute-done.36.refs_2_
  185.7 12.2 %back_own.1 = (f32[768,192]{1,0:T(8,128)S(1)}, f32[768,384]{1,0:T(8,128)S(1)}) custom-call(s32[1,12]{1,0:T(1,128)S(1)} %get-tuple-element.109.refs_0_.refs_1_, f32[2,768]{1,0:T(2,128)S(1)} %get-tuple-element.110.refs_1_.refs_2_, f32[2,768]{1,0:T(2,128)S(1)} %get-tuple-element.110.refs_1_.refs_2_, f32[768,384]{1,0:T(8,128)S(1)} %get-tuple-element.114.refs_4_.refs_3_, ...), custom_call_target="tpu_custom_call" | custom-call | flops 1 | bytes 1 | tf_op jit(solution)/shard_map/back_own/pallas_call | solution.py:52
  197.9 10.2 %last_grads.1 = (f32[2,192,768]{2,1,0:T(8,128)S(1)}, f32[2,192,768]{2,1,0:T(8,128)S(1)}, f32[2,30,24,128]{3,2,1,0:T(8,128)S(1)}, f32[2,30,24,128]{3,2,1,0:T(8,12...) custom-call(s32[1,100]{1,0:T(1,128)S(1)} %get-tuple-element.103.refs_0_, ...), custom_call_target="tpu_custom_call" | custom-call | flops 1 | bytes 1 | tf_op jit(solution)/shard_map/last_grads/pallas_call | solution.py:52
  214.9 5.3 %collective-permute-done.50 = f32[4,24,768]{2,1,0:T(8,128)S(1)} collective-permute-done((f32[4,24,768]{2,1,0:T(8,128)S(1)}, f32[4,24,768]{2,1,0:T(8,128)S(1)}, u32[]{:S(2)}, u32[]{:S(2)}) %collective-permute-start.50) | collective-permute-done | bytes 294944 | tf_op jit(solution)/shard_map/ppermute | solution.py:762
  225.4 9.5 %collective-permute-start.48 = (f32[96,768]{1,0:T(8,128)S(1)}, f32[96,768]{1,0:T(8,128)S(1)}, u32[]{:S(2)}, u32[]{:S(2)}) collective-permute-start(f32[96,768]{1,0:T(8,128)S(1)} %add_bitcast_fusion.refs_2_.refs_1_), channel_id=1, source_target_pairs={{0,8},{8,0},{16,24},{24,16},{1,9},{9,1},{17,25},{25,17},{2,10},{10... | collective-permute-start | bytes 884744 | tf_op jit(solution)/shard_map/ppermute | solution.py:762
  240.6 8.8 %collective-permute-done.41 = f32[2,30,24,128]{3,2,1,0:T(8,128)S(1)} collective-permute-done((f32[2,30,24,128]{3,2,1,0:T(8,128)S(1)}, f32[2,30,24,128]{3,2,1,0:T(8,128)S(1)}, u32[]{:S(2)}, u32[]{:S(2)}) %collective-permute-start.41) | collective-permute-done | bytes 737312 | tf_op jit(solution)/shard_map/ppermute | solution.py:762
  250.4 13.5 %collective-permute-done.53.refs_6_ = f32[4,24,768]{2,1,0:T(8,128)S(1)} collective-permute-done((f32[4,24,768]{2,1,0:T(8,128)S(1)}, f32[4,24,768]{2,1,0:T(8,128)S(1)}, u32[]{:S(2)}, u32[]{:S(2)}) %collective-permute-start.53) | collective-permute-done | bytes 294944 | tf_op jit(solution)/shard_map/ppermute | solution.py:762
  263.9 4.2 %collective-permute-done.49.refs_5_.refs_4_ = f32[96,768]{1,0:T(8,128)S(1)} collective-permute-done((f32[96,768]{1,0:T(8,128)S(1)}, f32[96,768]{1,0:T(8,128)S(1)}, u32[]{:S(2)}, u32[]{:S(2)}) %collective-permute-start.49) | collective-permute-done | bytes 294944 | tf_op jit(solution)/shard_map/ppermute | solution.py:762
  272.0 9.5 %collective-permute-done.54 = f32[1,30,24,128]{3,2,1,0:T(8,128)S(1)} collective-permute-done((f32[1,30,24,128]{3,2,1,0:T(8,128)S(1)}, f32[1,30,24,128]{3,2,1,0:T(8,128)S(1)}, u32[]{:S(2)}, u32[]{:S(2)}) %collective-permute-start.54) | collective-permute-done | bytes 368672 | tf_op jit(solution)/shard_map/ppermute | solution.py:762
  283.1 3.9 %collective-permute-done.55.refs_1_ = f32[14,24,128]{2,1,0:T(8,128)S(1)} collective-permute-done((f32[14,24,128]{2,1,0:T(8,128)S(1)}, f32[14,24,128]{2,1,0:T(8,128)S(1)}, u32[]{:S(2)}, u32[]{:S(2)}) %collective-permute-start.55) | collective-permute-done | bytes 172064 | tf_op jit(solution)/shard_map/ppermute | solution.py:762
  296.4 4.2 %collective-permute-start.59 = (f32[26,24,128]{2,1,0:T(8,128)S(1)}, f32[26,24,128]{2,1,0:T(8,128)S(1)}, u32[]{:S(2)}, u32[]{:S(2)}) collective-permute-start(f32[26,24,128]{2,1,0:T(8,128)S(1)} %constant_dynamic-update-slice_fusion.refs_1_), channel_id=1, source_target_pairs={{0,8},{8,0},{16,24},{24,16},{1,9},{9,1},{17,25},{25,17},{2,10},{10... | collective-permute-start | bytes 958472 | tf_op jit(solution)/shard_map/ppermute | solution.py:762
  301.4 6.1 %collective-permute-start.60 = (f32[26,24,128]{2,1,0:T(8,128)S(1)}, f32[26,24,128]{2,1,0:T(8,128)S(1)}, u32[]{:S(2)}, u32[]{:S(2)}) collective-permute-start(f32[26,24,128]{2,1,0:T(8,128)S(1)} %collective-permute-done.58.refs_2_), channel_id=1, source_target_pairs={{0,8},{8,0},{16,24},{24,16},{1,9},{9,1},{17,25},{25,17},{2,10},{10... | collective-permute-start | bytes 958472 | tf_op jit(solution)/shard_map/ppermute | solution.py:762
  308.2 7.0 %collective-permute-done.60.refs_4_ = f32[26,24,128]{2,1,0:T(8,128)S(1)} collective-permute-done((f32[26,24,128]{2,1,0:T(8,128)S(1)}, f32[26,24,128]{2,1,0:T(8,128)S(1)}, u32[]{:S(2)}, u32[]{:S(2)}) %collective-permute-start.60) | collective-permute-done | bytes 319520 | tf_op jit(solution)/shard_map/ppermute | solution.py:762
  (184 shorter events, 79.3 us)
Async XLA Ops:
  29.8 15.2 %collective-permute-start.3 = (f32[208,768]{1,0:T(8,128)S(1)}, f32[208,768]{1,0:T(8,128)S(1)}, u32[]{:S(2)}, u32[]{:S(2)}) collective-permute-start(f32[208,768]{1,0:T(8,128)S(1)} %base.1.refs_2_), channel_id=1, source_target_pairs={{0,1},{1,0},{2,3},{3,2},{4,5},{5,4},{6,7},{7,6},{8,9},{9,8},{10,11... | collective-permute-start | bytes 1916936 | tf_op jit(solution)/shard_map/ppermute | solution.py:762
  41.6 14.5 %collective-permute-start.5 = (f32[208,768]{1,0:T(8,128)S(1)}, f32[208,768]{1,0:T(8,128)S(1)}, u32[]{:S(2)}, u32[]{:S(2)}) collective-permute-start(f32[208,768]{1,0:T(8,128)S(1)} %collective-permute-done.4.refs_4_), channel_id=1, source_target_pairs={{0,1},{1,0},{2,3},{3,2},{4,5},{5,4},{6,7},{7,6},{8,9},{9,8},{10,11... | collective-permute-start | bytes 1916936 | tf_op jit(solution)/shard_map/ppermute | solution.py:762
  44.1 40.6 %collective-permute-start.12 = (f32[3,96,768]{2,1,0:T(8,128)S(1)}, f32[3,96,768]{2,1,0:T(8,128)S(1)}, u32[]{:S(2)}, u32[]{:S(2)}) collective-permute-start(f32[3,96,768]{2,1,0:T(8,128)S(1)} %get-tuple-element.119), channel_id=1, source_target_pairs={{0,2},{1,3},{2,0},{3,1},{4,6},{5,7},{6,4},{7,5},{8,10},{9,11},{10,... | collective-permute-start | bytes 2654216 | tf_op jit(solution)/shard_map/ppermute | solution.py:762
  45.0 39.7 %collective-permute-start.18 = (f32[3,96,768]{2,1,0:T(8,128)S(1)}, f32[3,96,768]{2,1,0:T(8,128)S(1)}, u32[]{:S(2)}, u32[]{:S(2)}) collective-permute-start(f32[3,96,768]{2,1,0:T(8,128)S(1)} %get-tuple-element.122.refs_1_), channel_id=1, source_target_pairs={{0,4},{4,0},{1,5},{5,1},{2,6},{6,2},{3,7},{7,3},{8,12},{12,8},{9,1... | collective-permute-start | bytes 2654216 | tf_op jit(solution)/shard_map/ppermute | solution.py:762
  62.0 22.8 %collective-permute-start.11 = (f32[384,384]{1,0:T(8,128)S(1)}, f32[384,384]{1,0:T(8,128)S(1)}, u32[]{:S(2)}, u32[]{:S(2)}) collective-permute-start(f32[384,384]{1,0:T(8,128)S(1)} %get-tuple-element.112), channel_id=1, source_target_pairs={{0,4},{4,0},{1,5},{5,1},{2,6},{6,2},{3,7},{7,3},{8,12},{12,8},{9,1... | collective-permute-start | bytes 1769480 | tf_op jit(solution)/shard_map/ppermute | solution.py:762
  64.3 20.4 %collective-permute-start.17 = (f32[192,768]{1,0:T(8,128)S(1)}, f32[192,768]{1,0:T(8,128)S(1)}, u32[]{:S(2)}, u32[]{:S(2)}) collective-permute-start(f32[192,768]{1,0:T(8,128)S(1)} %get-tuple-element.121.refs_1_), channel_id=1, source_target_pairs={{0,2},{1,3},{2,0},{3,1},{4,6},{5,7},{6,4},{7,5},{8,10},{9,11},{10,... | collective-permute-start | bytes 1769480 | tf_op jit(solution)/shard_map/ppermute | solution.py:762
  69.0 15.7 %collective-permute-start.16 = (f32[96,768]{1,0:T(8,128)S(1)}, f32[96,768]{1,0:T(8,128)S(1)}, u32[]{:S(2)}, u32[]{:S(2)}) collective-permute-start(f32[96,768]{1,0:T(8,128)S(1)} %collective-permute-done.13.refs_6_), channel_id=1, source_target_pairs={{0,16},{8,24},{16,0},{24,8},{1,17},{9,25},{17,1},{25,9},{2,18},{10... | collective-permute-start | bytes 884744 | tf_op jit(solution)/shard_map/ppermute | solution.py:762
  88.1 22.1 %collective-permute-start.25 = (f32[3,96,768]{2,1,0:T(8,128)S(1)}, f32[3,96,768]{2,1,0:T(8,128)S(1)}, u32[]{:S(2)}, u32[]{:S(2)}) collective-permute-start(f32[3,96,768]{2,1,0:T(8,128)S(1)} %get-tuple-element.124), channel_id=1, source_target_pairs={{0,4},{4,0},{1,5},{5,1},{2,6},{6,2},{3,7},{7,3},{8,12},{12,8},{9,1... | collective-permute-start | bytes 2654216 | tf_op jit(solution)/shard_map/ppermute | solution.py:762
  89.6 20.6 %collective-permute-start.20 = (f32[384,384]{1,0:T(8,128)S(1)}, f32[384,384]{1,0:T(8,128)S(1)}, u32[]{:S(2)}, u32[]{:S(2)}) collective-permute-start(f32[384,384]{1,0:T(8,128)S(1)} %get-tuple-element.123.refs_3_), channel_id=1, source_target_pairs={{0,2},{1,3},{2,0},{3,1},{4,6},{5,7},{6,4},{7,5},{8,10},{9,11},{10,... | collective-permute-start | bytes 1769480 | tf_op jit(solution)/shard_map/ppermute | solution.py:762
  90.5 20.3 %collective-permute-start.28 = (f32[192,768]{1,0:T(8,128)S(1)}, f32[192,768]{1,0:T(8,128)S(1)}, u32[]{:S(2)}, u32[]{:S(2)}) collective-permute-start(f32[192,768]{1,0:T(8,128)S(1)} %collective-permute-done.17.refs_12_.refs_3_), channel_id=1, source_target_pairs={{0,1},{1,0},{2,3},{3,2},{4,5},{5,4},{6,7},{7,6},{8,9},{9,8},{10,11... | collective-permute-start | bytes 1769480 | tf_op jit(solution)/shard_map/ppermute | solution.py:762
  90.5 24.8 %collective-permute-start.23 = (f32[3,96,768]{2,1,0:T(8,128)S(1)}, f32[3,96,768]{2,1,0:T(8,128)S(1)}, u32[]{:S(2)}, u32[]{:S(2)}) collective-permute-start(f32[3,96,768]{2,1,0:T(8,128)S(1)} %collective-permute-done.12.refs_8_.refs_3_), channel_id=1, source_target_pairs={{0,1},{1,0},{2,3},{3,2},{4,5},{5,4},{6,7},{7,6},{8,9},{9,8},{10,11... | collective-permute-start | bytes 2654216 | tf_op jit(solution)/shard_map/ppermute | solution.py:762
  91.4 23.9 %collective-permute-start.24 = (f32[3,96,768]{2,1,0:T(8,128)S(1)}, f32[3,96,768]{2,1,0:T(8,128)S(1)}, u32[]{:S(2)}, u32[]{:S(2)}) collective-permute-start(f32[3,96,768]{2,1,0:T(8,128)S(1)} %collective-permute-done.18.refs_13_.refs_5_), channel_id=1, source_target_pairs={{0,1},{1,0},{2,3},{3,2},{4,5},{5,4},{6,7},{7,6},{8,9},{9,8},{10,11... | collective-permute-start | bytes 2654216 | tf_op jit(solution)/shard_map/ppermute | solution.py:762
  138.2 15.7 %collective-permute-start.32 = (f32[192,768]{1,0:T(8,128)S(1)}, f32[192,768]{1,0:T(8,128)S(1)}, u32[]{:S(2)}, u32[]{:S(2)}) collective-permute-start(f32[192,768]{1,0:T(8,128)S(1)} %fusion.4.refs_11_), channel_id=1, source_target_pairs={{0,2},{1,3},{2,0},{3,1},{4,6},{5,7},{6,4},{7,5},{8,10},{9,11},{10,... | collective-permute-start | bytes 1769480 | tf_op jit(solution)/shard_map/ppermute | solution.py:762
  150.1 19.0 %collective-permute-start.30 = (f32[2,192,768]{2,1,0:T(8,128)S(1)}, f32[2,192,768]{2,1,0:T(8,128)S(1)}, u32[]{:S(2)}, u32[]{:S(2)}) collective-permute-start(f32[2,192,768]{2,1,0:T(8,128)S(1)} %get-tuple-element.144), channel_id=1, source_target_pairs={{0,1},{1,0},{2,3},{3,2},{4,5},{5,4},{6,7},{7,6},{8,9},{9,8},{10,11... | collective-permute-start | bytes 3538952 | tf_op jit(solution)/shard_map/ppermute | solution.py:762
  154.3 14.9 %collective-permute-start.34 = (f32[192,768]{1,0:T(8,128)S(1)}, f32[192,768]{1,0:T(8,128)S(1)}, u32[]{:S(2)}, u32[]{:S(2)}) collective-permute-start(f32[192,768]{1,0:T(8,128)S(1)} %get-tuple-element.148.refs_11_.refs_6_), channel_id=1, source_target_pairs={{0,2},{1,3},{2,0},{3,1},{4,6},{5,7},{6,4},{7,5},{8,10},{9,11},{10,... | collective-permute-start | bytes 1769480 | tf_op jit(solution)/shard_map/ppermute | solution.py:762
  155.0 27.7 %collective-permute-start.36 = (f32[4,96,768]{2,1,0:T(8,128)S(1)}, f32[4,96,768]{2,1,0:T(8,128)S(1)}, u32[]{:S(2)}, u32[]{:S(2)}) collective-permute-start(f32[4,96,768]{2,1,0:T(8,128)S(1)} %get-tuple-element.156), channel_id=1, source_target_pairs={{0,4},{4,0},{1,5},{5,1},{2,6},{6,2},{3,7},{7,3},{8,12},{12,8},{9,1... | collective-permute-start | bytes 3538952 | tf_op jit(solution)/shard_map/ppermute | solution.py:762
  156.4 26.9 %collective-permute-start.37 = (f32[16,24,768]{2,1,0:T(8,128)S(1)}, f32[16,24,768]{2,1,0:T(8,128)S(1)}, u32[]{:S(2)}, u32[]{:S(2)}) collective-permute-start(f32[16,24,768]{2,1,0:T(8,128)S(1)} %get-tuple-element.157), channel_id=1, source_target_pairs={{0,8},{8,0},{16,24},{24,16},{1,9},{9,1},{17,25},{25,17},{2,10},{10... | collective-permute-start | bytes 3538952 | tf_op jit(solution)/shard_map/ppermute | solution.py:762
  169.2 28.7 %collective-permute-start.31 = (f32[192,768]{1,0:T(8,128)S(1)}, f32[192,768]{1,0:T(8,128)S(1)}, u32[]{:S(2)}, u32[]{:S(2)}) collective-permute-start(f32[192,768]{1,0:T(8,128)S(1)} %fusion.1), channel_id=1, source_target_pairs={{0,2},{1,3},{2,0},{3,1},{4,6},{5,7},{6,4},{7,5},{8,10},{9,11},{10,... | collective-permute-start | bytes 1769480 | tf_op jit(solution)/shard_map/ppermute | solution.py:762
  178.7 19.2 %collective-permute-start.38 = (f32[384,384]{1,0:T(8,128)S(1)}, f32[384,384]{1,0:T(8,128)S(1)}, u32[]{:S(2)}, u32[]{:S(2)}) collective-permute-start(f32[384,384]{1,0:T(8,128)S(1)} %get-tuple-element.158.refs_4_), channel_id=1, source_target_pairs={{0,4},{4,0},{1,5},{5,1},{2,6},{6,2},{3,7},{7,3},{8,12},{12,8},{9,1... | collective-permute-start | bytes 1769480 | tf_op jit(solution)/shard_map/ppermute | solution.py:762
  183.5 24.7 %collective-permute-start.44 = (f32[2,96,768]{2,1,0:T(8,128)S(1)}, f32[2,96,768]{2,1,0:T(8,128)S(1)}, u32[]{:S(2)}, u32[]{:S(2)}) collective-permute-start(f32[2,96,768]{2,1,0:T(8,128)S(1)} %get-tuple-element.175), channel_id=1, source_target_pairs={{0,8},{8,0},{16,24},{24,16},{1,9},{9,1},{17,25},{25,17},{2,10},{10... | collective-permute-start | bytes 1769480 | tf_op jit(solution)/shard_map/ppermute | solution.py:762
  183.9 26.1 %collective-permute-start.45 = (f32[8,24,768]{2,1,0:T(8,128)S(1)}, f32[8,24,768]{2,1,0:T(8,128)S(1)}, u32[]{:S(2)}, u32[]{:S(2)}) collective-permute-start(f32[8,24,768]{2,1,0:T(8,128)S(1)} %get-tuple-element.176), channel_id=1, source_target_pairs={{0,24},{8,16},{16,8},{24,0},{1,25},{9,17},{17,9},{25,1},{2,26},{10... | collective-permute-start | bytes 1769480 | tf_op jit(solution)/shard_map/ppermute | solution.py:762
  208.1 27.9 %collective-permute-start.39 = (f32[2,192,768]{2,1,0:T(8,128)S(1)}, f32[2,192,768]{2,1,0:T(8,128)S(1)}, u32[]{:S(2)}, u32[]{:S(2)}) collective-permute-start(f32[2,192,768]{2,1,0:T(8,128)S(1)} %get-tuple-element.169), channel_id=1, source_target_pairs={{0,1},{1,0},{2,3},{3,2},{4,5},{5,4},{6,7},{7,6},{8,9},{9,8},{10,11... | collective-permute-start | bytes 3538952 | tf_op jit(solution)/shard_map/ppermute | solution.py:762
  212.8 23.1 %collective-permute-start.42 = (f32[2,30,24,128]{3,2,1,0:T(8,128)S(1)}, f32[2,30,24,128]{3,2,1,0:T(8,128)S(1)}, u32[]{:S(2)}, u32[]{:S(2)}) collective-permute-start(f32[2,30,24,128]{3,2,1,0:T(8,128)S(1)} %get-tuple-element.173), channel_id=1, source_target_pairs={{0,4},{4,0},{1,5},{5,1},{2,6},{6,2},{3,7},{7,3},{8,12},{12,8},{9,1... | collective-permute-start | bytes 2211848 | tf_op jit(solution)/shard_map/ppermute | solution.py:762
  214.3 35.2 %collective-permute-start.41 = (f32[2,30,24,128]{3,2,1,0:T(8,128)S(1)}, f32[2,30,24,128]{3,2,1,0:T(8,128)S(1)}, u32[]{:S(2)}, u32[]{:S(2)}) collective-permute-start(f32[2,30,24,128]{3,2,1,0:T(8,128)S(1)} %get-tuple-element.171), channel_id=1, source_target_pairs={{0,4},{4,0},{1,5},{5,1},{2,6},{6,2},{3,7},{7,3},{8,12},{12,8},{9,1... | collective-permute-start | bytes 2211848 | tf_op jit(solution)/shard_map/ppermute | solution.py:762
  221.4 17.3 %collective-permute-start.47 = (f32[96,768]{1,0:T(8,128)S(1)}, f32[96,768]{1,0:T(8,128)S(1)}, u32[]{:S(2)}, u32[]{:S(2)}) collective-permute-start(f32[96,768]{1,0:T(8,128)S(1)} %add_bitcast_fusion.refs_2_.refs_1_), channel_id=1, source_target_pairs={{0,24},{8,16},{16,8},{24,0},{1,25},{9,17},{17,9},{25,1},{2,26},{10... | collective-permute-start | bytes 884744 | tf_op jit(solution)/shard_map/ppermute | solution.py:762
  225.4 25.0 %collective-permute-start.48 = (f32[96,768]{1,0:T(8,128)S(1)}, f32[96,768]{1,0:T(8,128)S(1)}, u32[]{:S(2)}, u32[]{:S(2)}) collective-permute-start(f32[96,768]{1,0:T(8,128)S(1)} %add_bitcast_fusion.refs_2_.refs_1_), channel_id=1, source_target_pairs={{0,8},{8,0},{16,24},{24,16},{1,9},{9,1},{17,25},{25,17},{2,10},{10... | collective-permute-start | bytes 884744 | tf_op jit(solution)/shard_map/ppermute | solution.py:762
  236.0 32.0 %collective-permute-start.43 = (f32[2,30,24,128]{3,2,1,0:T(8,128)S(1)}, f32[2,30,24,128]{3,2,1,0:T(8,128)S(1)}, u32[]{:S(2)}, u32[]{:S(2)}) collective-permute-start(f32[2,30,24,128]{3,2,1,0:T(8,128)S(1)} %add.440), channel_id=1, source_target_pairs={{0,8},{8,0},{16,24},{24,16},{1,9},{9,1},{17,25},{25,17},{2,10},{10... | collective-permute-start | bytes 2211848 | tf_op jit(solution)/shard_map/ppermute | solution.py:762
  237.5 30.5 %collective-permute-start.40 = (f32[192,768]{1,0:T(8,128)S(1)}, f32[192,768]{1,0:T(8,128)S(1)}, u32[]{:S(2)}, u32[]{:S(2)}) collective-permute-start(f32[192,768]{1,0:T(8,128)S(1)} %fusion), channel_id=1, source_target_pairs={{0,2},{1,3},{2,0},{3,1},{4,6},{5,7},{6,4},{7,5},{8,10},{9,11},{10,... | collective-permute-start | bytes 1769480 | tf_op jit(solution)/shard_map/ppermute | solution.py:762
  238.8 25.1 %collective-permute-start.53 = (f32[4,24,768]{2,1,0:T(8,128)S(1)}, f32[4,24,768]{2,1,0:T(8,128)S(1)}, u32[]{:S(2)}, u32[]{:S(2)}) collective-permute-start(f32[4,24,768]{2,1,0:T(8,128)S(1)} %pad_maximum_fusion.refs_5_), channel_id=1, source_target_pairs={{0,24},{8,16},{16,8},{24,0},{1,25},{9,17},{17,9},{25,1},{2,26},{10... | collective-permute-start | bytes 884744 | tf_op jit(solution)/shard_map/ppermute | solution.py:762
  249.4 18.6 %collective-permute-start.49 = (f32[96,768]{1,0:T(8,128)S(1)}, f32[96,768]{1,0:T(8,128)S(1)}, u32[]{:S(2)}, u32[]{:S(2)}) collective-permute-start(f32[96,768]{1,0:T(8,128)S(1)} %collective-permute-done.47.refs_3_.refs_2_), channel_id=1, source_target_pairs={{0,8},{8,0},{16,24},{24,16},{1,9},{9,1},{17,25},{25,17},{2,10},{10... | collective-permute-start | bytes 884744 | tf_op jit(solution)/shard_map/ppermute | solution.py:762
  269.9 21.4 %collective-permute-start.61 = (f32[4,24,768]{2,1,0:T(8,128)S(1)}, f32[4,24,768]{2,1,0:T(8,128)S(1)}, u32[]{:S(2)}, u32[]{:S(2)}) collective-permute-start(f32[4,24,768]{2,1,0:T(8,128)S(1)} %pad_maximum_fusion.refs_5_), channel_id=1, source_target_pairs={{0,8},{8,0},{16,24},{24,16},{1,9},{9,1},{17,25},{25,17},{2,10},{10... | collective-permute-start | bytes 884744 | tf_op jit(solution)/shard_map/ppermute | solution.py:762
  270.9 21.7 %collective-permute-start.62 = (f32[4,24,768]{2,1,0:T(8,128)S(1)}, f32[4,24,768]{2,1,0:T(8,128)S(1)}, u32[]{:S(2)}, u32[]{:S(2)}) collective-permute-start(f32[4,24,768]{2,1,0:T(8,128)S(1)} %collective-permute-done.53.refs_6_), channel_id=1, source_target_pairs={{0,8},{8,0},{16,24},{24,16},{1,9},{9,1},{17,25},{25,17},{2,10},{10... | collective-permute-start | bytes 884744 | tf_op jit(solution)/shard_map/ppermute | solution.py:762
  (40 other events, 426.0 us)

commit v6 on v5

--- a/solution.py
+++ b/solution.py
@@ -1072,7 +1072,7 @@
         part_up = jnp.stack([part_up[0], core_up[0], far_up[0], core_up[1]])
         all_down = collect(part_down)
         all_up = collect(part_up)
-        (tail_keep,), (tail_send,) = fold((tail_near,), (tail_got,), [*all_down, all_up[1], far_in])
+        (tail_keep,), (tail_send,) = fold((tail_near,), (tail_got,), [all_down[1], all_down[2], all_up[1], far_in])
         part_tail = (tail_keep + swap(tail_send, "dp", 3))[0]
 
         far_tail = across(part_tail[near + outs:])

time: 321 us -> 322 us (level)
  starting transfers between devices: 70.6 us -> 46.3 us
  waiting for transfers between devices: 144 us -> 165 us
  Pallas kernels: 91 us -> 95.1 us
    ppermute x62, starting transfers between devices: 70 us -> 45.7 us  [swap(): return lax.ppermute(value, axis, [(i, i ^ mask) for i in range(count)])]
    ppermute x62, waiting for transfers between devices: 144 us -> 165 us  [swap(): return lax.ppermute(value, axis, [(i, i ^ mask) for i in range(count)])]
    pallas_call x21, Pallas kernels: 91 us -> 95.1 us  [call(): pl.pallas_call(kernel, out_shape=tuple(outs), in_specs=[SM] * smem + [VM]...]
  transfers between devices with their start and end apart: 63 -> 63, of which waited for: 30 -> 31; matrix products, arithmetic and copies ran while one was open for 1% -> 1% of each run, Pallas kernels for 22% -> 23%
where the time goes in v6:
time: 322 us; the launch traced here: 318 us
  waiting for transfers between devices  165 us (51%)
  Pallas kernels  95.1 us (30%)
  starting transfers between devices  46.3 us (14%)
  local copies, waits for them, and re-layouts  7.26 us (2%)
    ppermute x62, waiting for transfers between devices, swap(): return lax.ppermute(value, axis, [(i, i ^ mask) for i in range(count)])  165 us
    pallas_call x21, Pallas kernels, call(): pl.pallas_call(kernel, out_shape=tuple(outs), in_specs=[SM] * smem + [VM]...  95.1 us
    ppermute x62, starting transfers between devices, swap(): return lax.ppermute(value, axis, [(i, i ^ mask) for i in range(count)])  45.7 us
  transfers between devices with their start and end apart: 63, of which 31 were waited for; matrix products, arithmetic and copies ran while one was open for 1% of the time, Pallas kernels for 23%

profile of v6, /device:TPU:0, one launch (start us, length us, event | category | flops | bytes accessed | tf_op | source)
XLA Modules:
  0.0 317.5 jit_solution(15008878679332083599)
XLA Ops:
  3.8 2.9 collective-permute-start
  17.7 8.6 %collective-permute-done.1.refs_3_.refs_8_ = f32[2,96,576]{2,1,0:T(8,128)S(1)} collective-permute-done((f32[2,96,576]{2,1,0:T(8,128)S(1)}, f32[2,96,576]{2,1,0:T(8,128)S(1)}, u32[]{:S(2)}, u32[]{:S(2)}) %collective-permute-start.1) | collective-permute-done | bytes 442400 | tf_op jit(solution)/shard_map/ppermute | solution.py:762
  30.3 8.5 %collective-permute-done.9.refs_12_.refs_4_ = f32[2,96,576]{2,1,0:T(8,128)S(1)} collective-permute-done((f32[2,96,576]{2,1,0:T(8,128)S(1)}, f32[2,96,576]{2,1,0:T(8,128)S(1)}, u32[]{:S(2)}, u32[]{:S(2)}) %collective-permute-start.9) | collective-permute-done | bytes 442400 | tf_op jit(solution)/shard_map/ppermute | solution.py:762
  38.8 2.8 collective-permute-done.4.refs_4_
  45.6 6.9 %collective-permute-done.13.refs_6_ = f32[96,768]{1,0:T(8,128)S(1)} collective-permute-done((f32[96,768]{1,0:T(8,128)S(1)}, f32[96,768]{1,0:T(8,128)S(1)}, u32[]{:S(2)}, u32[]{:S(2)}) %collective-permute-start.13) | collective-permute-done | bytes 294944 | tf_op jit(solution)/shard_map/ppermute | solution.py:762
  52.5 3.6 %collective-permute-start.14 = (f32[96,768]{1,0:T(8,128)S(1)}, f32[96,768]{1,0:T(8,128)S(1)}, u32[]{:S(2)}, u32[]{:S(2)}) collective-permute-start(f32[96,768]{1,0:T(8,128)S(1)} %collective-permute-done.13.refs_6_), channel_id=1, source_target_pairs={{0,24},{8,16},{16,8},{24,0},{1,25},{9,17},{17,9},{25,1},{2,26},{10... | collective-permute-start | bytes 884744 | tf_op jit(solution)/shard_map/ppermute | solution.py:762
  56.1 5.8 %qkv.1 = (f32[768,192]{1,0:T(8,128)S(1)}, f32[768,384]{1,0:T(8,128)S(1)}, f32[384,384]{1,0:T(8,128)S(1)}, f32[768,768]{1,0:T(8,128)S(1)}, f32[16,768]{1,0:T(8,12...) custom-call(s32[1,100]{1,0:T(1,128)S(1)} %get-tuple-element.103.refs_0_, ...), custom_call_target="tpu_custom_call" | custom-call | flops 1 | bytes 1 | tf_op jit(solution)/shard_map/qkv/pallas_call | solution.py:52
  65.0 4.1 %collective-permute-done.15.refs_10_.refs_8_ = f32[96,768]{1,0:T(8,128)S(1)} collective-permute-done((f32[96,768]{1,0:T(8,128)S(1)}, f32[96,768]{1,0:T(8,128)S(1)}, u32[]{:S(2)}, u32[]{:S(2)}) %collective-permute-start.15) | collective-permute-done | bytes 294944 | tf_op jit(solution)/shard_map/ppermute | solution.py:762
  70.3 8.7 %attend_own.1 = (bf16[3,768,192]{2,1,0:T(8,128)(2,1)S(1)}, f32[3,3,1,256]{3,2,1,0:T(1,128)S(1)}, f32[3,3,1,256]{3,2,1,0:T(1,128)S(1)}, f32[3,3,128,256]{3,2,1,0:T(8,128)S(1)}) custom-call(s32[1,12]{1,0:T(1,128)S(1)} %get-tuple-element.109.refs_0_.refs_1_, f32[2,768]{1,0:T(2,128)S(1)} %get-tuple-element.110.refs_1_.refs_2_, ...), custom_call_target="tpu_custom_call" | custom-call | flops 1 | bytes 1 | tf_op jit(solution)/shard_map/attend_own/pallas_call | solution.py:52
  79.0 5.7 %collective-permute-done.16.refs_11_.refs_9_ = f32[96,768]{1,0:T(8,128)S(1)} collective-permute-done((f32[96,768]{1,0:T(8,128)S(1)}, f32[96,768]{1,0:T(8,128)S(1)}, u32[]{:S(2)}, u32[]{:S(2)}) %collective-permute-start.16) | collective-permute-done | bytes 294944 | tf_op jit(solution)/shard_map/ppermute | solution.py:762
  84.8 3.4 %attend_edge.1 = (f32[768,192]{1,0:T(8,128)S(1)}, f32[384,384]{1,0:T(8,128)S(1)}, f32[8,768]{1,0:T(8,128)S(1)}, f32[3,96,768]{2,1,0:T(8,128)S(1)}) custom-call(s32[1,12]{1,0:T(1,128)S(1)} %get-tuple-element.109.refs_0_.refs_1_, f32[2,768]{1,0:T(2,128)S(1)} %get-tuple-element.110.refs_1_.refs_2_, f32[2,384]{1,0:T(2,128)S(1)} %get-tuple-element.111.refs_2_.refs_3_, ...), custom_call_target="tpu_custom_call" | custom-call | flops 1 | bytes 1 | tf_op jit(solution)/shard_map/attend_edge/pallas_call | solution.py:52
  90.8 19.4 %collective-permute-done.25.refs_7_ = f32[3,96,768]{2,1,0:T(8,128)S(1)} collective-permute-done((f32[3,96,768]{2,1,0:T(8,128)S(1)}, f32[3,96,768]{2,1,0:T(8,128)S(1)}, u32[]{:S(2)}, u32[]{:S(2)}) %collective-permute-start.25) | collective-permute-done | bytes 884768 | tf_op jit(solution)/shard_map/ppermute | solution.py:762
  110.8 4.5 %act.1 = (bf16[768,768]{1,0:T(8,128)(2,1)S(1)}, bf16[768,768]{1,0:T(8,128)(2,1)S(1)}, bf16[768,768]{1,0:T(8,128)(2,1)S(1)}, bf16[768,768]{1,0:T(8,128)(2,1)S(1)}, f32[768,768]{1,0:T(8,128)S(1)}) custom-call(s32[1,100]{1,0:T(1,128)S(1)} %get-tuple-element.103.refs_0_, f32[192,768]{1,0:T(8,128)S(1)} %get-tuple-element.121.refs_1_, ...), custom_call_target="tpu_custom_call" | custom-call | flops 1 | bytes 1 | tf_op jit(solution)/shard_map/act/pallas_call | solution.py:52
  117.4 17.7 %feed.1 = (f32[2,192,768]{2,1,0:T(8,128)S(1)}, f32[2,192,768]{2,1,0:T(8,128)S(1)}, f32[2,192,768]{2,1,0:T(8,128)S(1)}, f32[192,128]{1,0:T(8,128)S(1)}, bf16[768,...) custom-call(s32[1,100]{1,0:T(1,128)S(1)} %get-tuple-element.103.refs, ...), custom_call_target="tpu_custom_call" | custom-call | flops 1 | bytes 1 | tf_op jit(solution)/shard_map/feed/pallas_call | solution.py:52
  135.6 2.5 collective-permute-done.29.refs_2_
  138.9 11.2 %feed_grads.1 = (f32[2,192,768]{2,1,0:T(8,128)S(1)}, f32[2,192,768]{2,1,0:T(8,128)S(1)}, f32[4,96,768]{2,1,0:T(8,128)S(1)}, f32[4,96,768]{2,1,0:T(8,128)S(1)}, f...) custom-call(s32[1,100]{1,0:T(1,128)S(1)} %get-tuple-element.103.refs_0_, ...), custom_call_target="tpu_custom_call" | custom-call | flops 1 | bytes 1 | tf_op jit(solution)/shard_map/feed_grads/pallas_call | solution.py:52
  150.2 3.6 %collective-permute-done.32.refs_3_ = f32[192,768]{1,0:T(8,128)S(1)} collective-permute-done((f32[192,768]{1,0:T(8,128)S(1)}, f32[192,768]{1,0:T(8,128)S(1)}, u32[]{:S(2)}, u32[]{:S(2)}) %collective-permute-start.32) | collective-permute-done | bytes 589856 | tf_op jit(solution)/shard_map/ppermute | solution.py:762
  157.0 12.1 %collective-permute-done.34.refs_13_ = f32[192,768]{1,0:T(8,128)S(1)} collective-permute-done((f32[192,768]{1,0:T(8,128)S(1)}, f32[192,768]{1,0:T(8,128)S(1)}, u32[]{:S(2)}, u32[]{:S(2)}) %collective-permute-start.34) | collective-permute-done | bytes 589856 | tf_op jit(solution)/shard_map/ppermute | solution.py:762
  171.1 7.6 %back_edge.1 = (f32[384,384]{1,0:T(8,128)S(1)}, bf16[3,768,128]{2,1,0:T(8,128)(2,1)S(1)}, bf16[3,768,192]{2,1,0:T(8,128)(2,1)S(1)}, bf16[3,768,128]{2,1,0:T(8,12...) custom-call(s32[1,100]{1,0:T(1,128)S(1)} %get-tuple-element.103.refs, ...), custom_call_target="tpu_custom_call" | custom-call | flops 1 | bytes 1 | tf_op jit(solution)/shard_map/back_edge/pallas_call | solution.py:52
  178.8 4.0 %collective-permute-done.36.refs_2_ = f32[4,96,768]{2,1,0:T(8,128)S(1)} collective-permute-done((f32[4,96,768]{2,1,0:T(8,128)S(1)}, f32[4,96,768]{2,1,0:T(8,128)S(1)}, u32[]{:S(2)}, u32[]{:S(2)}) %collective-permute-start.36) | collective-permute-done | bytes 1179680 | tf_op jit(solution)/shard_map/ppermute | solution.py:762
  185.8 14.8 %back_own.1 = (f32[768,192]{1,0:T(8,128)S(1)}, f32[768,384]{1,0:T(8,128)S(1)}) custom-call(s32[1,12]{1,0:T(1,128)S(1)} %get-tuple-element.109.refs_0_.refs_1_, f32[2,768]{1,0:T(2,128)S(1)} %get-tuple-element.110.refs_1_.refs_2_, f32[2,768]{1,0:T(2,128)S(1)} %get-tuple-element.110.refs_1_.refs_2_, f32[768,384]{1,0:T(8,128)S(1)} %get-tuple-element.114.refs_4_.refs_3_, ...), custom_call_target="tpu_custom_call" | custom-call | flops 1 | bytes 1 | tf_op jit(solution)/shard_map/back_own/pallas_call | solution.py:52
  200.7 10.2 %last_grads.1 = (f32[2,192,768]{2,1,0:T(8,128)S(1)}, f32[2,192,768]{2,1,0:T(8,128)S(1)}, f32[2,30,24,128]{3,2,1,0:T(8,128)S(1)}, f32[2,30,24,128]{3,2,1,0:T(8,12...) custom-call(s32[1,100]{1,0:T(1,128)S(1)} %get-tuple-element.103.refs_0_, ...), custom_call_target="tpu_custom_call" | custom-call | flops 1 | bytes 1 | tf_op jit(solution)/shard_map/last_grads/pallas_call | solution.py:52
  214.8 6.2 %collective-permute-done.49 = f32[4,24,768]{2,1,0:T(8,128)S(1)} collective-permute-done((f32[4,24,768]{2,1,0:T(8,128)S(1)}, f32[4,24,768]{2,1,0:T(8,128)S(1)}, u32[]{:S(2)}, u32[]{:S(2)}) %collective-permute-start.49) | collective-permute-done | bytes 294944 | tf_op jit(solution)/shard_map/ppermute | solution.py:762
  223.6 2.7 collective-permute-done.50
  226.7 10.1 %collective-permute-done.42 = f32[2,30,24,128]{3,2,1,0:T(8,128)S(1)} collective-permute-done((f32[2,30,24,128]{3,2,1,0:T(8,128)S(1)}, f32[2,30,24,128]{3,2,1,0:T(8,128)S(1)}, u32[]{:S(2)}, u32[]{:S(2)}) %collective-permute-start.42) | collective-permute-done | bytes 737312 | tf_op jit(solution)/shard_map/ppermute | solution.py:762
  239.4 12.8 %collective-permute-done.41 = f32[2,30,24,128]{3,2,1,0:T(8,128)S(1)} collective-permute-done((f32[2,30,24,128]{3,2,1,0:T(8,128)S(1)}, f32[2,30,24,128]{3,2,1,0:T(8,128)S(1)}, u32[]{:S(2)}, u32[]{:S(2)}) %collective-permute-start.41) | collective-permute-done | bytes 737312 | tf_op jit(solution)/shard_map/ppermute | solution.py:762
  252.3 10.4 %collective-permute-done.52.refs_4_.refs_6_ = f32[4,24,768]{2,1,0:T(8,128)S(1)} collective-permute-done((f32[4,24,768]{2,1,0:T(8,128)S(1)}, f32[4,24,768]{2,1,0:T(8,128)S(1)}, u32[]{:S(2)}, u32[]{:S(2)}) %collective-permute-start.52) | collective-permute-done | bytes 294944 | tf_op jit(solution)/shard_map/ppermute | solution.py:762
  266.8 9.5 %collective-permute-done.53 = f32[1,30,24,128]{3,2,1,0:T(8,128)S(1)} collective-permute-done((f32[1,30,24,128]{3,2,1,0:T(8,128)S(1)}, f32[1,30,24,128]{3,2,1,0:T(8,128)S(1)}, u32[]{:S(2)}, u32[]{:S(2)}) %collective-permute-start.53) | collective-permute-done | bytes 368672 | tf_op jit(solution)/shard_map/ppermute | solution.py:762
  278.2 3.6 %collective-permute-done.54.refs_1_ = f32[14,24,128]{2,1,0:T(8,128)S(1)} collective-permute-done((f32[14,24,128]{2,1,0:T(8,128)S(1)}, f32[14,24,128]{2,1,0:T(8,128)S(1)}, u32[]{:S(2)}, u32[]{:S(2)}) %collective-permute-start.54) | collective-permute-done | bytes 172064 | tf_op jit(solution)/shard_map/ppermute | solution.py:762
  286.8 8.4 %collective-permute-done.62.refs_8_ = f32[4,24,768]{2,1,0:T(8,128)S(1)} collective-permute-done((f32[4,24,768]{2,1,0:T(8,128)S(1)}, f32[4,24,768]{2,1,0:T(8,128)S(1)}, u32[]{:S(2)}, u32[]{:S(2)}) %collective-permute-start.62) | collective-permute-done | bytes 294944 | tf_op jit(solution)/shard_map/ppermute | solution.py:762
  303.6 5.9 %collective-permute-done.58.refs_3_ = f32[26,24,128]{2,1,0:T(8,128)S(1)} collective-permute-done((f32[26,24,128]{2,1,0:T(8,128)S(1)}, f32[26,24,128]{2,1,0:T(8,128)S(1)}, u32[]{:S(2)}, u32[]{:S(2)}) %collective-permute-start.58) | collective-permute-done | bytes 319520 | tf_op jit(solution)/shard_map/ppermute | solution.py:762
  309.6 5.8 %collective-permute-done.59.refs_4_ = f32[26,24,128]{2,1,0:T(8,128)S(1)} collective-permute-done((f32[26,24,128]{2,1,0:T(8,128)S(1)}, f32[26,24,128]{2,1,0:T(8,128)S(1)}, u32[]{:S(2)}, u32[]{:S(2)}) %collective-permute-start.59) | collective-permute-done | bytes 319520 | tf_op jit(solution)/shard_map/ppermute | solution.py:762
  (184 shorter events, 71.7 us)
Async XLA Ops:
  29.8 15.2 %collective-permute-start.3 = (f32[208,768]{1,0:T(8,128)S(1)}, f32[208,768]{1,0:T(8,128)S(1)}, u32[]{:S(2)}, u32[]{:S(2)}) collective-permute-start(f32[208,768]{1,0:T(8,128)S(1)} %base.1.refs_2_), channel_id=1, source_target_pairs={{0,1},{1,0},{2,3},{3,2},{4,5},{5,4},{6,7},{7,6},{8,9},{9,8},{10,11... | collective-permute-start | bytes 1916936 | tf_op jit(solution)/shard_map/ppermute | solution.py:762
  41.6 14.5 %collective-permute-start.5 = (f32[208,768]{1,0:T(8,128)S(1)}, f32[208,768]{1,0:T(8,128)S(1)}, u32[]{:S(2)}, u32[]{:S(2)}) collective-permute-start(f32[208,768]{1,0:T(8,128)S(1)} %collective-permute-done.4.refs_4_), channel_id=1, source_target_pairs={{0,1},{1,0},{2,3},{3,2},{4,5},{5,4},{6,7},{7,6},{8,9},{9,8},{10,11... | collective-permute-start | bytes 1916936 | tf_op jit(solution)/shard_map/ppermute | solution.py:762
  44.1 40.6 %collective-permute-start.12 = (f32[3,96,768]{2,1,0:T(8,128)S(1)}, f32[3,96,768]{2,1,0:T(8,128)S(1)}, u32[]{:S(2)}, u32[]{:S(2)}) collective-permute-start(f32[3,96,768]{2,1,0:T(8,128)S(1)} %get-tuple-element.119), channel_id=1, source_target_pairs={{0,2},{1,3},{2,0},{3,1},{4,6},{5,7},{6,4},{7,5},{8,10},{9,11},{10,... | collective-permute-start | bytes 2654216 | tf_op jit(solution)/shard_map/ppermute | solution.py:762
  45.0 39.7 %collective-permute-start.18 = (f32[3,96,768]{2,1,0:T(8,128)S(1)}, f32[3,96,768]{2,1,0:T(8,128)S(1)}, u32[]{:S(2)}, u32[]{:S(2)}) collective-permute-start(f32[3,96,768]{2,1,0:T(8,128)S(1)} %get-tuple-element.122.refs_1_), channel_id=1, source_target_pairs={{0,4},{4,0},{1,5},{5,1},{2,6},{6,2},{3,7},{7,3},{8,12},{12,8},{9,1... | collective-permute-start | bytes 2654216 | tf_op jit(solution)/shard_map/ppermute | solution.py:762
  62.0 22.8 %collective-permute-start.11 = (f32[384,384]{1,0:T(8,128)S(1)}, f32[384,384]{1,0:T(8,128)S(1)}, u32[]{:S(2)}, u32[]{:S(2)}) collective-permute-start(f32[384,384]{1,0:T(8,128)S(1)} %get-tuple-element.112), channel_id=1, source_target_pairs={{0,4},{4,0},{1,5},{5,1},{2,6},{6,2},{3,7},{7,3},{8,12},{12,8},{9,1... | collective-permute-start | bytes 1769480 | tf_op jit(solution)/shard_map/ppermute | solution.py:762
  64.3 20.4 %collective-permute-start.17 = (f32[192,768]{1,0:T(8,128)S(1)}, f32[192,768]{1,0:T(8,128)S(1)}, u32[]{:S(2)}, u32[]{:S(2)}) collective-permute-start(f32[192,768]{1,0:T(8,128)S(1)} %get-tuple-element.121.refs_1_), channel_id=1, source_target_pairs={{0,2},{1,3},{2,0},{3,1},{4,6},{5,7},{6,4},{7,5},{8,10},{9,11},{10,... | collective-permute-start | bytes 1769480 | tf_op jit(solution)/shard_map/ppermute | solution.py:762
  69.0 15.7 %collective-permute-start.16 = (f32[96,768]{1,0:T(8,128)S(1)}, f32[96,768]{1,0:T(8,128)S(1)}, u32[]{:S(2)}, u32[]{:S(2)}) collective-permute-start(f32[96,768]{1,0:T(8,128)S(1)} %collective-permute-done.13.refs_6_), channel_id=1, source_target_pairs={{0,16},{8,24},{16,0},{24,8},{1,17},{9,25},{17,1},{25,9},{2,18},{10... | collective-permute-start | bytes 884744 | tf_op jit(solution)/shard_map/ppermute | solution.py:762
  88.1 22.1 %collective-permute-start.25 = (f32[3,96,768]{2,1,0:T(8,128)S(1)}, f32[3,96,768]{2,1,0:T(8,128)S(1)}, u32[]{:S(2)}, u32[]{:S(2)}) collective-permute-start(f32[3,96,768]{2,1,0:T(8,128)S(1)} %get-tuple-element.124), channel_id=1, source_target_pairs={{0,4},{4,0},{1,5},{5,1},{2,6},{6,2},{3,7},{7,3},{8,12},{12,8},{9,1... | collective-permute-start | bytes 2654216 | tf_op jit(solution)/shard_map/ppermute | solution.py:762
  88.8 21.4 %collective-permute-start.20 = (f32[384,384]{1,0:T(8,128)S(1)}, f32[384,384]{1,0:T(8,128)S(1)}, u32[]{:S(2)}, u32[]{:S(2)}) collective-permute-start(f32[384,384]{1,0:T(8,128)S(1)} %get-tuple-element.123.refs_3_), channel_id=1, source_target_pairs={{0,2},{1,3},{2,0},{3,1},{4,6},{5,7},{6,4},{7,5},{8,10},{9,11},{10,... | collective-permute-start | bytes 1769480 | tf_op jit(solution)/shard_map/ppermute | solution.py:762
  89.7 21.1 %collective-permute-start.28 = (f32[192,768]{1,0:T(8,128)S(1)}, f32[192,768]{1,0:T(8,128)S(1)}, u32[]{:S(2)}, u32[]{:S(2)}) collective-permute-start(f32[192,768]{1,0:T(8,128)S(1)} %collective-permute-done.17.refs_12_.refs_3_), channel_id=1, source_target_pairs={{0,1},{1,0},{2,3},{3,2},{4,5},{5,4},{6,7},{7,6},{8,9},{9,8},{10,11... | collective-permute-start | bytes 1769480 | tf_op jit(solution)/shard_map/ppermute | solution.py:762
  89.7 25.6 %collective-permute-start.23 = (f32[3,96,768]{2,1,0:T(8,128)S(1)}, f32[3,96,768]{2,1,0:T(8,128)S(1)}, u32[]{:S(2)}, u32[]{:S(2)}) collective-permute-start(f32[3,96,768]{2,1,0:T(8,128)S(1)} %collective-permute-done.12.refs_8_.refs_3_), channel_id=1, source_target_pairs={{0,1},{1,0},{2,3},{3,2},{4,5},{5,4},{6,7},{7,6},{8,9},{9,8},{10,11... | collective-permute-start | bytes 2654216 | tf_op jit(solution)/shard_map/ppermute | solution.py:762
  90.6 24.7 %collective-permute-start.24 = (f32[3,96,768]{2,1,0:T(8,128)S(1)}, f32[3,96,768]{2,1,0:T(8,128)S(1)}, u32[]{:S(2)}, u32[]{:S(2)}) collective-permute-start(f32[3,96,768]{2,1,0:T(8,128)S(1)} %collective-permute-done.18.refs_13_.refs_5_), channel_id=1, source_target_pairs={{0,1},{1,0},{2,3},{3,2},{4,5},{5,4},{6,7},{7,6},{8,9},{9,8},{10,11... | collective-permute-start | bytes 2654216 | tf_op jit(solution)/shard_map/ppermute | solution.py:762
  138.2 15.7 %collective-permute-start.32 = (f32[192,768]{1,0:T(8,128)S(1)}, f32[192,768]{1,0:T(8,128)S(1)}, u32[]{:S(2)}, u32[]{:S(2)}) collective-permute-start(f32[192,768]{1,0:T(8,128)S(1)} %fusion.4.refs_11_), channel_id=1, source_target_pairs={{0,2},{1,3},{2,0},{3,1},{4,6},{5,7},{6,4},{7,5},{8,10},{9,11},{10,... | collective-permute-start | bytes 1769480 | tf_op jit(solution)/shard_map/ppermute | solution.py:762
  150.1 19.0 %collective-permute-start.30 = (f32[2,192,768]{2,1,0:T(8,128)S(1)}, f32[2,192,768]{2,1,0:T(8,128)S(1)}, u32[]{:S(2)}, u32[]{:S(2)}) collective-permute-start(f32[2,192,768]{2,1,0:T(8,128)S(1)} %get-tuple-element.144), channel_id=1, source_target_pairs={{0,1},{1,0},{2,3},{3,2},{4,5},{5,4},{6,7},{7,6},{8,9},{9,8},{10,11... | collective-permute-start | bytes 3538952 | tf_op jit(solution)/shard_map/ppermute | solution.py:762
  154.3 14.9 %collective-permute-start.34 = (f32[192,768]{1,0:T(8,128)S(1)}, f32[192,768]{1,0:T(8,128)S(1)}, u32[]{:S(2)}, u32[]{:S(2)}) collective-permute-start(f32[192,768]{1,0:T(8,128)S(1)} %get-tuple-element.148.refs_11_.refs_6_), channel_id=1, source_target_pairs={{0,2},{1,3},{2,0},{3,1},{4,6},{5,7},{6,4},{7,5},{8,10},{9,11},{10,... | collective-permute-start | bytes 1769480 | tf_op jit(solution)/shard_map/ppermute | solution.py:762
  155.0 27.7 %collective-permute-start.36 = (f32[4,96,768]{2,1,0:T(8,128)S(1)}, f32[4,96,768]{2,1,0:T(8,128)S(1)}, u32[]{:S(2)}, u32[]{:S(2)}) collective-permute-start(f32[4,96,768]{2,1,0:T(8,128)S(1)} %get-tuple-element.156), channel_id=1, source_target_pairs={{0,4},{4,0},{1,5},{5,1},{2,6},{6,2},{3,7},{7,3},{8,12},{12,8},{9,1... | collective-permute-start | bytes 3538952 | tf_op jit(solution)/shard_map/ppermute | solution.py:762
  155.6 27.1 %collective-permute-start.37 = (f32[16,24,768]{2,1,0:T(8,128)S(1)}, f32[16,24,768]{2,1,0:T(8,128)S(1)}, u32[]{:S(2)}, u32[]{:S(2)}) collective-permute-start(f32[16,24,768]{2,1,0:T(8,128)S(1)} %get-tuple-element.157), channel_id=1, source_target_pairs={{0,8},{8,0},{16,24},{24,16},{1,9},{9,1},{17,25},{25,17},{2,10},{10... | collective-permute-start | bytes 3538952 | tf_op jit(solution)/shard_map/ppermute | solution.py:762
  169.2 31.5 %collective-permute-start.31 = (f32[192,768]{1,0:T(8,128)S(1)}, f32[192,768]{1,0:T(8,128)S(1)}, u32[]{:S(2)}, u32[]{:S(2)}) collective-permute-start(f32[192,768]{1,0:T(8,128)S(1)} %fusion.1), channel_id=1, source_target_pairs={{0,2},{1,3},{2,0},{3,1},{4,6},{5,7},{6,4},{7,5},{8,10},{9,11},{10,... | collective-permute-start | bytes 1769480 | tf_op jit(solution)/shard_map/ppermute | solution.py:762
  178.7 22.0 %collective-permute-start.38 = (f32[384,384]{1,0:T(8,128)S(1)}, f32[384,384]{1,0:T(8,128)S(1)}, u32[]{:S(2)}, u32[]{:S(2)}) collective-permute-start(f32[384,384]{1,0:T(8,128)S(1)} %get-tuple-element.158.refs_4_), channel_id=1, source_target_pairs={{0,4},{4,0},{1,5},{5,1},{2,6},{6,2},{3,7},{7,3},{8,12},{12,8},{9,1... | collective-permute-start | bytes 1769480 | tf_op jit(solution)/shard_map/ppermute | solution.py:762
  183.0 28.0 %collective-permute-start.44 = (f32[2,96,768]{2,1,0:T(8,128)S(1)}, f32[2,96,768]{2,1,0:T(8,128)S(1)}, u32[]{:S(2)}, u32[]{:S(2)}) collective-permute-start(f32[2,96,768]{2,1,0:T(8,128)S(1)} %get-tuple-element.175), channel_id=1, source_target_pairs={{0,8},{8,0},{16,24},{24,16},{1,9},{9,1},{17,25},{25,17},{2,10},{10... | collective-permute-start | bytes 1769480 | tf_op jit(solution)/shard_map/ppermute | solution.py:762
  184.1 26.8 %collective-permute-start.45 = (f32[8,24,768]{2,1,0:T(8,128)S(1)}, f32[8,24,768]{2,1,0:T(8,128)S(1)}, u32[]{:S(2)}, u32[]{:S(2)}) collective-permute-start(f32[8,24,768]{2,1,0:T(8,128)S(1)} %get-tuple-element.176), channel_id=1, source_target_pairs={{0,24},{8,16},{16,8},{24,0},{1,25},{9,17},{17,9},{25,1},{2,26},{10... | collective-permute-start | bytes 1769480 | tf_op jit(solution)/shard_map/ppermute | solution.py:762
  210.9 26.1 %collective-permute-start.39 = (f32[2,192,768]{2,1,0:T(8,128)S(1)}, f32[2,192,768]{2,1,0:T(8,128)S(1)}, u32[]{:S(2)}, u32[]{:S(2)}) collective-permute-start(f32[2,192,768]{2,1,0:T(8,128)S(1)} %get-tuple-element.169), channel_id=1, source_target_pairs={{0,1},{1,0},{2,3},{3,2},{4,5},{5,4},{6,7},{7,6},{8,9},{9,8},{10,11... | collective-permute-start | bytes 3538952 | tf_op jit(solution)/shard_map/ppermute | solution.py:762
  212.8 24.0 %collective-permute-start.42 = (f32[2,30,24,128]{3,2,1,0:T(8,128)S(1)}, f32[2,30,24,128]{3,2,1,0:T(8,128)S(1)}, u32[]{:S(2)}, u32[]{:S(2)}) collective-permute-start(f32[2,30,24,128]{3,2,1,0:T(8,128)S(1)} %get-tuple-element.173), channel_id=1, source_target_pairs={{0,4},{4,0},{1,5},{5,1},{2,6},{6,2},{3,7},{7,3},{8,12},{12,8},{9,1... | collective-permute-start | bytes 2211848 | tf_op jit(solution)/shard_map/ppermute | solution.py:762
  214.3 37.9 %collective-permute-start.41 = (f32[2,30,24,128]{3,2,1,0:T(8,128)S(1)}, f32[2,30,24,128]{3,2,1,0:T(8,128)S(1)}, u32[]{:S(2)}, u32[]{:S(2)}) collective-permute-start(f32[2,30,24,128]{3,2,1,0:T(8,128)S(1)} %get-tuple-element.171), channel_id=1, source_target_pairs={{0,4},{4,0},{1,5},{5,1},{2,6},{6,2},{3,7},{7,3},{8,12},{12,8},{9,1... | collective-permute-start | bytes 2211848 | tf_op jit(solution)/shard_map/ppermute | solution.py:762
  222.6 29.7 %collective-permute-start.47 = (f32[96,768]{1,0:T(8,128)S(1)}, f32[96,768]{1,0:T(8,128)S(1)}, u32[]{:S(2)}, u32[]{:S(2)}) collective-permute-start(f32[96,768]{1,0:T(8,128)S(1)} %add_bitcast_fusion.refs_1_), channel_id=1, source_target_pairs={{0,24},{8,16},{16,8},{24,0},{1,25},{9,17},{17,9},{25,1},{2,26},{10... | collective-permute-start | bytes 884744 | tf_op jit(solution)/shard_map/ppermute | solution.py:762
  226.3 26.0 %collective-permute-start.48 = (f32[96,768]{1,0:T(8,128)S(1)}, f32[96,768]{1,0:T(8,128)S(1)}, u32[]{:S(2)}, u32[]{:S(2)}) collective-permute-start(f32[96,768]{1,0:T(8,128)S(1)} %add_bitcast_fusion.refs_1_), channel_id=1, source_target_pairs={{0,8},{8,0},{16,24},{24,16},{1,9},{9,1},{17,25},{25,17},{2,10},{10... | collective-permute-start | bytes 884744 | tf_op jit(solution)/shard_map/ppermute | solution.py:762
  236.9 25.8 %collective-permute-start.43 = (f32[2,30,24,128]{3,2,1,0:T(8,128)S(1)}, f32[2,30,24,128]{3,2,1,0:T(8,128)S(1)}, u32[]{:S(2)}, u32[]{:S(2)}) collective-permute-start(f32[2,30,24,128]{3,2,1,0:T(8,128)S(1)} %add.440), channel_id=1, source_target_pairs={{0,8},{8,0},{16,24},{24,16},{1,9},{9,1},{17,25},{25,17},{2,10},{10... | collective-permute-start | bytes 2211848 | tf_op jit(solution)/shard_map/ppermute | solution.py:762
  238.2 24.5 %collective-permute-start.40 = (f32[192,768]{1,0:T(8,128)S(1)}, f32[192,768]{1,0:T(8,128)S(1)}, u32[]{:S(2)}, u32[]{:S(2)}) collective-permute-start(f32[192,768]{1,0:T(8,128)S(1)} %fusion), channel_id=1, source_target_pairs={{0,2},{1,3},{2,0},{3,1},{4,6},{5,7},{6,4},{7,5},{8,10},{9,11},{10,... | collective-permute-start | bytes 1769480 | tf_op jit(solution)/shard_map/ppermute | solution.py:762
  264.6 21.4 %collective-permute-start.61 = (f32[4,24,768]{2,1,0:T(8,128)S(1)}, f32[4,24,768]{2,1,0:T(8,128)S(1)}, u32[]{:S(2)}, u32[]{:S(2)}) collective-permute-start(f32[4,24,768]{2,1,0:T(8,128)S(1)} %pad_maximum_fusion.refs_5_), channel_id=1, source_target_pairs={{0,8},{8,0},{16,24},{24,16},{1,9},{9,1},{17,25},{25,17},{2,10},{10... | collective-permute-start | bytes 884744 | tf_op jit(solution)/shard_map/ppermute | solution.py:762
  264.7 22.1 %collective-permute-start.60 = (f32[96,768]{1,0:T(8,128)S(1)}, f32[96,768]{1,0:T(8,128)S(1)}, u32[]{:S(2)}, u32[]{:S(2)}) collective-permute-start(f32[96,768]{1,0:T(8,128)S(1)} %collective-permute-done.47.refs_2_), channel_id=1, source_target_pairs={{0,8},{8,0},{16,24},{24,16},{1,9},{9,1},{17,25},{25,17},{2,10},{10... | collective-permute-start | bytes 884744 | tf_op jit(solution)/shard_map/ppermute | solution.py:762
  266.7 28.5 %collective-permute-start.62 = (f32[4,24,768]{2,1,0:T(8,128)S(1)}, f32[4,24,768]{2,1,0:T(8,128)S(1)}, u32[]{:S(2)}, u32[]{:S(2)}) collective-permute-start(f32[4,24,768]{2,1,0:T(8,128)S(1)} %collective-permute-done.52.refs_4_.refs_6_), channel_id=1, source_target_pairs={{0,8},{8,0},{16,24},{24,16},{1,9},{9,1},{17,25},{25,17},{2,10},{10... | collective-permute-start | bytes 884744 | tf_op jit(solution)/shard_map/ppermute | solution.py:762
  283.3 17.9 %collective-permute-start.57 = (f32[26,24,128]{2,1,0:T(8,128)S(1)}, f32[26,24,128]{2,1,0:T(8,128)S(1)}, u32[]{:S(2)}, u32[]{:S(2)}) collective-permute-start(f32[26,24,128]{2,1,0:T(8,128)S(1)} %constant_dynamic-update-slice_fusion.refs_1_), channel_id=1, source_target_pairs={{0,24},{8,16},{16,8},{24,0},{1,25},{9,17},{17,9},{25,1},{2,26},{10... | collective-permute-start | bytes 958472 | tf_op jit(solution)/shard_map/ppermute | solution.py:762
  (40 other events, 421.3 us)

commit v7 on v6

--- a/solution.py
+++ b/solution.py
@@ -159,7 +159,7 @@
     qb = pick(u, [small[0:1, i * part:(i + 1) * part] for i in range(splits)])
     vb = pick(u, [small[1:2, i * part:(i + 1) * part] for i in range(splits)])
     bias = jnp.concatenate([qb, jnp.zeros_like(qb), vb], axis=1)
-    step = nh.shape[0] // 2
+    step = nh.shape[0] // 3
 
     def rows_of(i, _):
         row = at(i * step, step, 16)
@@ -168,7 +168,7 @@
         kv_ref[row, :] = out[:, part:]
         return 0
 
-    lax.fori_loop(0, 2, rows_of, 0)
+    lax.fori_loop(0, 3, rows_of, 0)
     reach = edge_ref.shape[0]
     edge_ref[...] = kv_ref[at(idx[0, edge], reach), :]
     og_ref[...] = og[...]
@@ -495,14 +495,14 @@
             quarter = idx[0, place] ^ (0, 3, 1, 2)[z]
             row = at(idx[0, first + i] * unit + quarter * size, size, 16)
             dh[row, :], dl[row, :] = split(down[whole + 4 * (i - whole) + z][...])
-    step = gh.shape[0] // 2
+    step = gh.shape[0] // 3
 
     def rows_of(i, _):
         row = at(i * step, step, 16)
         act_ref[row, :] = mm3((gh[row, :], gl[row, :]), (dh[...], dl[...]), NT)
         return 0
 
-    lax.fori_loop(0, 2, rows_of, 0)
+    lax.fori_loop(0, 3, rows_of, 0)
 
 
 def feed_kernel(splits, idx, small, base, *refs):
@@ -565,7 +565,7 @@
     outs, r32 = refs[:-1], refs[-1]
     downs, ups = outs[:len(outs) // 2], outs[len(outs) // 2:]
     tokens = keep.shape[1]
-    step = r32.shape[0] // 2
+    step = r32.shape[0] // 3
 
     third = r32.shape[0] // 3
 
@@ -597,7 +597,7 @@
         r32[row, :] = mm3((ah[row, :], al[row, :]), (dh[...], dl[...]))
         return 0
 
-    lax.fori_loop(0, 2, rows_of, 0)
+    lax.fori_loop(0, 3, rows_of, 0)
 
     def pairs_of(h, _):
         keep[h] = r32[at(idx[0, 2 * h] * tokens, tokens), :]
@@ -631,7 +631,7 @@
     sums = jnp.sum(qkv, axis=0, keepdims=True)
     xhat[...], _ = norm(base[...])
     vec[...] = jnp.zeros_like(vec)
-    step = n32.shape[0] // 2
+    step = n32.shape[0] // 3
 
     def rows_of(i, _):
         row = at(i * step, step, 16)
@@ -641,7 +641,7 @@
         vec[5:6, :] += jnp.sum(grad, axis=0, keepdims=True)
         return 0
 
-    lax.fori_loop(0, 2, rows_of, 0)
+    lax.fori_loop(0, 3, rows_of, 0)
 
     def pairs_of(h, _):
         keep[h] = n32[at(idx[0, 2 * h] * tokens, tokens), :]

time: 322 us -> 322 us (level)
  starting transfers between devices: 46.3 us -> 69.5 us
  waiting for transfers between devices: 165 us -> 144 us
  Pallas kernels: 95.1 us -> 91.8 us
    ppermute x62, starting transfers between devices: 45.7 us -> 68.9 us  [swap(): return lax.ppermute(value, axis, [(i, i ^ mask) for i in range(count)])]
    ppermute x62, waiting for transfers between devices: 165 us -> 144 us  [swap(): return lax.ppermute(value, axis, [(i, i ^ mask) for i in range(count)])]
    pallas_call x21, Pallas kernels: 95.1 us -> 91.8 us  [call(): pl.pallas_call(kernel, out_shape=tuple(outs), in_specs=[SM] * smem + [VM]...]
  transfers between devices with their start and end apart: 63 -> 63, of which waited for: 31 -> 31; matrix products, arithmetic and copies ran while one was open for 1% -> 1% of each run, Pallas kernels for 23% -> 22%
where the time goes in v7:
time: 322 us; the launch traced here: 317 us
  waiting for transfers between devices  144 us (45%)
  Pallas kernels  91.8 us (29%)
  starting transfers between devices  69.5 us (22%)
  local copies, waits for them, and re-layouts  7.26 us (2%)
    ppermute x62, waiting for transfers between devices, swap(): return lax.ppermute(value, axis, [(i, i ^ mask) for i in range(count)])  144 us
    pallas_call x21, Pallas kernels, call(): pl.pallas_call(kernel, out_shape=tuple(outs), in_specs=[SM] * smem + [VM]...  91.8 us
    ppermute x62, starting transfers between devices, swap(): return lax.ppermute(value, axis, [(i, i ^ mask) for i in range(count)])  68.9 us
  transfers between devices with their start and end apart: 63, of which 31 were waited for; matrix products, arithmetic and copies ran while one was open for 1% of the time, Pallas kernels for 22%

profile of v7, /device:TPU:0, one launch (start us, length us, event | category | flops | bytes accessed | tf_op | source)
XLA Modules:
  0.0 316.6 jit_solution(11451803590607273758)
XLA Ops:
  3.8 2.9 collective-permute-start
  17.7 8.6 %collective-permute-done.1.refs_3_.refs_8_ = f32[2,96,576]{2,1,0:T(8,128)S(1)} collective-permute-done((f32[2,96,576]{2,1,0:T(8,128)S(1)}, f32[2,96,576]{2,1,0:T(8,128)S(1)}, u32[]{:S(2)}, u32[]{:S(2)}) %collective-permute-start.1) | collective-permute-done | bytes 442400 | tf_op jit(solution)/shard_map/ppermute | solution.py:762
  30.3 8.5 %collective-permute-done.9.refs_12_.refs_4_ = f32[2,96,576]{2,1,0:T(8,128)S(1)} collective-permute-done((f32[2,96,576]{2,1,0:T(8,128)S(1)}, f32[2,96,576]{2,1,0:T(8,128)S(1)}, u32[]{:S(2)}, u32[]{:S(2)}) %collective-permute-start.9) | collective-permute-done | bytes 442400 | tf_op jit(solution)/shard_map/ppermute | solution.py:762
  45.6 6.9 %collective-permute-done.13.refs_6_ = f32[96,768]{1,0:T(8,128)S(1)} collective-permute-done((f32[96,768]{1,0:T(8,128)S(1)}, f32[96,768]{1,0:T(8,128)S(1)}, u32[]{:S(2)}, u32[]{:S(2)}) %collective-permute-start.13) | collective-permute-done | bytes 294944 | tf_op jit(solution)/shard_map/ppermute | solution.py:762
  52.5 3.6 %collective-permute-start.14 = (f32[96,768]{1,0:T(8,128)S(1)}, f32[96,768]{1,0:T(8,128)S(1)}, u32[]{:S(2)}, u32[]{:S(2)}) collective-permute-start(f32[96,768]{1,0:T(8,128)S(1)} %collective-permute-done.13.refs_6_), channel_id=1, source_target_pairs={{0,24},{8,16},{16,8},{24,0},{1,25},{9,17},{17,9},{25,1},{2,26},{10... | collective-permute-start | bytes 884744 | tf_op jit(solution)/shard_map/ppermute | solution.py:762
  56.1 6.1 %qkv.1 = (f32[768,192]{1,0:T(8,128)S(1)}, f32[768,384]{1,0:T(8,128)S(1)}, f32[384,384]{1,0:T(8,128)S(1)}, f32[768,768]{1,0:T(8,128)S(1)}, f32[16,768]{1,0:T(8,12...) custom-call(s32[1,100]{1,0:T(1,128)S(1)} %get-tuple-element.103.refs_0_, ...), custom_call_target="tpu_custom_call" | custom-call | flops 1 | bytes 1 | tf_op jit(solution)/shard_map/qkv/pallas_call | solution.py:52
  65.0 4.1 %collective-permute-done.15.refs_10_.refs_8_ = f32[96,768]{1,0:T(8,128)S(1)} collective-permute-done((f32[96,768]{1,0:T(8,128)S(1)}, f32[96,768]{1,0:T(8,128)S(1)}, u32[]{:S(2)}, u32[]{:S(2)}) %collective-permute-start.15) | collective-permute-done | bytes 294944 | tf_op jit(solution)/shard_map/ppermute | solution.py:762
  70.3 7.2 %attend_own.1 = (bf16[3,768,192]{2,1,0:T(8,128)(2,1)S(1)}, f32[3,3,1,256]{3,2,1,0:T(1,128)S(1)}, f32[3,3,1,256]{3,2,1,0:T(1,128)S(1)}, f32[3,3,128,256]{3,2,1,0:T(8,128)S(1)}) custom-call(s32[1,12]{1,0:T(1,128)S(1)} %get-tuple-element.109.refs_0_.refs_1_, f32[2,768]{1,0:T(2,128)S(1)} %get-tuple-element.110.refs_1_.refs_2_, ...), custom_call_target="tpu_custom_call" | custom-call | flops 1 | bytes 1 | tf_op jit(solution)/shard_map/attend_own/pallas_call | solution.py:52
  77.5 7.2 %collective-permute-done.16.refs_11_.refs_9_ = f32[96,768]{1,0:T(8,128)S(1)} collective-permute-done((f32[96,768]{1,0:T(8,128)S(1)}, f32[96,768]{1,0:T(8,128)S(1)}, u32[]{:S(2)}, u32[]{:S(2)}) %collective-permute-start.16) | collective-permute-done | bytes 294944 | tf_op jit(solution)/shard_map/ppermute | solution.py:762
  84.8 3.4 %attend_edge.1 = (f32[768,192]{1,0:T(8,128)S(1)}, f32[384,384]{1,0:T(8,128)S(1)}, f32[8,768]{1,0:T(8,128)S(1)}, f32[3,96,768]{2,1,0:T(8,128)S(1)}) custom-call(s32[1,12]{1,0:T(1,128)S(1)} %get-tuple-element.109.refs_0_.refs_1_, f32[2,768]{1,0:T(2,128)S(1)} %get-tuple-element.110.refs_1_.refs_2_, f32[2,384]{1,0:T(2,128)S(1)} %get-tuple-element.111.refs_2_.refs_3_, ...), custom_call_target="tpu_custom_call" | custom-call | flops 1 | bytes 1 | tf_op jit(solution)/shard_map/attend_edge/pallas_call | solution.py:52
  91.6 18.6 %collective-permute-done.25.refs_7_ = f32[3,96,768]{2,1,0:T(8,128)S(1)} collective-permute-done((f32[3,96,768]{2,1,0:T(8,128)S(1)}, f32[3,96,768]{2,1,0:T(8,128)S(1)}, u32[]{:S(2)}, u32[]{:S(2)}) %collective-permute-start.25) | collective-permute-done | bytes 884768 | tf_op jit(solution)/shard_map/ppermute | solution.py:762
  110.8 4.7 %act.1 = (bf16[768,768]{1,0:T(8,128)(2,1)S(1)}, bf16[768,768]{1,0:T(8,128)(2,1)S(1)}, bf16[768,768]{1,0:T(8,128)(2,1)S(1)}, bf16[768,768]{1,0:T(8,128)(2,1)S(1)}, f32[768,768]{1,0:T(8,128)S(1)}) custom-call(s32[1,100]{1,0:T(1,128)S(1)} %get-tuple-element.103.refs_0_, f32[192,768]{1,0:T(8,128)S(1)} %get-tuple-element.121.refs_1_, ...), custom_call_target="tpu_custom_call" | custom-call | flops 1 | bytes 1 | tf_op jit(solution)/shard_map/act/pallas_call | solution.py:52
  117.6 17.7 %feed.1 = (f32[2,192,768]{2,1,0:T(8,128)S(1)}, f32[2,192,768]{2,1,0:T(8,128)S(1)}, f32[2,192,768]{2,1,0:T(8,128)S(1)}, f32[192,128]{1,0:T(8,128)S(1)}, bf16[768,...) custom-call(s32[1,100]{1,0:T(1,128)S(1)} %get-tuple-element.103.refs, ...), custom_call_target="tpu_custom_call" | custom-call | flops 1 | bytes 1 | tf_op jit(solution)/shard_map/feed/pallas_call | solution.py:52
  139.1 11.4 %feed_grads.1 = (f32[2,192,768]{2,1,0:T(8,128)S(1)}, f32[2,192,768]{2,1,0:T(8,128)S(1)}, f32[4,96,768]{2,1,0:T(8,128)S(1)}, f32[4,96,768]{2,1,0:T(8,128)S(1)}, f...) custom-call(s32[1,100]{1,0:T(1,128)S(1)} %get-tuple-element.103.refs_0_, ...), custom_call_target="tpu_custom_call" | custom-call | flops 1 | bytes 1 | tf_op jit(solution)/shard_map/feed_grads/pallas_call | solution.py:52
  150.6 3.4 %collective-permute-done.32.refs_3_ = f32[192,768]{1,0:T(8,128)S(1)} collective-permute-done((f32[192,768]{1,0:T(8,128)S(1)}, f32[192,768]{1,0:T(8,128)S(1)}, u32[]{:S(2)}, u32[]{:S(2)}) %collective-permute-start.32) | collective-permute-done | bytes 589856 | tf_op jit(solution)/shard_map/ppermute | solution.py:762
  156.6 12.7 %collective-permute-done.34.refs_13_ = f32[192,768]{1,0:T(8,128)S(1)} collective-permute-done((f32[192,768]{1,0:T(8,128)S(1)}, f32[192,768]{1,0:T(8,128)S(1)}, u32[]{:S(2)}, u32[]{:S(2)}) %collective-permute-start.34) | collective-permute-done | bytes 589856 | tf_op jit(solution)/shard_map/ppermute | solution.py:762
  171.3 7.5 %back_edge.1 = (f32[384,384]{1,0:T(8,128)S(1)}, bf16[3,768,128]{2,1,0:T(8,128)(2,1)S(1)}, bf16[3,768,192]{2,1,0:T(8,128)(2,1)S(1)}, bf16[3,768,128]{2,1,0:T(8,12...) custom-call(s32[1,100]{1,0:T(1,128)S(1)} %get-tuple-element.103.refs, ...), custom_call_target="tpu_custom_call" | custom-call | flops 1 | bytes 1 | tf_op jit(solution)/shard_map/back_edge/pallas_call | solution.py:52
  186.0 12.2 %back_own.1 = (f32[768,192]{1,0:T(8,128)S(1)}, f32[768,384]{1,0:T(8,128)S(1)}) custom-call(s32[1,12]{1,0:T(1,128)S(1)} %get-tuple-element.109.refs_0_.refs_1_, f32[2,768]{1,0:T(2,128)S(1)} %get-tuple-element.110.refs_1_.refs_2_, f32[2,768]{1,0:T(2,128)S(1)} %get-tuple-element.110.refs_1_.refs_2_, f32[768,384]{1,0:T(8,128)S(1)} %get-tuple-element.114.refs_4_.refs_3_, ...), custom_call_target="tpu_custom_call" | custom-call | flops 1 | bytes 1 | tf_op jit(solution)/shard_map/back_own/pallas_call | solution.py:52
  198.3 10.4 %last_grads.1 = (f32[2,192,768]{2,1,0:T(8,128)S(1)}, f32[2,192,768]{2,1,0:T(8,128)S(1)}, f32[2,30,24,128]{3,2,1,0:T(8,128)S(1)}, f32[2,30,24,128]{3,2,1,0:T(8,12...) custom-call(s32[1,100]{1,0:T(1,128)S(1)} %get-tuple-element.103.refs_0_, ...), custom_call_target="tpu_custom_call" | custom-call | flops 1 | bytes 1 | tf_op jit(solution)/shard_map/last_grads/pallas_call | solution.py:52
  210.9 3.5 %collective-permute-start.46 = (f32[1,96,768]{2,1,0:T(8,128)S(1)}, f32[1,96,768]{2,1,0:T(8,128)S(1)}, u32[]{:S(2)}, u32[]{:S(2)}) collective-permute-start(f32[1,96,768]{2,1,0:T(8,128)S(1)} %get-tuple-element.178), channel_id=1, source_target_pairs={{0,24},{8,16},{16,8},{24,0},{1,25},{9,17},{17,9},{25,1},{2,26},{10... | collective-permute-start | bytes 884744 | tf_op jit(solution)/shard_map/ppermute | solution.py:762
  216.4 3.4 %collective-permute-done.49 = f32[4,24,768]{2,1,0:T(8,128)S(1)} collective-permute-done((f32[4,24,768]{2,1,0:T(8,128)S(1)}, f32[4,24,768]{2,1,0:T(8,128)S(1)}, u32[]{:S(2)}, u32[]{:S(2)}) %collective-permute-start.49) | collective-permute-done | bytes 294944 | tf_op jit(solution)/shard_map/ppermute | solution.py:762
  221.9 3.6 %collective-permute-start.47 = (f32[96,768]{1,0:T(8,128)S(1)}, f32[96,768]{1,0:T(8,128)S(1)}, u32[]{:S(2)}, u32[]{:S(2)}) collective-permute-start(f32[96,768]{1,0:T(8,128)S(1)} %add_bitcast_fusion.refs_1_), channel_id=1, source_target_pairs={{0,24},{8,16},{16,8},{24,0},{1,25},{9,17},{17,9},{25,1},{2,26},{10... | collective-permute-start | bytes 884744 | tf_op jit(solution)/shard_map/ppermute | solution.py:762
  227.6 8.0 %collective-permute-done.42 = f32[2,30,24,128]{3,2,1,0:T(8,128)S(1)} collective-permute-done((f32[2,30,24,128]{3,2,1,0:T(8,128)S(1)}, f32[2,30,24,128]{3,2,1,0:T(8,128)S(1)}, u32[]{:S(2)}, u32[]{:S(2)}) %collective-permute-start.42) | collective-permute-done | bytes 737312 | tf_op jit(solution)/shard_map/ppermute | solution.py:762
  239.0 11.0 %collective-permute-done.41 = f32[2,30,24,128]{3,2,1,0:T(8,128)S(1)} collective-permute-done((f32[2,30,24,128]{3,2,1,0:T(8,128)S(1)}, f32[2,30,24,128]{3,2,1,0:T(8,128)S(1)}, u32[]{:S(2)}, u32[]{:S(2)}) %collective-permute-start.41) | collective-permute-done | bytes 737312 | tf_op jit(solution)/shard_map/ppermute | solution.py:762
  250.0 3.6 %collective-permute-start.52 = (f32[4,24,768]{2,1,0:T(8,128)S(1)}, f32[4,24,768]{2,1,0:T(8,128)S(1)}, u32[]{:S(2)}, u32[]{:S(2)}) collective-permute-start(f32[4,24,768]{2,1,0:T(8,128)S(1)} %pad_maximum_fusion.refs_5_), channel_id=1, source_target_pairs={{0,24},{8,16},{16,8},{24,0},{1,25},{9,17},{17,9},{25,1},{2,26},{10... | collective-permute-start | bytes 884744 | tf_op jit(solution)/shard_map/ppermute | solution.py:762
  253.8 8.1 %collective-permute-done.52.refs_4_.refs_6_ = f32[4,24,768]{2,1,0:T(8,128)S(1)} collective-permute-done((f32[4,24,768]{2,1,0:T(8,128)S(1)}, f32[4,24,768]{2,1,0:T(8,128)S(1)}, u32[]{:S(2)}, u32[]{:S(2)}) %collective-permute-start.52) | collective-permute-done | bytes 294944 | tf_op jit(solution)/shard_map/ppermute | solution.py:762
  261.9 3.0 collective-permute-start.53
  268.9 6.4 %collective-permute-done.53 = f32[1,30,24,128]{3,2,1,0:T(8,128)S(1)} collective-permute-done((f32[1,30,24,128]{3,2,1,0:T(8,128)S(1)}, f32[1,30,24,128]{3,2,1,0:T(8,128)S(1)}, u32[]{:S(2)}, u32[]{:S(2)}) %collective-permute-start.53) | collective-permute-done | bytes 368672 | tf_op jit(solution)/shard_map/ppermute | solution.py:762
  277.4 3.6 %collective-permute-done.54.refs_1_ = f32[14,24,128]{2,1,0:T(8,128)S(1)} collective-permute-done((f32[14,24,128]{2,1,0:T(8,128)S(1)}, f32[14,24,128]{2,1,0:T(8,128)S(1)}, u32[]{:S(2)}, u32[]{:S(2)}) %collective-permute-start.54) | collective-permute-done | bytes 172064 | tf_op jit(solution)/shard_map/ppermute | solution.py:762
  287.0 7.3 %collective-permute-done.62.refs_8_ = f32[4,24,768]{2,1,0:T(8,128)S(1)} collective-permute-done((f32[4,24,768]{2,1,0:T(8,128)S(1)}, f32[4,24,768]{2,1,0:T(8,128)S(1)}, u32[]{:S(2)}, u32[]{:S(2)}) %collective-permute-start.62) | collective-permute-done | bytes 294944 | tf_op jit(solution)/shard_map/ppermute | solution.py:762
  300.9 5.7 %collective-permute-start.59 = (f32[26,24,128]{2,1,0:T(8,128)S(1)}, f32[26,24,128]{2,1,0:T(8,128)S(1)}, u32[]{:S(2)}, u32[]{:S(2)}) collective-permute-start(f32[26,24,128]{2,1,0:T(8,128)S(1)} %collective-permute-done.57.refs_2_), channel_id=1, source_target_pairs={{0,8},{8,0},{16,24},{24,16},{1,9},{9,1},{17,25},{25,17},{2,10},{10... | collective-permute-start | bytes 958472 | tf_op jit(solution)/shard_map/ppermute | solution.py:762
  307.9 6.5 %collective-permute-done.59.refs_4_ = f32[26,24,128]{2,1,0:T(8,128)S(1)} collective-permute-done((f32[26,24,128]{2,1,0:T(8,128)S(1)}, f32[26,24,128]{2,1,0:T(8,128)S(1)}, u32[]{:S(2)}, u32[]{:S(2)}) %collective-permute-start.59) | collective-permute-done | bytes 319520 | tf_op jit(solution)/shard_map/ppermute | solution.py:762
  (184 shorter events, 84.0 us)
Async XLA Ops:
  29.8 15.2 %collective-permute-start.3 = (f32[208,768]{1,0:T(8,128)S(1)}, f32[208,768]{1,0:T(8,128)S(1)}, u32[]{:S(2)}, u32[]{:S(2)}) collective-permute-start(f32[208,768]{1,0:T(8,128)S(1)} %base.1.refs_2_), channel_id=1, source_target_pairs={{0,1},{1,0},{2,3},{3,2},{4,5},{5,4},{6,7},{7,6},{8,9},{9,8},{10,11... | collective-permute-start | bytes 1916936 | tf_op jit(solution)/shard_map/ppermute | solution.py:762
  41.6 14.5 %collective-permute-start.5 = (f32[208,768]{1,0:T(8,128)S(1)}, f32[208,768]{1,0:T(8,128)S(1)}, u32[]{:S(2)}, u32[]{:S(2)}) collective-permute-start(f32[208,768]{1,0:T(8,128)S(1)} %collective-permute-done.4.refs_4_), channel_id=1, source_target_pairs={{0,1},{1,0},{2,3},{3,2},{4,5},{5,4},{6,7},{7,6},{8,9},{9,8},{10,11... | collective-permute-start | bytes 1916936 | tf_op jit(solution)/shard_map/ppermute | solution.py:762
  44.1 40.6 %collective-permute-start.12 = (f32[3,96,768]{2,1,0:T(8,128)S(1)}, f32[3,96,768]{2,1,0:T(8,128)S(1)}, u32[]{:S(2)}, u32[]{:S(2)}) collective-permute-start(f32[3,96,768]{2,1,0:T(8,128)S(1)} %get-tuple-element.119), channel_id=1, source_target_pairs={{0,2},{1,3},{2,0},{3,1},{4,6},{5,7},{6,4},{7,5},{8,10},{9,11},{10,... | collective-permute-start | bytes 2654216 | tf_op jit(solution)/shard_map/ppermute | solution.py:762
  45.0 39.7 %collective-permute-start.18 = (f32[3,96,768]{2,1,0:T(8,128)S(1)}, f32[3,96,768]{2,1,0:T(8,128)S(1)}, u32[]{:S(2)}, u32[]{:S(2)}) collective-permute-start(f32[3,96,768]{2,1,0:T(8,128)S(1)} %get-tuple-element.122.refs_1_), channel_id=1, source_target_pairs={{0,4},{4,0},{1,5},{5,1},{2,6},{6,2},{3,7},{7,3},{8,12},{12,8},{9,1... | collective-permute-start | bytes 2654216 | tf_op jit(solution)/shard_map/ppermute | solution.py:762
  62.2 22.5 %collective-permute-start.11 = (f32[384,384]{1,0:T(8,128)S(1)}, f32[384,384]{1,0:T(8,128)S(1)}, u32[]{:S(2)}, u32[]{:S(2)}) collective-permute-start(f32[384,384]{1,0:T(8,128)S(1)} %get-tuple-element.112), channel_id=1, source_target_pairs={{0,4},{4,0},{1,5},{5,1},{2,6},{6,2},{3,7},{7,3},{8,12},{12,8},{9,1... | collective-permute-start | bytes 1769480 | tf_op jit(solution)/shard_map/ppermute | solution.py:762
  64.3 20.4 %collective-permute-start.17 = (f32[192,768]{1,0:T(8,128)S(1)}, f32[192,768]{1,0:T(8,128)S(1)}, u32[]{:S(2)}, u32[]{:S(2)}) collective-permute-start(f32[192,768]{1,0:T(8,128)S(1)} %get-tuple-element.121.refs_1_), channel_id=1, source_target_pairs={{0,2},{1,3},{2,0},{3,1},{4,6},{5,7},{6,4},{7,5},{8,10},{9,11},{10,... | collective-permute-start | bytes 1769480 | tf_op jit(solution)/shard_map/ppermute | solution.py:762
  69.0 15.7 %collective-permute-start.16 = (f32[96,768]{1,0:T(8,128)S(1)}, f32[96,768]{1,0:T(8,128)S(1)}, u32[]{:S(2)}, u32[]{:S(2)}) collective-permute-start(f32[96,768]{1,0:T(8,128)S(1)} %collective-permute-done.13.refs_6_), channel_id=1, source_target_pairs={{0,16},{8,24},{16,0},{24,8},{1,17},{9,25},{17,1},{25,9},{2,18},{10... | collective-permute-start | bytes 884744 | tf_op jit(solution)/shard_map/ppermute | solution.py:762
  88.1 22.1 %collective-permute-start.25 = (f32[3,96,768]{2,1,0:T(8,128)S(1)}, f32[3,96,768]{2,1,0:T(8,128)S(1)}, u32[]{:S(2)}, u32[]{:S(2)}) collective-permute-start(f32[3,96,768]{2,1,0:T(8,128)S(1)} %get-tuple-element.124), channel_id=1, source_target_pairs={{0,4},{4,0},{1,5},{5,1},{2,6},{6,2},{3,7},{7,3},{8,12},{12,8},{9,1... | collective-permute-start | bytes 2654216 | tf_op jit(solution)/shard_map/ppermute | solution.py:762
  89.6 20.6 %collective-permute-start.20 = (f32[384,384]{1,0:T(8,128)S(1)}, f32[384,384]{1,0:T(8,128)S(1)}, u32[]{:S(2)}, u32[]{:S(2)}) collective-permute-start(f32[384,384]{1,0:T(8,128)S(1)} %get-tuple-element.123.refs_3_), channel_id=1, source_target_pairs={{0,2},{1,3},{2,0},{3,1},{4,6},{5,7},{6,4},{7,5},{8,10},{9,11},{10,... | collective-permute-start | bytes 1769480 | tf_op jit(solution)/shard_map/ppermute | solution.py:762
  90.5 20.3 %collective-permute-start.28 = (f32[192,768]{1,0:T(8,128)S(1)}, f32[192,768]{1,0:T(8,128)S(1)}, u32[]{:S(2)}, u32[]{:S(2)}) collective-permute-start(f32[192,768]{1,0:T(8,128)S(1)} %collective-permute-done.17.refs_12_.refs_3_), channel_id=1, source_target_pairs={{0,1},{1,0},{2,3},{3,2},{4,5},{5,4},{6,7},{7,6},{8,9},{9,8},{10,11... | collective-permute-start | bytes 1769480 | tf_op jit(solution)/shard_map/ppermute | solution.py:762
  90.5 25.0 %collective-permute-start.23 = (f32[3,96,768]{2,1,0:T(8,128)S(1)}, f32[3,96,768]{2,1,0:T(8,128)S(1)}, u32[]{:S(2)}, u32[]{:S(2)}) collective-permute-start(f32[3,96,768]{2,1,0:T(8,128)S(1)} %collective-permute-done.12.refs_8_.refs_3_), channel_id=1, source_target_pairs={{0,1},{1,0},{2,3},{3,2},{4,5},{5,4},{6,7},{7,6},{8,9},{9,8},{10,11... | collective-permute-start | bytes 2654216 | tf_op jit(solution)/shard_map/ppermute | solution.py:762
  91.4 24.2 %collective-permute-start.24 = (f32[3,96,768]{2,1,0:T(8,128)S(1)}, f32[3,96,768]{2,1,0:T(8,128)S(1)}, u32[]{:S(2)}, u32[]{:S(2)}) collective-permute-start(f32[3,96,768]{2,1,0:T(8,128)S(1)} %collective-permute-done.18.refs_13_.refs_5_), channel_id=1, source_target_pairs={{0,1},{1,0},{2,3},{3,2},{4,5},{5,4},{6,7},{7,6},{8,9},{9,8},{10,11... | collective-permute-start | bytes 2654216 | tf_op jit(solution)/shard_map/ppermute | solution.py:762
  138.4 15.7 %collective-permute-start.32 = (f32[192,768]{1,0:T(8,128)S(1)}, f32[192,768]{1,0:T(8,128)S(1)}, u32[]{:S(2)}, u32[]{:S(2)}) collective-permute-start(f32[192,768]{1,0:T(8,128)S(1)} %fusion.4.refs_11_), channel_id=1, source_target_pairs={{0,2},{1,3},{2,0},{3,1},{4,6},{5,7},{6,4},{7,5},{8,10},{9,11},{10,... | collective-permute-start | bytes 1769480 | tf_op jit(solution)/shard_map/ppermute | solution.py:762
  150.5 18.8 %collective-permute-start.30 = (f32[2,192,768]{2,1,0:T(8,128)S(1)}, f32[2,192,768]{2,1,0:T(8,128)S(1)}, u32[]{:S(2)}, u32[]{:S(2)}) collective-permute-start(f32[2,192,768]{2,1,0:T(8,128)S(1)} %get-tuple-element.144), channel_id=1, source_target_pairs={{0,1},{1,0},{2,3},{3,2},{4,5},{5,4},{6,7},{7,6},{8,9},{9,8},{10,11... | collective-permute-start | bytes 3538952 | tf_op jit(solution)/shard_map/ppermute | solution.py:762
  154.5 14.9 %collective-permute-start.34 = (f32[192,768]{1,0:T(8,128)S(1)}, f32[192,768]{1,0:T(8,128)S(1)}, u32[]{:S(2)}, u32[]{:S(2)}) collective-permute-start(f32[192,768]{1,0:T(8,128)S(1)} %get-tuple-element.148.refs_11_.refs_6_), channel_id=1, source_target_pairs={{0,2},{1,3},{2,0},{3,1},{4,6},{5,7},{6,4},{7,5},{8,10},{9,11},{10,... | collective-permute-start | bytes 1769480 | tf_op jit(solution)/shard_map/ppermute | solution.py:762
  155.2 27.7 %collective-permute-start.36 = (f32[4,96,768]{2,1,0:T(8,128)S(1)}, f32[4,96,768]{2,1,0:T(8,128)S(1)}, u32[]{:S(2)}, u32[]{:S(2)}) collective-permute-start(f32[4,96,768]{2,1,0:T(8,128)S(1)} %get-tuple-element.156), channel_id=1, source_target_pairs={{0,4},{4,0},{1,5},{5,1},{2,6},{6,2},{3,7},{7,3},{8,12},{12,8},{9,1... | collective-permute-start | bytes 3538952 | tf_op jit(solution)/shard_map/ppermute | solution.py:762
  156.6 26.9 %collective-permute-start.37 = (f32[16,24,768]{2,1,0:T(8,128)S(1)}, f32[16,24,768]{2,1,0:T(8,128)S(1)}, u32[]{:S(2)}, u32[]{:S(2)}) collective-permute-start(f32[16,24,768]{2,1,0:T(8,128)S(1)} %get-tuple-element.157), channel_id=1, source_target_pairs={{0,8},{8,0},{16,24},{24,16},{1,9},{9,1},{17,25},{25,17},{2,10},{10... | collective-permute-start | bytes 3538952 | tf_op jit(solution)/shard_map/ppermute | solution.py:762
  169.4 28.9 %collective-permute-start.31 = (f32[192,768]{1,0:T(8,128)S(1)}, f32[192,768]{1,0:T(8,128)S(1)}, u32[]{:S(2)}, u32[]{:S(2)}) collective-permute-start(f32[192,768]{1,0:T(8,128)S(1)} %fusion.1), channel_id=1, source_target_pairs={{0,2},{1,3},{2,0},{3,1},{4,6},{5,7},{6,4},{7,5},{8,10},{9,11},{10,... | collective-permute-start | bytes 1769480 | tf_op jit(solution)/shard_map/ppermute | solution.py:762
  178.9 19.4 %collective-permute-start.38 = (f32[384,384]{1,0:T(8,128)S(1)}, f32[384,384]{1,0:T(8,128)S(1)}, u32[]{:S(2)}, u32[]{:S(2)}) collective-permute-start(f32[384,384]{1,0:T(8,128)S(1)} %get-tuple-element.158.refs_4_), channel_id=1, source_target_pairs={{0,4},{4,0},{1,5},{5,1},{2,6},{6,2},{3,7},{7,3},{8,12},{12,8},{9,1... | collective-permute-start | bytes 1769480 | tf_op jit(solution)/shard_map/ppermute | solution.py:762
  183.7 25.0 %collective-permute-start.44 = (f32[2,96,768]{2,1,0:T(8,128)S(1)}, f32[2,96,768]{2,1,0:T(8,128)S(1)}, u32[]{:S(2)}, u32[]{:S(2)}) collective-permute-start(f32[2,96,768]{2,1,0:T(8,128)S(1)} %get-tuple-element.175), channel_id=1, source_target_pairs={{0,8},{8,0},{16,24},{24,16},{1,9},{9,1},{17,25},{25,17},{2,10},{10... | collective-permute-start | bytes 1769480 | tf_op jit(solution)/shard_map/ppermute | solution.py:762
  184.1 26.0 %collective-permute-start.45 = (f32[8,24,768]{2,1,0:T(8,128)S(1)}, f32[8,24,768]{2,1,0:T(8,128)S(1)}, u32[]{:S(2)}, u32[]{:S(2)}) collective-permute-start(f32[8,24,768]{2,1,0:T(8,128)S(1)} %get-tuple-element.176), channel_id=1, source_target_pairs={{0,24},{8,16},{16,8},{24,0},{1,25},{9,17},{17,9},{25,1},{2,26},{10... | collective-permute-start | bytes 1769480 | tf_op jit(solution)/shard_map/ppermute | solution.py:762
  208.7 27.1 %collective-permute-start.39 = (f32[2,192,768]{2,1,0:T(8,128)S(1)}, f32[2,192,768]{2,1,0:T(8,128)S(1)}, u32[]{:S(2)}, u32[]{:S(2)}) collective-permute-start(f32[2,192,768]{2,1,0:T(8,128)S(1)} %get-tuple-element.169), channel_id=1, source_target_pairs={{0,1},{1,0},{2,3},{3,2},{4,5},{5,4},{6,7},{7,6},{8,9},{9,8},{10,11... | collective-permute-start | bytes 3538952 | tf_op jit(solution)/shard_map/ppermute | solution.py:762
  214.4 21.2 %collective-permute-start.42 = (f32[2,30,24,128]{3,2,1,0:T(8,128)S(1)}, f32[2,30,24,128]{3,2,1,0:T(8,128)S(1)}, u32[]{:S(2)}, u32[]{:S(2)}) collective-permute-start(f32[2,30,24,128]{3,2,1,0:T(8,128)S(1)} %get-tuple-element.173), channel_id=1, source_target_pairs={{0,4},{4,0},{1,5},{5,1},{2,6},{6,2},{3,7},{7,3},{8,12},{12,8},{9,1... | collective-permute-start | bytes 2211848 | tf_op jit(solution)/shard_map/ppermute | solution.py:762
  214.5 35.5 %collective-permute-start.41 = (f32[2,30,24,128]{3,2,1,0:T(8,128)S(1)}, f32[2,30,24,128]{3,2,1,0:T(8,128)S(1)}, u32[]{:S(2)}, u32[]{:S(2)}) collective-permute-start(f32[2,30,24,128]{3,2,1,0:T(8,128)S(1)} %get-tuple-element.171), channel_id=1, source_target_pairs={{0,4},{4,0},{1,5},{5,1},{2,6},{6,2},{3,7},{7,3},{8,12},{12,8},{9,1... | collective-permute-start | bytes 2211848 | tf_op jit(solution)/shard_map/ppermute | solution.py:762
  221.9 31.8 %collective-permute-start.47 = (f32[96,768]{1,0:T(8,128)S(1)}, f32[96,768]{1,0:T(8,128)S(1)}, u32[]{:S(2)}, u32[]{:S(2)}) collective-permute-start(f32[96,768]{1,0:T(8,128)S(1)} %add_bitcast_fusion.refs_1_), channel_id=1, source_target_pairs={{0,24},{8,16},{16,8},{24,0},{1,25},{9,17},{17,9},{25,1},{2,26},{10... | collective-permute-start | bytes 884744 | tf_op jit(solution)/shard_map/ppermute | solution.py:762
  225.5 28.2 %collective-permute-start.48 = (f32[96,768]{1,0:T(8,128)S(1)}, f32[96,768]{1,0:T(8,128)S(1)}, u32[]{:S(2)}, u32[]{:S(2)}) collective-permute-start(f32[96,768]{1,0:T(8,128)S(1)} %add_bitcast_fusion.refs_1_), channel_id=1, source_target_pairs={{0,8},{8,0},{16,24},{24,16},{1,9},{9,1},{17,25},{25,17},{2,10},{10... | collective-permute-start | bytes 884744 | tf_op jit(solution)/shard_map/ppermute | solution.py:762
  235.7 26.1 %collective-permute-start.43 = (f32[2,30,24,128]{3,2,1,0:T(8,128)S(1)}, f32[2,30,24,128]{3,2,1,0:T(8,128)S(1)}, u32[]{:S(2)}, u32[]{:S(2)}) collective-permute-start(f32[2,30,24,128]{3,2,1,0:T(8,128)S(1)} %add.440), channel_id=1, source_target_pairs={{0,8},{8,0},{16,24},{24,16},{1,9},{9,1},{17,25},{25,17},{2,10},{10... | collective-permute-start | bytes 2211848 | tf_op jit(solution)/shard_map/ppermute | solution.py:762
  237.7 24.1 %collective-permute-start.40 = (f32[192,768]{1,0:T(8,128)S(1)}, f32[192,768]{1,0:T(8,128)S(1)}, u32[]{:S(2)}, u32[]{:S(2)}) collective-permute-start(f32[192,768]{1,0:T(8,128)S(1)} %fusion), channel_id=1, source_target_pairs={{0,2},{1,3},{2,0},{3,1},{4,6},{5,7},{6,4},{7,5},{8,10},{9,11},{10,... | collective-permute-start | bytes 1769480 | tf_op jit(solution)/shard_map/ppermute | solution.py:762
  265.0 21.4 %collective-permute-start.61 = (f32[4,24,768]{2,1,0:T(8,128)S(1)}, f32[4,24,768]{2,1,0:T(8,128)S(1)}, u32[]{:S(2)}, u32[]{:S(2)}) collective-permute-start(f32[4,24,768]{2,1,0:T(8,128)S(1)} %pad_maximum_fusion.refs_5_), channel_id=1, source_target_pairs={{0,8},{8,0},{16,24},{24,16},{1,9},{9,1},{17,25},{25,17},{2,10},{10... | collective-permute-start | bytes 884744 | tf_op jit(solution)/shard_map/ppermute | solution.py:762
  266.9 20.1 %collective-permute-start.60 = (f32[96,768]{1,0:T(8,128)S(1)}, f32[96,768]{1,0:T(8,128)S(1)}, u32[]{:S(2)}, u32[]{:S(2)}) collective-permute-start(f32[96,768]{1,0:T(8,128)S(1)} %collective-permute-done.47.refs_2_), channel_id=1, source_target_pairs={{0,8},{8,0},{16,24},{24,16},{1,9},{9,1},{17,25},{25,17},{2,10},{10... | collective-permute-start | bytes 884744 | tf_op jit(solution)/shard_map/ppermute | solution.py:762
  267.1 27.2 %collective-permute-start.62 = (f32[4,24,768]{2,1,0:T(8,128)S(1)}, f32[4,24,768]{2,1,0:T(8,128)S(1)}, u32[]{:S(2)}, u32[]{:S(2)}) collective-permute-start(f32[4,24,768]{2,1,0:T(8,128)S(1)} %collective-permute-done.52.refs_4_.refs_6_), channel_id=1, source_target_pairs={{0,8},{8,0},{16,24},{24,16},{1,9},{9,1},{17,25},{25,17},{2,10},{10... | collective-permute-start | bytes 884744 | tf_op jit(solution)/shard_map/ppermute | solution.py:762
  282.6 18.3 %collective-permute-start.57 = (f32[26,24,128]{2,1,0:T(8,128)S(1)}, f32[26,24,128]{2,1,0:T(8,128)S(1)}, u32[]{:S(2)}, u32[]{:S(2)}) collective-permute-start(f32[26,24,128]{2,1,0:T(8,128)S(1)} %constant_dynamic-update-slice_fusion.refs_1_), channel_id=1, source_target_pairs={{0,24},{8,16},{16,8},{24,0},{1,25},{9,17},{17,9},{25,1},{2,26},{10... | collective-permute-start | bytes 958472 | tf_op jit(solution)/shard_map/ppermute | solution.py:762
  (40 other events, 424.0 us)
